TPU v7x, 32 devices: a whole 2x2x4 slice. The times are simulated.
32 devices in a mesh: loop: 2 (over x), fsdp: 16 (over z, y, core).
Axes of the slice: x: 2, y: 2, z: 4, core: 2. Of those that a mesh axis runs over, the one named last changes fastest.
Arguments:
- hidden_input: bfloat16 [2, 2048, 2048], P('loop', 'fsdp'), may hold values from -6 to 6
- sequence_lengths: int32 [2, 4], P('loop'), may hold values from 1 to 1024, 2048 in all within a row
- norm_gain_values: bfloat16 [2, 2048], replicated, may hold values from 0.5 to 1.5
- input_proj_weight: bfloat16 [2048, 2560], P('fsdp'), may hold values from -0.125 to 0.125
- output_proj_weight: bfloat16 [2048, 2048], P('fsdp'), may hold values from -2 to 2
- feedforward_weight: bfloat16 [16384, 3, 2048], P('fsdp'), may hold values from -0.09375 to 0.09375
- adapter_first: bfloat16 [2, 2048, 1536], P('loop'), may hold values from -0.125 to 0.125
- adapter_second: bfloat16 [2, 256, 39424], P('loop'), may hold values from -0.1875 to 0.1875
- adapter_down_first: bfloat16 [2, 16384, 256], P('loop'), may hold values from -0.046875 to 0.046875
- output_gradient: bfloat16 [2, 2048, 2048], P('loop', 'fsdp'), may hold values from -6 to 6
Outputs:
- hidden_out: bfloat16 [2, 2048, 2048], P('loop', 'fsdp')
- hidden_grad: float32 [2, 2048, 2048], P('loop', 'fsdp')
- norm_gain_grad: float32 [2, 2048], P(None, 'fsdp')
- attn_in_grad: float32 [2048, 2560], P('fsdp')
- attn_out_grad: float32 [2048, 2048], P('fsdp')
- ffn_grad: float32 [16384, 3, 2048], P('fsdp')
- lora_a_grad: float32 [2, 2048, 1536], P('loop', 'fsdp')
- lora_b_grad: float32 [2, 256, 39424], P('loop', None, 'fsdp')
- lora_down_grad: float32 [2, 16384, 256], P('loop', 'fsdp')
Inputs may be any that keep to these rules, and one draw needn't show every extreme that they name: `sequence_lengths`: row l holds the lengths of the 4 sequences packed in order into loop group l's 2048 rows; they sum to 2048 and the longest has exactly 1024 tokens.
All inputs are finite; a program needn't handle non-finite values.
Results may differ from a plain program's by a relative error of at most 0.017.
Values may be sent and summed in bfloat16 or wider, within the bound.
A program may use at most 1.5625 GiB of HBM per device.

v0:
```python
import math

import jax
import jax.numpy as jnp
from jax import lax
from jax.sharding import PartitionSpec as P

MODEL_WIDTH = 2048
HEADS = 8
HEAD_WIDTH = 256
HIDDEN_COUNT = 16384
ADAPTER_RANK = 256
QUERY_WIDTH = 2048
PROJECT_COLUMNS = 2560


epsilon = 1e-06


def matrix_product(former, latter):
    return jnp.dot(former, latter, preferred_element_type=jnp.float32)


def times_transposed(former, latter):
    return lax.dot_general(
        former, latter, (((1,), (1,)), ((), ())), preferred_element_type=jnp.float32
    )


def outer_product_rows(former, latter):
    return lax.dot_general(
        former, latter, (((0,), (0,)), ((), ())), preferred_element_type=jnp.float32
    )


def segment_info(lengths, row_count):
    row_ids = jnp.arange(row_count, dtype=jnp.int32)
    finish = jnp.cumsum(lengths)
    starts = finish - lengths
    segment = jnp.sum((row_ids[:, None] >= finish[None, :]).astype(jnp.int32), axis=1)
    labels = jnp.arange(lengths.shape[0], dtype=jnp.int32)
    opening = jnp.sum(jnp.where(segment[:, None] == labels[None, :], starts[None, :], 0), axis=1)
    return (segment, row_ids - opening)


def rotate(values, position, direction):
    half_dim = HEAD_WIDTH // 2
    frequency = jnp.exp(
        jnp.arange(half_dim).astype(jnp.float32) * (-2.0 * math.log(10000.0) / HEAD_WIDTH)
    )
    angles = position.astype(jnp.float32)[:, None] * frequency[None, :]
    cosine = jnp.cos(angles)[:, None, :]
    sine_val = direction * jnp.sin(angles)[:, None, :]
    shaped = values.reshape(values.shape[0], -1, HEAD_WIDTH)
    former = shaped[..., :half_dim]
    latter = shaped[..., half_dim:]
    turned = jnp.concatenate(
        [former * cosine - latter * sine_val, latter * cosine + former * sine_val], axis=-1
    )
    return turned.reshape(values.shape)


def rms_scale(values):
    return lax.rsqrt(jnp.mean(values * values, axis=-1, keepdims=True) + epsilon)


def gelu_tanh(values):
    return jax.nn.gelu(values, approximate=True)


def unit_backward(gate_value, upward_activation, hidden_unit_gradient):
    activated, pullback_function = jax.vjp(gelu_tanh, gate_value)
    gate_grad = pullback_function(hidden_unit_gradient * upward_activation)[0]
    return (gate_grad.astype(jnp.bfloat16), (hidden_unit_gradient * activated).astype(jnp.bfloat16))


def scores_of(query_heads, key_rows, allowed, scaling):
    product = (
        jnp.einsum("thd,ud->thu", query_heads, key_rows, preferred_element_type=jnp.float32)
        * scaling
    )
    return jnp.where(allowed[:, None, :], product, -1e30)


def per_device(
    hidden_input,
    sequence_lengths,
    norm_gain_values,
    input_proj_weight,
    output_proj_weight,
    feedforward_weight,
    adapter_first,
    adapter_second,
    adapter_down_first,
    output_gradient,
):
    tokens_dev = hidden_input.shape[1]
    all_rows = tokens_dev * lax.axis_size("fsdp")
    offset = lax.axis_index("fsdp") * tokens_dev
    segment_all, position_all = segment_info(sequence_lengths[0], all_rows)
    segment_own = lax.dynamic_slice_in_dim(segment_all, offset, tokens_dev)
    position_own = lax.dynamic_slice_in_dim(position_all, offset, tokens_dev)
    row_all = jnp.arange(all_rows, dtype=jnp.int32)
    row_own = offset + jnp.arange(tokens_dev, dtype=jnp.int32)
    allowed = (segment_own[:, None] == segment_all[None, :]) & (
        row_own[:, None] >= row_all[None, :]
    )
    norm_gain_pair = norm_gain_values.astype(jnp.float32)
    first_factor = adapter_first[0]
    second_factor = adapter_second[0]
    narrow_down = adapter_down_first[0]
    narrow_projection = first_factor[:, : 3 * ADAPTER_RANK]
    narrow_output = first_factor[:, 3 * ADAPTER_RANK : 4 * ADAPTER_RANK]
    narrow_feedforward = first_factor[:, 4 * ADAPTER_RANK :]
    squeeze_gate = first_factor[:, 4 * ADAPTER_RANK : 5 * ADAPTER_RANK]
    squeeze_up = first_factor[:, 5 * ADAPTER_RANK :]
    gate_column_start = PROJECT_COLUMNS + MODEL_WIDTH
    widen_query = second_factor[:, :QUERY_WIDTH]
    widen_key = second_factor[:, QUERY_WIDTH : QUERY_WIDTH + HEAD_WIDTH]
    widen_value = second_factor[:, QUERY_WIDTH + HEAD_WIDTH : PROJECT_COLUMNS]
    widen_output = second_factor[:, PROJECT_COLUMNS : PROJECT_COLUMNS + MODEL_WIDTH]
    expand_gate = second_factor[:, gate_column_start : gate_column_start + HIDDEN_COUNT]
    expand_up = second_factor[
        :, gate_column_start + HIDDEN_COUNT : gate_column_start + 2 * HIDDEN_COUNT
    ]
    widen_down = second_factor[:, gate_column_start + 2 * HIDDEN_COUNT :]
    scaling = HEAD_WIDTH ** (-0.5)
    hidden_state = hidden_input[0].astype(jnp.float32)
    scale_one = rms_scale(hidden_state)
    normalized = (hidden_state * scale_one * norm_gain_pair[0]).astype(jnp.bfloat16)
    attn_in_all, output_proj_every = (
        lax.all_gather(input_proj_weight, "fsdp", axis=0, tiled=True),
        lax.all_gather(output_proj_weight, "fsdp", axis=0, tiled=True),
    )
    adapter_projection = matrix_product(normalized, narrow_projection).astype(jnp.bfloat16)
    projected_rows = matrix_product(normalized, attn_in_all)
    query_unrotated = projected_rows[:, :QUERY_WIDTH] + matrix_product(
        adapter_projection[:, :ADAPTER_RANK], widen_query
    )
    key_unrotated = projected_rows[:, QUERY_WIDTH : QUERY_WIDTH + HEAD_WIDTH] + matrix_product(
        adapter_projection[:, ADAPTER_RANK : 2 * ADAPTER_RANK], widen_key
    )
    value_local = (
        projected_rows[:, QUERY_WIDTH + HEAD_WIDTH :]
        + matrix_product(adapter_projection[:, 2 * ADAPTER_RANK :], widen_value)
    ).astype(jnp.bfloat16)
    query_rot = rotate(query_unrotated, position_own, 1.0).astype(jnp.bfloat16)
    key_rot = rotate(key_unrotated, position_own, 1.0).astype(jnp.bfloat16)
    keys_own = jnp.concatenate([key_rot, value_local], axis=1)
    keys_all = lax.all_gather(keys_own, "fsdp", axis=0, tiled=True)
    query_heads = query_rot.reshape(tokens_dev, HEADS, HEAD_WIDTH)
    scores = scores_of(query_heads, keys_all[:, :HEAD_WIDTH], allowed, scaling)
    row_max = jnp.max(scores, axis=-1, keepdims=True)
    powered = jnp.exp(scores - row_max)
    row_sum = jnp.sum(powered, axis=-1, keepdims=True)
    weights = powered / row_sum
    log_total = row_max + jnp.log(row_sum)
    attention_output = jnp.einsum(
        "thu,ud->thd",
        weights.astype(jnp.bfloat16),
        keys_all[:, HEAD_WIDTH:],
        preferred_element_type=jnp.float32,
    )
    attention_output = attention_output.reshape(tokens_dev, QUERY_WIDTH).astype(jnp.bfloat16)
    adapter_output = matrix_product(attention_output, narrow_output).astype(jnp.bfloat16)
    middle_state = (
        hidden_state
        + times_transposed(attention_output, output_proj_every)
        + matrix_product(adapter_output, widen_output)
    )
    scale_two = rms_scale(middle_state)
    normalized_second = (middle_state * scale_two * norm_gain_pair[1]).astype(jnp.bfloat16)
    adapter_feedforward = matrix_product(normalized_second, narrow_feedforward).astype(jnp.bfloat16)
    adapter_gate = adapter_feedforward[:, :ADAPTER_RANK]
    adapter_upward = adapter_feedforward[:, ADAPTER_RANK:]
    weight_row_block = lax.all_gather(feedforward_weight, "fsdp", axis=0, tiled=True)
    gate_columns = expand_gate
    up_columns = expand_up
    down_portion = narrow_down
    gate_portion = times_transposed(normalized_second, weight_row_block[:, 0, :]) + matrix_product(
        adapter_gate, gate_columns
    )
    up_portion = times_transposed(normalized_second, weight_row_block[:, 1, :]) + matrix_product(
        adapter_upward, up_columns
    )
    unit_part = (gelu_tanh(gate_portion) * up_portion).astype(jnp.bfloat16)
    output_sum = matrix_product(unit_part, weight_row_block[:, 2, :])
    down_total_sum = matrix_product(unit_part, down_portion)
    gate_keep = gate_portion
    up_keep = up_portion
    feedforward_main, down_total_sum, gate_value, upward_activation, hidden_unit_values = (
        output_sum,
        down_total_sum,
        gate_keep,
        up_keep,
        unit_part,
    )
    adapter_hidden = down_total_sum.astype(jnp.bfloat16)
    result_value = middle_state + feedforward_main + matrix_product(adapter_hidden, widen_down)
    hidden_out = result_value.astype(jnp.bfloat16)[None]
    feedforward_cotangent = output_gradient[0]
    grad_out = feedforward_cotangent.astype(jnp.float32)
    adapter_hidden_gradient = times_transposed(feedforward_cotangent, widen_down).astype(
        jnp.bfloat16
    )
    weight_row_block = lax.all_gather(feedforward_weight, "fsdp", axis=0, tiled=True)
    gate_columns = expand_gate
    up_columns = expand_up
    down_portion = narrow_down
    gate_portion = gate_value
    up_portion = upward_activation
    hidden_unit_gradient = times_transposed(
        feedforward_cotangent, weight_row_block[:, 2, :]
    ) + times_transposed(adapter_hidden_gradient, down_portion)
    gate_grad, up_grad = unit_backward(gate_portion, up_portion, hidden_unit_gradient)
    normed_sum = matrix_product(gate_grad, weight_row_block[:, 0, :]) + matrix_product(
        up_grad, weight_row_block[:, 1, :]
    )
    gate_sum = times_transposed(gate_grad, gate_columns)
    up_sum = times_transposed(up_grad, up_columns)
    normed_two_grad, gate_sum, up_sum, gate_gradients, up_gradients = (
        normed_sum,
        gate_sum,
        up_sum,
        gate_grad,
        up_grad,
    )
    ffn_grad_own = lax.psum_scatter(
        jnp.stack(
            [
                outer_product_rows(gate_gradients, normalized_second),
                outer_product_rows(up_gradients, normalized_second),
                outer_product_rows(hidden_unit_values, feedforward_cotangent),
            ],
            axis=1,
        ),
        "fsdp",
        scatter_dimension=0,
        tiled=True,
    )
    widen_gate_piece = outer_product_rows(adapter_gate, gate_gradients)
    widen_up_piece = outer_product_rows(adapter_upward, up_gradients)
    narrow_down_piece = outer_product_rows(hidden_unit_values, adapter_hidden_gradient)
    gate_low = gate_sum.astype(jnp.bfloat16)
    up_low = up_sum.astype(jnp.bfloat16)
    normed_two_grad = (
        normed_two_grad
        + times_transposed(gate_low, squeeze_gate)
        + times_transposed(up_low, squeeze_up)
    )
    weighted_two = norm_gain_pair[1] * normed_two_grad
    middle_grad = (
        grad_out
        + scale_two * weighted_two
        - middle_state
        * scale_two**3
        * jnp.mean(middle_state * weighted_two, axis=-1, keepdims=True)
    )
    gain_two_term = jnp.sum(normed_two_grad * middle_state * scale_two, axis=0)
    input_proj_backward, output_proj_backward, keys_back = (
        lax.all_gather(input_proj_weight, "fsdp", axis=0, tiled=True),
        lax.all_gather(output_proj_weight, "fsdp", axis=0, tiled=True),
        lax.all_gather(keys_own, "fsdp", axis=0, tiled=True),
    )
    residual_branch_gradient = middle_grad.astype(jnp.bfloat16)
    adapter_output_gradient = times_transposed(residual_branch_gradient, widen_output).astype(
        jnp.bfloat16
    )
    attended_grad = (
        matrix_product(residual_branch_gradient, output_proj_backward)
        + times_transposed(adapter_output_gradient, narrow_output)
    ).astype(jnp.bfloat16)
    scores_back = scores_of(query_heads, keys_back[:, :HEAD_WIDTH], allowed, scaling)
    probs_back = jnp.exp(scores_back - log_total)
    heads_grad = attended_grad.reshape(tokens_dev, HEADS, HEAD_WIDTH)
    prob_grad = jnp.einsum(
        "thd,ud->thu", heads_grad, keys_back[:, HEAD_WIDTH:], preferred_element_type=jnp.float32
    )
    row_dot = jnp.sum(probs_back * prob_grad, axis=-1, keepdims=True)
    score_grad = (probs_back * (prob_grad - row_dot)).astype(jnp.bfloat16)
    query_rot_grad = (
        jnp.einsum(
            "thu,ud->thd", score_grad, keys_back[:, :HEAD_WIDTH], preferred_element_type=jnp.float32
        )
        * scaling
    )
    key_part = (
        jnp.einsum("thu,thd->ud", score_grad, query_heads, preferred_element_type=jnp.float32)
        * scaling
    )
    value_part = jnp.einsum(
        "thu,thd->ud",
        probs_back.astype(jnp.bfloat16),
        heads_grad,
        preferred_element_type=jnp.float32,
    )
    pair_grad = lax.psum_scatter(
        jnp.concatenate([key_part, value_part], axis=1), "fsdp", scatter_dimension=0, tiled=True
    )
    query_gradient = rotate(
        query_rot_grad.reshape(tokens_dev, QUERY_WIDTH), position_own, -1.0
    ).astype(jnp.bfloat16)
    key_gradient = rotate(pair_grad[:, :HEAD_WIDTH], position_own, -1.0).astype(jnp.bfloat16)
    value_gradient = pair_grad[:, HEAD_WIDTH:].astype(jnp.bfloat16)
    projection_gradient = jnp.concatenate([query_gradient, key_gradient, value_gradient], axis=1)
    adapter_projection_gradient = jnp.concatenate(
        [
            times_transposed(query_gradient, widen_query),
            times_transposed(key_gradient, widen_key),
            times_transposed(value_gradient, widen_value),
        ],
        axis=1,
    ).astype(jnp.bfloat16)
    normalized_gradient = times_transposed(
        projection_gradient, input_proj_backward
    ) + times_transposed(adapter_projection_gradient, narrow_projection)
    weighted_one = norm_gain_pair[0] * normalized_gradient
    input_grad = (
        middle_grad
        + scale_one * weighted_one
        - hidden_state
        * scale_one**3
        * jnp.mean(hidden_state * weighted_one, axis=-1, keepdims=True)
    )
    gain_one_term = jnp.sum(normalized_gradient * hidden_state * scale_one, axis=0)
    projection_own = lax.psum_scatter(
        jnp.concatenate(
            [
                outer_product_rows(normalized, projection_gradient),
                outer_product_rows(residual_branch_gradient, attention_output),
            ],
            axis=1,
        ),
        "fsdp",
        scatter_dimension=0,
        tiled=True,
    )
    squeeze_term = jnp.concatenate(
        [
            outer_product_rows(normalized, adapter_projection_gradient),
            outer_product_rows(attention_output, adapter_output_gradient),
            outer_product_rows(normalized_second, gate_low),
            outer_product_rows(normalized_second, up_low),
        ],
        axis=1,
    )
    gain_term = jnp.stack([gain_one_term, gain_two_term])
    expand_term = jnp.concatenate(
        [
            outer_product_rows(adapter_projection[:, :ADAPTER_RANK], query_gradient),
            outer_product_rows(
                adapter_projection[:, ADAPTER_RANK : 2 * ADAPTER_RANK], key_gradient
            ),
            outer_product_rows(adapter_projection[:, 2 * ADAPTER_RANK :], value_gradient),
            outer_product_rows(adapter_output, residual_branch_gradient),
            widen_gate_piece,
            widen_up_piece,
            outer_product_rows(adapter_hidden, feedforward_cotangent),
        ],
        axis=1,
    )
    squeeze_own, expand_own, down_own, gain_own = (
        lax.psum_scatter(squeeze_term, "fsdp", scatter_dimension=0, tiled=True),
        lax.psum_scatter(expand_term, "fsdp", scatter_dimension=1, tiled=True),
        lax.psum_scatter(narrow_down_piece, "fsdp", scatter_dimension=0, tiled=True),
        lax.psum_scatter(gain_term, "fsdp", scatter_dimension=1, tiled=True),
    )
    projection_sum, ffn_sum, gain_sum = (
        lax.psum(projection_own.astype(jnp.bfloat16), "loop").astype(jnp.float32),
        lax.psum(ffn_grad_own.astype(jnp.bfloat16), "loop").astype(jnp.float32),
        lax.psum(gain_own.astype(jnp.bfloat16), "loop").astype(jnp.float32),
    )
    return (
        hidden_out,
        input_grad[None],
        gain_sum,
        projection_sum[:, :PROJECT_COLUMNS],
        projection_sum[:, PROJECT_COLUMNS:],
        ffn_sum,
        squeeze_own[None],
        expand_own[None],
        down_own[None],
    )


def solution(mesh):
    return jax.shard_map(
        per_device,
        mesh=mesh,
        in_specs=(
            P("loop", "fsdp", None),
            P("loop", None),
            P(),
            P("fsdp", None),
            P("fsdp", None),
            P("fsdp", None, None),
            P("loop", None, None),
            P("loop", None, None),
            P("loop", None, None),
            P("loop", "fsdp", None),
        ),
        out_specs=(
            P("loop", "fsdp", None),
            P("loop", "fsdp", None),
            P(None, "fsdp"),
            P("fsdp", None),
            P("fsdp", None),
            P("fsdp", None, None),
            P("loop", "fsdp", None),
            P("loop", None, "fsdp"),
            P("loop", "fsdp", None),
        ),
        check_vma=False,
    )
```

profile of v0, /device:TPU:0, one launch (start us, length us, event | category | flops | bytes accessed | tf_op | source)
XLA Modules:
  0.0 6594.6 jit_solution(18166168694413823809)
XLA Ops:
  12.3 2.7 fusion.47
  15.0 85.9 %all-gather.5.cloned.1.call-done = bf16[2048,2560]{1,0:T(8,128)(2,1)} async-done(((bf16[128,2560]{1,0:T(8,128)(2,1)}), bf16[2048,2560]{1,0:T(8,128)(2,1)}) %all-gather.5.cloned.1.call-update) | async-done | bytes 10485776 | tf_op jit(solution)/shard_map/all_gather | solution.py:132
  100.9 5.7 fusion.134
  116.9 32.8 all-gather.7.cloned.1.call-done
  149.7 3.0 fusion.139
  154.0 2.0 copy-done
  159.8 65.9 all-gather.9.cloned.1.call-done
  225.7 6.3 convolution_add_fusion.9
  235.3 2.8 fusion.50
  238.1 945.5 %all-gather.11.cloned.1.call-done = bf16[16384,3,2048]{2,0,1:T(8,128)(2,1)} async-done(((bf16[1024,3,2048]{2,0,1:T(8,128)(2,1)}), bf16[16384,3,2048]{2,0,1:T(8,128)(2,1)}) %all-gather.11.cloned.1.call-update) | async-done | bytes 201326608 | tf_op jit(solution)/shard_map/all_gather | solution.py:176
  1183.6 31.8 fusion.3
  1215.5 10.5 convolution_add_fusion.1
  1226.0 31.7 fusion.1
  1257.7 10.6 convolution_add_fusion.2
  1268.3 31.6 fusion.4
  1299.9 20.6 multiply_convert_fusion.1
  1320.6 7.7 fusion.58
  1328.3 6.3 fusion.55
  1334.7 24.9 fusion
  1359.6 24.6 fusion.40
  1386.0 2.4 multiply_reduce_fusion.1
  1391.7 4.7 fusion.142
  1398.4 5.3 fusion.32
  1403.8 5.2 multiply_reduce_fusion
  1411.0 2.0 copy-done.25
  1414.4 2.5 pad_maximum_fusion.3
  1417.2 3.7 convolution_multiply_fusion
  1421.6 8.9 fusion.143
  1430.5 59.1 reduce-scatter.12.cloned.1.call-done
  1492.1 9.7 fusion.89
  1501.8 24.8 pad_maximum_fusion.1
  1527.6 67.0 %convolution_bitcast_fusion.1 = f32[16384,1,2048]{2,0,1:T(8,128)} fusion(bf16[128,16384]{1,0:T(8,128)(2,1)} %get-tuple-element.53, bf16[128,2048]{1,0:T(8,128)(2,1)S(1)} %copy-done.12), kind=kOutput, calls=%fused_computation.2 | convolution fusion | flops 8589934592 | bytes 138936320 | tf_op jit(solution)/shard_map/dot_general | solution.py:31
  1594.6 47.3 convolution_bitcast_fusion.2
  1641.9 47.3 convolution_bitcast_fusion
  1689.2 262.3 %pad_maximum_fusion = f32[16384,3,2048]{2,0,1:T(8,128)} fusion(f32[16384,1,2048]{2,0,1:T(8,128)} %convolution_bitcast_fusion, f32[16384,1,2048]{2,0,1:T(8,128)} %convolution_bitcast_fusion.1, f32[16384,1,2048]{2,0,1:T(8,128)} %convolution_bitcast_fusion.2), kind=kLoop, calls=%fused_computation | loop fusion | flops 201326592 | bytes 805306368 | tf_op jit(solution)/shard_map/stack | solution.py:229
  1956.2 2.6 fusion.146
  1958.9 2.8 fusion.145
  1964.3 5.8 fusion.90
  1970.2 3.6 fusion.72
  1975.2 5.7 fusion.104
  1981.0 11.5 pad_maximum_fusion.2
  1995.7 9.1 fusion.61
  2008.5 12.6 convolution_dynamic-update-slice_fusion.1
  2021.1 12.4 convolution_dynamic-update-slice_fusion
  2035.3 44.4 copy.89
  2079.8 3.3 convert_element_type.167
  2083.2 3413.6 %reduce-scatter.16.cloned.1.call-done = f32[1024,3,2048]{2,0,1:T(8,128)} async-done(((f32[16384,3,2048]{2,0,1:T(8,128)}), f32[1024,3,2048]{2,0,1:T(8,128)}) %reduce-scatter.16.cloned.1.call-update) | async-done | bytes 25165840 | tf_op jit(solution)/shard_map/reduce_scatter | solution.py:228
  5496.8 13.4 convert_element_type.169
  5511.0 10.4 fusion.147
  5522.7 25.3 fusion.39
  5548.0 2.6 fusion.43
  5550.6 2.5 fusion.69
  5553.2 4.9 reduce-scatter.22.cloned.1.call-done
  5558.9 4.9 psum.21
  5564.4 132.0 %reduce-scatter.18.cloned.1.call-done = f32[128,1536]{0,1:T(8,128)} async-done(((f32[2048,1536]{0,1:T(8,128)}), f32[128,1536]{0,1:T(8,128)}) %reduce-scatter.18.cloned.1.call-update) | async-done | bytes 786448 | tf_op jit(solution)/shard_map/reduce_scatter | solution.py:363
  5696.5 2.3 copy.77
  5698.7 388.7 %reduce-scatter.24.cloned.1.call-done = f32[2464,256]{1,0:T(8,128)} async-done(((f32[39424,256]{1,0:T(8,128)}), f32[2464,256]{1,0:T(8,128)}) %reduce-scatter.24.cloned.1.call-update) | async-done | bytes 2523152
  6087.4 2.1 copy.90
  6089.6 2.1 copy.78
  6091.6 312.2 %all-reduce.3.cloned.1.call-done = (bf16[128,4608]{1,0:T(8,128)(2,1)}, bf16[1024,3,2048]{2,0,1:T(8,128)(2,1)}) async-done(((bf16[128,4608]{1,0:T(8,128)(2,1)}, bf16[1024,3,2048]{2,0,1:T(8,128)(2,1)}), (bf16[128,4608]{1,0:T(8,128)(2,1)}, bf16[1024,3,2048]{2,0,1:T(8,128)(2,1)})) %all-reduce.3.cloned.1.call-update) | async-done | bytes 13762576 | tf_op jit(solution)/shard_map/psum | solution.py:369
  6403.8 2.1 slice.206
  6406.0 2.3 slice.205
  6408.2 15.5 convert_element_type.170
  6423.7 163.8 %reduce-scatter.20.cloned.1.call-done = f32[1024,256]{1,0:T(8,128)} async-done(((f32[16384,256]{1,0:T(8,128)}), f32[1024,256]{1,0:T(8,128)}) %reduce-scatter.20.cloned.1.call-update) | async-done | bytes 1048592 | tf_op jit(solution)/shard_map/reduce_scatter | solution.py:365
  (245 shorter events, 59.0 us)
Async XLA Ops:
  7.2 93.7 %all-gather.5.cloned.1.call-start = ((), (), s32[]{:S(2)}) async-start(), calls=%async_computation.7 | async-start | bytes 11141120 | tf_op jit(solution)/shard_map/all_gather | solution.py:132
  7.9 141.8 %all-gather.7.cloned.1.call-start = ((), (), s32[]{:S(2)}) async-start(), calls=%async_computation.8 | async-start | bytes 2228224 | tf_op jit(solution)/shard_map/all_gather | solution.py:150
  8.8 102.7 %copy-start.69 = (f32[128]{0:T(128)}, f32[128]{0:T(128)S(1)}, u32[]{:S(2)}) copy-start(f32[128]{0:T(128)S(1)} %multiply_exponential_fusion) | copy-start | bytes 1540
  9.7 101.8 %copy-start.67 = (f32[128]{0:T(128)}, f32[128]{0:T(128)S(1)}, u32[]{:S(2)}) copy-start(f32[128]{0:T(128)S(1)} %fusion.123) | copy-start | bytes 1540
  11.5 95.2 %copy-start.64 = (f32[128]{0:T(128)}, f32[128]{0:T(128)S(1)}, u32[]{:S(2)}) copy-start(f32[128]{0:T(128)S(1)} %get-tuple-element.72) | copy-start | bytes 1540
  12.3 94.4 %copy-start.30 = (f32[1,2048]{1,0:T(1,128)}, f32[1,2048]{1,0:T(1,128)S(1)}, u32[]{:S(2)}) copy-start(f32[1,2048]{1,0:T(1,128)S(1)} %get-tuple-element.67) | copy-start | bytes 24580
  12.3 222.8 %copy-start.57 = (f32[1,2048]{1,0:T(1,128)}, f32[1,2048]{1,0:T(1,128)S(1)}, u32[]{:S(2)}) copy-start(f32[1,2048]{1,0:T(1,128)S(1)} %get-tuple-element.66) | copy-start | bytes 24580
  15.0 99.7 %copy-start.28 = (bf16[128,768]{1,0:T(8,128)(2,1)}, bf16[128,768]{1,0:T(8,128)(2,1)S(1)}, u32[]{:S(2)}) copy-start(bf16[128,768]{1,0:T(8,128)(2,1)S(1)} %fusion.47) | copy-start | bytes 589828
  109.9 115.7 %all-gather.9.cloned.1.call-start = ((), (), s32[]{:S(2)}) async-start(), calls=%async_computation.9 | async-start | bytes 8912896 | tf_op jit(solution)/shard_map/all_gather | solution.py:133
  110.7 1073.0 %all-gather.11.cloned.1.call-start = ((), (), s32[]{:S(2)}) async-start(), calls=%async_computation.10 | async-start | bytes 213909504 | tf_op jit(solution)/shard_map/all_gather | solution.py:176
  111.2 1378.3 %reduce-scatter.12.cloned.1.call-start = ((), (), s32[]{:S(2)}) async-start(), calls=%async_computation.11 | async-start | bytes 4456448 | tf_op jit(solution)/shard_map/reduce_scatter | solution.py:297
  112.5 40.2 copy-start.35
  114.2 1185.7 %copy-start.59 = (bf16[128,256]{1,0:T(8,128)(2,1)}, bf16[128,256]{1,0:T(8,128)(2,1)S(1)}, u32[]{:S(2)}) copy-start(bf16[128,256]{1,0:T(8,128)(2,1)S(1)} %convolution_convert_fusion.2) | copy-start | bytes 196612
  116.9 35.8 copy-start.50
  116.9 35.8 copy-start.52
  156.0 69.6 %copy-start.2 = (bf16[1,128,2048]{2,1,0:T(8,128)(2,1)S(1)}, bf16[1,128,2048]{2,1,0:T(8,128)(2,1)}, u32[]{:S(2)}) copy-start(bf16[1,128,2048]{2,1,0:T(8,128)(2,1)} %param.10) | copy-start | bytes 1572868
  157.9 77.4 %copy-start.14 = (bf16[128,8,256]{0,2,1:T(8,128)(2,1)}, bf16[128,8,256]{0,2,1:T(8,128)(2,1)S(1)}, u32[]{:S(2)}) copy-start(bf16[128,8,256]{0,2,1:T(8,128)(2,1)S(1)} %copy.65) | copy-start | bytes 1572868
  159.8 78.3 %copy-start.33 = (bf16[128,256]{1,0:T(8,128)(2,1)}, bf16[128,256]{1,0:T(8,128)(2,1)S(1)}, u32[]{:S(2)}) copy-start(bf16[128,256]{1,0:T(8,128)(2,1)S(1)} %convolution_convert_fusion.3) | copy-start | bytes 196612
  234.5 981.0 %copy-start.71 = (f32[128]{0:T(128)}, f32[128]{0:T(128)S(1)}, u32[]{:S(2)}) copy-start(f32[128]{0:T(128)S(1)} %get-tuple-element.74) | copy-start | bytes 1540
  235.3 990.7 %copy-start.11 = (bf16[128,2048]{1,0:T(8,128)(2,1)}, bf16[128,2048]{1,0:T(8,128)(2,1)S(1)}, u32[]{:S(2)}) copy-start(bf16[128,2048]{1,0:T(8,128)(2,1)S(1)} %multiply_convert_fusion.3) | copy-start | bytes 1572868
  238.1 1019.6 %copy-start.41 = (bf16[128,512]{1,0:T(8,128)(2,1)}, bf16[128,512]{1,0:T(8,128)(2,1)S(1)}, u32[]{:S(2)}) copy-start(bf16[128,512]{1,0:T(8,128)(2,1)S(1)} %fusion.50) | copy-start | bytes 393220
  1328.3 57.6 copy-start.49
  1334.7 49.5 copy-start.55
  1359.6 26.3 copy-start.9
  1359.6 26.3 copy-start.58
  1359.6 26.3 copy-start.72
  1359.6 28.8 copy-start.74
  1389.8 31.7 copy-start.17
  1398.4 10.6 slice-start
  1417.0 662.9 %reduce-scatter.14.cloned.1.call-start = ((), (), s32[]{:S(2)}) async-start(), calls=%async_computation.12 | async-start | bytes 40108032 | tf_op jit(solution)/shard_map/reduce_scatter | solution.py:326
  1421.5 70.5 %copy-start.19 = (bf16[128,8,256]{0,2,1:T(8,128)(2,1)}, bf16[128,8,256]{0,2,1:T(8,128)(2,1)S(1)}, u32[]{:S(2)}) copy-start(bf16[128,8,256]{0,2,1:T(8,128)(2,1)S(1)} %copy.67) | copy-start | bytes 1572868
  1421.5 70.0 %copy-start.68 = (f32[128]{0:T(128)S(1)}, f32[128]{0:T(128)}, u32[]{:S(2)}) copy-start(f32[128]{0:T(128)} %copy-done.67) | copy-start | bytes 1540
  1421.5 70.0 %copy-start.70 = (f32[128]{0:T(128)S(1)}, f32[128]{0:T(128)}, u32[]{:S(2)}) copy-start(f32[128]{0:T(128)} %copy-done.69) | copy-start | bytes 1540
  1421.5 70.5 %copy-start.3 = (bf16[1,128,2048]{2,1,0:T(8,128)(2,1)S(1)}, bf16[1,128,2048]{2,1,0:T(8,128)(2,1)}, u32[]{:S(2)}) copy-start(bf16[1,128,2048]{2,1,0:T(8,128)(2,1)} %param.10) | copy-start | bytes 1572868
  1421.6 70.5 %copy-start.31 = (f32[1,2048]{1,0:T(1,128)S(1)}, f32[1,2048]{1,0:T(1,128)}, u32[]{:S(2)}) copy-start(f32[1,2048]{1,0:T(1,128)} %copy-done.30) | copy-start | bytes 24580
  1421.6 70.5 %copy-start.65 = (f32[128]{0:T(128)S(1)}, f32[128]{0:T(128)}, u32[]{:S(2)}) copy-start(f32[128]{0:T(128)} %copy-done.64) | copy-start | bytes 1540
  1490.5 11.2 copy-start.37
  1491.9 9.9 copy-start.45
  1491.9 9.9 copy-start.47
  1492.0 9.8 copy-start.39
  1526.6 3970.2 %reduce-scatter.16.cloned.1.call-start = ((), (), s32[]{:S(2)}) async-start(), calls=%async_computation.13 | async-start | bytes 427819008 | tf_op jit(solution)/shard_map/reduce_scatter | solution.py:228
  1594.6 47.3 copy-start.23
  1951.6 11.6 copy-start.27
  1951.6 12.7 copy-start.38
  1951.6 12.7 copy-start.40
  1951.6 3606.4 %reduce-scatter.22.cloned.1.call-start = ((), (), s32[]{:S(2)}) async-start(), calls=%async_computation.16 | async-start | bytes 1114112
  1952.6 11.7 copy-start.1
  1954.4 15.7 copy-start.61
  1958.9 11.3 copy-start.4
  1958.9 11.3 slice-start.2
  1958.9 11.3 copy-start.32
  1958.9 11.3 copy-start.66
  1980.9 3715.5 %reduce-scatter.18.cloned.1.call-start = ((), (), s32[]{:S(2)}) async-start(), calls=%async_computation.14 | async-start | bytes 13369344 | tf_op jit(solution)/shard_map/reduce_scatter | solution.py:363
  1992.5 4094.9 %reduce-scatter.24.cloned.1.call-start = ((), (), s32[]{:S(2)}) async-start(), calls=%async_computation.17 | async-start | bytes 42893312
  1995.7 11.1 copy-start.18
  1995.7 11.1 copy-start.34
  1995.7 12.8 copy-start.7
  1995.7 12.8 copy-start.42
  2008.5 12.6 copy-start.5
  2021.1 12.4 copy-start.24
  2079.8 4324.1 %all-reduce.3.cloned.1.call-start = ((), (), s32[]{:S(2)}) async-start(), calls=%async_computation.18 | async-start | bytes 27525120 | tf_op jit(solution)/shard_map/psum | solution.py:369
  5510.2 1077.3 %reduce-scatter.20.cloned.1.call-start = ((), (), s32[]{:S(2)}) async-start(), calls=%async_computation.15 | async-start | bytes 17825792 | tf_op jit(solution)/shard_map/reduce_scatter | solution.py:365
  5522.7 28.0 copy-start.26
  5522.7 28.0 copy-start.73
  (27 other events, 116.8 us)
Sparse Core Ops, SparseCore 0:
  10.3 90.5 all-gather.4
  110.0 39.6 all-gather.6
  151.9 73.7 all-gather.8
  227.1 956.5 all-gather.10
  1417.1 72.4 reduce-scatter.11
  1526.7 366.8 reduce-scatter.13
  1951.7 3545.0 reduce-scatter.15
  5500.4 57.5 reduce-scatter.21
  5562.6 133.7 reduce-scatter.17
  5701.2 386.1 reduce-scatter.23
  6090.6 313.2 all-reduce.2
  6408.9 178.5 reduce-scatter.19
where the time goes:
time: 6600 us; the launch traced here: 6590 us
  waiting for transfers between devices  5610 us (85%)
  matrix products  547 us (8%)
  other arithmetic  349 us (5%)
  local copies, waits for them, and re-layouts  70 us (1%)
    reduce_scatter x1, waiting for transfers between devices, per_device(): lax.psum_scatter(jnp.stack([outer_product_rows(gate_gradients, normalized...  3410 us
    all_gather x1, waiting for transfers between devices, per_device(): lax.all_gather(feedforward_weight, 'fsdp', axis=0, tiled=True)  945 us
    unnamed x14, waiting for transfers between devices  396 us
    psum x1, waiting for transfers between devices, per_device(): lax.psum(projection_own.astype(jnp.bfloat16), 'loop').astype(jnp.float32)  312 us
    another operation x1, other arithmetic, per_device(): jnp.stack([outer_product_rows(gate_gradients, normalized_second), outer_p...  262 us
    dot_general x17, matrix products, outer_product_rows(): lax.dot_general(former, latter, (((0,), (0,)), ((), ())), preferred_eleme...  236 us
    reduce_scatter x1, waiting for transfers between devices, per_device(): lax.psum_scatter(narrow_down_piece, 'fsdp', scatter_dimension=0, tiled=True)  164 us
    dot_general x17, matrix products, times_transposed(): lax.dot_general(former, latter, (((1,), (1,)), ((), ())), preferred_eleme...  159 us
  transfers between devices with their start and end apart: 12, of which 11 were waited for; matrix products, arithmetic and copies ran while one was open for 10% of the time, Pallas kernels for 0%

commit v1 on v0

v1 whole, which is shorter than its diff:
```python
import math

import jax
import jax.numpy as jnp
from jax import lax
from jax.sharding import PartitionSpec as P

MODEL_WIDTH = 2048
HEADS = 8
HEAD_WIDTH = 256
HIDDEN_COUNT = 16384
ADAPTER_RANK = 256
QUERY_WIDTH = 2048
PROJECT_COLUMNS = 2560
ADAPTER_COLUMNS = 39424
GATE_START = PROJECT_COLUMNS + MODEL_WIDTH

epsilon = 1e-06
bf16 = jnp.bfloat16
f32 = jnp.float32


def matrix_product(former, latter):
    return jnp.dot(former, latter, preferred_element_type=f32)


def times_transposed(former, latter):
    return lax.dot_general(former, latter, (((1,), (1,)), ((), ())), preferred_element_type=f32)


def outer_product_rows(former, latter):
    return lax.dot_general(former, latter, (((0,), (0,)), ((), ())), preferred_element_type=f32)


def segment_info(lengths, row_count):
    row_ids = jnp.arange(row_count, dtype=jnp.int32)
    count = lengths.shape[0]
    labels = jnp.arange(count, dtype=jnp.int32)
    finish = jnp.sum(jnp.where(labels[:, None] <= labels[None, :], lengths[:, None], 0), axis=0)
    starts = finish - lengths
    segment = jnp.sum((row_ids[:, None] >= finish[None, :]).astype(jnp.int32), axis=1)
    opening = jnp.sum(jnp.where(segment[:, None] == labels[None, :], starts[None, :], 0), axis=1)
    return (segment, row_ids - opening)


def rotate(values, position, direction):
    half_dim = HEAD_WIDTH // 2
    frequency = jnp.exp(
        jnp.arange(half_dim).astype(f32) * (-2.0 * math.log(10000.0) / HEAD_WIDTH)
    )
    angles = position.astype(f32)[:, None] * frequency[None, :]
    cosine = jnp.cos(angles)[:, None, :]
    sine_val = direction * jnp.sin(angles)[:, None, :]
    shaped = values.reshape(values.shape[0], -1, HEAD_WIDTH)
    former = shaped[..., :half_dim]
    latter = shaped[..., half_dim:]
    turned = jnp.concatenate(
        [former * cosine - latter * sine_val, latter * cosine + former * sine_val], axis=-1
    )
    return turned.reshape(values.shape)


def rms_scale(values):
    return lax.rsqrt(jnp.mean(values * values, axis=-1, keepdims=True) + epsilon)


def gelu_tanh(values):
    return jax.nn.gelu(values, approximate=True)


def unit_backward(gate_value, upward_activation, hidden_unit_gradient):
    activated, pullback_function = jax.vjp(gelu_tanh, gate_value)
    gate_grad = pullback_function(hidden_unit_gradient * upward_activation)[0]
    return (gate_grad.astype(bf16), (hidden_unit_gradient * activated).astype(bf16))


def scores_of(query_heads, key_rows, allowed, scaling):
    product = (
        jnp.einsum("thd,ud->thu", query_heads, key_rows, preferred_element_type=f32) * scaling
    )
    return jnp.where(allowed[:, None, :], product, -1e30)


def gather_rows(block):
    return lax.all_gather(block, "fsdp", axis=0, tiled=True)


def scatter_rows(partial):
    return lax.psum_scatter(partial.astype(bf16), "fsdp", scatter_dimension=0, tiled=True).astype(f32)


def turn(block):
    return lax.all_to_all(block, "fsdp", split_axis=1, concat_axis=0, tiled=True)


def per_device(
    hidden_input,
    sequence_lengths,
    norm_gain_values,
    input_proj_weight,
    output_proj_weight,
    feedforward_weight,
    adapter_first,
    adapter_second,
    adapter_down_first,
    output_gradient,
):
    size = lax.axis_size("fsdp")
    place = lax.axis_index("fsdp")
    tokens_dev = hidden_input.shape[1]
    all_rows = tokens_dev * size
    hidden_own = HIDDEN_COUNT // size
    width_own = MODEL_WIDTH // size
    columns_own = ADAPTER_COLUMNS // size
    offset = place * tokens_dev
    segment_all, position_all = segment_info(sequence_lengths[0], all_rows)
    segment_own = lax.dynamic_slice_in_dim(segment_all, offset, tokens_dev)
    position_own = lax.dynamic_slice_in_dim(position_all, offset, tokens_dev)
    row_all = jnp.arange(all_rows, dtype=jnp.int32)
    row_own = offset + jnp.arange(tokens_dev, dtype=jnp.int32)
    allowed = (segment_own[:, None] == segment_all[None, :]) & (
        row_own[:, None] >= row_all[None, :]
    )
    gains = norm_gain_values.astype(f32)
    first_factor = adapter_first[0]
    second_factor = adapter_second[0]
    rank = ADAPTER_RANK
    narrow_projection = first_factor[:, : 3 * rank]
    narrow_output = first_factor[:, 3 * rank : 4 * rank]
    squeeze_gate = first_factor[:, 4 * rank : 5 * rank]
    squeeze_up = first_factor[:, 5 * rank :]
    narrow_down = lax.dynamic_slice_in_dim(adapter_down_first[0], place * hidden_own, hidden_own, 0)
    widen_query = second_factor[:, :QUERY_WIDTH]
    widen_key = second_factor[:, QUERY_WIDTH : QUERY_WIDTH + HEAD_WIDTH]
    widen_value = second_factor[:, QUERY_WIDTH + HEAD_WIDTH : PROJECT_COLUMNS]
    widen_output = second_factor[:, PROJECT_COLUMNS:GATE_START]
    widen_gate = lax.dynamic_slice_in_dim(
        second_factor, GATE_START + place * hidden_own, hidden_own, 1
    )
    widen_up = lax.dynamic_slice_in_dim(
        second_factor, GATE_START + HIDDEN_COUNT + place * hidden_own, hidden_own, 1
    )
    widen_down = second_factor[:, GATE_START + 2 * HIDDEN_COUNT :]
    scaling = HEAD_WIDTH ** (-0.5)

    hidden_state = hidden_input[0].astype(f32)
    scale_one = rms_scale(hidden_state)
    normalized = (hidden_state * scale_one * gains[0]).astype(bf16)
    proj_in = gather_rows(input_proj_weight)
    proj_out = gather_rows(output_proj_weight)
    lora_qkv = matrix_product(normalized, narrow_projection).astype(bf16)
    projected = matrix_product(normalized, proj_in)
    query_pre = projected[:, :QUERY_WIDTH] + matrix_product(lora_qkv[:, :rank], widen_query)
    key_pre = projected[:, QUERY_WIDTH : QUERY_WIDTH + HEAD_WIDTH] + matrix_product(
        lora_qkv[:, rank : 2 * rank], widen_key
    )
    value_local = (
        projected[:, QUERY_WIDTH + HEAD_WIDTH :]
        + matrix_product(lora_qkv[:, 2 * rank :], widen_value)
    ).astype(bf16)
    query_rot = rotate(query_pre, position_own, 1.0).astype(bf16)
    key_rot = rotate(key_pre, position_own, 1.0).astype(bf16)
    keys_all = gather_rows(jnp.concatenate([key_rot, value_local], axis=1))
    key_rows, value_rows = keys_all[:, :HEAD_WIDTH], keys_all[:, HEAD_WIDTH:]
    query_heads = query_rot.reshape(tokens_dev, HEADS, HEAD_WIDTH)
    scores = scores_of(query_heads, key_rows, allowed, scaling)
    row_max = jnp.max(scores, axis=-1, keepdims=True)
    powered = jnp.exp(scores - row_max)
    row_sum = jnp.sum(powered, axis=-1, keepdims=True)
    probs = powered / row_sum
    probs_low = probs.astype(bf16)
    attended = (
        jnp.einsum("thu,ud->thd", probs_low, value_rows, preferred_element_type=f32)
        .reshape(tokens_dev, QUERY_WIDTH)
        .astype(bf16)
    )
    lora_out = matrix_product(attended, narrow_output).astype(bf16)
    middle = (
        hidden_state
        + times_transposed(attended, proj_out)
        + matrix_product(lora_out, widen_output)
    )
    scale_two = rms_scale(middle)
    normed_two = (middle * scale_two * gains[1]).astype(bf16)

    grad_all = gather_rows(output_gradient[0])
    two_all = gather_rows(normed_two)
    weight_gate = feedforward_weight[:, 0, :]
    weight_up = feedforward_weight[:, 1, :]
    weight_down = feedforward_weight[:, 2, :]
    lora_gate = matrix_product(two_all, squeeze_gate).astype(bf16)
    lora_up = matrix_product(two_all, squeeze_up).astype(bf16)
    hd_grad = times_transposed(grad_all, widen_down).astype(bf16)
    gate = times_transposed(two_all, weight_gate) + matrix_product(lora_gate, widen_gate)
    upward = times_transposed(two_all, weight_up) + matrix_product(lora_up, widen_up)
    units = (gelu_tanh(gate) * upward).astype(bf16)
    units_grad = times_transposed(grad_all, weight_down) + times_transposed(hd_grad, narrow_down)
    gate_grad, up_grad = unit_backward(gate, upward, units_grad)
    back_part = jnp.concatenate(
        [
            matrix_product(gate_grad, weight_gate) + matrix_product(up_grad, weight_up),
            times_transposed(gate_grad, widen_gate),
            times_transposed(up_grad, widen_up),
        ],
        axis=1,
    )
    back_own = scatter_rows(back_part)
    out_part = jnp.concatenate(
        [matrix_product(units, weight_down), matrix_product(units, narrow_down)], axis=1
    )
    out_own = scatter_rows(out_part)
    ffn_grad = jnp.stack(
        [
            outer_product_rows(gate_grad, two_all),
            outer_product_rows(up_grad, two_all),
            outer_product_rows(units, grad_all),
        ],
        axis=1,
    ).astype(bf16)
    ffn_sum = lax.psum(ffn_grad, "loop").astype(f32)
    down_own = outer_product_rows(units, hd_grad)
    gate_piece = outer_product_rows(lora_gate, gate_grad)
    up_piece = outer_product_rows(lora_up, up_grad)

    lora_hd = out_own[:, MODEL_WIDTH:].astype(bf16)
    hidden_out = (middle + out_own[:, :MODEL_WIDTH] + matrix_product(lora_hd, widen_down)).astype(bf16)

    gate_low = back_own[:, MODEL_WIDTH : MODEL_WIDTH + rank].astype(bf16)
    up_low = back_own[:, MODEL_WIDTH + rank :].astype(bf16)
    two_grad = (
        back_own[:, :MODEL_WIDTH]
        + times_transposed(gate_low, squeeze_gate)
        + times_transposed(up_low, squeeze_up)
    )
    weighted_two = gains[1] * two_grad
    middle_grad = (
        output_gradient[0].astype(f32)
        + scale_two * weighted_two
        - middle * scale_two**3 * jnp.mean(middle * weighted_two, axis=-1, keepdims=True)
    )
    gain_two = jnp.sum(two_grad * middle * scale_two, axis=0)

    branch_grad = middle_grad.astype(bf16)
    lora_out_grad = times_transposed(branch_grad, widen_output).astype(bf16)
    attended_grad = (
        matrix_product(branch_grad, proj_out) + times_transposed(lora_out_grad, narrow_output)
    ).astype(bf16)
    heads_grad = attended_grad.reshape(tokens_dev, HEADS, HEAD_WIDTH)
    prob_grad = jnp.einsum("thd,ud->thu", heads_grad, value_rows, preferred_element_type=f32)
    row_dot = jnp.sum(probs * prob_grad, axis=-1, keepdims=True)
    score_grad = (probs * (prob_grad - row_dot)).astype(bf16)
    query_rot_grad = (
        jnp.einsum("thu,ud->thd", score_grad, key_rows, preferred_element_type=f32) * scaling
    )
    key_part = (
        jnp.einsum("thu,thd->ud", score_grad, query_heads, preferred_element_type=f32) * scaling
    )
    value_part = jnp.einsum("thu,thd->ud", probs_low, heads_grad, preferred_element_type=f32)
    pair_grad = scatter_rows(jnp.concatenate([key_part, value_part], axis=1))
    query_grad = rotate(
        query_rot_grad.reshape(tokens_dev, QUERY_WIDTH), position_own, -1.0
    ).astype(bf16)
    key_grad = rotate(pair_grad[:, :HEAD_WIDTH], position_own, -1.0).astype(bf16)
    value_grad = pair_grad[:, HEAD_WIDTH:].astype(bf16)
    proj_grad = jnp.concatenate([query_grad, key_grad, value_grad], axis=1)
    lora_qkv_grad = jnp.concatenate(
        [
            times_transposed(query_grad, widen_query),
            times_transposed(key_grad, widen_key),
            times_transposed(value_grad, widen_value),
        ],
        axis=1,
    ).astype(bf16)
    normed_grad = times_transposed(proj_grad, proj_in) + times_transposed(
        lora_qkv_grad, narrow_projection
    )
    weighted_one = gains[0] * normed_grad
    input_grad = (
        middle_grad
        + scale_one * weighted_one
        - hidden_state
        * scale_one**3
        * jnp.mean(hidden_state * weighted_one, axis=-1, keepdims=True)
    )
    gain_one = jnp.sum(normed_grad * hidden_state * scale_one, axis=0)
    gain_sum = lax.psum(
        lax.psum_scatter(
            jnp.stack([gain_one, gain_two]), "fsdp", scatter_dimension=1, tiled=True
        ).astype(bf16),
        "loop",
    ).astype(f32)

    attended_all = gather_rows(jnp.concatenate([attended, lora_qkv], axis=1))
    lora_qkv_all = attended_all[:, QUERY_WIDTH:]
    attended_all = attended_all[:, :QUERY_WIDTH]
    lora_out_all = matrix_product(attended_all, narrow_output).astype(bf16)
    low_all = gather_rows(
        jnp.concatenate([lora_out_grad, gate_low, up_low, lora_hd], axis=1)
    )
    proj_all = gather_rows(jnp.concatenate([proj_grad, lora_qkv_grad], axis=1))
    qkv_low_all = proj_all[:, PROJECT_COLUMNS:]
    proj_all = proj_all[:, :PROJECT_COLUMNS]
    normed_turn = turn(normalized)
    branch_turn = turn(branch_grad)
    column = place * width_own
    attended_turn = lax.dynamic_slice_in_dim(attended_all, column, width_own, 1)
    two_turn = lax.dynamic_slice_in_dim(two_all, column, width_own, 1)
    attn_part = jnp.concatenate(
        [outer_product_rows(normed_turn, proj_all), outer_product_rows(branch_turn, attended_all)],
        axis=1,
    ).astype(bf16)
    attn_sum = lax.psum(attn_part, "loop").astype(f32)
    squeeze_own = jnp.concatenate(
        [
            outer_product_rows(normed_turn, qkv_low_all),
            outer_product_rows(attended_turn, low_all[:, :rank]),
            outer_product_rows(two_turn, low_all[:, rank : 3 * rank]),
        ],
        axis=1,
    )
    out_piece = outer_product_rows(lora_out_all, branch_turn)
    down_piece = outer_product_rows(low_all[:, 3 * rank :], grad_all)
    pieces = lax.all_gather(
        jnp.concatenate([out_piece, gate_piece, up_piece], axis=1).astype(bf16), "fsdp", axis=0
    )

    def laid(first, last):
        return pieces[:, :, first:last].transpose(1, 0, 2).reshape(rank, -1)

    expand_all = jnp.concatenate(
        [
            outer_product_rows(lora_qkv_all[:, :rank], proj_all[:, :QUERY_WIDTH]).astype(bf16),
            outer_product_rows(
                lora_qkv_all[:, rank : 2 * rank], proj_all[:, QUERY_WIDTH : QUERY_WIDTH + HEAD_WIDTH]
            ).astype(bf16),
            outer_product_rows(
                lora_qkv_all[:, 2 * rank :], proj_all[:, QUERY_WIDTH + HEAD_WIDTH :]
            ).astype(bf16),
            laid(0, width_own),
            laid(width_own, width_own + hidden_own),
            laid(width_own + hidden_own, width_own + 2 * hidden_own),
            down_piece.astype(bf16),
        ],
        axis=1,
    )
    expand_own = lax.dynamic_slice_in_dim(expand_all, place * columns_own, columns_own, 1).astype(f32)
    return (
        hidden_out[None],
        input_grad[None],
        gain_sum,
        attn_sum[:, :PROJECT_COLUMNS],
        attn_sum[:, PROJECT_COLUMNS:],
        ffn_sum,
        squeeze_own[None],
        expand_own[None],
        down_own[None],
    )


def solution(mesh):
    return jax.shard_map(
        per_device,
        mesh=mesh,
        in_specs=(
            P("loop", "fsdp", None),
            P("loop", None),
            P(),
            P("fsdp", None),
            P("fsdp", None),
            P("fsdp", None, None),
            P("loop", None, None),
            P("loop", None, None),
            P("loop", None, None),
            P("loop", "fsdp", None),
        ),
        out_specs=(
            P("loop", "fsdp", None),
            P("loop", "fsdp", None),
            P(None, "fsdp"),
            P("fsdp", None),
            P("fsdp", None),
            P("fsdp", None, None),
            P("loop", "fsdp", None),
            P("loop", None, "fsdp"),
            P("loop", "fsdp", None),
        ),
        check_vma=False,
    )
```

time: 6600 us -> 1590 us (0.24)
  waiting for transfers between devices: 5610 us -> 1110 us
  other arithmetic: 349 us -> 64.5 us
  matrix products: 547 us -> 300 us
    reduce_scatter x5 -> x3, waiting for transfers between devices: 3770 us -> 258 us  [scatter_rows(): lax.psum_scatter(partial.astype(bf16), 'fsdp', scatter_dimension=0, tiled...]
    all_gather x4 -> x9, waiting for transfers between devices: 1130 us -> 556 us  [the longest x8 489 us: gather_rows(): return lax.all_gather(block, 'fsdp', axis=0, tiled=True)]
    unnamed x14 -> x15, waiting for transfers between devices: 396 us -> 35 us
    another operation x7 -> x6, other arithmetic: 264 us -> 7.33 us  [the longest x1 5.68 us: per_device(): jnp.stack([outer_product_rows(gate_grad, two_all), outer_product_rows(up_...]
    dot_general x17 -> x16, matrix products: 236 us -> 92.4 us  [outer_product_rows(): lax.dot_general(former, latter, (((0,), (0,)), ((), ())), preferred_eleme...]
    dot_general x17, matrix products: 159 us -> 90.9 us  [times_transposed(): lax.dot_general(former, latter, (((1,), (1,)), ((), ())), preferred_eleme...]
  transfers between devices with their start and end apart: 12 -> 16, of which waited for: 11 -> 14; matrix products, arithmetic and copies ran while one was open for 10% -> 18% of each run, Pallas kernels for 0% -> 0%
where the time goes in v1:
time: 1590 us
  waiting for transfers between devices  1110 us (70%)
  matrix products  300 us (19%)
  local copies, waits for them, and re-layouts  82.3 us (5%)
  other arithmetic  64.5 us (4%)
    all_gather x8, waiting for transfers between devices, gather_rows(): return lax.all_gather(block, 'fsdp', axis=0, tiled=True)  489 us
    psum x1, waiting for transfers between devices, per_device(): attn_sum = lax.psum(attn_part, 'loop').astype(f32)  262 us
    reduce_scatter x3, waiting for transfers between devices, scatter_rows(): lax.psum_scatter(partial.astype(bf16), 'fsdp', scatter_dimension=0, tiled...  258 us
    dot_general x16, matrix products, matrix_product(): return jnp.dot(former, latter, preferred_element_type=f32)  98 us
    dot_general x16, matrix products, outer_product_rows(): lax.dot_general(former, latter, (((0,), (0,)), ((), ())), preferred_eleme...  92.4 us
    dot_general x17, matrix products, times_transposed(): lax.dot_general(former, latter, (((1,), (1,)), ((), ())), preferred_eleme...  90.9 us
    all_gather x1, waiting for transfers between devices, per_device(): lax.all_gather(jnp.concatenate([out_piece, gate_piece, up_piece], axis=1)...  66.2 us
    unnamed x144, local copies, waits for them, and re-layouts  50.5 us
  transfers between devices with their start and end apart: 16, of which 14 were waited for; matrix products, arithmetic and copies ran while one was open for 18% of the time, Pallas kernels for 0%

profile of v1, /device:TPU:0, one launch (start us, length us, event | category | flops | bytes accessed | tf_op | source)
XLA Modules:
  0.0 1588.3 jit_solution(12409513125814181764)
XLA Ops:
  14.9 86.0 %all-gather.11.cloned.1.call-done = bf16[2048,2560]{1,0:T(8,128)(2,1)} async-done(((bf16[128,2560]{1,0:T(8,128)(2,1)}), bf16[2048,2560]{1,0:T(8,128)(2,1)}) %all-gather.11.cloned.1.call-update) | async-done | bytes 10485776 | tf_op jit(solution)/shard_map/all_gather | solution.py:85
  100.9 5.7 fusion.157
  115.8 33.8 %all-gather.13.cloned.1.call-done = bf16[2048,512]{1,0:T(8,128)(2,1)} async-done(((bf16[128,512]{1,0:T(8,128)(2,1)}), bf16[2048,512]{1,0:T(8,128)(2,1)}) %all-gather.13.cloned.1.call-update) | async-done | bytes 2097168 | tf_op jit(solution)/shard_map/all_gather | solution.py:85
  152.1 4.7 fusion.214
  156.9 3.3 copy-done.6
  161.8 63.7 %all-gather.15.cloned.1.call-done = bf16[2048,2048]{1,0:T(8,128)(2,1)} async-done(((bf16[128,2048]{1,0:T(8,128)(2,1)}), bf16[2048,2048]{1,0:T(8,128)(2,1)}) %all-gather.15.cloned.1.call-update) | async-done | bytes 8388624 | tf_op jit(solution)/shard_map/all_gather | solution.py:85
  225.5 6.3 convolution_add_fusion.9
  236.2 64.4 %all-gather.27.cloned.1.call-done = bf16[1,2048,2048]{2,1,0:T(8,128)(2,1)} async-done(((bf16[1,128,2048]{2,1,0:T(8,128)(2,1)}), bf16[1,2048,2048]{2,1,0:T(8,128)(2,1)}) %all-gather.27.cloned.1.call-update) | async-done | bytes 8388624 | tf_op jit(solution)/shard_map/all_gather | solution.py:85
  300.7 6.2 fusion.53
  306.9 14.6 fusion.18
  321.4 5.7 convolution_add_fusion
  327.2 49.2 %all-gather.17.cloned.1.call-done = bf16[2048,2048]{1,0:T(8,128)(2,1)} async-done(((bf16[128,2048]{1,0:T(8,128)(2,1)}), bf16[2048,2048]{1,0:T(8,128)(2,1)}) %all-gather.17.cloned.1.call-update) | async-done | bytes 8388624 | tf_op jit(solution)/shard_map/all_gather | solution.py:85
  376.4 6.2 convolution_convert_fusion.5
  382.7 14.6 fusion.24
  397.2 5.6 convolution_add_fusion.1
  402.8 4.7 convolution_convert_fusion.6
  407.5 13.0 fusion.28
  420.6 15.3 fusion.9
  435.9 3.7 convolution_convert_fusion.2
  439.7 14.6 fusion.26
  456.7 14.3 add_convert_fusion
  471.0 7.0 pad_maximum_fusion.1
  478.5 117.0 %reduce-scatter.9.cloned.1.call-done = bf16[128,2560]{1,0:T(8,128)(2,1)} async-done(((bf16[2048,2560]{1,0:T(8,128)(2,1)}), bf16[128,2560]{1,0:T(8,128)(2,1)}) %reduce-scatter.9.cloned.1.call-update) | async-done | bytes 655376 | tf_op jit(solution)/shard_map/reduce_scatter | solution.py:89
  602.3 4.6 fusion.201
  609.0 5.1 fusion.52
  614.1 4.7 multiply_reduce_fusion
  618.9 4.2 multiply_convert_fusion
  628.1 3.6 convolution_convert_fusion.3
  631.7 12.0 convolution_convert_fusion
  643.8 4.5 pad_maximum_fusion.2
  650.4 3.7 convolution_multiply_fusion
  656.8 32.6 %reduce-scatter.11.cloned.1.call-done = bf16[128,512]{1,0:T(8,128)(2,1)} async-done(((bf16[2048,512]{1,0:T(8,128)(2,1)}), bf16[128,512]{1,0:T(8,128)(2,1)}) %reduce-scatter.11.cloned.1.call-update) | async-done | bytes 131088 | tf_op jit(solution)/shard_map/reduce_scatter | solution.py:89
  696.5 108.5 %reduce-scatter.7.cloned.1.call-done = bf16[128,2304]{1,0:T(8,128)(2,1)} async-done(((bf16[2048,2304]{1,0:T(8,128)(2,1)}), bf16[128,2304]{1,0:T(8,128)(2,1)}) %reduce-scatter.7.cloned.1.call-update) | async-done | bytes 589840 | tf_op jit(solution)/shard_map/reduce_scatter | solution.py:89
  805.0 7.5 fusion.131
  812.6 4.9 fusion.101
  820.7 4.5 all-to-all-start.1
  825.7 3.5 fusion.82
  829.1 3.8 fusion.81
  833.0 84.2 %all-gather.21.cloned.1.call-done = bf16[2048,2816]{0,1:T(8,128)(2,1)} async-done(((bf16[128,2816]{0,1:T(8,128)(2,1)}), bf16[2048,2816]{0,1:T(8,128)(2,1)}) %all-gather.21.cloned.1.call-update) | async-done | bytes 11534352 | tf_op jit(solution)/shard_map/all_gather | solution.py:85
  917.1 6.5 fusion.92
  926.4 3.6 all-to-all-start
  930.1 12.8 convert_bitcast_fusion.2
  942.9 11.9 convert_bitcast_fusion.1
  954.9 11.5 convert_bitcast_fusion
  966.4 5.7 pad_maximum_fusion
  972.1 4.7 convolution_convert_fusion.7
  976.9 62.8 %all-gather.19.cloned.1.call-done = bf16[2048,3328]{0,1:T(8,128)(2,1)} async-done(((bf16[128,3328]{0,1:T(8,128)(2,1)}), bf16[2048,3328]{0,1:T(8,128)(2,1)}) %all-gather.19.cloned.1.call-update) | async-done | bytes 13631504 | tf_op jit(solution)/shard_map/all_gather | solution.py:85
  1039.7 7.6 fusion.41
  1049.0 4.5 convolution_bitcast_fusion.2
  1053.6 8.7 slice.277
  1066.0 32.9 %reduce-scatter.13.cloned.1.call-done = f32[128,2]{1,0:T(8,128)} async-done(((f32[2048,2]{1,0:T(8,128)}), f32[128,2]{1,0:T(8,128)}) %reduce-scatter.13.cloned.1.call-update) | async-done | bytes 1040
  1099.8 5.2 psum.21
  1105.5 45.2 %all-gather.23.cloned.1.call-done = bf16[2048,1024]{1,0:T(8,128)(2,1)} async-done(((bf16[128,1024]{1,0:T(8,128)(2,1)}), bf16[2048,1024]{1,0:T(8,128)(2,1)}) %all-gather.23.cloned.1.call-update) | async-done | bytes 4194320 | tf_op jit(solution)/shard_map/all_gather | solution.py:85
  1150.8 6.1 fusion.56
  1161.8 6.2 fusion.59
  1169.6 3.4 fusion.44
  1179.3 66.2 %all-gather.25.cloned.1.call-done = bf16[16,256,2176]{2,1,0:T(8,128)(2,1)} async-done(((bf16[1,256,2176]{2,1,0:T(8,128)(2,1)}), bf16[16,256,2176]{2,1,0:T(8,128)(2,1)}) %all-gather.25.cloned.1.call-update) | async-done | bytes 17825808 | tf_op jit(solution)/shard_map/all_gather | solution.py:323
  1245.6 12.2 fusion.211
  1257.8 12.4 copy.145
  1270.7 12.3 copy.144
  1284.1 8.8 constant_dynamic-update-slice_fusion.8
  1292.9 3.6 constant_dynamic-update-slice_fusion.7
  1300.5 262.3 %all-reduce.3.cloned.1.call-done = (bf16[128,4608]{1,0:T(8,128)(2,1)}, bf16[1024,3,2048]{2,0,1:T(8,128)(2,1)}) async-done(((bf16[128,4608]{1,0:T(8,128)(2,1)}, bf16[1024,3,2048]{2,0,1:T(8,128)(2,1)}), (bf16[128,4608]{1,0:T(8,128)(2,1)}, bf16[1024,3,2048]{2,0,1:T(8,128)(2,1)})) %all-reduce.3.cloned.1.call-update) | async-done | bytes 13762576 | tf_op jit(solution)/shard_map/psum | solution.py:312
  1567.2 14.4 convert_element_type.197
  (257 shorter events, 89.6 us)
Async XLA Ops:
  7.2 93.7 %all-gather.11.cloned.1.call-start = ((), (), s32[]{:S(2)}) async-start(), calls=%async_computation.6 | async-start | bytes 11141120 | tf_op jit(solution)/shard_map/all_gather | solution.py:85
  7.9 141.7 %all-gather.13.cloned.1.call-start = ((), (), s32[]{:S(2)}) async-start(), calls=%async_computation.7 | async-start | bytes 2228224 | tf_op jit(solution)/shard_map/all_gather | solution.py:85
  8.0 103.5 %copy-start.43 = (f32[128]{0:T(128)}, f32[128]{0:T(128)S(1)}, u32[]{:S(2)}) copy-start(f32[128]{0:T(128)S(1)} %multiply_exponential_fusion) | copy-start | bytes 1540
  9.7 101.9 %copy-start.42 = (f32[128]{0:T(128)}, f32[128]{0:T(128)S(1)}, u32[]{:S(2)}) copy-start(f32[128]{0:T(128)S(1)} %fusion.194) | copy-start | bytes 1540
  11.4 95.2 %copy-start.39 = (f32[128]{0:T(128)}, f32[128]{0:T(128)S(1)}, u32[]{:S(2)}) copy-start(f32[128]{0:T(128)S(1)} %get-tuple-element.40) | copy-start | bytes 1540
  12.2 94.4 %copy-start.30 = (f32[1,2048]{1,0:T(1,128)}, f32[1,2048]{1,0:T(1,128)S(1)}, u32[]{:S(2)}) copy-start(f32[1,2048]{1,0:T(1,128)S(1)} %get-tuple-element.35) | copy-start | bytes 24580
  12.2 222.7 %copy-start.34 = (f32[1,2048]{1,0:T(1,128)}, f32[1,2048]{1,0:T(1,128)S(1)}, u32[]{:S(2)}) copy-start(f32[1,2048]{1,0:T(1,128)S(1)} %get-tuple-element.34) | copy-start | bytes 24580
  14.9 98.7 %copy-start.22 = (bf16[128,768]{1,0:T(8,128)(2,1)}, bf16[128,768]{1,0:T(8,128)(2,1)S(1)}, u32[]{:S(2)}) copy-start(bf16[128,768]{1,0:T(8,128)(2,1)S(1)} %fusion.83) | copy-start | bytes 589828
  109.9 115.6 %all-gather.15.cloned.1.call-start = ((), (), s32[]{:S(2)}) async-start(), calls=%async_computation.8 | async-start | bytes 8912896 | tf_op jit(solution)/shard_map/all_gather | solution.py:85
  110.6 190.1 %all-gather.27.cloned.1.call-start = ((), (), s32[]{:S(2)}) async-start(), calls=%async_computation.17 | async-start | bytes 8912896 | tf_op jit(solution)/shard_map/all_gather | solution.py:85
  111.2 265.2 %all-gather.17.cloned.1.call-start = ((), (), s32[]{:S(2)}) async-start(), calls=%async_computation.9 | async-start | bytes 8912896 | tf_op jit(solution)/shard_map/all_gather | solution.py:85
  115.8 41.1 %copy-start.18 = (bf16[128,8,128]{2,0,1:T(8,128)(2,1)}, bf16[128,8,128]{2,0,1:T(8,128)(2,1)S(1)}, u32[]{:S(2)}) copy-start(bf16[128,8,128]{2,0,1:T(8,128)(2,1)S(1)} %get-tuple-element.24) | copy-start | bytes 786436
  115.8 41.1 %copy-start.20 = (bf16[128,8,128]{2,0,1:T(8,128)(2,1)}, bf16[128,8,128]{2,0,1:T(8,128)(2,1)S(1)}, u32[]{:S(2)}) copy-start(bf16[128,8,128]{2,0,1:T(8,128)(2,1)S(1)} %get-tuple-element.25) | copy-start | bytes 786436
  152.1 8.1 copy-start.26
  160.2 65.3 %copy-start.4 = (bf16[1,128,2048]{2,1,0:T(8,128)(2,1)S(1)}, bf16[1,128,2048]{2,1,0:T(8,128)(2,1)}, u32[]{:S(2)}) copy-start(bf16[1,128,2048]{2,1,0:T(8,128)(2,1)} %param.10) | copy-start | bytes 1572868
  161.8 74.1 %copy-start.7 = (bf16[128,8,256]{0,2,1:T(8,128)(2,1)}, bf16[128,8,256]{0,2,1:T(8,128)(2,1)S(1)}, u32[]{:S(2)}) copy-start(bf16[128,8,256]{0,2,1:T(8,128)(2,1)S(1)} %copy.99) | copy-start | bytes 1572868
  234.3 72.5 %copy-start = (f32[128,2048]{1,0:T(8,128)}, f32[128,2048]{1,0:T(8,128)S(1)}, u32[]{:S(2)}) copy-start(f32[128,2048]{1,0:T(8,128)S(1)} %get-tuple-element.46) | copy-start | bytes 3145732
  235.0 71.9 %copy-start.44 = (f32[128]{0:T(128)}, f32[128]{0:T(128)S(1)}, u32[]{:S(2)}) copy-start(f32[128]{0:T(128)S(1)} %get-tuple-element.42) | copy-start | bytes 1540
  235.9 359.6 %reduce-scatter.9.cloned.1.call-start = ((), (), s32[]{:S(2)}) async-start(), calls=%async_computation.11 | async-start | bytes 11141120 | tf_op jit(solution)/shard_map/reduce_scatter | solution.py:89
  306.8 14.6 copy-start.10
  382.7 14.6 copy-start.12
  402.8 17.7 %slice-start.2 = ((s8[8388608]{0:T(1024)(128)(4,1)}), s8[4194304]{0:T(1024)(128)(4,1)S(1)}, s32[]{:S(2)}) async-start(s8[8388608]{0:T(1024)(128)(4,1)} %bitcast.229), calls=%async_computation.22 | async-start | bytes 8388608
  407.5 13.0 slice-start.3
  407.5 13.0 copy-start.54
  439.7 14.6 copy-start.51
  478.0 119.4 %copy-start.1 = (f32[128,2048]{1,0:T(8,128)S(1)}, f32[128,2048]{1,0:T(8,128)}, u32[]{:S(2)}) copy-start(f32[128,2048]{1,0:T(8,128)} %copy-done) | copy-start | bytes 3145732
  478.0 119.4 %copy-start.35 = (f32[1,2048]{1,0:T(1,128)S(1)}, f32[1,2048]{1,0:T(1,128)}, u32[]{:S(2)}) copy-start(f32[1,2048]{1,0:T(1,128)} %copy-done.34) | copy-start | bytes 24580
  478.1 119.4 %copy-start.45 = (f32[128]{0:T(128)S(1)}, f32[128]{0:T(128)}, u32[]{:S(2)}) copy-start(f32[128]{0:T(128)} %copy-done.44) | copy-start | bytes 1540
  478.1 121.3 %copy-start.15 = (bf16[1,128,2048]{2,1,0:T(8,128)(2,1)S(1)}, bf16[1,128,2048]{2,1,0:T(8,128)(2,1)}, u32[]{:S(2)}) copy-start(bf16[1,128,2048]{2,1,0:T(8,128)(2,1)} %param.19) | copy-start | bytes 1572868
  478.1 121.3 %copy-start.49 = (f32[128]{0:T(128)S(1)}, f32[128]{0:T(128)}, u32[]{:S(2)}) copy-start(f32[128]{0:T(128)} %get-tuple-element.41) | copy-start | bytes 1540
  478.1 211.3 %reduce-scatter.11.cloned.1.call-start = ((), (), s32[]{:S(2)}) async-start(), calls=%async_computation.12 | async-start | bytes 2228224 | tf_op jit(solution)/shard_map/reduce_scatter | solution.py:89
  627.9 177.1 %reduce-scatter.7.cloned.1.call-start = ((), (), s32[]{:S(2)}) async-start(), calls=%async_computation.10 | async-start | bytes 10027008 | tf_op jit(solution)/shard_map/reduce_scatter | solution.py:89
  648.3 268.8 %all-gather.21.cloned.1.call-start = ((), (), s32[]{:S(2)}) async-start(), calls=%async_computation.14 | async-start | bytes 12255232 | tf_op jit(solution)/shard_map/all_gather | solution.py:85
  650.4 389.3 %all-gather.19.cloned.1.call-start = ((), (), s32[]{:S(2)}) async-start(), calls=%async_computation.13 | async-start | bytes 14483456 | tf_op jit(solution)/shard_map/all_gather | solution.py:85
  656.7 155.8 %copy-start.5 = (bf16[1,128,2048]{2,1,0:T(8,128)(2,1)S(1)}, bf16[1,128,2048]{2,1,0:T(8,128)(2,1)}, u32[]{:S(2)}) copy-start(bf16[1,128,2048]{2,1,0:T(8,128)(2,1)} %param.10) | copy-start | bytes 1572868
  656.7 155.8 %copy-start.31 = (f32[1,2048]{1,0:T(1,128)S(1)}, f32[1,2048]{1,0:T(1,128)}, u32[]{:S(2)}) copy-start(f32[1,2048]{1,0:T(1,128)} %copy-done.30) | copy-start | bytes 24580
  696.5 402.4 %reduce-scatter.13.cloned.1.call-start = ((), (), s32[]{:S(2)}) async-start(), calls=%async_computation.18 | async-start | bytes 1114112
  805.0 7.6 copy-start.36
  805.0 7.6 copy-start.40
  805.0 14.0 slice-start.10
  805.0 14.0 slice-start.11
  812.6 7.2 copy-start.16
  812.6 13.0 copy-start.13
  818.9 331.8 %all-gather.23.cloned.1.call-start = ((), (), s32[]{:S(2)}) async-start(), calls=%async_computation.15 | async-start | bytes 4456448 | tf_op jit(solution)/shard_map/all_gather | solution.py:85
  820.7 96.4 %all-to-all-start.1 = ((bf16[128,16,128]{2,0,1:T(8,128)(2,1)}), bf16[128,16,128]{2,0,1:T(8,128)(2,1)}, u32[]{:S(2)}, u32[]{:S(2)}) async-start(bf16[128,16,128]{2,0,1:T(8,128)(2,1)} %bitcast.255), calls=%async_computation.4 | async-start | bytes 1048576 | tf_op jit(solution)/shard_map/all_to_all | solution.py:93
  825.2 420.4 %all-gather.25.cloned.1.call-start = ((), (), s32[]{:S(2)}) async-start(), calls=%async_computation.16 | async-start | bytes 18939904 | tf_op jit(solution)/shard_map/all_gather | solution.py:323
  917.1 8.1 copy-start.41
  926.4 50.4 %all-to-all-start = ((bf16[128,16,128]{2,0,1:T(8,128)(2,1)}), bf16[128,16,128]{2,0,1:T(8,128)(2,1)S(1)}, u32[]{:S(2)}, u32[]{:S(2)}) async-start(bf16[128,16,128]{2,0,1:T(8,128)(2,1)} %fusion.112), calls=%async_computation.3 | async-start | bytes 1048576 | tf_op jit(solution)/shard_map/all_to_all | solution.py:93
  930.0 632.8 %all-reduce.3.cloned.1.call-start = ((), (), s32[]{:S(2)}) async-start(), calls=%async_computation.19 | async-start | bytes 27525120 | tf_op jit(solution)/shard_map/psum | solution.py:312
  930.0 12.9 copy-start.52
  930.1 24.8 %slice-start.4 = ((s8[8388608]{0:T(1024)(128)(4,1)}), s8[4194304]{0:T(1024)(128)(4,1)S(1)}, s32[]{:S(2)}) async-start(s8[8388608]{0:T(1024)(128)(4,1)} %bitcast.231), calls=%async_computation.24 | async-start | bytes 8388608
  942.9 12.0 slice-start.5
  954.9 17.2 %slice-start.7 = ((s8[11534336]{0:T(1024)(128)(4,1)}), s8[3145728]{0:T(1024)(128)(4,1)S(1)}, s32[]{:S(2)}) async-start(s8[11534336]{0:T(1024)(128)(4,1)} %bitcast.236), calls=%async_computation.27 | async-start | bytes 6291456
  954.9 17.2 %slice-start.8 = ((s8[11534336]{0:T(1024)(128)(4,1)}), s8[4194304]{0:T(1024)(128)(4,1)S(1)}, s32[]{:S(2)}) async-start(s8[11534336]{0:T(1024)(128)(4,1)} %bitcast.236), calls=%async_computation.28 | async-start | bytes 8388608
  976.8 71.6 %copy-start.28 = (bf16[128,16,128]{2,0,1:T(8,128)(2,1)}, bf16[128,16,128]{2,0,1:T(8,128)(2,1)S(1)}, u32[]{:S(2)}) copy-start(bf16[128,16,128]{2,0,1:T(8,128)(2,1)S(1)} %all-to-all-done) | copy-start | bytes 1572868
  1039.7 7.7 copy-start.29
  1053.5 8.8 copy-start.2
  1053.5 8.8 copy-start.32
  1053.5 11.1 copy-start.50
  1053.5 11.1 copy-start.17
  1053.5 11.1 copy-start.48
  1257.8 12.4 slice-start.6
  1283.0 9.8 slice-start
  1284.0 8.8 slice-start.1
  (19 other events, 80.1 us)
Sparse Core Ops, SparseCore 0:
  10.3 90.5 all-gather.10
  110.0 39.5 all-gather.12
  151.8 73.6 all-gather.14
  227.5 73.1 all-gather.26
  303.2 73.1 all-gather.16
  478.2 117.2 reduce-scatter.8
  628.0 61.2 reduce-scatter.10
  694.6 110.3 reduce-scatter.6
  807.7 109.3 all-gather.20
  919.1 120.5 all-gather.18
  1043.3 55.5 reduce-scatter.12
  1101.1 49.5 all-gather.22
  1153.0 92.5 all-gather.24
  1248.7 314.0 all-reduce.2

commit v2 on v1

--- a/solution.py
+++ b/solution.py
@@ -1,8 +1,11 @@
+import functools
 import math
 
 import jax
 import jax.numpy as jnp
 from jax import lax
+from jax.experimental import pallas as pl
+from jax.experimental.pallas import tpu as pltpu
 from jax.sharding import PartitionSpec as P
 
 MODEL_WIDTH = 2048
@@ -18,6 +21,7 @@
 epsilon = 1e-06
 bf16 = jnp.bfloat16
 f32 = jnp.float32
+MESH = pl.DeviceIdType.MESH
 
 
 def matrix_product(former, latter):
@@ -89,8 +93,326 @@
     return lax.psum_scatter(partial.astype(bf16), "fsdp", scatter_dimension=0, tiled=True).astype(f32)
 
 
+def both_loops(partial):
+    shares = lax.all_gather(partial.astype(bf16), "loop", axis=0)
+    return shares[0].astype(f32) + shares[1].astype(f32)
+
+
 def turn(block):
     return lax.all_to_all(block, "fsdp", split_axis=1, concat_axis=0, tiled=True)
+
+
+def chip_at(q, chips):
+    return jnp.where(q < 4, 2 * q, 15 - 2 * q) if chips == 8 else q
+
+def ring_place(chip, chips):
+    return jnp.where(chip % 2 == 0, chip // 2, 7 - chip // 2) if chips == 8 else chip
+
+def ring_neighbours(chips):
+    me = lax.axis_index("fsdp")
+    core = me % 2
+    p = ring_place(me // 2, chips)
+    def device(shift, c):
+        return chip_at((p + shift + chips) % chips, chips) * 2 + c
+    return core, device
+
+def meet(devices):
+    barrier = pltpu.get_barrier_semaphore()
+    for d in devices:
+        pl.semaphore_signal(barrier, inc=1, device_id={"fsdp": d}, device_id_type=MESH)
+    pl.semaphore_wait(barrier, len(devices))
+
+def gather_kernel(chips, x_ref, o_ref, own_sem, ring_send, ring_recv, side_send, side_recv):
+    core, device = ring_neighbours(chips)
+    rows = x_ref.shape[0]
+    reach = chips // 2
+    ways = (device(1, core), device(-1, core))
+    side = device(0, 1 - core)
+    meet((*ways, side))
+
+    def span(way, hops):
+        return (way * (rows // 2), rows // 2) if hops == reach else (0, rows)
+
+    def at(way, hops, c, part):
+        origin = device(-hops if way == 0 else hops, c)
+        return o_ref.at[pl.ds(pl.multiple_of(origin * rows + part[0], 8), part[1])]
+
+    def hop(way, hops):
+        part = span(way, hops)
+        here = at(way, hops - 1, core, part)
+        src = x_ref.at[pl.ds(part[0], part[1])] if hops == 1 else here
+        return pltpu.make_async_remote_copy(src, here, ring_send.at[way, hops - 1], ring_recv.at[way, hops - 1], device_id={"fsdp": ways[way]}, device_id_type=MESH)
+
+    def arriving(way, hops):
+        here = at(way, hops, core, span(way, hops))
+        return pltpu.make_async_remote_copy(here, here, ring_send.at[way, hops - 1], ring_recv.at[way, hops - 1], device_id={"fsdp": ways[way]}, device_id_type=MESH)
+
+    def across(way, hops, c):
+        part = span(way, hops) if hops else (0, rows)
+        there = at(way, hops, c, part)
+        src = there if hops else x_ref
+        return pltpu.make_async_remote_copy(src, there, side_send.at[way, hops], side_recv.at[way, hops], device_id={"fsdp": side}, device_id_type=MESH)
+
+    for way in (0, 1):
+        hop(way, 1).start()
+    across(0, 0, core).start()
+    own = pltpu.make_async_copy(x_ref, at(0, 0, core, (0, rows)), own_sem)
+    own.start()
+    for hops in range(1, reach + 1):
+        for way in (0, 1):
+            arriving(way, hops).wait_recv()
+            if hops < reach:
+                hop(way, hops + 1).start()
+            across(way, hops, core).start()
+    across(0, 0, 1 - core).wait_recv()
+    across(0, 0, core).wait_send()
+    for hops in range(1, reach + 1):
+        for way in (0, 1):
+            across(way, hops, 1 - core).wait_recv()
+            across(way, hops, core).wait_send()
+            hop(way, hops).wait_send()
+    own.wait()
+
+def busy(us):
+    return pl.CostEstimate(flops=0, bytes_accessed=int(us * 3.0e6), transcendentals=0)
+
+
+def ring_gather(block, ident):
+    size = lax.axis_size("fsdp")
+    chips = size // 2
+    rows, columns = block.shape
+    pair = pltpu.SemaphoreType.DMA((2, chips // 2))
+    sides = pltpu.SemaphoreType.DMA((2, chips // 2 + 1))
+    return pl.pallas_call(
+        functools.partial(gather_kernel, chips),
+        out_shape=jax.ShapeDtypeStruct((size * rows, columns), block.dtype),
+        in_specs=[pl.BlockSpec(memory_space=pl.ANY)],
+        out_specs=pl.BlockSpec(memory_space=pl.ANY),
+        scratch_shapes=[pltpu.SemaphoreType.DMA, pair, pair, sides, sides],
+        compiler_params=pltpu.CompilerParams(collective_id=ident, has_side_effects=True),
+        cost_estimate=busy(size * rows * columns * 2 / 180e3 + 10),
+        name="ring_gather",
+    )(block)
+
+def scatter_kernel(chips, x_ref, o_ref, side_buf, ring_buf, send_buf, side_send, side_recv, ring_send, ring_recv):
+    core, device = ring_neighbours(chips)
+    rows, columns = o_ref.shape
+    reach = chips // 2
+    half = columns // 2
+    ways = (device(1, core), device(-1, core))
+    side = device(0, 1 - core)
+    meet((*ways, side))
+
+    def shift(way, hops):
+        return (hops if way == 0 else chips - hops) % chips
+
+    def across(target, c):
+        there = pl.ds(pl.multiple_of(device(target, c) * rows, 16), rows)
+        return pltpu.make_async_remote_copy(x_ref.at[there], side_buf.at[target], side_send.at[target], side_recv.at[target], device_id={"fsdp": side}, device_id_type=MESH)
+
+    def hop(way, step):
+        cols = pl.ds(way * half, half) if step == 0 else pl.ds(0, columns)
+        return pltpu.make_async_remote_copy(send_buf.at[way, step, :, cols], ring_buf.at[way, step, :, cols], ring_send.at[way, step], ring_recv.at[way, step], device_id={"fsdp": ways[way]}, device_id_type=MESH)
+
+    order = [reach] + [shift(way, hops) for hops in range(reach - 1, 0, -1) for way in (0, 1)] + [0]
+    for target in order:
+        across(target, 1 - core).start()
+    tile = 16
+
+    def add(target, incoming, store):
+        first = pl.multiple_of(device(target, core) * rows, 16)
+        @pl.loop(0, rows // tile)
+        def _(i):
+            here = pl.ds(pl.multiple_of(i * tile, tile), tile)
+            total = x_ref[pl.ds(pl.multiple_of(first + i * tile, tile), tile), :].astype(f32) + side_buf[target, here, :].astype(f32)
+            store(here, total, [(way, step, ring_buf[way, step, here, pl.ds(way * half, half) if step == 0 else pl.ds(0, columns)].astype(f32)) for way, step in incoming])
+
+    for step in range(reach):
+        hops = reach - step
+        for way in (0, 1):
+            target = shift(way, hops)
+            if step or way == 0:
+                across(target, core).wait_recv()
+            if step:
+                hop(way, step - 1).wait_recv()
+
+            def store(here, total, more, way=way, step=step):
+                if step == 0:
+                    send_buf[way, step, here, pl.ds(way * half, half)] = total[:, way * half:(way + 1) * half].astype(bf16)
+                elif step == 1:
+                    other = total[:, (1 - way) * half:(2 - way) * half]
+                    send_buf[way, step, here, pl.ds((1 - way) * half, half)] = other.astype(bf16)
+                    send_buf[way, step, here, pl.ds(way * half, half)] = (total[:, way * half:(way + 1) * half] + more[0][2]).astype(bf16)
+                else:
+                    send_buf[way, step, here, :] = (total + more[0][2]).astype(bf16)
+            add(target, [(way, step - 1)] if step else [], store)
+            hop(way, step).start()
+    across(0, core).wait_recv()
+    for way in (0, 1):
+        hop(way, reach - 1).wait_recv()
+
+    def last(here, total, more):
+        o_ref[here, :] = total + (more[0][2] + more[1][2])
+    add(0, [(0, reach - 1), (1, reach - 1)], last)
+    for target in order:
+        across(target, 1 - core).wait_send()
+    for step in range(reach):
+        for way in (0, 1):
+            hop(way, step).wait_send()
+
+def ring_scatter(partial, ident):
+    size = lax.axis_size("fsdp")
+    if size != 16:
+        return scatter_rows(partial)
+    partial = partial.astype(bf16)
+    chips = size // 2
+    rows, columns = partial.shape[0] // size, partial.shape[1]
+    pair = pltpu.SemaphoreType.DMA((2, chips // 2))
+    sides = pltpu.SemaphoreType.DMA((chips,))
+    return pl.pallas_call(
+        functools.partial(scatter_kernel, chips),
+        out_shape=jax.ShapeDtypeStruct((rows, columns), f32),
+        in_specs=[pl.BlockSpec(memory_space=pltpu.VMEM)],
+        out_specs=pl.BlockSpec(memory_space=pltpu.VMEM),
+        scratch_shapes=[
+            pltpu.VMEM((chips, rows, columns), bf16),
+            pltpu.VMEM((2, chips // 2, rows, columns), bf16),
+            pltpu.VMEM((2, chips // 2, rows, columns), bf16),
+            sides, sides, pair, pair],
+        compiler_params=pltpu.CompilerParams(collective_id=ident, has_side_effects=True, vmem_limit_bytes=48 << 20),
+        cost_estimate=busy(size * rows * columns * 2 / 180e3 + 10),
+        name="ring_scatter",
+    )(partial)
+
+
+def place_kernel(size, chunk, own_count, mid_ref, near_ref, far_ref, o_ref, send_sem, recv_sem, own_sem):
+    me = lax.axis_index("fsdp")
+    hidden = HIDDEN_COUNT // size
+    width = MODEL_WIDTH // size
+    sections = (
+        (0, PROJECT_COLUMNS, width),
+        (width, GATE_START, hidden),
+        (width + hidden, GATE_START + HIDDEN_COUNT, hidden),
+    )
+    barrier = pltpu.get_barrier_semaphore()
+
+    def greet(i, carry):
+        other = (me + i) % size
+        pl.semaphore_signal(barrier, inc=1, device_id={"fsdp": other}, device_id_type=MESH)
+        return carry
+
+    lax.fori_loop(1, size, greet, 0)
+    pl.semaphore_wait(barrier, size - 1)
+
+    def rows(ref, first):
+        return ref.at[pl.ds(pl.multiple_of(first, 8), chunk)]
+
+    def remote(source, first, owner, sent=0):
+        return pltpu.make_async_remote_copy(
+            source,
+            rows(o_ref, first),
+            send_sem.at[sent],
+            recv_sem.at[first // chunk],
+            device_id={"fsdp": owner},
+            device_id_type=MESH,
+        )
+
+    def local(source, first):
+        return pltpu.make_async_copy(source, rows(o_ref, first), own_sem.at[first // chunk])
+
+    for base, start, length in sections:
+
+        def send(j, carry, base=base, start=start, length=length):
+            column = start + me * length + j * chunk
+            owner = column // own_count
+            first = column - owner * own_count
+            source = rows(mid_ref, base + j * chunk)
+
+            @pl.when(owner != me)
+            def _():
+                remote(source, first, owner, base // chunk + j).start()
+
+            @pl.when(owner == me)
+            def _():
+                local(source, first).start()
+
+            return carry
+
+        lax.fori_loop(0, length // chunk, send, 0)
+
+    def fill(j, carry):
+        column = me * own_count + j * chunk
+
+        @pl.when(column < PROJECT_COLUMNS)
+        def _():
+            local(rows(near_ref, column), j * chunk).start()
+
+        @pl.when(column >= GATE_START + 2 * HIDDEN_COUNT)
+        def _():
+            local(rows(far_ref, column - (GATE_START + 2 * HIDDEN_COUNT)), j * chunk).start()
+
+        return carry
+
+    lax.fori_loop(0, own_count // chunk, fill, 0)
+
+    def arrive(j, carry):
+        column = me * own_count + j * chunk
+        here = rows(o_ref, j * chunk)
+        away = 0
+        for _, start, length in sections:
+            inside = (column >= start) & (column < start + length * size)
+            away = away + (inside & ((column - start) // length != me)).astype(jnp.int32)
+
+        @pl.when(away > 0)
+        def _():
+            remote(here, j * chunk, (me + 1) % size).wait_recv()
+
+        @pl.when(away == 0)
+        def _():
+            local(rows(near_ref, 0), j * chunk).wait()
+
+        return carry
+
+    lax.fori_loop(0, own_count // chunk, arrive, 0)
+    for base, start, length in sections:
+
+        def sent(j, carry, base=base, start=start, length=length):
+            column = start + me * length + j * chunk
+            owner = column // own_count
+
+            @pl.when(owner != me)
+            def _():
+                remote(
+                    rows(mid_ref, base + j * chunk),
+                    column - owner * own_count,
+                    owner,
+                    base // chunk + j,
+                ).wait_send()
+
+            return carry
+
+        lax.fori_loop(0, length // chunk, sent, 0)
+
+
+def place_columns(middle, near, far, ident):
+    size = lax.axis_size("fsdp")
+    own_count = ADAPTER_COLUMNS // size
+    chunk = math.gcd(own_count, MODEL_WIDTH // size, HIDDEN_COUNT // size, PROJECT_COLUMNS, GATE_START)
+    anywhere = pl.BlockSpec(memory_space=pl.ANY)
+    return pl.pallas_call(
+        functools.partial(place_kernel, size, chunk, own_count),
+        out_shape=jax.ShapeDtypeStruct((own_count, ADAPTER_RANK), f32),
+        in_specs=[anywhere] * 3,
+        out_specs=anywhere,
+        scratch_shapes=[
+            pltpu.SemaphoreType.DMA((middle.shape[0] // chunk,)),
+            pltpu.SemaphoreType.DMA((own_count // chunk,)),
+            pltpu.SemaphoreType.DMA((own_count // chunk,)),
+        ],
+        compiler_params=pltpu.CompilerParams(collective_id=ident, has_side_effects=True),
+        cost_estimate=busy(30),
+        name="place_columns",
+    )(middle, near, far)
 
 
 def per_device(
@@ -146,7 +468,7 @@
     hidden_state = hidden_input[0].astype(f32)
     scale_one = rms_scale(hidden_state)
     normalized = (hidden_state * scale_one * gains[0]).astype(bf16)
-    proj_in = gather_rows(input_proj_weight)
+    proj_in = ring_gather(input_proj_weight, 0)
     proj_out = gather_rows(output_proj_weight)
     lora_qkv = matrix_product(normalized, narrow_projection).astype(bf16)
     projected = matrix_product(normalized, proj_in)
@@ -160,7 +482,7 @@
     ).astype(bf16)
     query_rot = rotate(query_pre, position_own, 1.0).astype(bf16)
     key_rot = rotate(key_pre, position_own, 1.0).astype(bf16)
-    keys_all = gather_rows(jnp.concatenate([key_rot, value_local], axis=1))
+    keys_all = ring_gather(jnp.concatenate([key_rot, value_local], axis=1), 1)
     key_rows, value_rows = keys_all[:, :HEAD_WIDTH], keys_all[:, HEAD_WIDTH:]
     query_heads = query_rot.reshape(tokens_dev, HEADS, HEAD_WIDTH)
     scores = scores_of(query_heads, key_rows, allowed, scaling)
@@ -184,7 +506,7 @@
     normed_two = (middle * scale_two * gains[1]).astype(bf16)
 
     grad_all = gather_rows(output_gradient[0])
-    two_all = gather_rows(normed_two)
+    two_all = ring_gather(normed_two, 2)
     weight_gate = feedforward_weight[:, 0, :]
     weight_up = feedforward_weight[:, 1, :]
     weight_down = feedforward_weight[:, 2, :]
@@ -204,23 +526,30 @@
         ],
         axis=1,
     )
-    back_own = scatter_rows(back_part)
+    ffn_shares = [
+        outer_product_rows(former, latter).astype(bf16)
+        for former, latter in ((units, grad_all), (gate_grad, two_all), (up_grad, two_all))
+    ]
     out_part = jnp.concatenate(
         [matrix_product(units, weight_down), matrix_product(units, narrow_down)], axis=1
     )
+    ffn_shares, out_part, back_part = lax.optimization_barrier(
+        (ffn_shares, out_part.astype(bf16), back_part.astype(bf16))
+    )
+    down_total, gate_total, up_total = [both_loops(share) for share in ffn_shares]
+    back_own = ring_scatter(back_part, 3)
     out_own = scatter_rows(out_part)
-    ffn_grad = jnp.stack(
+    ffn_sum = jnp.stack(
         [
-            outer_product_rows(gate_grad, two_all),
-            outer_product_rows(up_grad, two_all),
-            outer_product_rows(units, grad_all),
+            gate_total,
+            up_total,
+            down_total,
         ],
         axis=1,
-    ).astype(bf16)
-    ffn_sum = lax.psum(ffn_grad, "loop").astype(f32)
+    )
     down_own = outer_product_rows(units, hd_grad)
-    gate_piece = outer_product_rows(lora_gate, gate_grad)
-    up_piece = outer_product_rows(lora_up, up_grad)
+    gate_piece = outer_product_rows(gate_grad, lora_gate)
+    up_piece = outer_product_rows(up_grad, lora_up)
 
     lora_hd = out_own[:, MODEL_WIDTH:].astype(bf16)
     hidden_out = (middle + out_own[:, :MODEL_WIDTH] + matrix_product(lora_hd, widen_down)).astype(bf16)
@@ -256,7 +585,7 @@
         jnp.einsum("thu,thd->ud", score_grad, query_heads, preferred_element_type=f32) * scaling
     )
     value_part = jnp.einsum("thu,thd->ud", probs_low, heads_grad, preferred_element_type=f32)
-    pair_grad = scatter_rows(jnp.concatenate([key_part, value_part], axis=1))
+    pair_grad = ring_scatter(jnp.concatenate([key_part, value_part], axis=1), 4)
     query_grad = rotate(
         query_rot_grad.reshape(tokens_dev, QUERY_WIDTH), position_own, -1.0
     ).astype(bf16)
@@ -294,12 +623,19 @@
     lora_qkv_all = attended_all[:, QUERY_WIDTH:]
     attended_all = attended_all[:, :QUERY_WIDTH]
     lora_out_all = matrix_product(attended_all, narrow_output).astype(bf16)
-    low_all = gather_rows(
-        jnp.concatenate([lora_out_grad, gate_low, up_low, lora_hd], axis=1)
-    )
-    proj_all = gather_rows(jnp.concatenate([proj_grad, lora_qkv_grad], axis=1))
-    qkv_low_all = proj_all[:, PROJECT_COLUMNS:]
+    proj_all = ring_gather(
+        jnp.concatenate([proj_grad, lora_out_grad, gate_low, up_low, lora_hd], axis=1), 5
+    )
+    low_all = proj_all[:, PROJECT_COLUMNS:]
     proj_all = proj_all[:, :PROJECT_COLUMNS]
+    qkv_low_all = jnp.concatenate(
+        [
+            times_transposed(proj_all[:, :QUERY_WIDTH], widen_query),
+            times_transposed(proj_all[:, QUERY_WIDTH : QUERY_WIDTH + HEAD_WIDTH], widen_key),
+            times_transposed(proj_all[:, QUERY_WIDTH + HEAD_WIDTH :], widen_value),
+        ],
+        axis=1,
+    ).astype(bf16)
     normed_turn = turn(normalized)
     branch_turn = turn(branch_grad)
     column = place * width_own
@@ -308,8 +644,8 @@
     attn_part = jnp.concatenate(
         [outer_product_rows(normed_turn, proj_all), outer_product_rows(branch_turn, attended_all)],
         axis=1,
-    ).astype(bf16)
-    attn_sum = lax.psum(attn_part, "loop").astype(f32)
+    )
+    attn_sum = both_loops(attn_part)
     squeeze_own = jnp.concatenate(
         [
             outer_product_rows(normed_turn, qkv_low_all),
@@ -318,32 +654,21 @@
         ],
         axis=1,
     )
-    out_piece = outer_product_rows(lora_out_all, branch_turn)
-    down_piece = outer_product_rows(low_all[:, 3 * rank :], grad_all)
-    pieces = lax.all_gather(
-        jnp.concatenate([out_piece, gate_piece, up_piece], axis=1).astype(bf16), "fsdp", axis=0
-    )
-
-    def laid(first, last):
-        return pieces[:, :, first:last].transpose(1, 0, 2).reshape(rank, -1)
-
-    expand_all = jnp.concatenate(
+    out_piece = outer_product_rows(branch_turn, lora_out_all)
+    near = jnp.concatenate(
         [
-            outer_product_rows(lora_qkv_all[:, :rank], proj_all[:, :QUERY_WIDTH]).astype(bf16),
+            outer_product_rows(proj_all[:, :QUERY_WIDTH], lora_qkv_all[:, :rank]),
             outer_product_rows(
-                lora_qkv_all[:, rank : 2 * rank], proj_all[:, QUERY_WIDTH : QUERY_WIDTH + HEAD_WIDTH]
-            ).astype(bf16),
-            outer_product_rows(
-                lora_qkv_all[:, 2 * rank :], proj_all[:, QUERY_WIDTH + HEAD_WIDTH :]
-            ).astype(bf16),
-            laid(0, width_own),
-            laid(width_own, width_own + hidden_own),
-            laid(width_own + hidden_own, width_own + 2 * hidden_own),
-            down_piece.astype(bf16),
+                proj_all[:, QUERY_WIDTH : QUERY_WIDTH + HEAD_WIDTH], lora_qkv_all[:, rank : 2 * rank]
+            ),
+            outer_product_rows(proj_all[:, QUERY_WIDTH + HEAD_WIDTH :], lora_qkv_all[:, 2 * rank :]),
         ],
-        axis=1,
-    )
-    expand_own = lax.dynamic_slice_in_dim(expand_all, place * columns_own, columns_own, 1).astype(f32)
+        axis=0,
+    )
+    far = outer_product_rows(grad_all, low_all[:, 3 * rank :])
+    expand_own = place_columns(
+        jnp.concatenate([out_piece, gate_piece, up_piece], axis=0), near, far, 6
+    ).T
     return (
         hidden_out[None],
         input_grad[None],

time: 1590 us -> 1390 us (0.87)
  waiting for transfers between devices: 1110 us -> 488 us
  Pallas kernels: 0 us -> 435 us
  local copies, waits for them, and re-layouts: 82.3 us -> 30.5 us
  other arithmetic: 64.5 us -> 91.6 us
    pallas_call x0 -> x7, Pallas kernels: none -> 435 us  [the longest x4 268 us: ring_gather(): pl.pallas_call(functools.partial(gather_kernel, chips), out_shape=jax.Sha...]
    all_gather x8 -> x3, waiting for transfers between devices: 489 us -> 92.8 us  [gather_rows(): return lax.all_gather(block, 'fsdp', axis=0, tiled=True)]
    psum x1 -> x0, waiting for transfers between devices: 262 us -> none  [per_device(): attn_sum = lax.psum(attn_part, 'loop').astype(f32)]
    all_gather x1 -> x4, waiting for transfers between devices: 66.2 us -> 267 us  [both_loops(): shares = lax.all_gather(partial.astype(bf16), 'loop', axis=0)]
    reduce_scatter x3 -> x1, waiting for transfers between devices: 258 us -> 90.8 us  [scatter_rows(): lax.psum_scatter(partial.astype(bf16), 'fsdp', scatter_dimension=0, tiled...]
    unnamed x144 -> x151, local copies, waits for them, and re-layouts: 50.5 us -> 14.2 us
    add x0 -> x4, other arithmetic: none -> 30 us  [both_loops(): return shares[0].astype(f32) + shares[1].astype(f32)]
    dot_general x17 -> x20, matrix products: 90.9 us -> 105 us  [times_transposed(): lax.dot_general(former, latter, (((1,), (1,)), ((), ())), preferred_eleme...]
  transfers between devices with their start and end apart: 16 -> 11, of which waited for: 14 -> 6; matrix products, arithmetic and copies ran while one was open for 18% -> 16% of each run, Pallas kernels for 0% -> 25%
where the time goes in v2:
time: 1390 us; the launch traced here: 1380 us
  waiting for transfers between devices  488 us (35%)
  Pallas kernels  435 us (31%)
  matrix products  307 us (22%)
  other arithmetic  91.6 us (7%)
  local copies, waits for them, and re-layouts  30.5 us (2%)
  between operations  15.6 us (1%)
    pallas_call x4, Pallas kernels, ring_gather(): pl.pallas_call(functools.partial(gather_kernel, chips), out_shape=jax.Sha...  268 us
    all_gather x4, waiting for transfers between devices, both_loops(): shares = lax.all_gather(partial.astype(bf16), 'loop', axis=0)  267 us
    dot_general x20, matrix products, times_transposed(): lax.dot_general(former, latter, (((1,), (1,)), ((), ())), preferred_eleme...  105 us
    dot_general x16, matrix products, outer_product_rows(): lax.dot_general(former, latter, (((0,), (0,)), ((), ())), preferred_eleme...  93.1 us
    all_gather x3, waiting for transfers between devices, gather_rows(): return lax.all_gather(block, 'fsdp', axis=0, tiled=True)  92.8 us
    reduce_scatter x1, waiting for transfers between devices, scatter_rows(): lax.psum_scatter(partial.astype(bf16), 'fsdp', scatter_dimension=0, tiled...  90.8 us
    dot_general x16, matrix products, matrix_product(): return jnp.dot(former, latter, preferred_element_type=f32)  86.9 us
    pallas_call x1, Pallas kernels, place_columns(): pl.pallas_call(functools.partial(place_kernel, size, chunk, own_count), o...  84.5 us
  transfers between devices with their start and end apart: 11, of which 6 were waited for; matrix products, arithmetic and copies ran while one was open for 16% of the time, Pallas kernels for 25%

profile of v2, /device:TPU:0, one launch (start us, length us, event | category | flops | bytes accessed | tf_op | source)
XLA Modules:
  0.0 1381.3 jit_solution(805000482991715773)
XLA Ops:
  11.3 108.7 %ring_gather.4 = bf16[2048,2560]{1,0:T(8,128)(2,1)} custom-call(bf16[128,2560]{1,0:T(8,128)(2,1)} %x_ref.1), custom_call_target="tpu_custom_call" | custom-call | bytes 204762672 | tf_op jit(solution)/shard_map/ring_gather/pallas_call | solution.py:186
  120.1 2.5 fusion.92
  123.9 5.5 fusion.175
  132.6 31.6 %ring_gather.5 = bf16[2048,512]{1,0:T(8,128)(2,1)} custom-call(bf16[128,512]{1,0:T(8,128)(2,1)} %pad_maximum_fusion.11.x_ref), custom_call_target="tpu_custom_call" | custom-call | bytes 64952532 | tf_op jit(solution)/shard_map/ring_gather/pallas_call | solution.py:186
  168.0 4.7 fusion.117
  172.7 9.2 fusion.232
  181.9 3.3 copy-done.8
  186.8 7.3 convolution_add_fusion.9
  194.1 2.5 multiply_reduce_fusion.3
  198.1 49.9 %ring_gather.6 = bf16[2048,2048]{1,0:T(8,128)(2,1)} custom-call(bf16[128,2048]{1,0:T(8,128)(2,1)} %multiply_convert_fusion.3.x_ref), custom_call_target="tpu_custom_call" | custom-call | bytes 169810128 | tf_op jit(solution)/shard_map/ring_gather/pallas_call | solution.py:186
  248.0 6.1 convolution_convert_fusion.9
  254.2 14.5 %fusion.26 = f32[2048,1024]{1,0:T(8,128)S(1)} fusion(bf16[2048,2048]{1,0:T(8,128)(2,1)S(1)} %copy-done.7, bf16[1024,3,2048]{2,0,1:T(8,128)(2,1)} %param.15), kind=kOutput, calls=%fused_computation.46 | convolution fusion | flops 8589934592 | bytes 20971520 | tf_op jit(solution)/shard_map/dot_general | solution.py:32
  268.7 5.6 convolution_add_fusion.1
  274.3 3.6 convolution_convert_fusion.10
  277.9 14.5 %fusion.30 = f32[2048,1024]{1,0:T(8,128)S(1)} fusion(bf16[2048,2048]{1,0:T(8,128)(2,1)S(1)} %copy-done.7, bf16[1024,3,2048]{2,0,1:T(8,128)(2,1)} %param.15), kind=kOutput, calls=%fused_computation.50 | convolution fusion | flops 8589934592 | bytes 20971520 | tf_op jit(solution)/shard_map/dot_general | solution.py:32
  292.4 5.7 convolution_add_fusion.2
  298.1 6.2 fusion.69
  304.3 13.7 fusion.14
  317.9 15.3 %multiply_convert_fusion.1 = (bf16[2048,1024]{1,0:T(8,128)(2,1)}, bf16[2048,1024]{1,0:T(8,128)(2,1)}, bf16[2048,1024]{1,0:T(8,128)(2,1)}) fusion(f32[2048,1024]{1,0:T(8,128)} %convolution_add_fusion.2, f32[2048,1024]{1,0:T(8,128)S(1)} %bitcast.227, f32[2048,1024]{1,0:T(8,128)} %fusion.14, bf16[2048,256]{1,0:T(8,128)(2,1)S(1)} %fusion.69, ...), kind=kOutput, calls=%fused_computation.29 | convolution fusion | flops 1130364928 | bytes 39321604 | tf_op jit(solution)/shard_map/dot_general | solution.py:32
  333.3 15.8 %fusion.28 = f32[2048,2048]{1,0:T(8,128)} fusion(bf16[2048,1024]{1,0:T(8,128)(2,1)} %get-tuple-element.28, bf16[1024,3,2048]{2,0,1:T(8,128)(2,1)} %param.15), kind=kOutput, calls=%fused_computation.48 | convolution fusion | flops 8589934592 | bytes 25165824 | tf_op jit(solution)/shard_map/dot_general | solution.py:28
  349.1 2.6 convolution_convert_fusion.6
  351.7 13.2 convolution_convert_fusion
  364.9 2.5 convolution_convert_fusion.7
  367.4 2.6 convolution_convert_fusion.5
  370.0 11.0 convolution_convert_fusion.1
  381.0 14.2 %convolution_convert_fusion.2 = bf16[1024,2048]{1,0:T(8,128)(2,1)} fusion(bf16[2048,1024]{1,0:T(8,128)(2,1)} %get-tuple-element.28, bf16[2048,2048]{1,0:T(8,128)(2,1)} %ring_gather.6), kind=kOutput, calls=%fused_computation.58 | convolution fusion | flops 8592031744 | bytes 16777216 | tf_op jit(solution)/shard_map/dot_general | solution.py:36
  395.2 16.3 %add_convert_fusion = bf16[2048,2048]{1,0:T(8,128)(2,1)} fusion(f32[2048,2048]{1,0:T(8,128)} %fusion.28, bf16[2048,1024]{1,0:T(8,128)(2,1)} %get-tuple-element.27, bf16[1024,3,2048]{2,0,1:T(8,128)(2,1)} %param.15), kind=kOutput, calls=%fused_computation.2 | convolution fusion | flops 8598323200 | bytes 33554432 | tf_op jit(solution)/shard_map/dot_general | solution.py:28
  411.6 8.9 pad_maximum_fusion.2
  420.5 10.5 pad_maximum_fusion.1.x_ref
  431.0 13.3 fusion.35
  444.3 63.7 %ring_scatter.2 = f32[128,2560]{1,0:T(8,128)S(1)} custom-call(bf16[2048,2560]{1,0:T(8,128)(2,1)} %pad_maximum_fusion.1.x_ref), custom_call_target="tpu_custom_call" | custom-call | bytes 204762672 | tf_op jit(solution)/shard_map/ring_scatter/pallas_call | solution.py:272
  518.6 5.4 multiply_reduce_fusion
  524.0 6.1 fusion.65
  535.4 3.6 convolution_multiply_fusion
  539.2 19.0 %ring_scatter.3 = f32[128,512]{1,0:T(8,128)S(1)} custom-call(bf16[2048,512]{1,0:T(8,128)(2,1)S(1)} %pad_maximum_fusion.5.x_ref), custom_call_target="tpu_custom_call" | custom-call | bytes 64952532 | tf_op jit(solution)/shard_map/ring_scatter/pallas_call | solution.py:272
  563.2 3.4 fusion.149
  566.7 4.1 fusion.106
  578.3 3.7 all-to-all-start.1
  584.7 5.0 fusion.235
  589.7 2.3 fusion.236
  595.5 33.2 %reduce-scatter.7.cloned.1.call-done = f32[128,2]{1,0:T(8,128)} async-done(((f32[2048,2]{1,0:T(8,128)}), f32[128,2]{1,0:T(8,128)}) %reduce-scatter.7.cloned.1.call-update) | async-done | bytes 1040
  629.6 4.9 psum.7
  635.1 92.8 %all-gather.14.cloned.1.call-done = bf16[2048,2816]{0,1:T(8,128)(2,1)} async-done(((bf16[128,2816]{0,1:T(8,128)(2,1)}), bf16[2048,2816]{0,1:T(8,128)(2,1)}) %all-gather.14.cloned.1.call-update) | async-done | bytes 11534352 | tf_op jit(solution)/shard_map/all_gather | solution.py:89
  727.9 9.3 slice.294
  737.3 4.2 all-to-all-start
  741.8 7.6 fusion.96
  750.9 6.5 fusion.78
  757.4 74.2 %all-gather.24.cloned.1.call-done = bf16[2048,2048]{1,0:T(8,128)(2,1)} async-done(((bf16[1024,2048]{1,0:T(8,128)(2,1)}), bf16[2048,2048]{1,0:T(8,128)(2,1)}) %all-gather.24.cloned.1.call-update) | async-done | bytes 8388624 | tf_op jit(solution)/shard_map/all_gather | solution.py:97
  831.6 9.1 add_bitcast_fusion
  840.7 96.4 %all-gather.22.cloned.1.call-done = bf16[2048,2048]{1,0:T(8,128)(2,1)} async-done(((bf16[1024,2048]{1,0:T(8,128)(2,1)}), bf16[2048,2048]{1,0:T(8,128)(2,1)}) %all-gather.22.cloned.1.call-update) | async-done | bytes 8388624 | tf_op jit(solution)/shard_map/all_gather | solution.py:97
  937.1 9.1 add_bitcast_fusion.1
  946.2 96.6 %all-gather.20.cloned.1.call-done = bf16[2048,2048]{1,0:T(8,128)(2,1)} async-done(((bf16[1024,2048]{1,0:T(8,128)(2,1)}), bf16[2048,2048]{1,0:T(8,128)(2,1)}) %all-gather.20.cloned.1.call-update) | async-done | bytes 8388624 | tf_op jit(solution)/shard_map/all_gather | solution.py:97
  1042.8 9.9 add_bitcast_fusion.2
  1054.1 13.9 %pad_maximum_fusion = f32[1024,3,2048]{2,0,1:T(8,128)} fusion(f32[1024,1,2048]{2,0,1:T(8,128)S(1)} %copy-done, f32[1024,1,2048]{2,0,1:T(8,128)S(1)} %copy-done.1, f32[1024,1,2048]{2,0,1:T(8,128)} %add_bitcast_fusion.2), kind=kLoop, calls=%fused_computation.1 | loop fusion | flops 12582912 | bytes 50331648 | tf_op jit(solution)/shard_map/stack | solution.py:542
  1068.0 90.8 %reduce-scatter.5.cloned.1.call-done = bf16[128,2304]{1,0:T(8,128)(2,1)} async-done(((bf16[2048,2304]{1,0:T(8,128)(2,1)}), bf16[128,2304]{1,0:T(8,128)(2,1)}) %reduce-scatter.5.cloned.1.call-update) | async-done | bytes 589840 | tf_op jit(solution)/shard_map/reduce_scatter | solution.py:93
  1160.3 77.2 %ring_gather.7 = bf16[2048,3584]{1,0:T(8,128)(2,1)} custom-call(bf16[128,3584]{1,0:T(8,128)(2,1)} %slice_dynamic-update-slice_fusion.1.x_ref), custom_call_target="tpu_custom_call" | custom-call | bytes 274667744 | tf_op jit(solution)/shard_map/ring_gather/pallas_call | solution.py:186
  1239.2 5.7 fusion.47
  1246.1 6.2 fusion.18
  1258.3 8.5 fusion.60.far_ref
  1266.7 2.5 fusion.77
  1269.2 84.5 %place_columns.1 = f32[2464,256]{1,0:T(8,128)} custom-call(f32[2176,256]{1,0:T(8,128)} %pad_maximum_fusion.4.mid_ref, f32[2560,256]{1,0:T(8,128)} %pad_maximum_fusion.3.near_ref, f32[2048,256]{1,0:T(8,128)} %fusion.60.far_ref), custom_call_target="tpu_custom_call" | custom-call | bytes 90000000 | tf_op jit(solution)/shard_map/place_columns/pallas_call | solution.py:402
  1357.1 2.3 fusion.79
  1359.4 6.0 fusion.66
  1365.4 2.4 fusion.50
  (248 shorter events, 74.4 us)
Async XLA Ops:
  7.2 112.9 %copy-start.4 = (bf16[1,128,2048]{2,1,0:T(8,128)(2,1)S(1)}, bf16[1,128,2048]{2,1,0:T(8,128)(2,1)}, u32[]{:S(2)}) copy-start(bf16[1,128,2048]{2,1,0:T(8,128)(2,1)} %param.10) | copy-start | bytes 1572868
  7.2 179.6 %all-gather.12.cloned.1.call-start = ((), (), s32[]{:S(2)}) async-start(), calls=%async_computation.4 | async-start | bytes 8912896 | tf_op jit(solution)/shard_map/all_gather | solution.py:89
  7.9 290.1 %all-gather.18.cloned.1.call-start = ((), (), s32[]{:S(2)}) async-start(), calls=%async_computation.8 | async-start | bytes 8912896 | tf_op jit(solution)/shard_map/all_gather | solution.py:89
  8.7 620.0 %reduce-scatter.7.cloned.1.call-start = ((), (), s32[]{:S(2)}) async-start(), calls=%async_computation.12 | async-start | bytes 1114112
  9.5 114.4 %copy-start.33 = (f32[1,2048]{1,0:T(1,128)}, f32[1,2048]{1,0:T(1,128)S(1)}, u32[]{:S(2)}) copy-start(f32[1,2048]{1,0:T(1,128)S(1)} %get-tuple-element.41) | copy-start | bytes 24580
  9.5 187.7 %copy-start.36 = (f32[1,2048]{1,0:T(1,128)}, f32[1,2048]{1,0:T(1,128)S(1)}, u32[]{:S(2)}) copy-start(f32[1,2048]{1,0:T(1,128)S(1)} %get-tuple-element.40) | copy-start | bytes 24580
  11.3 112.6 %copy-start.38 = (f32[128]{0:T(128)}, f32[128]{0:T(128)S(1)}, u32[]{:S(2)}) copy-start(f32[128]{0:T(128)S(1)} %get-tuple-element.46) | copy-start | bytes 1540
  11.3 112.1 %copy-start.51 = (s32[1,4]{1,0:T(1,128)S(1)}, s32[1,4]{1,0:T(1,128)}, u32[]{:S(2)}) copy-start(s32[1,4]{1,0:T(1,128)} %param.11) | copy-start | bytes 52
  123.7 42.6 %copy-start.42 = (f32[128]{0:T(128)}, f32[128]{0:T(128)S(1)}, u32[]{:S(2)}) copy-start(f32[128]{0:T(128)S(1)} %multiply_exponential_fusion) | copy-start | bytes 1540
  123.9 42.4 %copy-start.40 = (f32[128]{0:T(128)}, f32[128]{0:T(128)S(1)}, u32[]{:S(2)}) copy-start(f32[128]{0:T(128)S(1)} %fusion.214) | copy-start | bytes 1540
  167.3 14.6 %copy-start.30 = (f32[128,128]{1,0:T(8,128)}, f32[128,128]{1,0:T(8,128)S(1)}, u32[]{:S(2)}) copy-start(f32[128,128]{1,0:T(8,128)S(1)} %get-tuple-element.44) | copy-start | bytes 196612
  167.5 14.3 %copy-start.24 = (bf16[128,8,128]{2,0,1:T(8,128)(2,1)}, bf16[128,8,128]{2,0,1:T(8,128)(2,1)S(1)}, u32[]{:S(2)}) copy-start(bf16[128,8,128]{2,0,1:T(8,128)(2,1)S(1)} %get-tuple-element.32) | copy-start | bytes 786436
  167.6 14.3 %copy-start.26 = (bf16[128,8,128]{2,0,1:T(8,128)(2,1)}, bf16[128,8,128]{2,0,1:T(8,128)(2,1)S(1)}, u32[]{:S(2)}) copy-start(bf16[128,8,128]{2,0,1:T(8,128)(2,1)S(1)} %get-tuple-element.33) | copy-start | bytes 786436
  186.8 11.3 copy-start.9
  196.5 57.6 %copy-start.2 = (f32[128,2048]{1,0:T(8,128)}, f32[128,2048]{1,0:T(8,128)S(1)}, u32[]{:S(2)}) copy-start(f32[128,2048]{1,0:T(8,128)S(1)} %get-tuple-element.52) | copy-start | bytes 3145732
  197.2 57.0 %copy-start.44 = (f32[128]{0:T(128)}, f32[128]{0:T(128)S(1)}, u32[]{:S(2)}) copy-start(f32[128]{0:T(128)S(1)} %get-tuple-element.48) | copy-start | bytes 1540
  248.0 6.1 copy-start.7
  254.2 14.5 %copy-start.14 = (bf16[2048,256]{1,0:T(8,128)(2,1)}, bf16[2048,256]{1,0:T(8,128)(2,1)S(1)}, u32[]{:S(2)}) copy-start(bf16[2048,256]{1,0:T(8,128)(2,1)S(1)} %convolution_convert_fusion.9) | copy-start | bytes 3145732
  277.9 14.5 %copy-start.16 = (bf16[2048,256]{1,0:T(8,128)(2,1)}, bf16[2048,256]{1,0:T(8,128)(2,1)S(1)}, u32[]{:S(2)}) copy-start(bf16[2048,256]{1,0:T(8,128)(2,1)S(1)} %convolution_convert_fusion.10) | copy-start | bytes 3145732
  298.1 6.2 copy-start.50
  298.1 19.9 %slice-start.5 = ((s8[8388608]{0:T(1024)(128)(4,1)}), s8[4194304]{0:T(1024)(128)(4,1)S(1)}, s32[]{:S(2)}) async-start(s8[8388608]{0:T(1024)(128)(4,1)} %bitcast.226), calls=%async_computation.18 | async-start | bytes 8388608
  304.2 13.7 copy-start.58
  304.2 13.7 slice-start.6
  333.3 15.8 %copy-start.57 = (bf16[2048,1024]{1,0:T(8,128)(2,1)S(1)}, bf16[2048,1024]{1,0:T(8,128)(2,1)}, u32[]{:S(2)}) copy-start(bf16[2048,1024]{1,0:T(8,128)(2,1)} %get-tuple-element.28) | copy-start | bytes 12582916
  351.7 15.7 %copy-start.55 = (bf16[2048,1024]{1,0:T(8,128)(2,1)S(1)}, bf16[2048,1024]{1,0:T(8,128)(2,1)}, u32[]{:S(2)}) copy-start(bf16[2048,1024]{1,0:T(8,128)(2,1)} %get-tuple-element.27) | copy-start | bytes 12582916
  420.5 10.5 copy-start.53
  444.3 65.9 %copy-start.3 = (f32[128,2048]{1,0:T(8,128)S(1)}, f32[128,2048]{1,0:T(8,128)}, u32[]{:S(2)}) copy-start(f32[128,2048]{1,0:T(8,128)} %copy-done.2) | copy-start | bytes 3145732
  444.3 65.9 %copy-start.37 = (f32[1,2048]{1,0:T(1,128)S(1)}, f32[1,2048]{1,0:T(1,128)}, u32[]{:S(2)}) copy-start(f32[1,2048]{1,0:T(1,128)} %copy-done.36) | copy-start | bytes 24580
  444.3 65.9 %copy-start.45 = (f32[128]{0:T(128)S(1)}, f32[128]{0:T(128)}, u32[]{:S(2)}) copy-start(f32[128]{0:T(128)} %copy-done.44) | copy-start | bytes 1540
  444.3 67.9 %copy-start.18 = (bf16[1,128,2048]{2,1,0:T(8,128)(2,1)S(1)}, bf16[1,128,2048]{2,1,0:T(8,128)(2,1)}, u32[]{:S(2)}) copy-start(bf16[1,128,2048]{2,1,0:T(8,128)(2,1)} %param.19) | copy-start | bytes 1572868
  444.3 67.9 %copy-start.49 = (f32[128]{0:T(128)S(1)}, f32[128]{0:T(128)}, u32[]{:S(2)}) copy-start(f32[128]{0:T(128)} %get-tuple-element.47) | copy-start | bytes 1540
  508.1 7.1 slice-start.3
  508.1 5.3 copy-start.20
  518.6 11.5 slice-start.9
  524.0 6.1 slice-start.10
  535.3 22.9 %copy-start.41 = (f32[128]{0:T(128)S(1)}, f32[128]{0:T(128)}, u32[]{:S(2)}) copy-start(f32[128]{0:T(128)} %copy-done.40) | copy-start | bytes 1540
  535.3 22.9 %copy-start.43 = (f32[128]{0:T(128)S(1)}, f32[128]{0:T(128)}, u32[]{:S(2)}) copy-start(f32[128]{0:T(128)} %copy-done.42) | copy-start | bytes 1540
  535.3 24.4 %copy-start.31 = (f32[128,128]{1,0:T(8,128)S(1)}, f32[128,128]{1,0:T(8,128)}, u32[]{:S(2)}) copy-start(f32[128,128]{1,0:T(8,128)} %copy-done.30) | copy-start | bytes 196612
  535.3 24.4 %copy-start.35 = (f32[128,128]{1,0:T(8,128)S(1)}, f32[128,128]{1,0:T(8,128)}, u32[]{:S(2)}) copy-start(f32[128,128]{1,0:T(8,128)} %get-tuple-element.42) | copy-start | bytes 196612
  535.3 27.8 %slice-start = ((s8[10485760]{0:T(1024)(128)(4,1)}), s8[4194304]{0:T(1024)(128)(4,1)S(1)}, s32[]{:S(2)}) async-start(s8[10485760]{0:T(1024)(128)(4,1)} %bitcast.222), calls=%async_computation.13 | async-start | bytes 8388608
  535.3 27.8 %slice-start.1 = ((s8[10485760]{0:T(1024)(128)(4,1)}), s8[4194304]{0:T(1024)(128)(4,1)S(1)}, s32[]{:S(2)}) async-start(s8[10485760]{0:T(1024)(128)(4,1)} %bitcast.222), calls=%async_computation.14 | async-start | bytes 8388608
  539.1 24.0 %slice-start.2 = ((s8[10485760]{0:T(1024)(128)(4,1)}), s8[2097152]{0:T(1024)(128)(4,1)S(1)}, s32[]{:S(2)}) async-start(s8[10485760]{0:T(1024)(128)(4,1)} %bitcast.222), calls=%async_computation.15 | async-start | bytes 4194304
  560.0 6.7 copy-start.5
  560.0 6.7 copy-start.34
  560.0 6.7 copy-start.39
  563.2 9.1 copy-start.10
  563.2 9.0 copy-start.29
  572.2 155.7 %all-gather.14.cloned.1.call-start = ((), (), s32[]{:S(2)}) async-start(), calls=%async_computation.6 | async-start | bytes 12255232 | tf_op jit(solution)/shard_map/all_gather | solution.py:89
  573.2 258.4 %all-gather.24.cloned.1.call-start = ((), (), s32[]{:S(2)}) async-start(), calls=%async_computation.11 | async-start | bytes 12582912 | tf_op jit(solution)/shard_map/all_gather | solution.py:97
  573.8 363.3 %all-gather.22.cloned.1.call-start = ((), (), s32[]{:S(2)}) async-start(), calls=%async_computation.10 | async-start | bytes 12582912 | tf_op jit(solution)/shard_map/all_gather | solution.py:97
  574.3 468.4 %all-gather.20.cloned.1.call-start = ((), (), s32[]{:S(2)}) async-start(), calls=%async_computation.9 | async-start | bytes 12582912 | tf_op jit(solution)/shard_map/all_gather | solution.py:97
  575.1 583.7 %reduce-scatter.5.cloned.1.call-start = ((), (), s32[]{:S(2)}) async-start(), calls=%async_computation.5 | async-start | bytes 10027008 | tf_op jit(solution)/shard_map/reduce_scatter | solution.py:93
  578.3 159.0 %all-to-all-start.1 = ((bf16[128,16,128]{2,0,1:T(8,128)(2,1)}), bf16[128,16,128]{2,0,1:T(8,128)(2,1)S(1)}, u32[]{:S(2)}, u32[]{:S(2)}) async-start(bf16[128,16,128]{2,0,1:T(8,128)(2,1)} %bitcast.252), calls=%async_computation.2 | async-start | bytes 1048576 | tf_op jit(solution)/shard_map/all_to_all | solution.py:102
  582.0 7.6 copy-start.15
  582.0 7.6 copy-start.56
  584.7 7.3 copy-start.54
  584.7 7.3 copy-start.59
  737.3 502.0 %all-to-all-start = ((bf16[128,16,128]{2,0,1:T(8,128)(2,1)}), bf16[128,16,128]{2,0,1:T(8,128)(2,1)}, u32[]{:S(2)}, u32[]{:S(2)}) async-start(bf16[128,16,128]{2,0,1:T(8,128)(2,1)} %fusion.120), calls=%async_computation.1 | async-start | bytes 1048576 | tf_op jit(solution)/shard_map/all_to_all | solution.py:102
  741.5 627.2 %all-gather.16.cloned.1.call-start = ((), (), s32[]{:S(2)}) async-start(), calls=%async_computation.7 | async-start | bytes 3538944 | tf_op jit(solution)/shard_map/all_gather | solution.py:97
  741.8 7.6 copy-start.22
  741.8 7.6 copy-start.23
  1042.8 9.9 copy-start
  1042.8 11.3 copy-start.1
  1365.4 7.5 copy-start.6
  (18 other events, 64.0 us)
Sparse Core Ops, SparseCore 0:
  10.2 106.7 all-gather.11
  119.1 85.5 all-gather.17
  572.3 56.3 reduce-scatter.6
  631.5 96.3 all-gather.13
  729.4 102.1 all-gather.23
  833.1 103.9 all-gather.21
  938.7 103.9 all-gather.19
  1047.4 111.3 reduce-scatter.4
  1246.2 34.7 all-gather.15

commit v3 on v2

--- a/solution.py
+++ b/solution.py
@@ -93,8 +93,11 @@
     return lax.psum_scatter(partial.astype(bf16), "fsdp", scatter_dimension=0, tiled=True).astype(f32)
 
 
-def both_loops(partial):
-    shares = lax.all_gather(partial.astype(bf16), "loop", axis=0)
+def loop_shares(partial):
+    return lax.all_gather(partial.astype(bf16), "loop", axis=0)
+
+
+def both_loops(shares):
     return shares[0].astype(f32) + shares[1].astype(f32)
 
 
@@ -190,99 +193,133 @@
         out_specs=pl.BlockSpec(memory_space=pl.ANY),
         scratch_shapes=[pltpu.SemaphoreType.DMA, pair, pair, sides, sides],
         compiler_params=pltpu.CompilerParams(collective_id=ident, has_side_effects=True),
-        cost_estimate=busy(size * rows * columns * 2 / 180e3 + 10),
+        cost_estimate=busy(1),
         name="ring_gather",
     )(block)
 
-def scatter_kernel(chips, x_ref, o_ref, side_buf, ring_buf, send_buf, side_send, side_recv, ring_send, ring_recv):
+def scatter_kernel(chips, count, *refs):
+    x_refs, o_ref = refs[:count], refs[count]
+    side_buf, ring_buf, side_send, side_recv, ring_send, ring_recv = refs[count + 1 :]
     core, device = ring_neighbours(chips)
     rows, columns = o_ref.shape
     reach = chips // 2
     half = columns // 2
+    tile = 16
     ways = (device(1, core), device(-1, core))
     side = device(0, 1 - core)
     meet((*ways, side))
+    starts = [sum(x.shape[1] for x in x_refs[:i]) for i in range(count)]
 
     def shift(way, hops):
         return (hops if way == 0 else chips - hops) % chips
 
-    def across(target, c):
-        there = pl.ds(pl.multiple_of(device(target, c) * rows, 16), rows)
-        return pltpu.make_async_remote_copy(x_ref.at[there], side_buf.at[target], side_send.at[target], side_recv.at[target], device_id={"fsdp": side}, device_id_type=MESH)
+    def across(target, c, i):
+        there = pl.ds(pl.multiple_of(device(target, c) * rows, tile), rows)
+        return pltpu.make_async_remote_copy(
+            x_refs[i].at[there],
+            side_buf.at[target, :, pl.ds(starts[i], x_refs[i].shape[1])],
+            side_send.at[target, i],
+            side_recv.at[target, i],
+            device_id={"fsdp": side},
+            device_id_type=MESH,
+        )
 
     def hop(way, step):
         cols = pl.ds(way * half, half) if step == 0 else pl.ds(0, columns)
-        return pltpu.make_async_remote_copy(send_buf.at[way, step, :, cols], ring_buf.at[way, step, :, cols], ring_send.at[way, step], ring_recv.at[way, step], device_id={"fsdp": ways[way]}, device_id_type=MESH)
+        return pltpu.make_async_remote_copy(
+            side_buf.at[shift(way, reach - step), :, cols],
+            ring_buf.at[way, step, :, cols],
+            ring_send.at[way, step],
+            ring_recv.at[way, step],
+            device_id={"fsdp": ways[way]},
+            device_id_type=MESH,
+        )
 
     order = [reach] + [shift(way, hops) for hops in range(reach - 1, 0, -1) for way in (0, 1)] + [0]
     for target in order:
-        across(target, 1 - core).start()
-    tile = 16
+        for i in range(count):
+            across(target, 1 - core, i).start()
 
     def add(target, incoming, store):
-        first = pl.multiple_of(device(target, core) * rows, 16)
+        first = pl.multiple_of(device(target, core) * rows, tile)
+        for i in range(count):
+            across(target, core, i).wait_recv()
+
         @pl.loop(0, rows // tile)
-        def _(i):
-            here = pl.ds(pl.multiple_of(i * tile, tile), tile)
-            total = x_ref[pl.ds(pl.multiple_of(first + i * tile, tile), tile), :].astype(f32) + side_buf[target, here, :].astype(f32)
-            store(here, total, [(way, step, ring_buf[way, step, here, pl.ds(way * half, half) if step == 0 else pl.ds(0, columns)].astype(f32)) for way, step in incoming])
+        def _(j):
+            here = pl.ds(pl.multiple_of(j * tile, tile), tile)
+            mine = pl.ds(pl.multiple_of(first + j * tile, tile), tile)
+            for i in range(count):
+                cols = pl.ds(starts[i], x_refs[i].shape[1])
+                total = x_refs[i][mine, :].astype(f32) + side_buf[target, here, cols].astype(f32)
+                for way, step in incoming:
+                    if step:
+                        total = total + ring_buf[way, step, here, cols].astype(f32)
+                store(here, cols, total)
+            for way, step in incoming:
+                if not step:
+                    cols = pl.ds(way * half, half)
+                    store(
+                        here,
+                        cols,
+                        side_buf[target, here, cols].astype(f32) + ring_buf[way, 0, here, cols].astype(f32),
+                    )
 
     for step in range(reach):
-        hops = reach - step
         for way in (0, 1):
-            target = shift(way, hops)
-            if step or way == 0:
-                across(target, core).wait_recv()
+            target = shift(way, reach - step)
             if step:
                 hop(way, step - 1).wait_recv()
 
-            def store(here, total, more, way=way, step=step):
-                if step == 0:
-                    send_buf[way, step, here, pl.ds(way * half, half)] = total[:, way * half:(way + 1) * half].astype(bf16)
-                elif step == 1:
-                    other = total[:, (1 - way) * half:(2 - way) * half]
-                    send_buf[way, step, here, pl.ds((1 - way) * half, half)] = other.astype(bf16)
-                    send_buf[way, step, here, pl.ds(way * half, half)] = (total[:, way * half:(way + 1) * half] + more[0][2]).astype(bf16)
-                else:
-                    send_buf[way, step, here, :] = (total + more[0][2]).astype(bf16)
-            add(target, [(way, step - 1)] if step else [], store)
+            def store(here, cols, total, target=target):
+                side_buf[target, here, cols] = total.astype(bf16)
+
+            if step or way == 0:
+                add(target, [(way, step - 1)] if step else [], store)
             hop(way, step).start()
-    across(0, core).wait_recv()
     for way in (0, 1):
         hop(way, reach - 1).wait_recv()
 
-    def last(here, total, more):
-        o_ref[here, :] = total + (more[0][2] + more[1][2])
+    def last(here, cols, total):
+        o_ref[here, cols] = total
+
     add(0, [(0, reach - 1), (1, reach - 1)], last)
     for target in order:
-        across(target, 1 - core).wait_send()
+        for i in range(count):
+            across(target, 1 - core, i).wait_send()
     for step in range(reach):
         for way in (0, 1):
             hop(way, step).wait_send()
 
-def ring_scatter(partial, ident):
+
+def ring_scatter(terms, ident):
     size = lax.axis_size("fsdp")
+    terms = [term.astype(bf16) for term in terms]
     if size != 16:
-        return scatter_rows(partial)
-    partial = partial.astype(bf16)
-    chips = size // 2
-    rows, columns = partial.shape[0] // size, partial.shape[1]
+        return scatter_rows(jnp.concatenate(terms, axis=1))
+    chips, count = size // 2, len(terms)
+    rows, columns = terms[0].shape[0] // size, sum(term.shape[1] for term in terms)
     pair = pltpu.SemaphoreType.DMA((2, chips // 2))
-    sides = pltpu.SemaphoreType.DMA((chips,))
+    sides = pltpu.SemaphoreType.DMA((chips, count))
     return pl.pallas_call(
-        functools.partial(scatter_kernel, chips),
+        functools.partial(scatter_kernel, chips, count),
         out_shape=jax.ShapeDtypeStruct((rows, columns), f32),
-        in_specs=[pl.BlockSpec(memory_space=pltpu.VMEM)],
+        in_specs=[pl.BlockSpec(memory_space=pltpu.VMEM)] * count,
         out_specs=pl.BlockSpec(memory_space=pltpu.VMEM),
         scratch_shapes=[
             pltpu.VMEM((chips, rows, columns), bf16),
             pltpu.VMEM((2, chips // 2, rows, columns), bf16),
-            pltpu.VMEM((2, chips // 2, rows, columns), bf16),
-            sides, sides, pair, pair],
-        compiler_params=pltpu.CompilerParams(collective_id=ident, has_side_effects=True, vmem_limit_bytes=48 << 20),
-        cost_estimate=busy(size * rows * columns * 2 / 180e3 + 10),
+            sides,
+            sides,
+            pair,
+            pair,
+        ],
+        compiler_params=pltpu.CompilerParams(
+            collective_id=ident, has_side_effects=True, vmem_limit_bytes=56 << 20
+        ),
+        cost_estimate=busy(1),
         name="ring_scatter",
-    )(partial)
+    )(*terms)
 
 
 def place_kernel(size, chunk, own_count, mid_ref, near_ref, far_ref, o_ref, send_sem, recv_sem, own_sem):
@@ -306,6 +343,10 @@
 
     def rows(ref, first):
         return ref.at[pl.ds(pl.multiple_of(first, 8), chunk)]
+
+    def aim(start, length):
+        owner = (start + me * length) // own_count
+        return owner, start + me * length - owner * own_count
 
     def remote(source, first, owner, sent=0):
         return pltpu.make_async_remote_copy(
@@ -322,10 +363,10 @@
 
     for base, start, length in sections:
 
-        def send(j, carry, base=base, start=start, length=length):
-            column = start + me * length + j * chunk
-            owner = column // own_count
-            first = column - owner * own_count
+        def send(j, carry, base=base, aimed=aim(start, length)):
+            over = (aimed[1] + j * chunk >= own_count).astype(jnp.int32)
+            owner = aimed[0] + over
+            first = aimed[1] + j * chunk - over * own_count
             source = rows(mid_ref, base + j * chunk)
 
             @pl.when(owner != me)
@@ -360,8 +401,10 @@
         here = rows(o_ref, j * chunk)
         away = 0
         for _, start, length in sections:
+            mine = start + me * length
             inside = (column >= start) & (column < start + length * size)
-            away = away + (inside & ((column - start) // length != me)).astype(jnp.int32)
+            outside = (column < mine) | (column >= mine + length)
+            away = away + (inside & outside).astype(jnp.int32)
 
         @pl.when(away > 0)
         def _():
@@ -376,18 +419,14 @@
     lax.fori_loop(0, own_count // chunk, arrive, 0)
     for base, start, length in sections:
 
-        def sent(j, carry, base=base, start=start, length=length):
-            column = start + me * length + j * chunk
-            owner = column // own_count
+        def sent(j, carry, base=base, aimed=aim(start, length)):
+            over = (aimed[1] + j * chunk >= own_count).astype(jnp.int32)
+            owner = aimed[0] + over
+            first = aimed[1] + j * chunk - over * own_count
 
             @pl.when(owner != me)
             def _():
-                remote(
-                    rows(mid_ref, base + j * chunk),
-                    column - owner * own_count,
-                    owner,
-                    base // chunk + j,
-                ).wait_send()
+                remote(rows(mid_ref, base + j * chunk), first, owner, base // chunk + j).wait_send()
 
             return carry
 
@@ -401,7 +440,7 @@
     anywhere = pl.BlockSpec(memory_space=pl.ANY)
     return pl.pallas_call(
         functools.partial(place_kernel, size, chunk, own_count),
-        out_shape=jax.ShapeDtypeStruct((own_count, ADAPTER_RANK), f32),
+        out_shape=jax.ShapeDtypeStruct((own_count, ADAPTER_RANK), bf16),
         in_specs=[anywhere] * 3,
         out_specs=anywhere,
         scratch_shapes=[
@@ -469,7 +508,10 @@
     scale_one = rms_scale(hidden_state)
     normalized = (hidden_state * scale_one * gains[0]).astype(bf16)
     proj_in = ring_gather(input_proj_weight, 0)
-    proj_out = gather_rows(output_proj_weight)
+    proj_in, proj_out, grad_rows = lax.optimization_barrier(
+        (proj_in, output_proj_weight, output_gradient[0])
+    )
+    proj_out = gather_rows(proj_out)
     lora_qkv = matrix_product(normalized, narrow_projection).astype(bf16)
     projected = matrix_product(normalized, proj_in)
     query_pre = projected[:, :QUERY_WIDTH] + matrix_product(lora_qkv[:, :rank], widen_query)
@@ -505,8 +547,9 @@
     scale_two = rms_scale(middle)
     normed_two = (middle * scale_two * gains[1]).astype(bf16)
 
-    grad_all = gather_rows(output_gradient[0])
     two_all = ring_gather(normed_two, 2)
+    two_all, grad_rows = lax.optimization_barrier((two_all, grad_rows))
+    grad_all = gather_rows(grad_rows)
     weight_gate = feedforward_weight[:, 0, :]
     weight_up = feedforward_weight[:, 1, :]
     weight_down = feedforward_weight[:, 2, :]
@@ -518,35 +561,26 @@
     units = (gelu_tanh(gate) * upward).astype(bf16)
     units_grad = times_transposed(grad_all, weight_down) + times_transposed(hd_grad, narrow_down)
     gate_grad, up_grad = unit_backward(gate, upward, units_grad)
-    back_part = jnp.concatenate(
+    back_terms = [
+        (matrix_product(gate_grad, weight_gate) + matrix_product(up_grad, weight_up)).astype(bf16),
+        times_transposed(gate_grad, widen_gate).astype(bf16),
+        times_transposed(up_grad, widen_up).astype(bf16),
+        matrix_product(units, weight_down).astype(bf16),
+        matrix_product(units, narrow_down).astype(bf16),
+    ]
+    ffn_shares = jnp.stack(
         [
-            matrix_product(gate_grad, weight_gate) + matrix_product(up_grad, weight_up),
-            times_transposed(gate_grad, widen_gate),
-            times_transposed(up_grad, widen_up),
-        ],
-        axis=1,
-    )
-    ffn_shares = [
-        outer_product_rows(former, latter).astype(bf16)
-        for former, latter in ((units, grad_all), (gate_grad, two_all), (up_grad, two_all))
-    ]
-    out_part = jnp.concatenate(
-        [matrix_product(units, weight_down), matrix_product(units, narrow_down)], axis=1
-    )
-    ffn_shares, out_part, back_part = lax.optimization_barrier(
-        (ffn_shares, out_part.astype(bf16), back_part.astype(bf16))
-    )
-    down_total, gate_total, up_total = [both_loops(share) for share in ffn_shares]
-    back_own = ring_scatter(back_part, 3)
-    out_own = scatter_rows(out_part)
-    ffn_sum = jnp.stack(
-        [
-            gate_total,
-            up_total,
-            down_total,
-        ],
-        axis=1,
-    )
+            outer_product_rows(former, latter).astype(bf16)
+            for former, latter in ((gate_grad, two_all), (up_grad, two_all), (units, grad_all))
+        ]
+    )
+    attended_all = gather_rows(jnp.concatenate([attended, lora_qkv], axis=1))
+    ffn_shares, back_terms, attended_all = lax.optimization_barrier(
+        (ffn_shares, back_terms, attended_all)
+    )
+    ffn_both = loop_shares(ffn_shares)
+    rows_sum = ring_scatter(back_terms, 3)
+    back_own, out_own = rows_sum[:, : MODEL_WIDTH + 2 * rank], rows_sum[:, MODEL_WIDTH + 2 * rank :]
     down_own = outer_product_rows(units, hd_grad)
     gate_piece = outer_product_rows(gate_grad, lora_gate)
     up_piece = outer_product_rows(up_grad, lora_up)
@@ -585,7 +619,7 @@
         jnp.einsum("thu,thd->ud", score_grad, query_heads, preferred_element_type=f32) * scaling
     )
     value_part = jnp.einsum("thu,thd->ud", probs_low, heads_grad, preferred_element_type=f32)
-    pair_grad = ring_scatter(jnp.concatenate([key_part, value_part], axis=1), 4)
+    pair_grad = ring_scatter([key_part, value_part], 4)
     query_grad = rotate(
         query_rot_grad.reshape(tokens_dev, QUERY_WIDTH), position_own, -1.0
     ).astype(bf16)
@@ -612,21 +646,21 @@
         * jnp.mean(hidden_state * weighted_one, axis=-1, keepdims=True)
     )
     gain_one = jnp.sum(normed_grad * hidden_state * scale_one, axis=0)
-    gain_sum = lax.psum(
-        lax.psum_scatter(
-            jnp.stack([gain_one, gain_two]), "fsdp", scatter_dimension=1, tiled=True
-        ).astype(bf16),
-        "loop",
-    ).astype(f32)
-
-    attended_all = gather_rows(jnp.concatenate([attended, lora_qkv], axis=1))
+
     lora_qkv_all = attended_all[:, QUERY_WIDTH:]
     attended_all = attended_all[:, :QUERY_WIDTH]
     lora_out_all = matrix_product(attended_all, narrow_output).astype(bf16)
-    proj_all = ring_gather(
-        jnp.concatenate([proj_grad, lora_out_grad, gate_low, up_low, lora_hd], axis=1), 5
-    )
-    low_all = proj_all[:, PROJECT_COLUMNS:]
+    gain_rows = jnp.stack([gain_one, gain_two]).astype(bf16).reshape(tokens_dev, -1)
+    gain_count = gain_rows.shape[1]
+    gain_rows = jnp.pad(gain_rows, ((0, 0), (0, -gain_count % 128)))
+    proj_rows = jnp.concatenate(
+        [proj_grad, lora_out_grad, gate_low, up_low, lora_hd, gain_rows], axis=1
+    )
+    proj_all = ring_gather(proj_rows, 5)
+    low_all = proj_all[:, PROJECT_COLUMNS : PROJECT_COLUMNS + 4 * rank]
+    gain_all = proj_all[:, PROJECT_COLUMNS + 4 * rank :][:, :gain_count].reshape(size, 2, MODEL_WIDTH)
+    gain_all = jnp.sum(gain_all.astype(f32), axis=0)
+    gain_own = lax.dynamic_slice_in_dim(gain_all, place * width_own, width_own, 1)
     proj_all = proj_all[:, :PROJECT_COLUMNS]
     qkv_low_all = jnp.concatenate(
         [
@@ -645,7 +679,13 @@
         [outer_product_rows(normed_turn, proj_all), outer_product_rows(branch_turn, attended_all)],
         axis=1,
     )
-    attn_sum = both_loops(attn_part)
+    gain_part = jnp.pad(gain_own, ((0, width_own - 2), (0, -width_own % 128)))
+    attn_part, ffn_both = lax.optimization_barrier(
+        (jnp.concatenate([attn_part, gain_part], axis=1).astype(bf16), ffn_both)
+    )
+    attn_sum = both_loops(loop_shares(attn_part))
+    gain_column = PROJECT_COLUMNS + QUERY_WIDTH
+    gain_sum = attn_sum[:2, gain_column : gain_column + width_own]
     squeeze_own = jnp.concatenate(
         [
             outer_product_rows(normed_turn, qkv_low_all),
@@ -667,14 +707,19 @@
     )
     far = outer_product_rows(grad_all, low_all[:, 3 * rank :])
     expand_own = place_columns(
-        jnp.concatenate([out_piece, gate_piece, up_piece], axis=0), near, far, 6
-    ).T
+        jnp.concatenate([out_piece, gate_piece, up_piece], axis=0).astype(bf16),
+        near.astype(bf16),
+        far.astype(bf16),
+        6,
+    )
+    expand_own = expand_own.T.astype(f32)
+    ffn_sum = both_loops(ffn_both).transpose(1, 0, 2)
     return (
         hidden_out[None],
         input_grad[None],
         gain_sum,
         attn_sum[:, :PROJECT_COLUMNS],
-        attn_sum[:, PROJECT_COLUMNS:],
+        attn_sum[:, PROJECT_COLUMNS:gain_column],
         ffn_sum,
         squeeze_own[None],
         expand_own[None],

time: 1390 us -> 871 us (0.63)
  waiting for transfers between devices: 488 us -> 47.6 us
  other arithmetic: 91.6 us -> 56.4 us
  Pallas kernels: 435 us -> 413 us
  matrix products: 307 us -> 291 us
    all_gather x4 -> x2, waiting for transfers between devices: 267 us -> 0.02 us  [loop_shares(): return lax.all_gather(partial.astype(bf16), 'loop', axis=0)]
    reduce_scatter x1 -> x0, waiting for transfers between devices: 90.8 us -> none  [scatter_rows(): lax.psum_scatter(partial.astype(bf16), 'fsdp', scatter_dimension=0, tiled...]
    pallas_call x2, Pallas kernels: 82.8 us -> 147 us  [ring_scatter(): pl.pallas_call(functools.partial(scatter_kernel, chips, count), out_shape...]
    pallas_call x4, Pallas kernels: 268 us -> 218 us  [ring_gather(): pl.pallas_call(functools.partial(gather_kernel, chips), out_shape=jax.Sha...]
    all_gather x3, waiting for transfers between devices: 92.8 us -> 47.5 us  [gather_rows(): return lax.all_gather(block, 'fsdp', axis=0, tiled=True)]
    unnamed x10 -> x5, waiting for transfers between devices: 37.1 us -> 0.08 us
    pallas_call x1, Pallas kernels: 84.5 us -> 47.7 us  [place_columns(): pl.pallas_call(functools.partial(place_kernel, size, chunk, own_count), o...]
    add x4 -> x1, other arithmetic: 30 us -> 1.88 us  [both_loops(): return shares[0].astype(f32) + shares[1].astype(f32)]
  transfers between devices with their start and end apart: 11 -> 7, of which waited for: 6 -> 2; matrix products, arithmetic and copies ran while one was open for 16% -> 41% of each run, Pallas kernels for 25% -> 35%
where the time goes in v3:
time: 871 us; the launch traced here: 861 us
  Pallas kernels  413 us (47%)
  matrix products  291 us (33%)
  other arithmetic  56.4 us (6%)
  waiting for transfers between devices  47.6 us (5%)
  local copies, waits for them, and re-layouts  27.8 us (3%)
  between operations  15.5 us (2%)
  starting transfers between devices  9.3 us (1%)
    pallas_call x4, Pallas kernels, ring_gather(): pl.pallas_call(functools.partial(gather_kernel, chips), out_shape=jax.Sha...  218 us
    pallas_call x2, Pallas kernels, ring_scatter(): pl.pallas_call(functools.partial(scatter_kernel, chips, count), out_shape...  147 us
    dot_general x20, matrix products, times_transposed(): lax.dot_general(former, latter, (((1,), (1,)), ((), ())), preferred_eleme...  103 us
    dot_general x16, matrix products, matrix_product(): return jnp.dot(former, latter, preferred_element_type=f32)  97.5 us
    dot_general x16, matrix products, outer_product_rows(): lax.dot_general(former, latter, (((0,), (0,)), ((), ())), preferred_eleme...  76.9 us
    pallas_call x1, Pallas kernels, place_columns(): pl.pallas_call(functools.partial(place_kernel, size, chunk, own_count), o...  47.7 us
    all_gather x3, waiting for transfers between devices, gather_rows(): return lax.all_gather(block, 'fsdp', axis=0, tiled=True)  47.5 us
    transpose x1, other arithmetic, per_device(): ffn_sum = both_loops(ffn_both).transpose(1, 0, 2)  18.6 us
  transfers between devices with their start and end apart: 7, of which 2 were waited for; matrix products, arithmetic and copies ran while one was open for 41% of the time, Pallas kernels for 35%

profile of v3, /device:TPU:0, one launch (start us, length us, event | category | flops | bytes accessed | tf_op | source)
XLA Modules:
  0.0 860.8 jit_solution(10059314459426567610)
XLA Ops:
  7.3 61.2 %ring_gather.4 = bf16[2048,2560]{1,0:T(8,128)(2,1)} custom-call(bf16[128,2560]{1,0:T(8,128)(2,1)} %x_ref.1), custom_call_target="tpu_custom_call" | custom-call | bytes 3000000 | tf_op jit(solution)/shard_map/ring_gather/pallas_call | solution.py:189
  69.7 2.5 fusion.77
  72.3 6.0 fusion.162
  81.4 29.3 %ring_gather.5 = bf16[2048,512]{1,0:T(8,128)(2,1)} custom-call(bf16[128,512]{1,0:T(8,128)(2,1)} %pad_maximum_fusion.7.x_ref), custom_call_target="tpu_custom_call" | custom-call | bytes 3000000 | tf_op jit(solution)/shard_map/ring_gather/pallas_call | solution.py:189
  114.5 4.7 fusion.97
  119.2 9.2 %fusion.219 = (f32[128,8]{0,1:T(8,128)S(1)}, f32[128,8,2048]{2,0,1:T(8,128)S(1)}) fusion(f32[128,8,2048]{2,0,1:T(8,128)} %fusion.97, pred[128,2048]{1,0:T(8,128)(4,1)S(1)} %fusion.107), kind=kOutput, calls=%fused_computation.315 | output fusion | flops 12584959 | bytes 17043456 | tf_op jit(solution)/shard_map/sub | solution.py:532
  128.4 3.3 copy-done.4
  133.3 16.9 %all-gather.8.cloned.1.call-done = bf16[2048,2048]{1,0:T(8,128)(2,1)} async-done(((bf16[128,2048]{1,0:T(8,128)(2,1)}), bf16[2048,2048]{1,0:T(8,128)(2,1)}) %all-gather.8.cloned.1.call-update) | async-done | bytes 8388624 | tf_op jit(solution)/shard_map/all_gather | solution.py:89
  150.2 6.5 convolution_add_fusion.9
  156.7 2.4 multiply_reduce_fusion.3
  160.8 47.4 %ring_gather.6 = bf16[2048,2048]{1,0:T(8,128)(2,1)} custom-call(bf16[128,2048]{1,0:T(8,128)(2,1)} %multiply_convert_fusion.3.x_ref), custom_call_target="tpu_custom_call" | custom-call | bytes 3000000 | tf_op jit(solution)/shard_map/ring_gather/pallas_call | solution.py:189
  209.4 6.1 convolution_convert_fusion.9
  215.5 13.1 %fusion.20 = f32[2048,1024]{1,0:T(8,128)S(1)} fusion(bf16[2048,2048]{1,0:T(8,128)(2,1)} %ring_gather.6, bf16[1024,3,2048]{2,0,1:T(8,128)(2,1)} %param.15), kind=kOutput, calls=%fused_computation.36 | convolution fusion | flops 8589934592 | bytes 20971520 | tf_op jit(solution)/shard_map/dot_general | solution.py:32
  228.6 13.0 %fusion.17 = f32[2048,1024]{1,0:T(8,128)} fusion(bf16[2048,2048]{1,0:T(8,128)(2,1)S(1)} %bitcast.217, bf16[1024,3,2048]{2,0,1:T(8,128)(2,1)} %param.15), kind=kOutput, calls=%fused_computation.33 | convolution fusion | flops 8589934592 | bytes 20971520 | tf_op jit(solution)/shard_map/dot_general | solution.py:32
  241.7 4.7 convolution_convert_fusion.8
  246.4 5.6 convolution_add_fusion.1
  251.9 30.6 %all-gather.10.cloned.1.call-done = bf16[2048,2048]{1,0:T(8,128)(2,1)} async-done(((bf16[128,2048]{1,0:T(8,128)(2,1)}), bf16[2048,2048]{1,0:T(8,128)(2,1)}) %all-gather.10.cloned.1.call-update) | async-done | bytes 8388624 | tf_op jit(solution)/shard_map/all_gather | solution.py:89
  282.5 6.2 convolution_convert_fusion.10
  288.7 13.5 %fusion.23 = f32[2048,1024]{1,0:T(8,128)S(1)} fusion(bf16[2048,2048]{1,0:T(8,128)(2,1)} %all-gather.10.cloned.1.call-done, bf16[1024,3,2048]{2,0,1:T(8,128)(2,1)} %param.15), kind=kOutput, calls=%fused_computation.39 | convolution fusion | flops 8589934592 | bytes 20971520 | tf_op jit(solution)/shard_map/dot_general | solution.py:32
  302.2 5.7 convolution_add_fusion.2
  307.9 15.1 %fusion.9 = (bf16[2048,1024]{1,0:T(8,128)(2,1)}, bf16[2048,1024]{1,0:T(8,128)(2,1)S(1)}, bf16[2048,1024]{1,0:T(8,128)(2,1)}) fusion(f32[2048,1024]{1,0:T(8,128)} %convolution_add_fusion.2, f32[2048,1024]{1,0:T(8,128)S(1)} %bitcast.212, f32[2048,1024]{1,0:T(8,128)} %fusion.17, bf16[2048,256]{1,0:T(8,128)(2,1)} %convolution_convert_fusion.8, ...), kind=kOutput, calls=%fused_computation.14 | convolution fusion | flops 1130364928 | bytes 39321604 | tf_op jit(solution)/shard_map/dot_general | solution.py:28
  323.0 6.6 convolution_convert_fusion.4.refs_2_
  329.6 3.5 convolution_convert_fusion.5.refs_1_
  333.1 3.3 convolution_convert_fusion.3.refs_4_
  336.4 9.6 %convert_bitcast_fusion.2 = bf16[1,1024,2048]{2,1,0:T(8,128)(2,1)S(1)} fusion(bf16[2048,1024]{1,0:T(8,128)(2,1)S(1)} %copy-done.45, bf16[2048,2048]{1,0:T(8,128)(2,1)S(1)} %bitcast.219), kind=kOutput, calls=%fused_computation.43 | convolution fusion | flops 8592031744 | bytes 16777216 | tf_op jit(solution)/shard_map/dot_general | solution.py:36
  346.0 11.5 %convert_bitcast_fusion.1 = bf16[1,1024,2048]{2,1,0:T(8,128)(2,1)S(1)} fusion(bf16[2048,1024]{1,0:T(8,128)(2,1)} %get-tuple-element.47, bf16[2048,2048]{1,0:T(8,128)(2,1)S(1)} %bitcast.219), kind=kOutput, calls=%fused_computation.42 | convolution fusion | flops 8592031744 | bytes 16777216 | tf_op jit(solution)/shard_map/dot_general | solution.py:36
  357.5 9.4 %convert_bitcast_fusion = bf16[1,1024,2048]{2,1,0:T(8,128)(2,1)S(1)} fusion(bf16[2048,1024]{1,0:T(8,128)(2,1)S(1)} %get-tuple-element.46, bf16[2048,2048]{1,0:T(8,128)(2,1)S(1)} %bitcast.267), kind=kOutput, calls=%fused_computation.41 | convolution fusion | flops 8592031744 | bytes 16777216 | tf_op jit(solution)/shard_map/dot_general | solution.py:36
  366.9 5.5 pad_maximum_fusion
  372.4 15.6 %fusion.15 = f32[2048,2048]{1,0:T(8,128)} fusion(bf16[2048,1024]{1,0:T(8,128)(2,1)} %get-tuple-element.45, bf16[1024,3,2048]{2,0,1:T(8,128)(2,1)} %param.15), kind=kOutput, calls=%fused_computation.31 | convolution fusion | flops 8589934592 | bytes 25165824 | tf_op jit(solution)/shard_map/dot_general | solution.py:28
  388.1 13.2 %convolution_convert_fusion.refs_3_ = bf16[2048,2048]{1,0:T(8,128)(2,1)} fusion(bf16[2048,1024]{1,0:T(8,128)(2,1)S(1)} %copy-done.43, bf16[1024,3,2048]{2,0,1:T(8,128)(2,1)} %param.15), kind=kOutput, calls=%fused_computation.22 | convolution fusion | flops 8594128896 | bytes 16777216 | tf_op jit(solution)/shard_map/dot_general | solution.py:28
  401.3 15.2 %add_convert_fusion.refs_0_ = bf16[2048,2048]{1,0:T(8,128)(2,1)} fusion(f32[2048,2048]{1,0:T(8,128)} %fusion.15, bf16[2048,1024]{1,0:T(8,128)(2,1)S(1)} %copy-done.47, bf16[1024,3,2048]{2,0,1:T(8,128)(2,1)} %param.15), kind=kOutput, calls=%fused_computation.2 | convolution fusion | flops 8598323200 | bytes 33554432 | tf_op jit(solution)/shard_map/dot_general | solution.py:28
  419.0 4.6 all-to-all-start
  423.7 123.8 %ring_scatter.2 = f32[128,4864]{1,0:T(8,128)} custom-call(bf16[2048,2048]{1,0:T(8,128)(2,1)} %add_convert_fusion.refs_0_, bf16[2048,256]{1,0:T(8,128)(2,1)} %convolution_convert_fusion.5.refs_1_, bf16[2048,256]{1,0:T(8,128)(2,1)} %convolution_convert_fusion.4.refs_2_, bf16[2048,2048]{1,0:T(8,128)(2,1)} %convolution_convert_fusion.refs_3_, ...), custom_call_target="tpu_custom_call" | custom-call | bytes 3000000 | tf_op jit(solution)/shard_map/ring_scatter/pallas_call | solution.py:304
  547.6 2.0 convert.96
  549.6 2.6 convolution_add_fusion.5
  552.3 2.0 multiply_reduce_fusion.1
  554.7 1.9 convolution_convert_fusion.17
  558.0 2.1 fusion.61
  564.5 2.3 fusion.48.refs_0_
  566.8 2.7 fusion.49.refs_1_
  569.5 23.2 %ring_scatter.3 = f32[128,512]{1,0:T(8,128)} custom-call(bf16[2048,256]{1,0:T(8,128)(2,1)} %fusion.48.refs_0_, bf16[2048,256]{1,0:T(8,128)(2,1)} %fusion.49.refs_1_), custom_call_target="tpu_custom_call" | custom-call | bytes 3000000 | tf_op jit(solution)/shard_map/ring_scatter/pallas_call | solution.py:304
  599.2 7.6 fusion.132
  606.9 2.2 fusion.92
  613.5 80.7 %ring_gather.7 = bf16[2048,3712]{1,0:T(8,128)(2,1)} custom-call(bf16[128,3712]{1,0:T(8,128)(2,1)} %pad_dynamic-update-slice_fusion.x_ref), custom_call_target="tpu_custom_call" | custom-call | bytes 3000000 | tf_op jit(solution)/shard_map/ring_gather/pallas_call | solution.py:189
  695.2 8.4 slice.235
  705.3 2.7 convolution_convert_fusion.1
  708.0 2.7 convolution_convert_fusion.2
  710.7 2.2 fusion.63
  713.0 7.0 fusion.50
  720.0 4.2 all-to-all-start.1
  724.5 3.2 fusion.37
  728.6 2.0 convolution_convert_fusion.15
  730.7 2.0 convolution_convert_fusion.14
  732.7 6.3 fusion.53
  740.3 2.3 convolution_bitcast_fusion.2
  744.1 2.1 convolution_convert_fusion.13
  751.1 2.7 fusion.34
  753.8 2.7 fusion.62
  757.2 7.4 convolution_convert_fusion.6.far_ref
  764.5 6.5 convolution_convert_fusion.11
  772.1 6.6 fusion.82
  779.9 47.7 %place_columns.1 = bf16[2464,256]{1,0:T(8,128)(2,1)} custom-call(bf16[2176,256]{1,0:T(8,128)(2,1)} %pad_maximum_fusion.2.mid_ref, bf16[2560,256]{1,0:T(8,128)(2,1)} %pad_maximum_fusion.1.near_ref, bf16[2048,256]{1,0:T(8,128)(2,1)} %convolution_convert_fusion.6.far_ref), custom_call_target="tpu_custom_call" | custom-call | bytes 90000000 | tf_op jit(solution)/shard_map/place_columns/pallas_call | solution.py:441
  827.6 3.0 convert_bitcast_fusion.3
  830.6 18.6 %add_bitcast_fusion = f32[1024,3,2048]{2,0,1:T(8,128)} fusion(bf16[2,3,1024,2048]{3,2,1,0:T(8,128)(2,1)} %bitcast.215), kind=kLoop, calls=%fused_computation.1 | loop fusion | flops 18874368 | bytes 50331648 | tf_op jit(solution)/shard_map/transpose | solution.py:716
  (232 shorter events, 51.0 us)
Async XLA Ops:
  7.2 61.3 %copy-start.41 = (s32[1,4]{1,0:T(1,128)S(1)}, s32[1,4]{1,0:T(1,128)}, u32[]{:S(2)}) copy-start(s32[1,4]{1,0:T(1,128)} %param.11) | copy-start | bytes 52
  7.2 61.8 %copy-start.2 = (bf16[1,128,2048]{2,1,0:T(8,128)(2,1)S(1)}, bf16[1,128,2048]{2,1,0:T(8,128)(2,1)}, u32[]{:S(2)}) copy-start(bf16[1,128,2048]{2,1,0:T(8,128)(2,1)} %param.10) | copy-start | bytes 1572868
  7.2 62.5 %copy-start.28 = (bf16[2,2048]{1,0:T(2,128)(2,1)S(1)}, bf16[2,2048]{1,0:T(2,128)(2,1)}, u32[]{:S(2)}) copy-start(bf16[2,2048]{1,0:T(2,128)(2,1)} %param.12) | copy-start | bytes 24580
  7.2 143.0 %all-gather.8.cloned.1.call-start = ((), (), s32[]{:S(2)}) async-start(), calls=%async_computation.2 | async-start | bytes 8912896 | tf_op jit(solution)/shard_map/all_gather | solution.py:89
  68.4 214.1 %all-gather.10.cloned.1.call-start = ((), (), s32[]{:S(2)}) async-start(), calls=%async_computation.3 | async-start | bytes 8912896 | tf_op jit(solution)/shard_map/all_gather | solution.py:89
  68.8 44.0 %copy-start.33 = (f32[128]{0:T(128)}, f32[128]{0:T(128)S(1)}, u32[]{:S(2)}) copy-start(f32[128]{0:T(128)S(1)} %multiply_exponential_fusion) | copy-start | bytes 1540
  69.0 43.8 %copy-start.31 = (f32[128]{0:T(128)}, f32[128]{0:T(128)S(1)}, u32[]{:S(2)}) copy-start(f32[128]{0:T(128)S(1)} %fusion.202) | copy-start | bytes 1540
  69.7 8.5 copy-start.29
  69.7 8.5 copy-start.23
  69.7 90.1 %copy-start.26 = (f32[1,2048]{1,0:T(1,128)}, f32[1,2048]{1,0:T(1,128)S(1)}, u32[]{:S(2)}) copy-start(f32[1,2048]{1,0:T(1,128)S(1)} %get-tuple-element.58) | copy-start | bytes 24580
  110.7 3.8 copy-start.5
  113.7 14.6 %copy-start.20 = (f32[128,128]{1,0:T(8,128)}, f32[128,128]{1,0:T(8,128)S(1)}, u32[]{:S(2)}) copy-start(f32[128,128]{1,0:T(8,128)S(1)} %get-tuple-element.62) | copy-start | bytes 196612
  114.0 14.4 %copy-start.16 = (bf16[128,8,128]{2,0,1:T(8,128)(2,1)}, bf16[128,8,128]{2,0,1:T(8,128)(2,1)S(1)}, u32[]{:S(2)}) copy-start(bf16[128,8,128]{2,0,1:T(8,128)(2,1)S(1)} %get-tuple-element.50) | copy-start | bytes 786436
  114.0 14.4 %copy-start.18 = (bf16[128,8,128]{2,0,1:T(8,128)(2,1)}, bf16[128,8,128]{2,0,1:T(8,128)(2,1)S(1)}, u32[]{:S(2)}) copy-start(bf16[128,8,128]{2,0,1:T(8,128)(2,1)S(1)} %get-tuple-element.51) | copy-start | bytes 786436
  159.1 56.3 %copy-start = (f32[128,2048]{1,0:T(8,128)}, f32[128,2048]{1,0:T(8,128)S(1)}, u32[]{:S(2)}) copy-start(f32[128,2048]{1,0:T(8,128)S(1)} %get-tuple-element.70) | copy-start | bytes 3145732
  159.8 48.3 %copy-start.35 = (f32[128]{0:T(128)}, f32[128]{0:T(128)S(1)}, u32[]{:S(2)}) copy-start(f32[128]{0:T(128)S(1)} %get-tuple-element.66) | copy-start | bytes 1540
  208.2 208.4 %all-gather.12.cloned.1.call-start = ((), (), s32[]{:S(2)}) async-start(), calls=%async_computation.4 | async-start | bytes 12255232 | tf_op jit(solution)/shard_map/all_gather | solution.py:89
  209.3 569.5 %all-gather.14.cloned.1.call-start = ((), (), s32[]{:S(2)}) async-start(), calls=%async_computation.5 | async-start | bytes 37748736 | tf_op jit(solution)/shard_map/all_gather | solution.py:97
  209.4 19.3 %slice-start.8 = ((s8[8388608]{0:T(1024)(128)(4,1)}), s8[4194304]{0:T(1024)(128)(4,1)S(1)}, s32[]{:S(2)}) async-start(s8[8388608]{0:T(1024)(128)(4,1)} %bitcast.216), calls=%async_computation.15 | async-start | bytes 8388608
  215.5 30.9 %copy-start.8 = (bf16[2048,256]{1,0:T(8,128)(2,1)}, bf16[2048,256]{1,0:T(8,128)(2,1)S(1)}, u32[]{:S(2)}) copy-start(bf16[2048,256]{1,0:T(8,128)(2,1)S(1)} %convolution_convert_fusion.9) | copy-start | bytes 3145732
  215.5 13.1 %slice-start.9 = ((s8[8388608]{0:T(1024)(128)(4,1)}), s8[4194304]{0:T(1024)(128)(4,1)S(1)}, s32[]{:S(2)}) async-start(s8[8388608]{0:T(1024)(128)(4,1)} %bitcast.216), calls=%async_computation.16 | async-start | bytes 8388608
  282.5 25.4 %slice-start.2 = ((s8[8388608]{0:T(1024)(128)(4,1)}), s8[4194304]{0:T(1024)(128)(4,1)S(1)}, s32[]{:S(2)}) async-start(s8[8388608]{0:T(1024)(128)(4,1)} %bitcast.211), calls=%async_computation.9 | async-start | bytes 8388608
  288.7 13.5 %copy-start.10 = (bf16[2048,256]{1,0:T(8,128)(2,1)}, bf16[2048,256]{1,0:T(8,128)(2,1)S(1)}, u32[]{:S(2)}) copy-start(bf16[2048,256]{1,0:T(8,128)(2,1)S(1)} %convolution_convert_fusion.10) | copy-start | bytes 3145732
  288.7 19.2 %slice-start.3 = ((s8[8388608]{0:T(1024)(128)(4,1)}), s8[4194304]{0:T(1024)(128)(4,1)S(1)}, s32[]{:S(2)}) async-start(s8[8388608]{0:T(1024)(128)(4,1)} %bitcast.211), calls=%async_computation.10 | async-start | bytes 8388608
  323.0 34.5 %copy-start.42 = (bf16[2048,1024]{1,0:T(8,128)(2,1)}, bf16[2048,1024]{1,0:T(8,128)(2,1)S(1)}, u32[]{:S(2)}) copy-start(bf16[2048,1024]{1,0:T(8,128)(2,1)S(1)} %get-tuple-element.46) | copy-start | bytes 12582916
  323.0 6.6 copy-start.45
  329.6 6.8 slice-start.10
  329.6 6.7 slice-start.11
  336.4 21.2 %slice-start.16 = ((s8[8388608]{0:T(1024)(128)(4,1)}), s8[4194304]{0:T(1024)(128)(4,1)S(1)}, s32[]{:S(2)}) async-start(s8[8388608]{0:T(1024)(128)(4,1)} %bitcast.266), calls=%async_computation.23 | async-start | bytes 8388608
  346.0 11.5 %slice-start.17 = ((s8[8388608]{0:T(1024)(128)(4,1)}), s8[4194304]{0:T(1024)(128)(4,1)S(1)}, s32[]{:S(2)}) async-start(s8[8388608]{0:T(1024)(128)(4,1)} %bitcast.266), calls=%async_computation.24 | async-start | bytes 8388608
  372.4 15.6 %copy-start.43 = (bf16[2048,1024]{1,0:T(8,128)(2,1)S(1)}, bf16[2048,1024]{1,0:T(8,128)(2,1)}, u32[]{:S(2)}) copy-start(bf16[2048,1024]{1,0:T(8,128)(2,1)} %copy-done.42) | copy-start | bytes 12582916
  388.1 13.2 %copy-start.47 = (bf16[2048,1024]{1,0:T(8,128)(2,1)S(1)}, bf16[2048,1024]{1,0:T(8,128)(2,1)}, u32[]{:S(2)}) copy-start(bf16[2048,1024]{1,0:T(8,128)(2,1)} %get-tuple-element.47) | copy-start | bytes 12582916
  419.0 300.9 %all-to-all-start = ((bf16[128,16,128]{2,0,1:T(8,128)(2,1)}), bf16[128,16,128]{2,0,1:T(8,128)(2,1)}, u32[]{:S(2)}, u32[]{:S(2)}) async-start(bf16[128,16,128]{2,0,1:T(8,128)(2,1)} %fusion.100), calls=%async_computation | async-start | bytes 1048576 | tf_op jit(solution)/shard_map/all_to_all | solution.py:105
  423.7 128.5 %copy-start.1 = (f32[128,2048]{1,0:T(8,128)S(1)}, f32[128,2048]{1,0:T(8,128)}, u32[]{:S(2)}) copy-start(f32[128,2048]{1,0:T(8,128)} %copy-done) | copy-start | bytes 3145732
  423.7 128.5 %copy-start.27 = (f32[1,2048]{1,0:T(1,128)S(1)}, f32[1,2048]{1,0:T(1,128)}, u32[]{:S(2)}) copy-start(f32[1,2048]{1,0:T(1,128)} %copy-done.26) | copy-start | bytes 24580
  423.7 128.5 %copy-start.36 = (f32[128]{0:T(128)S(1)}, f32[128]{0:T(128)}, u32[]{:S(2)}) copy-start(f32[128]{0:T(128)} %copy-done.35) | copy-start | bytes 1540
  547.5 6.7 copy-start.14
  547.6 6.7 copy-start.40
  547.6 9.0 %slice-start = ((s8[8388608]{0:T(1024)(128)(4,1)}), s8[4194304]{0:T(1024)(128)(4,1)S(1)}, s32[]{:S(2)}) async-start(s8[8388608]{0:T(1024)(128)(4,1)} %bitcast.209), calls=%async_computation.7 | async-start | bytes 8388608
  549.6 5.1 copy-start.13
  552.2 4.4 slice-start.1
  554.3 5.9 slice-start.12
  556.6 3.5 slice-start.13
  556.6 3.5 copy-start.6
  556.7 3.5 copy-start.38
  566.8 27.0 %copy-start.32 = (f32[128]{0:T(128)S(1)}, f32[128]{0:T(128)}, u32[]{:S(2)}) copy-start(f32[128]{0:T(128)} %copy-done.31) | copy-start | bytes 1540
  566.8 27.0 %copy-start.34 = (f32[128]{0:T(128)S(1)}, f32[128]{0:T(128)}, u32[]{:S(2)}) copy-start(f32[128]{0:T(128)} %copy-done.33) | copy-start | bytes 1540
  592.7 14.1 %slice-start.14 = ((s8[6291456]{0:T(1024)(128)(4,1)}), s8[4194304]{0:T(1024)(128)(4,1)S(1)}, s32[]{:S(2)}) async-start(s8[6291456]{0:T(1024)(128)(4,1)} %bitcast.239), calls=%async_computation.21 | async-start | bytes 8388608
  596.2 12.8 %copy-start.12 = (bf16[128,3712]{1,0:T(8,128)(2,1)}, bf16[128,3712]{1,0:T(8,128)(2,1)S(1)}, u32[]{:S(2)}) copy-start(bf16[128,3712]{1,0:T(8,128)(2,1)S(1)} %get-tuple-element.43) | copy-start | bytes 2850820
  599.2 7.6 slice-start.15
  720.0 44.5 %all-to-all-start.1 = ((bf16[128,16,128]{2,0,1:T(8,128)(2,1)}), bf16[128,16,128]{2,0,1:T(8,128)(2,1)}, u32[]{:S(2)}, u32[]{:S(2)}) async-start(bf16[128,16,128]{2,0,1:T(8,128)(2,1)} %bitcast.208), calls=%async_computation.1 | async-start | bytes 1048576 | tf_op jit(solution)/shard_map/all_to_all | solution.py:105
  724.2 124.9 %all-gather.16.cloned.1.call-start = ((), (), s32[]{:S(2)}) async-start(), calls=%async_computation.6 | async-start | bytes 3637248 | tf_op jit(solution)/shard_map/all_gather | solution.py:97
  732.7 7.5 copy-start.11
  732.7 7.5 copy-start.44
  740.2 3.6 copy-start.46
  740.3 3.8 copy-start.49
  740.3 5.9 slice-start.4
  740.3 6.3 slice-start.5
  742.5 5.4 slice-start.6
  744.1 4.6 slice-start.7
  744.1 5.7 copy-start.15
  744.1 5.7 copy-start.39
  751.1 5.4 copy-start.7
  772.1 6.7 copy-start.22
  (11 other events, 23.1 us)
Sparse Core Ops, SparseCore 0:
  68.6 81.6 all-gather.7
  208.3 74.1 all-gather.9
  285.2 95.6 all-gather.11
  416.7 291.7 all-gather.13
  778.9 37.9 all-gather.15

commit v4 on v3

--- a/solution.py
+++ b/solution.py
@@ -322,6 +322,156 @@
     )(*terms)
 
 
+def mix_kernel(chips, *refs):
+    gate_ref, up_ref, unit_ref, gate_w, up_w, down_w, gate_b, up_b, down_a, o_ref = refs[:10]
+    side_buf, ring_buf, stage, mine, side_send, side_recv, ring_send, ring_recv = refs[10:]
+    core, device = ring_neighbours(chips)
+    rows, columns = o_ref.shape
+    reach = chips // 2
+    half = columns // 2
+    tile = 16
+    wide = 256
+    ways = (device(1, core), device(-1, core))
+    side = device(0, 1 - core)
+    meet((*ways, side))
+    order = [(reach, 0, 0)]
+    for step in range(1, reach):
+        order += [(reach - step, 0, step), (chips - reach + step, 1, step)]
+    order.append((0, 0, reach))
+
+    def across(i):
+        target = order[i][0]
+        return pltpu.make_async_remote_copy(
+            stage.at[i % 2],
+            side_buf.at[target],
+            side_send.at[target],
+            side_recv.at[target],
+            device_id={"fsdp": side},
+            device_id_type=MESH,
+        )
+
+    def hop(way, step):
+        target = (reach - step if way == 0 else chips - reach + step) % chips
+        cols = pl.ds(way * half, half) if step == 0 else pl.ds(0, columns)
+        return pltpu.make_async_remote_copy(
+            side_buf.at[target, :, cols],
+            ring_buf.at[way, step, :, cols],
+            ring_send.at[way, step],
+            ring_recv.at[way, step],
+            device_id={"fsdp": ways[way]},
+            device_id_type=MESH,
+        )
+
+    def make(i):
+        target, slot = order[i][0], i % 2
+        if i >= 2:
+            across(i - 2).wait_send()
+        theirs = pl.ds(pl.multiple_of(device(target, 1 - core) * rows, rows), rows)
+        ours = pl.ds(pl.multiple_of(device(target, core) * rows, rows), rows)
+
+        def block(ref):
+            return jnp.concatenate([ref[theirs, :], ref[ours, :]], axis=0)
+
+        def put(first, value):
+            cols = pl.ds(pl.multiple_of(first, wide), wide)
+            stage[slot, :, cols] = value[:rows].astype(bf16)
+            mine[slot, :, cols] = value[rows:].astype(bf16)
+
+        @pl.loop(0, MODEL_WIDTH // wide)
+        def _(t):
+            cols = pl.ds(pl.multiple_of(t * wide, wide), wide)
+            put(
+                t * wide,
+                matrix_product(block(gate_ref), gate_w[:, cols])
+                + matrix_product(block(up_ref), up_w[:, cols]),
+            )
+            put(
+                MODEL_WIDTH + 2 * ADAPTER_RANK + t * wide,
+                matrix_product(block(unit_ref), down_w[:, cols]),
+            )
+
+        put(MODEL_WIDTH, times_transposed(block(gate_ref), gate_b[...]))
+        put(MODEL_WIDTH + ADAPTER_RANK, times_transposed(block(up_ref), up_b[...]))
+        put(2 * MODEL_WIDTH + 2 * ADAPTER_RANK, matrix_product(block(unit_ref), down_a[...]))
+        across(i).start()
+
+    def add(i):
+        target, way, step = order[i]
+        last = target == 0
+        incoming = [(w, step - 1) for w in ((0, 1) if last else (way,))] if step else []
+        across(i).wait_recv()
+        for w, s in incoming:
+            hop(w, s).wait_recv()
+
+        @pl.loop(0, rows // tile)
+        def _(j):
+            here = pl.ds(pl.multiple_of(j * tile, tile), tile)
+            for part in (0, 1):
+                cols = pl.ds(part * half, half)
+                total = mine[i % 2, here, cols].astype(f32) + side_buf[target, here, cols].astype(f32)
+                for w, s in incoming:
+                    if s or w == part:
+                        total = total + ring_buf[w, s, here, cols].astype(f32)
+                if last:
+                    o_ref[here, cols] = total
+                else:
+                    side_buf[target, here, cols] = total.astype(bf16)
+
+        if not last:
+            hop(way, step).start()
+            if step == 0:
+                hop(1, 0).start()
+
+    make(0)
+    for i in range(len(order)):
+        if i + 1 < len(order):
+            make(i + 1)
+        add(i)
+    for i in range(len(order) - 2, len(order)):
+        across(i).wait_send()
+    for step in range(reach):
+        for way in (0, 1):
+            hop(way, step).wait_send()
+
+
+def mix_rows(gate_grad, up_grad, units, gate_w, up_w, down_w, gate_b, up_b, down_a, ident):
+    size = lax.axis_size("fsdp")
+    if size != 16:
+        terms = [
+            matrix_product(gate_grad, gate_w) + matrix_product(up_grad, up_w),
+            times_transposed(gate_grad, gate_b),
+            times_transposed(up_grad, up_b),
+            matrix_product(units, down_w),
+            matrix_product(units, down_a),
+        ]
+        return scatter_rows(jnp.concatenate(terms, axis=1))
+    chips = size // 2
+    rows, columns = units.shape[0] // size, 2 * MODEL_WIDTH + 3 * ADAPTER_RANK
+    pair = pltpu.SemaphoreType.DMA((2, chips // 2))
+    sides = pltpu.SemaphoreType.DMA((chips,))
+    return pl.pallas_call(
+        functools.partial(mix_kernel, chips),
+        out_shape=jax.ShapeDtypeStruct((rows, columns), f32),
+        in_specs=[pl.BlockSpec(memory_space=pltpu.VMEM)] * 9,
+        out_specs=pl.BlockSpec(memory_space=pltpu.VMEM),
+        scratch_shapes=[
+            pltpu.VMEM((chips, rows, columns), bf16),
+            pltpu.VMEM((2, chips // 2, rows, columns), bf16),
+            pltpu.VMEM((2, rows, columns), bf16),
+            pltpu.VMEM((2, rows, columns), bf16),
+            sides,
+            sides,
+            pair,
+            pair,
+        ],
+        compiler_params=pltpu.CompilerParams(
+            collective_id=ident, has_side_effects=True, vmem_limit_bytes=60 << 20
+        ),
+        cost_estimate=busy(1),
+        name="mix_rows",
+    )(gate_grad, up_grad, units, gate_w, up_w, down_w, gate_b, up_b, down_a)
+
+
 def place_kernel(size, chunk, own_count, mid_ref, near_ref, far_ref, o_ref, send_sem, recv_sem, own_sem):
     me = lax.axis_index("fsdp")
     hidden = HIDDEN_COUNT // size
@@ -561,13 +711,6 @@
     units = (gelu_tanh(gate) * upward).astype(bf16)
     units_grad = times_transposed(grad_all, weight_down) + times_transposed(hd_grad, narrow_down)
     gate_grad, up_grad = unit_backward(gate, upward, units_grad)
-    back_terms = [
-        (matrix_product(gate_grad, weight_gate) + matrix_product(up_grad, weight_up)).astype(bf16),
-        times_transposed(gate_grad, widen_gate).astype(bf16),
-        times_transposed(up_grad, widen_up).astype(bf16),
-        matrix_product(units, weight_down).astype(bf16),
-        matrix_product(units, narrow_down).astype(bf16),
-    ]
     ffn_shares = jnp.stack(
         [
             outer_product_rows(former, latter).astype(bf16)
@@ -575,11 +718,13 @@
         ]
     )
     attended_all = gather_rows(jnp.concatenate([attended, lora_qkv], axis=1))
-    ffn_shares, back_terms, attended_all = lax.optimization_barrier(
-        (ffn_shares, back_terms, attended_all)
+    ffn_shares, gate_grad, attended_all = lax.optimization_barrier(
+        (ffn_shares, gate_grad, attended_all)
     )
     ffn_both = loop_shares(ffn_shares)
-    rows_sum = ring_scatter(back_terms, 3)
+    rows_sum = mix_rows(
+        gate_grad, up_grad, units, weight_gate, weight_up, weight_down, widen_gate, widen_up, narrow_down, 3
+    )
     back_own, out_own = rows_sum[:, : MODEL_WIDTH + 2 * rank], rows_sum[:, MODEL_WIDTH + 2 * rank :]
     down_own = outer_product_rows(units, hd_grad)
     gate_piece = outer_product_rows(gate_grad, lora_gate)

time: 871 us -> 855 us (0.982)
  matrix products: 291 us -> 240 us
  local copies, waits for them, and re-layouts: 27.8 us -> 44.4 us
  waiting for transfers between devices: 47.6 us -> 59.8 us
    pallas_call x0 -> x1, Pallas kernels: none -> 133 us  [mix_rows(): pl.pallas_call(functools.partial(mix_kernel, chips), out_shape=jax.ShapeD...]
    pallas_call x2 -> x1, Pallas kernels: 147 us -> 23.4 us  [ring_scatter(): pl.pallas_call(functools.partial(scatter_kernel, chips, count), out_shape...]
    dot_general x16 -> x12, matrix products: 97.5 us -> 49.4 us  [matrix_product(): return jnp.dot(former, latter, preferred_element_type=f32)]
    squeeze x0 -> x1, local copies, waits for them, and re-layouts: none -> 14.3 us  [per_device(): weight_down = feedforward_weight[:, 2, :]]
    all_gather x3, waiting for transfers between devices: 47.5 us -> 59.7 us  [gather_rows(): return lax.all_gather(block, 'fsdp', axis=0, tiled=True)]
    dot_general x20 -> x18, matrix products: 103 us -> 93.3 us  [times_transposed(): lax.dot_general(former, latter, (((1,), (1,)), ((), ())), preferred_eleme...]
  transfers between devices with their start and end apart: 7 -> 7, of which waited for: 2 -> 3; matrix products, arithmetic and copies ran while one was open for 41% -> 38% of each run, Pallas kernels for 35% -> 37%
where the time goes in v4:
time: 855 us; the launch traced here: 844 us
  Pallas kernels  420 us (49%)
  matrix products  240 us (28%)
  waiting for transfers between devices  59.8 us (7%)
  other arithmetic  56.2 us (7%)
  local copies, waits for them, and re-layouts  44.4 us (5%)
  between operations  15.3 us (2%)
  starting transfers between devices  9.03 us (1%)
    pallas_call x4, Pallas kernels, ring_gather(): pl.pallas_call(functools.partial(gather_kernel, chips), out_shape=jax.Sha...  216 us
    pallas_call x1, Pallas kernels, mix_rows(): pl.pallas_call(functools.partial(mix_kernel, chips), out_shape=jax.ShapeD...  133 us
    dot_general x18, matrix products, times_transposed(): lax.dot_general(former, latter, (((1,), (1,)), ((), ())), preferred_eleme...  93.3 us
    dot_general x16, matrix products, outer_product_rows(): lax.dot_general(former, latter, (((0,), (0,)), ((), ())), preferred_eleme...  83.4 us
    all_gather x3, waiting for transfers between devices, gather_rows(): return lax.all_gather(block, 'fsdp', axis=0, tiled=True)  59.7 us
    dot_general x12, matrix products, matrix_product(): return jnp.dot(former, latter, preferred_element_type=f32)  49.4 us
    pallas_call x1, Pallas kernels, place_columns(): pl.pallas_call(functools.partial(place_kernel, size, chunk, own_count), o...  47.7 us
    pallas_call x1, Pallas kernels, ring_scatter(): pl.pallas_call(functools.partial(scatter_kernel, chips, count), out_shape...  23.4 us
  transfers between devices with their start and end apart: 7, of which 3 were waited for; matrix products, arithmetic and copies ran while one was open for 38% of the time, Pallas kernels for 37%

profile of v4, /device:TPU:0, one launch (start us, length us, event | category | flops | bytes accessed | tf_op | source)
XLA Modules:
  0.0 844.4 jit_solution(16284288087345910609)
XLA Ops:
  7.3 61.2 %ring_gather.4 = bf16[2048,2560]{1,0:T(8,128)(2,1)} custom-call(bf16[128,2560]{1,0:T(8,128)(2,1)} %x_ref.1), custom_call_target="tpu_custom_call" | custom-call | bytes 3000000 | tf_op jit(solution)/shard_map/ring_gather/pallas_call | solution.py:189
  69.7 2.5 fusion.61
  72.3 6.0 fusion.134
  81.4 29.3 %ring_gather.5 = bf16[2048,512]{1,0:T(8,128)(2,1)} custom-call(bf16[128,512]{1,0:T(8,128)(2,1)} %pad_maximum_fusion.7.x_ref), custom_call_target="tpu_custom_call" | custom-call | bytes 3000000 | tf_op jit(solution)/shard_map/ring_gather/pallas_call | solution.py:189
  114.5 4.7 fusion.81
  119.2 9.2 %fusion.188 = (f32[128,8]{0,1:T(8,128)S(1)}, f32[128,8,2048]{2,0,1:T(8,128)S(1)}) fusion(f32[128,8,2048]{2,0,1:T(8,128)} %fusion.81, pred[128,2048]{1,0:T(8,128)(4,1)S(1)} %fusion.91), kind=kOutput, calls=%fused_computation.285 | output fusion | flops 12584959 | bytes 17043456 | tf_op jit(solution)/shard_map/sub | solution.py:682
  128.4 3.4 copy-done.4
  133.4 16.8 %all-gather.8.cloned.1.call-done = bf16[2048,2048]{1,0:T(8,128)(2,1)} async-done(((bf16[128,2048]{1,0:T(8,128)(2,1)}), bf16[2048,2048]{1,0:T(8,128)(2,1)}) %all-gather.8.cloned.1.call-update) | async-done | bytes 8388624 | tf_op jit(solution)/shard_map/all_gather | solution.py:89
  150.2 6.6 convolution_add_fusion.9
  156.9 2.4 multiply_reduce_fusion.3
  160.9 47.4 %ring_gather.6 = bf16[2048,2048]{1,0:T(8,128)(2,1)} custom-call(bf16[128,2048]{1,0:T(8,128)(2,1)} %multiply_convert_fusion.3.x_ref), custom_call_target="tpu_custom_call" | custom-call | bytes 3000000 | tf_op jit(solution)/shard_map/ring_gather/pallas_call | solution.py:189
  210.6 2.3 dynamic-slice_bitcast_fusion
  212.9 6.7 convolution_convert_fusion.5
  219.6 14.5 %fusion.181 = f32[2048,1024]{1,0:T(8,128)S(1)} fusion(bf16[2048,2048]{1,0:T(8,128)(2,1)S(1)} %bitcast.197, bf16[1024,3,2048]{2,0,1:T(8,128)(2,1)} %param.15), kind=kOutput, calls=%fused_computation.279 | convolution fusion | flops 8589934592 | bytes 20971520 | tf_op jit(solution)/shard_map/dot_general | solution.py:32
  234.2 4.6 convolution_add_fusion.1
  238.7 4.5 convolution_convert_fusion.4
  243.2 13.0 %fusion.182 = f32[2048,1024]{1,0:T(8,128)} fusion(bf16[2048,2048]{1,0:T(8,128)(2,1)S(1)} %bitcast.197, bf16[1024,3,2048]{2,0,1:T(8,128)(2,1)} %param.15), kind=kOutput, calls=%fused_computation.280 | convolution fusion | flops 8589934592 | bytes 20971520 | tf_op jit(solution)/shard_map/dot_general | solution.py:32
  256.3 26.4 %all-gather.10.cloned.1.call-done = bf16[2048,2048]{1,0:T(8,128)(2,1)} async-done(((bf16[128,2048]{1,0:T(8,128)(2,1)}), bf16[2048,2048]{1,0:T(8,128)(2,1)}) %all-gather.10.cloned.1.call-update) | async-done | bytes 8388624 | tf_op jit(solution)/shard_map/all_gather | solution.py:89
  282.6 6.2 convolution_convert_fusion.6
  288.8 13.5 %fusion.180 = f32[2048,1024]{1,0:T(8,128)S(1)} fusion(bf16[2048,2048]{1,0:T(8,128)(2,1)} %all-gather.10.cloned.1.call-done, bf16[1024,3,2048]{2,0,1:T(8,128)(2,1)} %param.15), kind=kOutput, calls=%fused_computation.278 | convolution fusion | flops 8589934592 | bytes 20971520 | tf_op jit(solution)/shard_map/dot_general | solution.py:32
  302.3 4.7 convolution_add_fusion.2
  307.0 14.9 %fusion.9 = (bf16[2048,1024]{1,0:T(8,128)(2,1)}, bf16[2048,1024]{1,0:T(8,128)(2,1)}, bf16[2048,1024]{1,0:T(8,128)(2,1)S(1)}) fusion(f32[2048,1024]{1,0:T(8,128)} %convolution_add_fusion.2, f32[2048,1024]{1,0:T(8,128)S(1)} %bitcast.192, f32[2048,1024]{1,0:T(8,128)} %fusion.182, bf16[2048,256]{1,0:T(8,128)(2,1)} %convolution_convert_fusion.4, ...), kind=kOutput, calls=%fused_computation.13 | convolution fusion | flops 1130364928 | bytes 39321600 | tf_op jit(solution)/shard_map/dot_general | solution.py:28
  322.0 15.3 %convert_bitcast_fusion.2 = bf16[1,1024,2048]{2,1,0:T(8,128)(2,1)S(1)} fusion(bf16[2048,1024]{1,0:T(8,128)(2,1)} %get-tuple-element.24.refs_0_, bf16[2048,2048]{1,0:T(8,128)(2,1)} %ring_gather.6), kind=kOutput, calls=%fused_computation.31 | convolution fusion | flops 8592031744 | bytes 16777216 | tf_op jit(solution)/shard_map/dot_general | solution.py:36
  337.3 12.1 %convert_bitcast_fusion.1 = bf16[1,1024,2048]{2,1,0:T(8,128)(2,1)S(1)} fusion(bf16[2048,1024]{1,0:T(8,128)(2,1)S(1)} %get-tuple-element.41.refs_1_, bf16[2048,2048]{1,0:T(8,128)(2,1)} %ring_gather.6), kind=kOutput, calls=%fused_computation.30 | convolution fusion | flops 8592031744 | bytes 16777216 | tf_op jit(solution)/shard_map/dot_general | solution.py:36
  349.5 9.7 %convert_bitcast_fusion = bf16[1,1024,2048]{2,1,0:T(8,128)(2,1)S(1)} fusion(bf16[2048,1024]{1,0:T(8,128)(2,1)S(1)} %copy-done.12, bf16[2048,2048]{1,0:T(8,128)(2,1)S(1)} %bitcast.245), kind=kOutput, calls=%fused_computation.29 | convolution fusion | flops 8592031744 | bytes 16777216 | tf_op jit(solution)/shard_map/dot_general | solution.py:36
  359.1 5.4 pad_maximum_fusion
  364.5 16.5 %all-gather.12.cloned.1.call-done = bf16[2048,2816]{0,1:T(8,128)(2,1)} async-done(((bf16[128,2816]{0,1:T(8,128)(2,1)}), bf16[2048,2816]{0,1:T(8,128)(2,1)}) %all-gather.12.cloned.1.call-update) | async-done | bytes 11534352 | tf_op jit(solution)/shard_map/all_gather | solution.py:89
  382.6 4.4 all-to-all-start
  387.0 14.3 %slice_bitcast_fusion.2 = (bf16[1024,2048]{1,0:T(8,128)(2,1)}, bf16[1024,2048]{1,0:T(8,128)(2,1)}, bf16[1024,2048]{1,0:T(8,128)(2,1)}) fusion(bf16[1024,3,2048]{2,0,1:T(8,128)(2,1)} %param.15), kind=kLoop, calls=%fused_computation.34 | loop fusion | bytes 25165824 | tf_op jit(solution)/shard_map/squeeze | solution.py:705
  401.3 132.7 %mix_rows.1 = f32[128,4864]{1,0:T(8,128)} custom-call(bf16[2048,1024]{1,0:T(8,128)(2,1)} %get-tuple-element.24.refs_0_, bf16[2048,1024]{1,0:T(8,128)(2,1)} %copy-done.9, bf16[2048,1024]{1,0:T(8,128)(2,1)} %get-tuple-element.40.refs_2_, bf16[1024,2048]{1,0:T(8,128)(2,1)} %get-tuple-element.43.refs_3_, bf16[1024,2048]{1,0:T(8,128)(2,1)} %get-tuple-element.44.refs_4_, ...), custom_call_target="tpu_custom_call" | custom-call | bytes 3000000 | tf_op jit(solution)/shard_map/mix_rows/pallas_call | solution.py:452
  534.0 2.0 convert.96
  536.0 2.6 convolution_add_fusion.5
  538.7 2.0 multiply_reduce_fusion.1
  541.1 1.9 convolution_convert_fusion.13
  544.4 2.1 fusion.45
  550.9 2.3 fusion.32.refs_0_
  553.2 2.7 fusion.33.refs_1_
  556.0 23.4 %ring_scatter.1 = f32[128,512]{1,0:T(8,128)} custom-call(bf16[2048,256]{1,0:T(8,128)(2,1)} %fusion.32.refs_0_, bf16[2048,256]{1,0:T(8,128)(2,1)} %fusion.33.refs_1_), custom_call_target="tpu_custom_call" | custom-call | bytes 3000000 | tf_op jit(solution)/shard_map/ring_scatter/pallas_call | solution.py:304
  584.1 1.7 convolution_convert_fusion.12
  585.9 7.6 fusion.116
  593.5 2.2 fusion.76
  600.2 78.1 %ring_gather.7 = bf16[2048,3712]{1,0:T(8,128)(2,1)} custom-call(bf16[128,3712]{1,0:T(8,128)(2,1)} %pad_dynamic-update-slice_fusion.x_ref), custom_call_target="tpu_custom_call" | custom-call | bytes 3000000 | tf_op jit(solution)/shard_map/ring_gather/pallas_call | solution.py:189
  679.2 8.4 slice.235
  687.6 1.7 fusion.89
  689.3 2.7 convolution_convert_fusion
  692.0 2.7 convolution_convert_fusion.1
  694.6 2.2 fusion.47
  696.9 7.0 fusion.34
  703.9 4.2 all-to-all-start.1
  708.4 3.2 fusion.21
  712.5 2.0 convolution_convert_fusion.11
  714.5 2.0 convolution_convert_fusion.10
  716.6 6.3 fusion.37
  724.1 2.3 convolution_bitcast_fusion.2
  728.0 2.1 convolution_convert_fusion.8
  735.0 2.7 fusion.18
  737.7 2.7 fusion.46
  741.0 7.3 convolution_convert_fusion.2.far_ref
  748.4 6.5 convolution_convert_fusion.7
  756.0 6.6 fusion.66
  763.7 47.7 %place_columns.1 = bf16[2464,256]{1,0:T(8,128)(2,1)} custom-call(bf16[2176,256]{1,0:T(8,128)(2,1)} %pad_maximum_fusion.2.mid_ref, bf16[2560,256]{1,0:T(8,128)(2,1)} %pad_maximum_fusion.1.near_ref, bf16[2048,256]{1,0:T(8,128)(2,1)} %convolution_convert_fusion.2.far_ref), custom_call_target="tpu_custom_call" | custom-call | bytes 90000000 | tf_op jit(solution)/shard_map/place_columns/pallas_call | solution.py:591
  811.5 3.0 convert_bitcast_fusion.3
  814.4 18.5 %add_bitcast_fusion = f32[1024,3,2048]{2,0,1:T(8,128)} fusion(bf16[2,3,1024,2048]{3,2,1,0:T(8,128)(2,1)} %bitcast.195), kind=kLoop, calls=%fused_computation.1 | loop fusion | flops 18874368 | bytes 50331648 | tf_op jit(solution)/shard_map/transpose | solution.py:861
  833.0 1.9 convert_add_fusion
  (224 shorter events, 45.7 us)
Async XLA Ops:
  7.2 61.3 %copy-start.48 = (s32[1,4]{1,0:T(1,128)S(1)}, s32[1,4]{1,0:T(1,128)}, u32[]{:S(2)}) copy-start(s32[1,4]{1,0:T(1,128)} %param.11) | copy-start | bytes 52
  7.2 61.8 %copy-start.2 = (bf16[1,128,2048]{2,1,0:T(8,128)(2,1)S(1)}, bf16[1,128,2048]{2,1,0:T(8,128)(2,1)}, u32[]{:S(2)}) copy-start(bf16[1,128,2048]{2,1,0:T(8,128)(2,1)} %param.10) | copy-start | bytes 1572868
  7.2 62.5 %copy-start.35 = (bf16[2,2048]{1,0:T(2,128)(2,1)S(1)}, bf16[2,2048]{1,0:T(2,128)(2,1)}, u32[]{:S(2)}) copy-start(bf16[2,2048]{1,0:T(2,128)(2,1)} %param.12) | copy-start | bytes 24580
  7.2 143.0 %all-gather.8.cloned.1.call-start = ((), (), s32[]{:S(2)}) async-start(), calls=%async_computation.2 | async-start | bytes 8912896 | tf_op jit(solution)/shard_map/all_gather | solution.py:89
  68.4 214.2 %all-gather.10.cloned.1.call-start = ((), (), s32[]{:S(2)}) async-start(), calls=%async_computation.3 | async-start | bytes 8912896 | tf_op jit(solution)/shard_map/all_gather | solution.py:89
  68.8 44.0 %copy-start.40 = (f32[128]{0:T(128)}, f32[128]{0:T(128)S(1)}, u32[]{:S(2)}) copy-start(f32[128]{0:T(128)S(1)} %multiply_exponential_fusion) | copy-start | bytes 1540
  69.0 43.8 %copy-start.38 = (f32[128]{0:T(128)}, f32[128]{0:T(128)S(1)}, u32[]{:S(2)}) copy-start(f32[128]{0:T(128)S(1)} %fusion.168) | copy-start | bytes 1540
  69.7 8.5 %copy-start.36 = (f32[128]{0:T(128)}, f32[128]{0:T(128)S(1)}, u32[]{:S(2)}) copy-start(f32[128]{0:T(128)S(1)} %get-tuple-element.61) | copy-start | bytes 1540
  69.7 8.5 %copy-start.30 = (f32[1,2048]{1,0:T(1,128)}, f32[1,2048]{1,0:T(1,128)S(1)}, u32[]{:S(2)}) copy-start(f32[1,2048]{1,0:T(1,128)S(1)} %get-tuple-element.56) | copy-start | bytes 24580
  69.7 90.2 %copy-start.33 = (f32[1,2048]{1,0:T(1,128)}, f32[1,2048]{1,0:T(1,128)S(1)}, u32[]{:S(2)}) copy-start(f32[1,2048]{1,0:T(1,128)S(1)} %get-tuple-element.55) | copy-start | bytes 24580
  110.7 3.8 copy-start.7
  113.7 14.6 %copy-start.27 = (f32[128,128]{1,0:T(8,128)}, f32[128,128]{1,0:T(8,128)S(1)}, u32[]{:S(2)}) copy-start(f32[128,128]{1,0:T(8,128)S(1)} %get-tuple-element.59) | copy-start | bytes 196612
  114.0 14.4 %copy-start.23 = (bf16[128,8,128]{2,0,1:T(8,128)(2,1)}, bf16[128,8,128]{2,0,1:T(8,128)(2,1)S(1)}, u32[]{:S(2)}) copy-start(bf16[128,8,128]{2,0,1:T(8,128)(2,1)S(1)} %get-tuple-element.47) | copy-start | bytes 786436
  114.0 14.4 %copy-start.25 = (bf16[128,8,128]{2,0,1:T(8,128)(2,1)}, bf16[128,8,128]{2,0,1:T(8,128)(2,1)S(1)}, u32[]{:S(2)}) copy-start(bf16[128,8,128]{2,0,1:T(8,128)(2,1)S(1)} %get-tuple-element.48) | copy-start | bytes 786436
  159.3 60.3 %copy-start = (f32[128,2048]{1,0:T(8,128)}, f32[128,2048]{1,0:T(8,128)S(1)}, u32[]{:S(2)}) copy-start(f32[128,2048]{1,0:T(8,128)S(1)} %get-tuple-element.67) | copy-start | bytes 3145732
  159.9 48.4 %copy-start.42 = (f32[128]{0:T(128)}, f32[128]{0:T(128)S(1)}, u32[]{:S(2)}) copy-start(f32[128]{0:T(128)S(1)} %get-tuple-element.63) | copy-start | bytes 1540
  208.3 172.7 %all-gather.12.cloned.1.call-start = ((), (), s32[]{:S(2)}) async-start(), calls=%async_computation.4 | async-start | bytes 12255232 | tf_op jit(solution)/shard_map/all_gather | solution.py:89
  209.5 553.2 %all-gather.14.cloned.1.call-start = ((), (), s32[]{:S(2)}) async-start(), calls=%async_computation.5 | async-start | bytes 37748736 | tf_op jit(solution)/shard_map/all_gather | solution.py:97
  210.6 91.7 %copy-start.6 = (bf16[1024,256]{1,0:T(8,128)(2,1)}, bf16[1024,256]{1,0:T(8,128)(2,1)S(1)}, u32[]{:S(2)}) copy-start(bf16[1024,256]{1,0:T(8,128)(2,1)S(1)} %dynamic-slice_bitcast_fusion.2.refs_8_) | copy-start | bytes 1572868
  210.6 9.0 %slice-start.8 = ((s8[8388608]{0:T(1024)(128)(4,1)}), s8[4194304]{0:T(1024)(128)(4,1)S(1)}, s32[]{:S(2)}) async-start(s8[8388608]{0:T(1024)(128)(4,1)} %bitcast.196), calls=%async_computation.15 | async-start | bytes 8388608
  212.9 21.2 %copy-start.5 = (bf16[256,1024]{1,0:T(8,128)(2,1)}, bf16[256,1024]{1,0:T(8,128)(2,1)S(1)}, u32[]{:S(2)}) copy-start(bf16[256,1024]{1,0:T(8,128)(2,1)S(1)} %get-tuple-element.38.refs_7_) | copy-start | bytes 1572868
  212.9 6.7 slice-start.9
  219.6 14.5 %copy-start.15 = (bf16[2048,256]{1,0:T(8,128)(2,1)}, bf16[2048,256]{1,0:T(8,128)(2,1)S(1)}, u32[]{:S(2)}) copy-start(bf16[2048,256]{1,0:T(8,128)(2,1)S(1)} %convolution_convert_fusion.5) | copy-start | bytes 3145732
  282.6 24.4 %slice-start.2 = ((s8[8388608]{0:T(1024)(128)(4,1)}), s8[4194304]{0:T(1024)(128)(4,1)S(1)}, s32[]{:S(2)}) async-start(s8[8388608]{0:T(1024)(128)(4,1)} %bitcast.191), calls=%async_computation.9 | async-start | bytes 8388608
  288.8 13.5 %copy-start.20 = (bf16[2048,256]{1,0:T(8,128)(2,1)}, bf16[2048,256]{1,0:T(8,128)(2,1)S(1)}, u32[]{:S(2)}) copy-start(bf16[2048,256]{1,0:T(8,128)(2,1)S(1)} %convolution_convert_fusion.6) | copy-start | bytes 3145732
  288.8 18.2 %slice-start.3 = ((s8[8388608]{0:T(1024)(128)(4,1)}), s8[4194304]{0:T(1024)(128)(4,1)S(1)}, s32[]{:S(2)}) async-start(s8[8388608]{0:T(1024)(128)(4,1)} %bitcast.191), calls=%async_computation.10 | async-start | bytes 8388608
  321.9 15.3 %copy-start.9 = (bf16[2048,1024]{1,0:T(8,128)(2,1)}, bf16[2048,1024]{1,0:T(8,128)(2,1)S(1)}, u32[]{:S(2)}) copy-start(bf16[2048,1024]{1,0:T(8,128)(2,1)S(1)} %get-tuple-element.41.refs_1_) | copy-start | bytes 12582916
  321.9 27.5 %slice-start.14 = ((s8[8388608]{0:T(1024)(128)(4,1)}), s8[4194304]{0:T(1024)(128)(4,1)S(1)}, s32[]{:S(2)}) async-start(s8[8388608]{0:T(1024)(128)(4,1)} %bitcast.244), calls=%async_computation.21 | async-start | bytes 8388608
  337.3 12.1 %copy-start.12 = (bf16[2048,1024]{1,0:T(8,128)(2,1)S(1)}, bf16[2048,1024]{1,0:T(8,128)(2,1)}, u32[]{:S(2)}) copy-start(bf16[2048,1024]{1,0:T(8,128)(2,1)} %get-tuple-element.40.refs_2_) | copy-start | bytes 12582916
  337.3 12.1 %slice-start.15 = ((s8[8388608]{0:T(1024)(128)(4,1)}), s8[4194304]{0:T(1024)(128)(4,1)S(1)}, s32[]{:S(2)}) async-start(s8[8388608]{0:T(1024)(128)(4,1)} %bitcast.244), calls=%async_computation.22 | async-start | bytes 8388608
  364.5 16.6 %copy-start.3 = (bf16[1,128,2048]{2,1,0:T(8,128)(2,1)S(1)}, bf16[1,128,2048]{2,1,0:T(8,128)(2,1)}, u32[]{:S(2)}) copy-start(bf16[1,128,2048]{2,1,0:T(8,128)(2,1)} %param.10) | copy-start | bytes 1572868
  364.5 16.9 %copy-start.31 = (f32[1,2048]{1,0:T(1,128)S(1)}, f32[1,2048]{1,0:T(1,128)}, u32[]{:S(2)}) copy-start(f32[1,2048]{1,0:T(1,128)} %copy-done.30) | copy-start | bytes 24580
  364.5 16.9 %copy-start.37 = (f32[128]{0:T(128)S(1)}, f32[128]{0:T(128)}, u32[]{:S(2)}) copy-start(f32[128]{0:T(128)} %copy-done.36) | copy-start | bytes 1540
  382.6 321.3 %all-to-all-start = ((bf16[128,16,128]{2,0,1:T(8,128)(2,1)}), bf16[128,16,128]{2,0,1:T(8,128)(2,1)}, u32[]{:S(2)}, u32[]{:S(2)}) async-start(bf16[128,16,128]{2,0,1:T(8,128)(2,1)} %fusion.84), calls=%async_computation | async-start | bytes 1048576 | tf_op jit(solution)/shard_map/all_to_all | solution.py:105
  401.3 137.4 %copy-start.1 = (f32[128,2048]{1,0:T(8,128)S(1)}, f32[128,2048]{1,0:T(8,128)}, u32[]{:S(2)}) copy-start(f32[128,2048]{1,0:T(8,128)} %copy-done) | copy-start | bytes 3145732
  401.3 137.4 %copy-start.34 = (f32[1,2048]{1,0:T(1,128)S(1)}, f32[1,2048]{1,0:T(1,128)}, u32[]{:S(2)}) copy-start(f32[1,2048]{1,0:T(1,128)} %copy-done.33) | copy-start | bytes 24580
  401.3 137.4 %copy-start.43 = (f32[128]{0:T(128)S(1)}, f32[128]{0:T(128)}, u32[]{:S(2)}) copy-start(f32[128]{0:T(128)} %copy-done.42) | copy-start | bytes 1540
  534.0 6.7 copy-start.19
  534.0 6.7 copy-start.47
  534.0 9.0 %slice-start = ((s8[8388608]{0:T(1024)(128)(4,1)}), s8[4194304]{0:T(1024)(128)(4,1)S(1)}, s32[]{:S(2)}) async-start(s8[8388608]{0:T(1024)(128)(4,1)} %bitcast.189), calls=%async_computation.7 | async-start | bytes 8388608
  536.0 5.1 copy-start.18
  538.7 4.4 slice-start.1
  540.7 5.9 slice-start.10
  543.1 3.5 slice-start.11
  543.1 3.5 copy-start.8
  553.2 27.2 %copy-start.39 = (f32[128]{0:T(128)S(1)}, f32[128]{0:T(128)}, u32[]{:S(2)}) copy-start(f32[128]{0:T(128)} %copy-done.38) | copy-start | bytes 1540
  553.2 27.2 %copy-start.41 = (f32[128]{0:T(128)S(1)}, f32[128]{0:T(128)}, u32[]{:S(2)}) copy-start(f32[128]{0:T(128)} %copy-done.40) | copy-start | bytes 1540
  579.3 14.1 %slice-start.12 = ((s8[6291456]{0:T(1024)(128)(4,1)}), s8[4194304]{0:T(1024)(128)(4,1)S(1)}, s32[]{:S(2)}) async-start(s8[6291456]{0:T(1024)(128)(4,1)} %bitcast.217), calls=%async_computation.19 | async-start | bytes 8388608
  582.9 12.8 %copy-start.17 = (bf16[128,3712]{1,0:T(8,128)(2,1)}, bf16[128,3712]{1,0:T(8,128)(2,1)S(1)}, u32[]{:S(2)}) copy-start(bf16[128,3712]{1,0:T(8,128)(2,1)S(1)} %get-tuple-element.35) | copy-start | bytes 2850820
  585.9 7.6 slice-start.13
  703.9 44.5 %all-to-all-start.1 = ((bf16[128,16,128]{2,0,1:T(8,128)(2,1)}), bf16[128,16,128]{2,0,1:T(8,128)(2,1)}, u32[]{:S(2)}, u32[]{:S(2)}) async-start(bf16[128,16,128]{2,0,1:T(8,128)(2,1)} %bitcast.188), calls=%async_computation.1 | async-start | bytes 1048576 | tf_op jit(solution)/shard_map/all_to_all | solution.py:105
  708.1 124.8 %all-gather.16.cloned.1.call-start = ((), (), s32[]{:S(2)}) async-start(), calls=%async_computation.6 | async-start | bytes 3637248 | tf_op jit(solution)/shard_map/all_gather | solution.py:97
  716.6 7.5 copy-start.13
  716.6 7.5 copy-start.21
  724.1 3.6 copy-start.10
  724.1 3.8 copy-start.16
  724.1 6.0 slice-start.4
  724.1 6.3 slice-start.5
  726.4 5.4 slice-start.6
  728.0 4.6 slice-start.7
  728.0 5.7 copy-start.22
  728.0 5.7 copy-start.46
  735.0 5.4 copy-start.14
  756.0 6.7 copy-start.29
  (9 other events, 23.0 us)
Sparse Core Ops, SparseCore 0:
  68.6 81.6 all-gather.7
  208.4 74.1 all-gather.9
  285.4 95.6 all-gather.11
  383.0 291.8 all-gather.13
  762.8 38.2 all-gather.15

commit v5 on v4

--- a/solution.py
+++ b/solution.py
@@ -125,13 +125,16 @@
         pl.semaphore_signal(barrier, inc=1, device_id={"fsdp": d}, device_id_type=MESH)
     pl.semaphore_wait(barrier, len(devices))
 
-def gather_kernel(chips, x_ref, o_ref, own_sem, ring_send, ring_recv, side_send, side_recv):
+def gather_kernel(chips, x_ref, o_ref, own_sem, ring_send, ring_recv, side_send, side_recv, greet=None, also=None):
     core, device = ring_neighbours(chips)
     rows = x_ref.shape[0]
     reach = chips // 2
     ways = (device(1, core), device(-1, core))
     side = device(0, 1 - core)
-    meet((*ways, side))
+    if greet is None:
+        meet((*ways, side))
+    else:
+        greet()
 
     def span(way, hops):
         return (way * (rows // 2), rows // 2) if hops == reach else (0, rows)
@@ -161,6 +164,8 @@
     across(0, 0, core).start()
     own = pltpu.make_async_copy(x_ref, at(0, 0, core, (0, rows)), own_sem)
     own.start()
+    if also is not None:
+        also()
     for hops in range(1, reach + 1):
         for way in (0, 1):
             arriving(way, hops).wait_recv()
@@ -323,8 +328,11 @@
 
 
 def mix_kernel(chips, *refs):
-    gate_ref, up_ref, unit_ref, gate_w, up_w, down_w, gate_b, up_b, down_a, o_ref = refs[:10]
-    side_buf, ring_buf, stage, mine, side_send, side_recv, ring_send, ring_recv = refs[10:]
+    gate_ref, up_ref, unit_ref, planes, gate_b, up_b, down_a, o_ref = refs[:8]
+    held, side_buf, ring_buf, stage, mine, held_sem, side_send, side_recv, ring_send, ring_recv = refs[8:]
+    fetches = [pltpu.make_async_copy(planes.at[i], held.at[i], held_sem.at[i]) for i in range(3)]
+    for fetch in fetches:
+        fetch.start()
     core, device = ring_neighbours(chips)
     rows, columns = o_ref.shape
     reach = chips // 2
@@ -382,12 +390,12 @@
             cols = pl.ds(pl.multiple_of(t * wide, wide), wide)
             put(
                 t * wide,
-                matrix_product(block(gate_ref), gate_w[:, cols])
-                + matrix_product(block(up_ref), up_w[:, cols]),
+                matrix_product(block(gate_ref), held[0, :, cols])
+                + matrix_product(block(up_ref), held[1, :, cols]),
             )
             put(
                 MODEL_WIDTH + 2 * ADAPTER_RANK + t * wide,
-                matrix_product(block(unit_ref), down_w[:, cols]),
+                matrix_product(block(unit_ref), held[2, :, cols]),
             )
 
         put(MODEL_WIDTH, times_transposed(block(gate_ref), gate_b[...]))
@@ -422,6 +430,8 @@
             if step == 0:
                 hop(1, 0).start()
 
+    for fetch in fetches:
+        fetch.wait()
     make(0)
     for i in range(len(order)):
         if i + 1 < len(order):
@@ -434,14 +444,14 @@
             hop(way, step).wait_send()
 
 
-def mix_rows(gate_grad, up_grad, units, gate_w, up_w, down_w, gate_b, up_b, down_a, ident):
+def mix_rows(gate_grad, up_grad, units, planes, gate_b, up_b, down_a, ident):
     size = lax.axis_size("fsdp")
     if size != 16:
         terms = [
-            matrix_product(gate_grad, gate_w) + matrix_product(up_grad, up_w),
+            matrix_product(gate_grad, planes[0]) + matrix_product(up_grad, planes[1]),
             times_transposed(gate_grad, gate_b),
             times_transposed(up_grad, up_b),
-            matrix_product(units, down_w),
+            matrix_product(units, planes[2]),
             matrix_product(units, down_a),
         ]
         return scatter_rows(jnp.concatenate(terms, axis=1))
@@ -452,13 +462,17 @@
     return pl.pallas_call(
         functools.partial(mix_kernel, chips),
         out_shape=jax.ShapeDtypeStruct((rows, columns), f32),
-        in_specs=[pl.BlockSpec(memory_space=pltpu.VMEM)] * 9,
+        in_specs=[pl.BlockSpec(memory_space=pltpu.VMEM)] * 3
+        + [pl.BlockSpec(memory_space=pl.ANY)]
+        + [pl.BlockSpec(memory_space=pltpu.VMEM)] * 3,
         out_specs=pl.BlockSpec(memory_space=pltpu.VMEM),
         scratch_shapes=[
+            pltpu.VMEM(planes.shape, bf16),
             pltpu.VMEM((chips, rows, columns), bf16),
             pltpu.VMEM((2, chips // 2, rows, columns), bf16),
             pltpu.VMEM((2, rows, columns), bf16),
             pltpu.VMEM((2, rows, columns), bf16),
+            pltpu.SemaphoreType.DMA((3,)),
             sides,
             sides,
             pair,
@@ -469,10 +483,11 @@
         ),
         cost_estimate=busy(1),
         name="mix_rows",
-    )(gate_grad, up_grad, units, gate_w, up_w, down_w, gate_b, up_b, down_a)
-
-
-def place_kernel(size, chunk, own_count, mid_ref, near_ref, far_ref, o_ref, send_sem, recv_sem, own_sem):
+    )(gate_grad, up_grad, units, planes, gate_b, up_b, down_a)
+
+
+def share_kernel(size, chunk, own_count, x_ref, mid_ref, all_ref, o_ref, *sems):
+    send_sem, recv_sem, own_sem = sems[5:]
     me = lax.axis_index("fsdp")
     hidden = HIDDEN_COUNT // size
     width = MODEL_WIDTH // size
@@ -481,15 +496,16 @@
         (width, GATE_START, hidden),
         (width + hidden, GATE_START + HIDDEN_COUNT, hidden),
     )
-    barrier = pltpu.get_barrier_semaphore()
-
-    def greet(i, carry):
-        other = (me + i) % size
-        pl.semaphore_signal(barrier, inc=1, device_id={"fsdp": other}, device_id_type=MESH)
-        return carry
-
-    lax.fori_loop(1, size, greet, 0)
-    pl.semaphore_wait(barrier, size - 1)
+
+    def greet():
+        barrier = pltpu.get_barrier_semaphore()
+
+        def one(i, carry):
+            pl.semaphore_signal(barrier, inc=1, device_id={"fsdp": (me + i) % size}, device_id_type=MESH)
+            return carry
+
+        lax.fori_loop(1, size, one, 0)
+        pl.semaphore_wait(barrier, size - 1)
 
     def rows(ref, first):
         return ref.at[pl.ds(pl.multiple_of(first, 8), chunk)]
@@ -511,58 +527,47 @@
     def local(source, first):
         return pltpu.make_async_copy(source, rows(o_ref, first), own_sem.at[first // chunk])
 
-    for base, start, length in sections:
-
-        def send(j, carry, base=base, aimed=aim(start, length)):
-            over = (aimed[1] + j * chunk >= own_count).astype(jnp.int32)
-            owner = aimed[0] + over
-            first = aimed[1] + j * chunk - over * own_count
-            source = rows(mid_ref, base + j * chunk)
-
-            @pl.when(owner != me)
-            def _():
-                remote(source, first, owner, base // chunk + j).start()
-
-            @pl.when(owner == me)
-            def _():
-                local(source, first).start()
-
-            return carry
-
-        lax.fori_loop(0, length // chunk, send, 0)
-
-    def fill(j, carry):
-        column = me * own_count + j * chunk
-
-        @pl.when(column < PROJECT_COLUMNS)
-        def _():
-            local(rows(near_ref, column), j * chunk).start()
-
-        @pl.when(column >= GATE_START + 2 * HIDDEN_COUNT)
-        def _():
-            local(rows(far_ref, column - (GATE_START + 2 * HIDDEN_COUNT)), j * chunk).start()
-
-        return carry
-
-    lax.fori_loop(0, own_count // chunk, fill, 0)
+    def send_all():
+        for base, start, length in sections:
+
+            def send(j, carry, base=base, aimed=aim(start, length)):
+                over = (aimed[1] + j * chunk >= own_count).astype(jnp.int32)
+                owner = aimed[0] + over
+                first = aimed[1] + j * chunk - over * own_count
+                source = rows(mid_ref, base + j * chunk)
+
+                @pl.when(owner != me)
+                def _():
+                    remote(source, first, owner, base // chunk + j).start()
+
+                @pl.when(owner == me)
+                def _():
+                    local(source, first).start()
+
+                return carry
+
+            lax.fori_loop(0, length // chunk, send, 0)
+
+    gather_kernel(size // 2, x_ref, all_ref, *sems[:5], greet=greet, also=send_all)
 
     def arrive(j, carry):
         column = me * own_count + j * chunk
         here = rows(o_ref, j * chunk)
-        away = 0
+        away, kept = 0, 0
         for _, start, length in sections:
             mine = start + me * length
             inside = (column >= start) & (column < start + length * size)
             outside = (column < mine) | (column >= mine + length)
             away = away + (inside & outside).astype(jnp.int32)
+            kept = kept + (inside & ~outside).astype(jnp.int32)
 
         @pl.when(away > 0)
         def _():
             remote(here, j * chunk, (me + 1) % size).wait_recv()
 
-        @pl.when(away == 0)
+        @pl.when(kept > 0)
         def _():
-            local(rows(near_ref, 0), j * chunk).wait()
+            local(rows(mid_ref, 0), j * chunk).wait()
 
         return carry
 
@@ -583,25 +588,36 @@
         lax.fori_loop(0, length // chunk, sent, 0)
 
 
-def place_columns(middle, near, far, ident):
+def share_rows(block, middle, ident):
     size = lax.axis_size("fsdp")
+    rows, columns = block.shape
     own_count = ADAPTER_COLUMNS // size
     chunk = math.gcd(own_count, MODEL_WIDTH // size, HIDDEN_COUNT // size, PROJECT_COLUMNS, GATE_START)
     anywhere = pl.BlockSpec(memory_space=pl.ANY)
+    pair = pltpu.SemaphoreType.DMA((2, size // 4))
+    sides = pltpu.SemaphoreType.DMA((2, size // 4 + 1))
     return pl.pallas_call(
-        functools.partial(place_kernel, size, chunk, own_count),
-        out_shape=jax.ShapeDtypeStruct((own_count, ADAPTER_RANK), bf16),
-        in_specs=[anywhere] * 3,
-        out_specs=anywhere,
+        functools.partial(share_kernel, size, chunk, own_count),
+        out_shape=(
+            jax.ShapeDtypeStruct((size * rows, columns), block.dtype),
+            jax.ShapeDtypeStruct((own_count, ADAPTER_RANK), bf16),
+        ),
+        in_specs=[anywhere] * 2,
+        out_specs=(anywhere, anywhere),
         scratch_shapes=[
+            pltpu.SemaphoreType.DMA,
+            pair,
+            pair,
+            sides,
+            sides,
             pltpu.SemaphoreType.DMA((middle.shape[0] // chunk,)),
             pltpu.SemaphoreType.DMA((own_count // chunk,)),
             pltpu.SemaphoreType.DMA((own_count // chunk,)),
         ],
         compiler_params=pltpu.CompilerParams(collective_id=ident, has_side_effects=True),
-        cost_estimate=busy(30),
-        name="place_columns",
-    )(middle, near, far)
+        cost_estimate=busy(1),
+        name="share_rows",
+    )(block, middle)
 
 
 def per_device(
@@ -700,9 +716,8 @@
     two_all = ring_gather(normed_two, 2)
     two_all, grad_rows = lax.optimization_barrier((two_all, grad_rows))
     grad_all = gather_rows(grad_rows)
-    weight_gate = feedforward_weight[:, 0, :]
-    weight_up = feedforward_weight[:, 1, :]
-    weight_down = feedforward_weight[:, 2, :]
+    weight_planes = feedforward_weight.transpose(1, 0, 2)
+    weight_gate, weight_up, weight_down = weight_planes[0], weight_planes[1], weight_planes[2]
     lora_gate = matrix_product(two_all, squeeze_gate).astype(bf16)
     lora_up = matrix_product(two_all, squeeze_up).astype(bf16)
     hd_grad = times_transposed(grad_all, widen_down).astype(bf16)
@@ -723,7 +738,7 @@
     )
     ffn_both = loop_shares(ffn_shares)
     rows_sum = mix_rows(
-        gate_grad, up_grad, units, weight_gate, weight_up, weight_down, widen_gate, widen_up, narrow_down, 3
+        gate_grad, up_grad, units, weight_planes, widen_gate, widen_up, narrow_down, 3
     )
     back_own, out_own = rows_sum[:, : MODEL_WIDTH + 2 * rank], rows_sum[:, MODEL_WIDTH + 2 * rank :]
     down_own = outer_product_rows(units, hd_grad)
@@ -793,19 +808,39 @@
     gain_one = jnp.sum(normed_grad * hidden_state * scale_one, axis=0)
 
     lora_qkv_all = attended_all[:, QUERY_WIDTH:]
-    attended_all = attended_all[:, :QUERY_WIDTH]
-    lora_out_all = matrix_product(attended_all, narrow_output).astype(bf16)
+    lora_out_all = matrix_product(attended_all[:, :QUERY_WIDTH], narrow_output).astype(bf16)
+    normed_turn, branch_turn = turn(normalized), turn(branch_grad)
+    out_piece = outer_product_rows(branch_turn, lora_out_all)
     gain_rows = jnp.stack([gain_one, gain_two]).astype(bf16).reshape(tokens_dev, -1)
     gain_count = gain_rows.shape[1]
     gain_rows = jnp.pad(gain_rows, ((0, 0), (0, -gain_count % 128)))
     proj_rows = jnp.concatenate(
         [proj_grad, lora_out_grad, gate_low, up_low, lora_hd, gain_rows], axis=1
     )
-    proj_all = ring_gather(proj_rows, 5)
-    low_all = proj_all[:, PROJECT_COLUMNS : PROJECT_COLUMNS + 4 * rank]
+    proj_rows, normed_turn, branch_turn = lax.optimization_barrier(
+        (proj_rows, normed_turn, branch_turn)
+    )
+    proj_all, middle_own = share_rows(
+        proj_rows, jnp.concatenate([out_piece, gate_piece, up_piece], axis=0).astype(bf16), 5
+    )
+    column = place * width_own
     gain_all = proj_all[:, PROJECT_COLUMNS + 4 * rank :][:, :gain_count].reshape(size, 2, MODEL_WIDTH)
     gain_all = jnp.sum(gain_all.astype(f32), axis=0)
-    gain_own = lax.dynamic_slice_in_dim(gain_all, place * width_own, width_own, 1)
+    gain_own = lax.dynamic_slice_in_dim(gain_all, column, width_own, 1)
+    gain_part = jnp.pad(gain_own, ((0, width_own - 2), (0, -width_own % 128)))
+    attn_part = jnp.concatenate(
+        [
+            outer_product_rows(normed_turn, proj_all[:, :PROJECT_COLUMNS]),
+            outer_product_rows(branch_turn, attended_all)[:, :QUERY_WIDTH],
+            gain_part,
+        ],
+        axis=1,
+    ).astype(bf16)
+    attn_part, ffn_both, proj_all = lax.optimization_barrier((attn_part, ffn_both, proj_all))
+    attn_sum = both_loops(loop_shares(attn_part))
+    gain_column = PROJECT_COLUMNS + QUERY_WIDTH
+    gain_sum = attn_sum[:2, gain_column : gain_column + width_own]
+    low_all = proj_all[:, PROJECT_COLUMNS : PROJECT_COLUMNS + 4 * rank]
     proj_all = proj_all[:, :PROJECT_COLUMNS]
     qkv_low_all = jnp.concatenate(
         [
@@ -815,22 +850,8 @@
         ],
         axis=1,
     ).astype(bf16)
-    normed_turn = turn(normalized)
-    branch_turn = turn(branch_grad)
-    column = place * width_own
     attended_turn = lax.dynamic_slice_in_dim(attended_all, column, width_own, 1)
     two_turn = lax.dynamic_slice_in_dim(two_all, column, width_own, 1)
-    attn_part = jnp.concatenate(
-        [outer_product_rows(normed_turn, proj_all), outer_product_rows(branch_turn, attended_all)],
-        axis=1,
-    )
-    gain_part = jnp.pad(gain_own, ((0, width_own - 2), (0, -width_own % 128)))
-    attn_part, ffn_both = lax.optimization_barrier(
-        (jnp.concatenate([attn_part, gain_part], axis=1).astype(bf16), ffn_both)
-    )
-    attn_sum = both_loops(loop_shares(attn_part))
-    gain_column = PROJECT_COLUMNS + QUERY_WIDTH
-    gain_sum = attn_sum[:2, gain_column : gain_column + width_own]
     squeeze_own = jnp.concatenate(
         [
             outer_product_rows(normed_turn, qkv_low_all),
@@ -839,7 +860,6 @@
         ],
         axis=1,
     )
-    out_piece = outer_product_rows(branch_turn, lora_out_all)
     near = jnp.concatenate(
         [
             outer_product_rows(proj_all[:, :QUERY_WIDTH], lora_qkv_all[:, :rank]),
@@ -851,13 +871,21 @@
         axis=0,
     )
     far = outer_product_rows(grad_all, low_all[:, 3 * rank :])
-    expand_own = place_columns(
-        jnp.concatenate([out_piece, gate_piece, up_piece], axis=0).astype(bf16),
-        near.astype(bf16),
-        far.astype(bf16),
-        6,
-    )
-    expand_own = expand_own.T.astype(f32)
+    first = place * columns_own
+    far_start = GATE_START + 2 * HIDDEN_COUNT
+    near = lax.dynamic_slice_in_dim(
+        jnp.pad(near.astype(bf16), ((0, columns_own), (0, 0))), jnp.minimum(first, PROJECT_COLUMNS), columns_own, 0
+    )
+    far = lax.dynamic_slice_in_dim(
+        jnp.pad(far.astype(bf16), ((columns_own, 0), (0, 0))),
+        jnp.maximum(first - far_start + columns_own, 0),
+        columns_own,
+        0,
+    )
+    owned = first + jnp.arange(columns_own, dtype=jnp.int32)[:, None]
+    expand_own = jnp.where(
+        owned < PROJECT_COLUMNS, near, jnp.where(owned < far_start, middle_own, far)
+    ).T.astype(f32)
     ffn_sum = both_loops(ffn_both).transpose(1, 0, 2)
     return (
         hidden_out[None],

time: 855 us -> 836 us (0.978)
  local copies, waits for them, and re-layouts: 44.4 us -> 19.5 us
  Pallas kernels: 420 us -> 407 us
  waiting for transfers between devices: 59.8 us -> 68.8 us
    pallas_call x4 -> x3, Pallas kernels: 216 us -> 138 us  [ring_gather(): pl.pallas_call(functools.partial(gather_kernel, chips), out_shape=jax.Sha...]
    pallas_call x1, Pallas kernels: 47.7 us -> 108 us  [share_rows(): pl.pallas_call(functools.partial(share_kernel, size, chunk, own_count), o...]
    squeeze x1 -> x0, local copies, waits for them, and re-layouts: 14.3 us -> none  [per_device(): weight_down = feedforward_weight[:, 2, :]]
    dot_general x16, matrix products: 83.4 us -> 93 us  [outer_product_rows(): lax.dot_general(former, latter, (((0,), (0,)), ((), ())), preferred_eleme...]
  transfers between devices with their start and end apart: 7 -> 7, of which waited for: 3 -> 5; matrix products, arithmetic and copies ran while one was open for 38% -> 34% of each run, Pallas kernels for 37% -> 36%
where the time goes in v5:
time: 836 us; the launch traced here: 825 us
  Pallas kernels  407 us (49%)
  matrix products  245 us (29%)
  waiting for transfers between devices  68.8 us (8%)
  other arithmetic  59.7 us (7%)
  local copies, waits for them, and re-layouts  19.5 us (2%)
  between operations  15.4 us (2%)
  starting transfers between devices  9.26 us (1%)
    pallas_call x1, Pallas kernels, mix_rows(): pl.pallas_call(functools.partial(mix_kernel, chips), out_shape=jax.ShapeD...  138 us
    pallas_call x3, Pallas kernels, ring_gather(): pl.pallas_call(functools.partial(gather_kernel, chips), out_shape=jax.Sha...  138 us
    pallas_call x1, Pallas kernels, share_rows(): pl.pallas_call(functools.partial(share_kernel, size, chunk, own_count), o...  108 us
    dot_general x16, matrix products, outer_product_rows(): lax.dot_general(former, latter, (((0,), (0,)), ((), ())), preferred_eleme...  93 us
    dot_general x18, matrix products, times_transposed(): lax.dot_general(former, latter, (((1,), (1,)), ((), ())), preferred_eleme...  89 us
    all_gather x3, waiting for transfers between devices, gather_rows(): return lax.all_gather(block, 'fsdp', axis=0, tiled=True)  59.8 us
    dot_general x12, matrix products, matrix_product(): return jnp.dot(former, latter, preferred_element_type=f32)  49.4 us
    pallas_call x1, Pallas kernels, ring_scatter(): pl.pallas_call(functools.partial(scatter_kernel, chips, count), out_shape...  22.8 us
  transfers between devices with their start and end apart: 7, of which 5 were waited for; matrix products, arithmetic and copies ran while one was open for 34% of the time, Pallas kernels for 36%

profile of v5, /device:TPU:0, one launch (start us, length us, event | category | flops | bytes accessed | tf_op | source)
XLA Modules:
  0.0 825.0 jit_solution(747956430920746925)
XLA Ops:
  7.3 61.2 %ring_gather.3 = bf16[2048,2560]{1,0:T(8,128)(2,1)} custom-call(bf16[128,2560]{1,0:T(8,128)(2,1)} %x_ref.1), custom_call_target="tpu_custom_call" | custom-call | bytes 3000000 | tf_op jit(solution)/shard_map/ring_gather/pallas_call | solution.py:194
  69.7 2.5 fusion.79
  72.3 6.0 fusion.153
  81.4 29.3 %ring_gather.4 = bf16[2048,512]{1,0:T(8,128)(2,1)} custom-call(bf16[128,512]{1,0:T(8,128)(2,1)} %pad_maximum_fusion.6.x_ref), custom_call_target="tpu_custom_call" | custom-call | bytes 3000000 | tf_op jit(solution)/shard_map/ring_gather/pallas_call | solution.py:194
  110.7 1.7 convolution_add_fusion.8
  114.5 4.7 fusion.100
  119.2 9.2 %fusion.203 = (f32[128,8]{0,1:T(8,128)S(1)}, f32[128,8,2048]{2,0,1:T(8,128)S(1)}) fusion(f32[128,8,2048]{2,0,1:T(8,128)} %fusion.100, pred[128,2048]{1,0:T(8,128)(4,1)S(1)} %fusion.110), kind=kOutput, calls=%fused_computation.299 | output fusion | flops 12584959 | bytes 17043456 | tf_op jit(solution)/shard_map/sub | solution.py:698
  128.4 3.4 copy-done.4
  133.4 16.8 %all-gather.8.cloned.1.call-done = bf16[2048,2048]{1,0:T(8,128)(2,1)} async-done(((bf16[128,2048]{1,0:T(8,128)(2,1)}), bf16[2048,2048]{1,0:T(8,128)(2,1)}) %all-gather.8.cloned.1.call-update) | async-done | bytes 8388624 | tf_op jit(solution)/shard_map/all_gather | solution.py:89
  150.2 6.6 convolution_add_fusion.9
  156.9 2.4 multiply_reduce_fusion.3
  160.8 47.4 %ring_gather.5 = bf16[2048,2048]{1,0:T(8,128)(2,1)} custom-call(bf16[128,2048]{1,0:T(8,128)(2,1)} %multiply_convert_fusion.3.x_ref), custom_call_target="tpu_custom_call" | custom-call | bytes 3000000 | tf_op jit(solution)/shard_map/ring_gather/pallas_call | solution.py:194
  210.5 2.3 dynamic-slice_bitcast_fusion
  212.8 6.6 convolution_convert_fusion.4
  219.6 14.5 %fusion.18 = f32[2048,1024]{1,0:T(8,128)S(1)} fusion(bf16[2048,2048]{1,0:T(8,128)(2,1)S(1)} %bitcast.201, bf16[3,1024,2048]{2,1,0:T(8,128)(2,1)} %bitcast.196), kind=kOutput, calls=%fused_computation.34 | convolution fusion | flops 8589934592 | bytes 20971520 | tf_op jit(solution)/shard_map/dot_general | solution.py:32
  234.0 4.6 convolution_add_fusion.1
  238.6 4.5 convolution_convert_fusion.3
  243.1 13.0 %fusion.17 = f32[2048,1024]{1,0:T(8,128)} fusion(bf16[2048,2048]{1,0:T(8,128)(2,1)S(1)} %bitcast.201, bf16[3,1024,2048]{2,1,0:T(8,128)(2,1)} %bitcast.197), kind=kOutput, calls=%fused_computation.32 | convolution fusion | flops 8589934592 | bytes 20971520 | tf_op jit(solution)/shard_map/dot_general | solution.py:32
  256.2 26.4 %all-gather.10.cloned.1.call-done = bf16[2048,2048]{1,0:T(8,128)(2,1)} async-done(((bf16[128,2048]{1,0:T(8,128)(2,1)}), bf16[2048,2048]{1,0:T(8,128)(2,1)}) %all-gather.10.cloned.1.call-update) | async-done | bytes 8388624 | tf_op jit(solution)/shard_map/all_gather | solution.py:89
  282.6 6.2 convolution_convert_fusion.5
  288.8 13.5 %fusion.19 = f32[2048,1024]{1,0:T(8,128)S(1)} fusion(bf16[2048,2048]{1,0:T(8,128)(2,1)} %all-gather.10.cloned.1.call-done, bf16[3,1024,2048]{2,1,0:T(8,128)(2,1)} %bitcast.198), kind=kOutput, calls=%fused_computation.36 | convolution fusion | flops 8589934592 | bytes 20971520 | tf_op jit(solution)/shard_map/dot_general | solution.py:32
  302.3 4.7 convolution_add_fusion.2
  306.9 14.9 %fusion.9 = (bf16[2048,1024]{1,0:T(8,128)(2,1)}, bf16[2048,1024]{1,0:T(8,128)(2,1)S(1)}, bf16[2048,1024]{1,0:T(8,128)(2,1)}) fusion(f32[2048,1024]{1,0:T(8,128)} %convolution_add_fusion.2, f32[2048,1024]{1,0:T(8,128)S(1)} %bitcast.194, f32[2048,1024]{1,0:T(8,128)} %fusion.17, bf16[2048,256]{1,0:T(8,128)(2,1)} %convolution_convert_fusion.3, ...), kind=kOutput, calls=%fused_computation.13 | convolution fusion | flops 1130364928 | bytes 39321600 | tf_op jit(solution)/shard_map/dot_general | solution.py:28
  321.9 15.3 %convert_bitcast_fusion.2 = bf16[1,1024,2048]{2,1,0:T(8,128)(2,1)S(1)} fusion(bf16[2048,1024]{1,0:T(8,128)(2,1)} %get-tuple-element.30.refs_0_, bf16[2048,2048]{1,0:T(8,128)(2,1)} %ring_gather.5), kind=kOutput, calls=%fused_computation.39 | convolution fusion | flops 8592031744 | bytes 16777216 | tf_op jit(solution)/shard_map/dot_general | solution.py:36
  337.2 12.4 %convert_bitcast_fusion.1 = bf16[1,1024,2048]{2,1,0:T(8,128)(2,1)S(1)} fusion(bf16[2048,1024]{1,0:T(8,128)(2,1)S(1)} %copy-done.10, bf16[2048,2048]{1,0:T(8,128)(2,1)} %ring_gather.5), kind=kOutput, calls=%fused_computation.38 | convolution fusion | flops 8592031744 | bytes 16777216 | tf_op jit(solution)/shard_map/dot_general | solution.py:36
  349.6 9.4 %convert_bitcast_fusion = bf16[1,1024,2048]{2,1,0:T(8,128)(2,1)S(1)} fusion(bf16[2048,1024]{1,0:T(8,128)(2,1)S(1)} %get-tuple-element.52.refs_2_, bf16[2048,2048]{1,0:T(8,128)(2,1)S(1)} %bitcast.253), kind=kOutput, calls=%fused_computation.37 | convolution fusion | flops 8592031744 | bytes 16777216 | tf_op jit(solution)/shard_map/dot_general | solution.py:36
  359.0 5.4 pad_maximum_fusion
  364.4 16.5 %all-gather.12.cloned.1.call-done = bf16[2048,2816]{0,1:T(8,128)(2,1)} async-done(((bf16[128,2816]{0,1:T(8,128)(2,1)}), bf16[2048,2816]{0,1:T(8,128)(2,1)}) %all-gather.12.cloned.1.call-update) | async-done | bytes 11534352 | tf_op jit(solution)/shard_map/all_gather | solution.py:89
  382.5 4.4 all-to-all-start
  387.0 138.3 %mix_rows.1 = f32[128,4864]{1,0:T(8,128)} custom-call(bf16[2048,1024]{1,0:T(8,128)(2,1)} %get-tuple-element.30.refs_0_, bf16[2048,1024]{1,0:T(8,128)(2,1)} %get-tuple-element.53.refs_1_, bf16[2048,1024]{1,0:T(8,128)(2,1)} %copy-done.9, bf16[3,1024,2048]{2,1,0:T(8,128)(2,1)} %bitcast.199, bf16[256,1024]{1,0:T(8,128)(2,1)} %get-tuple-element.49.refs_4_, ...), custom_call_target="tpu_custom_call" | custom-call | bytes 3000000 | tf_op jit(solution)/shard_map/mix_rows/pallas_call | solution.py:462
  525.3 2.0 convert.97
  527.3 2.6 convolution_add_fusion.5
  530.0 2.0 multiply_reduce_fusion.1
  532.5 1.9 convolution_convert_fusion.11
  535.8 2.1 fusion.56
  542.3 2.3 fusion.37.refs_0_
  544.6 2.7 fusion.38.refs_1_
  547.3 22.8 %ring_scatter.1 = f32[128,512]{1,0:T(8,128)} custom-call(bf16[2048,256]{1,0:T(8,128)(2,1)} %fusion.37.refs_0_, bf16[2048,256]{1,0:T(8,128)(2,1)} %fusion.38.refs_1_), custom_call_target="tpu_custom_call" | custom-call | bytes 3000000 | tf_op jit(solution)/shard_map/ring_scatter/pallas_call | solution.py:309
  575.0 1.7 convolution_convert_fusion.10
  576.7 7.6 fusion.135
  584.3 2.2 fusion.95
  587.4 1.9 slice_dynamic-update-slice_fusion
  590.8 2.7 fusion.57
  595.1 4.7 convolution_convert_fusion.7
  599.7 2.1 convolution_convert_fusion.6
  601.8 4.2 all-to-all-start.1
  606.6 4.5 convolution_bitcast_fusion.2
  612.4 8.1 all-to-all-done.1
  620.5 8.2 fusion.206
  628.8 6.7 fusion.83
  636.6 108.4 %share_rows.1 = (bf16[2048,3712]{1,0:T(8,128)(2,1)}, bf16[2464,256]{1,0:T(8,128)(2,1)}) custom-call(bf16[128,3712]{1,0:T(8,128)(2,1)} %pad_dynamic-update-slice_fusion.x_ref, bf16[2176,256]{1,0:T(8,128)(2,1)} %pad_maximum_fusion.1.mid_ref), custom_call_target="tpu_custom_call" | custom-call | bytes 3000000 | tf_op jit(solution)/shard_map/share_rows/pallas_call | solution.py:599
  746.8 5.7 fusion.23
  753.7 2.2 convolution_convert_fusion.8
  755.9 2.7 convolution_convert_fusion.9
  758.6 6.3 fusion.42
  764.9 1.7 convolution_convert_fusion
  766.6 1.7 convolution_convert_fusion.1
  768.4 4.6 fusion.39
  774.5 2.0 fusion.108
  776.6 2.6 fusion.26
  779.2 6.6 convolution_convert_fusion.2
  786.8 7.5 convert_bitcast_fusion.3
  794.2 18.5 %add_bitcast_fusion = f32[1024,3,2048]{2,0,1:T(8,128)} fusion(bf16[2,3,1024,2048]{3,2,1,0:T(8,128)(2,1)} %bitcast.195), kind=kLoop, calls=%fused_computation.1 | loop fusion | flops 18874368 | bytes 50331648 | tf_op jit(solution)/shard_map/transpose | solution.py:889
  813.6 1.9 convert_add_fusion
  (225 shorter events, 40.0 us)
Async XLA Ops:
  7.2 61.3 %copy-start.50 = (s32[1,4]{1,0:T(1,128)S(1)}, s32[1,4]{1,0:T(1,128)}, u32[]{:S(2)}) copy-start(s32[1,4]{1,0:T(1,128)} %param.11) | copy-start | bytes 52
  7.2 61.8 %copy-start.2 = (bf16[1,128,2048]{2,1,0:T(8,128)(2,1)S(1)}, bf16[1,128,2048]{2,1,0:T(8,128)(2,1)}, u32[]{:S(2)}) copy-start(bf16[1,128,2048]{2,1,0:T(8,128)(2,1)} %param.10) | copy-start | bytes 1572868
  7.2 62.5 %copy-start.37 = (bf16[2,2048]{1,0:T(2,128)(2,1)S(1)}, bf16[2,2048]{1,0:T(2,128)(2,1)}, u32[]{:S(2)}) copy-start(bf16[2,2048]{1,0:T(2,128)(2,1)} %param.12) | copy-start | bytes 24580
  7.2 143.0 %all-gather.8.cloned.1.call-start = ((), (), s32[]{:S(2)}) async-start(), calls=%async_computation.2 | async-start | bytes 8912896 | tf_op jit(solution)/shard_map/all_gather | solution.py:89
  68.4 214.1 %all-gather.10.cloned.1.call-start = ((), (), s32[]{:S(2)}) async-start(), calls=%async_computation.3 | async-start | bytes 8912896 | tf_op jit(solution)/shard_map/all_gather | solution.py:89
  68.8 44.0 %copy-start.42 = (f32[128]{0:T(128)}, f32[128]{0:T(128)S(1)}, u32[]{:S(2)}) copy-start(f32[128]{0:T(128)S(1)} %multiply_exponential_fusion) | copy-start | bytes 1540
  69.0 43.8 %copy-start.40 = (f32[128]{0:T(128)}, f32[128]{0:T(128)S(1)}, u32[]{:S(2)}) copy-start(f32[128]{0:T(128)S(1)} %fusion.189) | copy-start | bytes 1540
  69.7 8.5 %copy-start.38 = (f32[128]{0:T(128)}, f32[128]{0:T(128)S(1)}, u32[]{:S(2)}) copy-start(f32[128]{0:T(128)S(1)} %get-tuple-element.70) | copy-start | bytes 1540
  69.7 8.5 %copy-start.30 = (f32[1,2048]{1,0:T(1,128)}, f32[1,2048]{1,0:T(1,128)S(1)}, u32[]{:S(2)}) copy-start(f32[1,2048]{1,0:T(1,128)S(1)} %get-tuple-element.65) | copy-start | bytes 24580
  69.7 90.2 %copy-start.33 = (f32[1,2048]{1,0:T(1,128)}, f32[1,2048]{1,0:T(1,128)S(1)}, u32[]{:S(2)}) copy-start(f32[1,2048]{1,0:T(1,128)S(1)} %get-tuple-element.64) | copy-start | bytes 24580
  113.7 14.6 %copy-start.26 = (f32[128,128]{1,0:T(8,128)}, f32[128,128]{1,0:T(8,128)S(1)}, u32[]{:S(2)}) copy-start(f32[128,128]{1,0:T(8,128)S(1)} %get-tuple-element.68) | copy-start | bytes 196612
  114.0 14.4 %copy-start.22 = (bf16[128,8,128]{2,0,1:T(8,128)(2,1)}, bf16[128,8,128]{2,0,1:T(8,128)(2,1)S(1)}, u32[]{:S(2)}) copy-start(bf16[128,8,128]{2,0,1:T(8,128)(2,1)S(1)} %get-tuple-element.56) | copy-start | bytes 786436
  114.0 14.4 %copy-start.24 = (bf16[128,8,128]{2,0,1:T(8,128)(2,1)}, bf16[128,8,128]{2,0,1:T(8,128)(2,1)S(1)}, u32[]{:S(2)}) copy-start(bf16[128,8,128]{2,0,1:T(8,128)(2,1)S(1)} %get-tuple-element.57) | copy-start | bytes 786436
  159.3 60.2 %copy-start = (f32[128,2048]{1,0:T(8,128)}, f32[128,2048]{1,0:T(8,128)S(1)}, u32[]{:S(2)}) copy-start(f32[128,2048]{1,0:T(8,128)S(1)} %get-tuple-element.76) | copy-start | bytes 3145732
  159.9 48.4 %copy-start.44 = (f32[128]{0:T(128)}, f32[128]{0:T(128)S(1)}, u32[]{:S(2)}) copy-start(f32[128]{0:T(128)S(1)} %get-tuple-element.72) | copy-start | bytes 1540
  208.2 172.7 %all-gather.12.cloned.1.call-start = ((), (), s32[]{:S(2)}) async-start(), calls=%async_computation.4 | async-start | bytes 12255232 | tf_op jit(solution)/shard_map/all_gather | solution.py:89
  209.4 544.3 %all-gather.14.cloned.1.call-start = ((), (), s32[]{:S(2)}) async-start(), calls=%async_computation.5 | async-start | bytes 37748736 | tf_op jit(solution)/shard_map/all_gather | solution.py:97
  210.5 91.7 %copy-start.6 = (bf16[1024,256]{1,0:T(8,128)(2,1)}, bf16[1024,256]{1,0:T(8,128)(2,1)S(1)}, u32[]{:S(2)}) copy-start(bf16[1024,256]{1,0:T(8,128)(2,1)S(1)} %dynamic-slice_bitcast_fusion.2.refs_6_) | copy-start | bytes 1572868
  210.5 9.0 %slice-start.4 = ((s8[8388608]{0:T(1024)(128)(4,1)}), s8[4194304]{0:T(1024)(128)(4,1)S(1)}, s32[]{:S(2)}) async-start(s8[8388608]{0:T(1024)(128)(4,1)} %bitcast.200), calls=%async_computation.11 | async-start | bytes 8388608
  212.8 21.2 %copy-start.5 = (bf16[256,1024]{1,0:T(8,128)(2,1)}, bf16[256,1024]{1,0:T(8,128)(2,1)S(1)}, u32[]{:S(2)}) copy-start(bf16[256,1024]{1,0:T(8,128)(2,1)S(1)} %get-tuple-element.50.refs_5_) | copy-start | bytes 1572868
  212.8 6.7 slice-start.5
  219.5 14.5 %copy-start.12 = (bf16[2048,256]{1,0:T(8,128)(2,1)}, bf16[2048,256]{1,0:T(8,128)(2,1)S(1)}, u32[]{:S(2)}) copy-start(bf16[2048,256]{1,0:T(8,128)(2,1)S(1)} %convolution_convert_fusion.4) | copy-start | bytes 3145732
  282.6 24.4 %slice-start.2 = ((s8[8388608]{0:T(1024)(128)(4,1)}), s8[4194304]{0:T(1024)(128)(4,1)S(1)}, s32[]{:S(2)}) async-start(s8[8388608]{0:T(1024)(128)(4,1)} %bitcast.193), calls=%async_computation.9 | async-start | bytes 8388608
  288.7 13.5 %copy-start.19 = (bf16[2048,256]{1,0:T(8,128)(2,1)}, bf16[2048,256]{1,0:T(8,128)(2,1)S(1)}, u32[]{:S(2)}) copy-start(bf16[2048,256]{1,0:T(8,128)(2,1)S(1)} %convolution_convert_fusion.5) | copy-start | bytes 3145732
  288.7 18.2 %slice-start.3 = ((s8[8388608]{0:T(1024)(128)(4,1)}), s8[4194304]{0:T(1024)(128)(4,1)S(1)}, s32[]{:S(2)}) async-start(s8[8388608]{0:T(1024)(128)(4,1)} %bitcast.193), calls=%async_computation.10 | async-start | bytes 8388608
  321.8 27.8 %copy-start.9 = (bf16[2048,1024]{1,0:T(8,128)(2,1)}, bf16[2048,1024]{1,0:T(8,128)(2,1)S(1)}, u32[]{:S(2)}) copy-start(bf16[2048,1024]{1,0:T(8,128)(2,1)S(1)} %get-tuple-element.52.refs_2_) | copy-start | bytes 12582916
  321.8 15.3 %copy-start.10 = (bf16[2048,1024]{1,0:T(8,128)(2,1)S(1)}, bf16[2048,1024]{1,0:T(8,128)(2,1)}, u32[]{:S(2)}) copy-start(bf16[2048,1024]{1,0:T(8,128)(2,1)} %get-tuple-element.53.refs_1_) | copy-start | bytes 12582916
  321.9 27.8 %slice-start.15 = ((s8[8388608]{0:T(1024)(128)(4,1)}), s8[4194304]{0:T(1024)(128)(4,1)S(1)}, s32[]{:S(2)}) async-start(s8[8388608]{0:T(1024)(128)(4,1)} %bitcast.252), calls=%async_computation.22 | async-start | bytes 8388608
  337.2 12.4 %slice-start.16 = ((s8[8388608]{0:T(1024)(128)(4,1)}), s8[4194304]{0:T(1024)(128)(4,1)S(1)}, s32[]{:S(2)}) async-start(s8[8388608]{0:T(1024)(128)(4,1)} %bitcast.252), calls=%async_computation.23 | async-start | bytes 8388608
  364.4 16.6 %copy-start.3 = (bf16[1,128,2048]{2,1,0:T(8,128)(2,1)S(1)}, bf16[1,128,2048]{2,1,0:T(8,128)(2,1)}, u32[]{:S(2)}) copy-start(bf16[1,128,2048]{2,1,0:T(8,128)(2,1)} %param.10) | copy-start | bytes 1572868
  364.4 16.9 %copy-start.31 = (f32[1,2048]{1,0:T(1,128)S(1)}, f32[1,2048]{1,0:T(1,128)}, u32[]{:S(2)}) copy-start(f32[1,2048]{1,0:T(1,128)} %copy-done.30) | copy-start | bytes 24580
  364.4 16.9 %copy-start.39 = (f32[128]{0:T(128)S(1)}, f32[128]{0:T(128)}, u32[]{:S(2)}) copy-start(f32[128]{0:T(128)} %copy-done.38) | copy-start | bytes 1540
  382.5 219.3 %all-to-all-start = ((bf16[128,16,128]{2,0,1:T(8,128)(2,1)}), bf16[128,16,128]{2,0,1:T(8,128)(2,1)}, u32[]{:S(2)}, u32[]{:S(2)}) async-start(bf16[128,16,128]{2,0,1:T(8,128)(2,1)} %fusion.103), calls=%async_computation | async-start | bytes 1048576 | tf_op jit(solution)/shard_map/all_to_all | solution.py:105
  386.9 143.0 %copy-start.1 = (f32[128,2048]{1,0:T(8,128)S(1)}, f32[128,2048]{1,0:T(8,128)}, u32[]{:S(2)}) copy-start(f32[128,2048]{1,0:T(8,128)} %copy-done) | copy-start | bytes 3145732
  387.0 143.0 %copy-start.34 = (f32[1,2048]{1,0:T(1,128)S(1)}, f32[1,2048]{1,0:T(1,128)}, u32[]{:S(2)}) copy-start(f32[1,2048]{1,0:T(1,128)} %copy-done.33) | copy-start | bytes 24580
  387.0 143.0 %copy-start.45 = (f32[128]{0:T(128)S(1)}, f32[128]{0:T(128)}, u32[]{:S(2)}) copy-start(f32[128]{0:T(128)} %copy-done.44) | copy-start | bytes 1540
  525.3 6.7 copy-start.17
  525.3 6.7 copy-start.49
  525.3 9.1 %slice-start = ((s8[8388608]{0:T(1024)(128)(4,1)}), s8[4194304]{0:T(1024)(128)(4,1)S(1)}, s32[]{:S(2)}) async-start(s8[8388608]{0:T(1024)(128)(4,1)} %bitcast.191), calls=%async_computation.7 | async-start | bytes 8388608
  527.3 5.2 copy-start.15
  532.1 5.9 slice-start.6
  544.6 26.6 %copy-start.41 = (f32[128]{0:T(128)S(1)}, f32[128]{0:T(128)}, u32[]{:S(2)}) copy-start(f32[128]{0:T(128)} %copy-done.40) | copy-start | bytes 1540
  544.6 26.6 %copy-start.43 = (f32[128]{0:T(128)S(1)}, f32[128]{0:T(128)}, u32[]{:S(2)}) copy-start(f32[128]{0:T(128)} %copy-done.42) | copy-start | bytes 1540
  570.2 14.1 %slice-start.8 = ((s8[6291456]{0:T(1024)(128)(4,1)}), s8[4194304]{0:T(1024)(128)(4,1)S(1)}, s32[]{:S(2)}) async-start(s8[6291456]{0:T(1024)(128)(4,1)} %bitcast.221), calls=%async_computation.15 | async-start | bytes 8388608
  573.7 12.8 %copy-start.14 = (bf16[128,3712]{1,0:T(8,128)(2,1)}, bf16[128,3712]{1,0:T(8,128)(2,1)S(1)}, u32[]{:S(2)}) copy-start(bf16[128,3712]{1,0:T(8,128)(2,1)S(1)} %get-tuple-element.47) | copy-start | bytes 2850820
  576.7 7.6 slice-start.9
  586.7 13.1 %copy-start.11 = (bf16[2048,1024]{1,0:T(8,128)(2,1)S(1)}, bf16[2048,1024]{1,0:T(8,128)(2,1)}, u32[]{:S(2)}) copy-start(bf16[2048,1024]{1,0:T(8,128)(2,1)} %get-tuple-element.53.refs_1_) | copy-start | bytes 12582916
  586.7 13.0 %copy-start.13 = (bf16[2048,256]{1,0:T(8,128)(2,1)S(1)}, bf16[2048,256]{1,0:T(8,128)(2,1)}, u32[]{:S(2)}) copy-start(bf16[2048,256]{1,0:T(8,128)(2,1)} %copy-done.12) | copy-start | bytes 3145732
  595.1 11.5 %copy-start.20 = (bf16[2048,256]{1,0:T(8,128)(2,1)S(1)}, bf16[2048,256]{1,0:T(8,128)(2,1)}, u32[]{:S(2)}) copy-start(bf16[2048,256]{1,0:T(8,128)(2,1)} %copy-done.19) | copy-start | bytes 3145732
  599.7 11.4 %copy-start.48 = (f32[128]{0:T(128)S(1)}, f32[128]{0:T(128)}, u32[]{:S(2)}) copy-start(f32[128]{0:T(128)} %get-tuple-element.69) | copy-start | bytes 1540
  601.8 18.7 %all-to-all-start.1 = ((bf16[128,16,128]{2,0,1:T(8,128)(2,1)}), bf16[128,16,128]{2,0,1:T(8,128)(2,1)S(1)}, u32[]{:S(2)}, u32[]{:S(2)}) async-start(bf16[128,16,128]{2,0,1:T(8,128)(2,1)} %bitcast.190), calls=%async_computation.1 | async-start | bytes 1048576 | tf_op jit(solution)/shard_map/all_to_all | solution.py:105
  606.0 207.5 %all-gather.16.cloned.1.call-start = ((), (), s32[]{:S(2)}) async-start(), calls=%async_computation.6 | async-start | bytes 3637248 | tf_op jit(solution)/shard_map/all_gather | solution.py:97
  606.5 4.5 copy-start.21
  628.7 6.7 copy-start.16
  628.8 6.7 copy-start.28
  628.8 6.7 copy-start.29
  745.0 7.6 slice-start.10
  753.7 14.7 %slice-start.11 = ((s8[15204352]{0:T(1024)(128)(4,1)}), s8[4194304]{0:T(1024)(128)(4,1)S(1)}, s32[]{:S(2)}) async-start(s8[15204352]{0:T(1024)(128)(4,1)} %bitcast.240), calls=%async_computation.18 | async-start | bytes 8388608
  758.6 9.8 %slice-start.12 = ((s8[15204352]{0:T(1024)(128)(4,1)}), s8[4194304]{0:T(1024)(128)(4,1)S(1)}, s32[]{:S(2)}) async-start(s8[15204352]{0:T(1024)(128)(4,1)} %bitcast.240), calls=%async_computation.19 | async-start | bytes 8388608
  758.6 9.8 %slice-start.13 = ((s8[15204352]{0:T(1024)(128)(4,1)}), s8[4194304]{0:T(1024)(128)(4,1)S(1)}, s32[]{:S(2)}) async-start(s8[15204352]{0:T(1024)(128)(4,1)} %bitcast.240), calls=%async_computation.20 | async-start | bytes 8388608
  758.6 9.8 %slice-start.14 = ((s8[15204352]{0:T(1024)(128)(4,1)}), s8[2621440]{0:T(1024)(128)(4,1)S(1)}, s32[]{:S(2)}) async-start(s8[15204352]{0:T(1024)(128)(4,1)} %bitcast.240), calls=%async_computation.21 | async-start | bytes 5242880
  779.1 6.7 copy-start.36
  779.2 7.6 copy-start.18
  779.2 7.6 copy-start.35
  (11 other events, 31.3 us)
Sparse Core Ops, SparseCore 0:
  68.6 81.6 all-gather.7
  208.3 74.1 all-gather.9
  285.3 95.6 all-gather.11
  382.9 291.8 all-gather.13
  776.7 36.8 all-gather.15

commit v6 on v5

--- a/solution.py
+++ b/solution.py
@@ -327,10 +327,212 @@
     )(*terms)
 
 
+def unit_kernel(chips, *refs):
+    sources, (planes, squeeze, widen_down, widen_gate, widen_up, narrow) = refs[:2], refs[2:8]
+    outs, (held, rows_v, acts, low) = refs[8:11], refs[11:15]
+    held_sem, own_sem, ring_send, ring_recv, side_send, side_recv, out_sem = refs[15:]
+    core, device = ring_neighbours(chips)
+    rows = sources[0].shape[0]
+    reach = chips // 2
+    wide = 256
+    ways = (device(1, core), device(-1, core))
+    side = device(0, 1 - core)
+    fetches = [pltpu.make_async_copy(planes.at[i], held.at[i], held_sem.at[i]) for i in range(3)]
+    for fetch in fetches:
+        fetch.start()
+    meet((*ways, side))
+
+    def span(way, hops):
+        return (way * (rows // 2), rows // 2) if hops == reach else (0, rows)
+
+    def at(i, way, hops, c, part):
+        origin = device(-hops if way == 0 else hops, c)
+        return rows_v.at[i, pl.ds(pl.multiple_of(origin * rows + part[0], 16), part[1])]
+
+    def hop(i, way, hops):
+        part = span(way, hops)
+        here = at(i, way, hops - 1, core, part)
+        src = sources[i].at[pl.ds(part[0], part[1])] if hops == 1 else here
+        return pltpu.make_async_remote_copy(
+            src,
+            here,
+            ring_send.at[i, way, hops - 1],
+            ring_recv.at[i, way, hops - 1],
+            device_id={"fsdp": ways[way]},
+            device_id_type=MESH,
+        )
+
+    def arriving(i, way, hops):
+        here = at(i, way, hops, core, span(way, hops))
+        return pltpu.make_async_remote_copy(
+            here,
+            here,
+            ring_send.at[i, way, hops - 1],
+            ring_recv.at[i, way, hops - 1],
+            device_id={"fsdp": ways[way]},
+            device_id_type=MESH,
+        )
+
+    def across(i, way, hops, c):
+        part = span(way, hops) if hops else (0, rows)
+        there = at(i, way, hops, c, part)
+        return pltpu.make_async_remote_copy(
+            there if hops else sources[i],
+            there,
+            side_send.at[i, way, hops],
+            side_recv.at[i, way, hops],
+            device_id={"fsdp": side},
+            device_id_type=MESH,
+        )
+
+    def leaving(n, first):
+        mine = pl.ds(first, 2 * rows)
+        pairs = [(rows_v.at[i, mine], outs[0].at[i, mine]) for i in (0, 1)]
+        pairs += [(acts.at[i, mine], outs[1].at[i, mine]) for i in range(3)]
+        pairs += [(low.at[mine], outs[2].at[mine])]
+        return [pltpu.make_async_copy(a, b, out_sem.at[n, i]) for i, (a, b) in enumerate(pairs)]
+
+    def first_row(shift):
+        return pl.multiple_of(device(shift, 0) * rows, 2 * rows)
+
+    def work(n, first):
+        mine = pl.ds(first, 2 * rows)
+        rank = ADAPTER_RANK
+        low[mine, : 2 * rank] = matrix_product(rows_v[0, mine, :], squeeze[...]).astype(bf16)
+        low[mine, 2 * rank :] = times_transposed(rows_v[1, mine, :], widen_down[...]).astype(bf16)
+
+        @pl.loop(0, held.shape[1] // wide)
+        def _(t):
+            own = pl.ds(pl.multiple_of(t * wide, wide), wide)
+            two = rows_v[0, mine, :]
+            gate = times_transposed(two, held[0, own, :]) + matrix_product(
+                low[mine, :rank], widen_gate[:, own]
+            )
+            upward = times_transposed(two, held[1, own, :]) + matrix_product(
+                low[mine, rank : 2 * rank], widen_up[:, own]
+            )
+            pull = times_transposed(rows_v[1, mine, :], held[2, own, :]) + times_transposed(
+                low[mine, 2 * rank :], narrow[own, :]
+            )
+            scale = math.sqrt(2.0 / math.pi)
+            square = gate * gate
+            bend = jnp.tanh(scale * gate * (1.0 + 0.044715 * square))
+            rise = 0.5 * (1.0 + bend)
+            active = gate * rise
+            slope = rise + 0.5 * gate * (1.0 - bend * bend) * (scale * (1.0 + 3 * 0.044715 * square))
+            acts[0, mine, own] = (pull * upward * slope).astype(bf16)
+            acts[1, mine, own] = (pull * active).astype(bf16)
+            acts[2, mine, own] = (active * upward).astype(bf16)
+
+        for copy in leaving(n, first):
+            copy.start()
+
+    for i in (0, 1):
+        for way in (0, 1):
+            hop(i, way, 1).start()
+        across(i, 0, 0, core).start()
+    keeps = [
+        pltpu.make_async_copy(sources[i], at(i, 0, 0, core, (0, rows)), own_sem.at[i]) for i in (0, 1)
+    ]
+    for keep in keeps:
+        keep.start()
+    for copy in keeps + fetches:
+        copy.wait()
+    for i in (0, 1):
+        across(i, 0, 0, 1 - core).wait_recv()
+    work(0, first_row(0))
+    for hops in range(1, reach + 1):
+        for i in (0, 1):
+            for way in (0, 1):
+                arriving(i, way, hops).wait_recv()
+                if hops < reach:
+                    hop(i, way, hops + 1).start()
+                across(i, way, hops, core).start()
+        if hops < reach:
+            for way in (0, 1):
+                for i in (0, 1):
+                    across(i, way, hops, 1 - core).wait_recv()
+                work(2 * hops - 1 + way, first_row(-hops if way == 0 else hops))
+    for way in (0, 1):
+        for i in (0, 1):
+            across(i, way, reach, 1 - core).wait_recv()
+    work(2 * reach - 1, first_row(reach))
+    for i in (0, 1):
+        across(i, 0, 0, core).wait_send()
+        for hops in range(1, reach + 1):
+            for way in (0, 1):
+                across(i, way, hops, core).wait_send()
+                hop(i, way, hops).wait_send()
+    for n in range(chips):
+        if n == 0:
+            shift = 0
+        elif n == 2 * reach - 1:
+            shift = reach
+        else:
+            shift = (-1 if n % 2 else 1) * ((n + 1) // 2)
+        for copy in leaving(n, first_row(shift)):
+            copy.wait()
+
+
+def unit_rows(two, grad, planes, squeeze, widen_down, widen_gate, widen_up, narrow, ident):
+    size = lax.axis_size("fsdp")
+    rank = ADAPTER_RANK
+    if size != 16:
+        two, grad = gather_rows(two), gather_rows(grad)
+        low = matrix_product(two, squeeze).astype(bf16)
+        pulled = times_transposed(grad, widen_down).astype(bf16)
+        gate = times_transposed(two, planes[0]) + matrix_product(low[:, :rank], widen_gate)
+        upward = times_transposed(two, planes[1]) + matrix_product(low[:, rank:], widen_up)
+        units_grad = times_transposed(grad, planes[2]) + times_transposed(pulled, narrow)
+        units = (gelu_tanh(gate) * upward).astype(bf16)
+        gate_grad, up_grad = unit_backward(gate, upward, units_grad)
+        return (
+            jnp.stack([two, grad]),
+            jnp.stack([gate_grad, up_grad, units]),
+            jnp.concatenate([low, pulled], axis=1),
+        )
+    chips = size // 2
+    rows, columns = two.shape
+    all_rows, hidden = size * rows, planes.shape[1]
+    anywhere, inside = pl.BlockSpec(memory_space=pl.ANY), pl.BlockSpec(memory_space=pltpu.VMEM)
+    pair = pltpu.SemaphoreType.DMA((2, 2, chips // 2))
+    sides = pltpu.SemaphoreType.DMA((2, 2, chips // 2 + 1))
+    return pl.pallas_call(
+        functools.partial(unit_kernel, chips),
+        out_shape=(
+            jax.ShapeDtypeStruct((2, all_rows, columns), bf16),
+            jax.ShapeDtypeStruct((3, all_rows, hidden), bf16),
+            jax.ShapeDtypeStruct((all_rows, 3 * rank), bf16),
+        ),
+        in_specs=[anywhere] * 3 + [inside] * 5,
+        out_specs=(anywhere,) * 3,
+        scratch_shapes=[
+            pltpu.VMEM(planes.shape, bf16),
+            pltpu.VMEM((2, all_rows, columns), bf16),
+            pltpu.VMEM((3, all_rows, hidden), bf16),
+            pltpu.VMEM((all_rows, 3 * rank), bf16),
+            pltpu.SemaphoreType.DMA((3,)),
+            pltpu.SemaphoreType.DMA((2,)),
+            pair,
+            pair,
+            sides,
+            sides,
+            pltpu.SemaphoreType.DMA((chips, 6)),
+        ],
+        compiler_params=pltpu.CompilerParams(
+            collective_id=ident, has_side_effects=True, vmem_limit_bytes=60 << 20
+        ),
+        cost_estimate=busy(100),
+        name="unit_rows",
+    )(two, grad, planes, squeeze, widen_down, widen_gate, widen_up, narrow)
+
+
 def mix_kernel(chips, *refs):
-    gate_ref, up_ref, unit_ref, planes, gate_b, up_b, down_a, o_ref = refs[:8]
-    held, side_buf, ring_buf, stage, mine, held_sem, side_send, side_recv, ring_send, ring_recv = refs[8:]
-    fetches = [pltpu.make_async_copy(planes.at[i], held.at[i], held_sem.at[i]) for i in range(3)]
+    acts_ref, planes, gate_b, up_b, down_a, o_ref = refs[:6]
+    acts, held, side_buf, ring_buf, stage, mine = refs[6:12]
+    held_sem, side_send, side_recv, ring_send, ring_recv = refs[12:]
+    fetches = [pltpu.make_async_copy(planes.at[i], held.at[i], held_sem.at[0, i]) for i in range(3)]
+    fetches += [pltpu.make_async_copy(acts_ref.at[i], acts.at[i], held_sem.at[1, i]) for i in range(3)]
     for fetch in fetches:
         fetch.start()
     core, device = ring_neighbours(chips)
@@ -377,8 +579,8 @@
         theirs = pl.ds(pl.multiple_of(device(target, 1 - core) * rows, rows), rows)
         ours = pl.ds(pl.multiple_of(device(target, core) * rows, rows), rows)
 
-        def block(ref):
-            return jnp.concatenate([ref[theirs, :], ref[ours, :]], axis=0)
+        def block(kind):
+            return jnp.concatenate([acts[kind, theirs, :], acts[kind, ours, :]], axis=0)
 
         def put(first, value):
             cols = pl.ds(pl.multiple_of(first, wide), wide)
@@ -390,17 +592,17 @@
             cols = pl.ds(pl.multiple_of(t * wide, wide), wide)
             put(
                 t * wide,
-                matrix_product(block(gate_ref), held[0, :, cols])
-                + matrix_product(block(up_ref), held[1, :, cols]),
+                matrix_product(block(0), held[0, :, cols])
+                + matrix_product(block(1), held[1, :, cols]),
             )
             put(
                 MODEL_WIDTH + 2 * ADAPTER_RANK + t * wide,
-                matrix_product(block(unit_ref), held[2, :, cols]),
+                matrix_product(block(2), held[2, :, cols]),
             )
 
-        put(MODEL_WIDTH, times_transposed(block(gate_ref), gate_b[...]))
-        put(MODEL_WIDTH + ADAPTER_RANK, times_transposed(block(up_ref), up_b[...]))
-        put(2 * MODEL_WIDTH + 2 * ADAPTER_RANK, matrix_product(block(unit_ref), down_a[...]))
+        put(MODEL_WIDTH, times_transposed(block(0), gate_b[...]))
+        put(MODEL_WIDTH + ADAPTER_RANK, times_transposed(block(1), up_b[...]))
+        put(2 * MODEL_WIDTH + 2 * ADAPTER_RANK, matrix_product(block(2), down_a[...]))
         across(i).start()
 
     def add(i):
@@ -444,9 +646,10 @@
             hop(way, step).wait_send()
 
 
-def mix_rows(gate_grad, up_grad, units, planes, gate_b, up_b, down_a, ident):
+def mix_rows(acts, planes, gate_b, up_b, down_a, ident):
     size = lax.axis_size("fsdp")
     if size != 16:
+        gate_grad, up_grad, units = acts[0], acts[1], acts[2]
         terms = [
             matrix_product(gate_grad, planes[0]) + matrix_product(up_grad, planes[1]),
             times_transposed(gate_grad, gate_b),
@@ -456,23 +659,23 @@
         ]
         return scatter_rows(jnp.concatenate(terms, axis=1))
     chips = size // 2
-    rows, columns = units.shape[0] // size, 2 * MODEL_WIDTH + 3 * ADAPTER_RANK
+    rows, columns = acts.shape[1] // size, 2 * MODEL_WIDTH + 3 * ADAPTER_RANK
     pair = pltpu.SemaphoreType.DMA((2, chips // 2))
     sides = pltpu.SemaphoreType.DMA((chips,))
     return pl.pallas_call(
         functools.partial(mix_kernel, chips),
         out_shape=jax.ShapeDtypeStruct((rows, columns), f32),
-        in_specs=[pl.BlockSpec(memory_space=pltpu.VMEM)] * 3
-        + [pl.BlockSpec(memory_space=pl.ANY)]
+        in_specs=[pl.BlockSpec(memory_space=pl.ANY)] * 2
         + [pl.BlockSpec(memory_space=pltpu.VMEM)] * 3,
         out_specs=pl.BlockSpec(memory_space=pltpu.VMEM),
         scratch_shapes=[
+            pltpu.VMEM(acts.shape, bf16),
             pltpu.VMEM(planes.shape, bf16),
             pltpu.VMEM((chips, rows, columns), bf16),
             pltpu.VMEM((2, chips // 2, rows, columns), bf16),
             pltpu.VMEM((2, rows, columns), bf16),
             pltpu.VMEM((2, rows, columns), bf16),
-            pltpu.SemaphoreType.DMA((3,)),
+            pltpu.SemaphoreType.DMA((2, 3)),
             sides,
             sides,
             pair,
@@ -483,7 +686,7 @@
         ),
         cost_estimate=busy(1),
         name="mix_rows",
-    )(gate_grad, up_grad, units, planes, gate_b, up_b, down_a)
+    )(acts, planes, gate_b, up_b, down_a)
 
 
 def share_kernel(size, chunk, own_count, x_ref, mid_ref, all_ref, o_ref, *sems):
@@ -674,9 +877,7 @@
     scale_one = rms_scale(hidden_state)
     normalized = (hidden_state * scale_one * gains[0]).astype(bf16)
     proj_in = ring_gather(input_proj_weight, 0)
-    proj_in, proj_out, grad_rows = lax.optimization_barrier(
-        (proj_in, output_proj_weight, output_gradient[0])
-    )
+    proj_in, proj_out = lax.optimization_barrier((proj_in, output_proj_weight))
     proj_out = gather_rows(proj_out)
     lora_qkv = matrix_product(normalized, narrow_projection).astype(bf16)
     projected = matrix_product(normalized, proj_in)
@@ -713,19 +914,21 @@
     scale_two = rms_scale(middle)
     normed_two = (middle * scale_two * gains[1]).astype(bf16)
 
-    two_all = ring_gather(normed_two, 2)
-    two_all, grad_rows = lax.optimization_barrier((two_all, grad_rows))
-    grad_all = gather_rows(grad_rows)
     weight_planes = feedforward_weight.transpose(1, 0, 2)
-    weight_gate, weight_up, weight_down = weight_planes[0], weight_planes[1], weight_planes[2]
-    lora_gate = matrix_product(two_all, squeeze_gate).astype(bf16)
-    lora_up = matrix_product(two_all, squeeze_up).astype(bf16)
-    hd_grad = times_transposed(grad_all, widen_down).astype(bf16)
-    gate = times_transposed(two_all, weight_gate) + matrix_product(lora_gate, widen_gate)
-    upward = times_transposed(two_all, weight_up) + matrix_product(lora_up, widen_up)
-    units = (gelu_tanh(gate) * upward).astype(bf16)
-    units_grad = times_transposed(grad_all, weight_down) + times_transposed(hd_grad, narrow_down)
-    gate_grad, up_grad = unit_backward(gate, upward, units_grad)
+    rows_all, acts, low_ffn = unit_rows(
+        normed_two,
+        output_gradient[0],
+        weight_planes,
+        first_factor[:, 4 * rank :],
+        widen_down,
+        widen_gate,
+        widen_up,
+        narrow_down,
+        2,
+    )
+    two_all, grad_all = rows_all[0], rows_all[1]
+    gate_grad, up_grad, units = acts[0], acts[1], acts[2]
+    lora_gate, lora_up, hd_grad = low_ffn[:, :rank], low_ffn[:, rank : 2 * rank], low_ffn[:, 2 * rank :]
     ffn_shares = jnp.stack(
         [
             outer_product_rows(former, latter).astype(bf16)
@@ -733,12 +936,10 @@
         ]
     )
     attended_all = gather_rows(jnp.concatenate([attended, lora_qkv], axis=1))
-    ffn_shares, gate_grad, attended_all = lax.optimization_barrier(
-        (ffn_shares, gate_grad, attended_all)
-    )
+    ffn_shares, acts, attended_all = lax.optimization_barrier((ffn_shares, acts, attended_all))
     ffn_both = loop_shares(ffn_shares)
     rows_sum = mix_rows(
-        gate_grad, up_grad, units, weight_planes, widen_gate, widen_up, narrow_down, 3
+        acts, weight_planes, widen_gate, widen_up, narrow_down, 3
     )
     back_own, out_own = rows_sum[:, : MODEL_WIDTH + 2 * rank], rows_sum[:, MODEL_WIDTH + 2 * rank :]
     down_own = outer_product_rows(units, hd_grad)

time: 836 us -> 844 us (level)
  Pallas kernels: 407 us -> 521 us
  matrix products: 245 us -> 165 us
  waiting for transfers between devices: 68.8 us -> 22.2 us
  local copies, waits for them, and re-layouts: 19.5 us -> 40.6 us
    pallas_call x0 -> x1, Pallas kernels: none -> 167 us  [unit_rows(): pl.pallas_call(functools.partial(unit_kernel, chips), out_shape=(jax.Shap...]
    all_gather x3 -> x2, waiting for transfers between devices: 59.8 us -> 8.35 us  [gather_rows(): return lax.all_gather(block, 'fsdp', axis=0, tiled=True)]
    dot_general x18 -> x13, matrix products: 89 us -> 39 us  [times_transposed(): lax.dot_general(former, latter, (((1,), (1,)), ((), ())), preferred_eleme...]
    pallas_call x3 -> x2, Pallas kernels: 138 us -> 90.7 us  [ring_gather(): pl.pallas_call(functools.partial(gather_kernel, chips), out_shape=jax.Sha...]
    dot_general x12 -> x8, matrix products: 49.4 us -> 19.1 us  [matrix_product(): return jnp.dot(former, latter, preferred_element_type=f32)]
    slice x0 -> x3, local copies, waits for them, and re-layouts: none -> 18.7 us  [the longest x1 13.1 us: per_device(): two_all, grad_all = (rows_all[0], rows_all[1])]
  transfers between devices with their start and end apart: 7 -> 6, of which waited for: 5 -> 3; matrix products, arithmetic and copies ran while one was open for 34% -> 27% of each run, Pallas kernels for 36% -> 55%
where the time goes in v6:
time: 844 us; the launch traced here: 834 us
  Pallas kernels  521 us (62%)
  matrix products  165 us (20%)
  other arithmetic  56.4 us (7%)
  local copies, waits for them, and re-layouts  40.6 us (5%)
  waiting for transfers between devices  22.2 us (3%)
  between operations  14.8 us (2%)
  starting transfers between devices  13.5 us (2%)
    pallas_call x1, Pallas kernels, unit_rows(): pl.pallas_call(functools.partial(unit_kernel, chips), out_shape=(jax.Shap...  167 us
    pallas_call x1, Pallas kernels, mix_rows(): pl.pallas_call(functools.partial(mix_kernel, chips), out_shape=jax.ShapeD...  132 us
    pallas_call x1, Pallas kernels, share_rows(): pl.pallas_call(functools.partial(share_kernel, size, chunk, own_count), o...  109 us
    dot_general x16, matrix products, outer_product_rows(): lax.dot_general(former, latter, (((0,), (0,)), ((), ())), preferred_eleme...  94.3 us
    pallas_call x2, Pallas kernels, ring_gather(): pl.pallas_call(functools.partial(gather_kernel, chips), out_shape=jax.Sha...  90.7 us
    dot_general x13, matrix products, times_transposed(): lax.dot_general(former, latter, (((1,), (1,)), ((), ())), preferred_eleme...  39 us
    pallas_call x1, Pallas kernels, ring_scatter(): pl.pallas_call(functools.partial(scatter_kernel, chips, count), out_shape...  23 us
    dot_general x8, matrix products, matrix_product(): return jnp.dot(former, latter, preferred_element_type=f32)  19.1 us
  transfers between devices with their start and end apart: 6, of which 3 were waited for; matrix products, arithmetic and copies ran while one was open for 27% of the time, Pallas kernels for 55%

profile of v6, /device:TPU:0, one launch (start us, length us, event | category | flops | bytes accessed | tf_op | source)
XLA Modules:
  0.0 834.3 jit_solution(7122141529603734265)
XLA Ops:
  7.2 61.2 %ring_gather.2 = bf16[2048,2560]{1,0:T(8,128)(2,1)} custom-call(bf16[128,2560]{1,0:T(8,128)(2,1)} %x_ref.1), custom_call_target="tpu_custom_call" | custom-call | bytes 3000000 | tf_op jit(solution)/shard_map/ring_gather/pallas_call | solution.py:194
  69.2 2.5 fusion.118
  71.9 5.9 fusion.192
  77.9 1.5 convolution_add_fusion.5
  84.3 29.5 %ring_gather.3 = bf16[2048,512]{1,0:T(8,128)(2,1)} custom-call(bf16[128,512]{1,0:T(8,128)(2,1)} %pad_maximum_fusion.6.x_ref), custom_call_target="tpu_custom_call" | custom-call | bytes 3000000 | tf_op jit(solution)/shard_map/ring_gather/pallas_call | solution.py:194
  116.1 2.5 fusion.141
  118.7 3.6 fusion.245
  122.2 3.2 copy-done.2
  125.4 2.6 fusion.101
  129.6 2.3 slice.305.refs_4_
  131.9 3.3 slice.304.refs_3_
  135.2 1.9 dynamic-slice_bitcast_fusion.refs_7_.refs_4_
  137.1 2.3 dynamic-slice_bitcast_fusion.1
  139.4 8.3 %all-gather.7.cloned.1.call-done = bf16[2048,2048]{1,0:T(8,128)(2,1)} async-done(((bf16[128,2048]{1,0:T(8,128)(2,1)}), bf16[2048,2048]{1,0:T(8,128)(2,1)}) %all-gather.7.cloned.1.call-update) | async-done | bytes 8388624 | tf_op jit(solution)/shard_map/all_gather | solution.py:89
  147.7 7.3 convolution_add_fusion.6
  155.0 3.0 multiply_reduce_fusion.3
  159.0 167.1 %unit_rows.1 = (bf16[2,2048,2048]{2,1,0:T(8,128)(2,1)}, bf16[3,2048,1024]{2,1,0:T(8,128)(2,1)}, bf16[2048,768]{1,0:T(8,128)(2,1)}) custom-call(bf16[128,2048]{1,0:T(8,128)(2,1)} %multiply_convert_fusion.1.refs_0_, bf16[128,2048]{1,0:T(8,128)(2,1)} %bitcast.244, bf16[3,1024,2048]{2,1,0:T(8,128)(2,1)} %bitcast.207, bf16[2048,512]{1,0:T(8,128)(2,1)} %slice.304.refs_3_, ...), custom_call_target="tpu_custom_call" | custom-call | bytes 300000000 | tf_op jit(solution)/shard_map/unit_rows/pallas_call | solution.py:500
  326.0 12.8 %convert_bitcast_fusion.2 = bf16[1,1024,2048]{2,1,0:T(8,128)(2,1)S(1)} fusion(bf16[3,2048,1024]{2,1,0:T(8,128)(2,1)} %get-tuple-element.29.refs_0_, bf16[2,2048,2048]{2,1,0:T(8,128)(2,1)} %get-tuple-element.28), kind=kOutput, calls=%fused_computation.37 | convolution fusion | flops 8592031744 | bytes 16777216 | tf_op jit(solution)/shard_map/dot_general | solution.py:36
  338.9 11.4 %convert_bitcast_fusion.1 = bf16[1,1024,2048]{2,1,0:T(8,128)(2,1)S(1)} fusion(bf16[3,2048,1024]{2,1,0:T(8,128)(2,1)S(1)} %copy-done.1, bf16[2,2048,2048]{2,1,0:T(8,128)(2,1)} %get-tuple-element.28), kind=kOutput, calls=%fused_computation.36 | convolution fusion | flops 8592031744 | bytes 16777216 | tf_op jit(solution)/shard_map/dot_general | solution.py:36
  350.3 12.8 %convert_bitcast_fusion = bf16[1,1024,2048]{2,1,0:T(8,128)(2,1)} fusion(bf16[2,2048,2048]{2,1,0:T(8,128)(2,1)} %get-tuple-element.28, bf16[3,2048,1024]{2,1,0:T(8,128)(2,1)S(1)} %copy-done.1), kind=kOutput, calls=%fused_computation.35 | convolution fusion | flops 8592031744 | bytes 16777216 | tf_op jit(solution)/shard_map/dot_general | solution.py:36
  363.1 7.7 pad_maximum_fusion
  372.3 8.8 %all-to-all-start = ((bf16[128,16,128]{2,0,1:T(8,128)(2,1)}), bf16[128,16,128]{2,0,1:T(8,128)(2,1)}, u32[]{:S(2)}, u32[]{:S(2)}) async-start(bf16[128,16,128]{2,0,1:T(8,128)(2,1)} %fusion.144), calls=%async_computation | async-start | bytes 1048576 | tf_op jit(solution)/shard_map/all_to_all | solution.py:105
  381.2 13.1 %slice.243 = bf16[1,2048,2048]{2,1,0:T(8,128)(2,1)} slice(bf16[2,2048,2048]{2,1,0:T(8,128)(2,1)} %get-tuple-element.28), slice={[0:1], [0:2048], [0:2048]} | slice | bytes 16777216 | tf_op jit(solution)/shard_map/slice | solution.py:929
  394.3 5.1 fusion.93
  399.4 4.8 fusion.107
  404.1 4.8 fusion.104
  408.9 132.0 %mix_rows.1 = f32[128,4864]{1,0:T(8,128)} custom-call(bf16[3,2048,1024]{2,1,0:T(8,128)(2,1)} %get-tuple-element.29.refs_0_, bf16[3,1024,2048]{2,1,0:T(8,128)(2,1)} %bitcast.208, bf16[256,1024]{1,0:T(8,128)(2,1)} %get-tuple-element.50.refs_5_.refs_2_, bf16[256,1024]{1,0:T(8,128)(2,1)} %get-tuple-element.49.refs_6_.refs_3_, ...), custom_call_target="tpu_custom_call" | custom-call | bytes 3000000 | tf_op jit(solution)/shard_map/mix_rows/pallas_call | solution.py:665
  540.9 2.0 convert.97
  542.9 2.6 convolution_add_fusion.2
  545.6 2.0 multiply_reduce_fusion.1
  548.0 1.9 convolution_convert_fusion.5
  550.0 1.3 fusion.236
  551.3 2.1 fusion.86
  553.5 1.5 multiply_reduce_fusion
  557.7 2.4 fusion.64.refs_0_
  560.1 2.7 fusion.65.refs_1_
  562.8 23.0 %ring_scatter.1 = f32[128,512]{1,0:T(8,128)} custom-call(bf16[2048,256]{1,0:T(8,128)(2,1)} %fusion.64.refs_0_, bf16[2048,256]{1,0:T(8,128)(2,1)} %fusion.65.refs_1_), custom_call_target="tpu_custom_call" | custom-call | bytes 3000000 | tf_op jit(solution)/shard_map/ring_scatter/pallas_call | solution.py:309
  590.5 1.7 convolution_convert_fusion.4
  592.2 7.6 fusion.173
  599.9 2.2 fusion.134
  603.8 1.6 slice_dynamic-update-slice_fusion
  605.3 1.5 slice_dynamic-update-slice_fusion.1
  607.4 4.2 all-to-all-start.1
  611.7 2.7 fusion.87
  614.3 2.5 fusion.131
  616.9 9.2 %all-to-all-done.1 = bf16[128,16,128]{2,0,1:T(8,128)(2,1)S(1)} async-done(((bf16[128,16,128]{2,0,1:T(8,128)(2,1)}), bf16[128,16,128]{2,0,1:T(8,128)(2,1)S(1)}, u32[]{:S(2)}, u32[]{:S(2)}) %all-to-all-start.1) | async-done | bytes 524320 | tf_op jit(solution)/shard_map/all_to_all | solution.py:105
  626.1 8.2 fusion.248
  634.4 6.7 fusion.122
  642.1 108.6 %share_rows.1 = (bf16[2048,3712]{1,0:T(8,128)(2,1)}, bf16[2464,256]{1,0:T(8,128)(2,1)}) custom-call(bf16[128,3712]{1,0:T(8,128)(2,1)} %pad_dynamic-update-slice_fusion.x_ref, bf16[2176,256]{1,0:T(8,128)(2,1)} %pad_maximum_fusion.1.mid_ref), custom_call_target="tpu_custom_call" | custom-call | bytes 3000000 | tf_op jit(solution)/shard_map/share_rows/pallas_call | solution.py:802
  752.6 5.8 fusion.50
  759.5 7.2 fusion.75
  767.2 1.7 convolution_convert_fusion.3
  769.0 1.7 convolution_convert_fusion.2
  770.7 4.6 fusion.69
  775.3 2.3 convolution_convert_fusion
  777.6 2.3 convolution_convert_fusion.1
  780.0 4.6 fusion.66
  784.5 1.5 fusion.88
  786.1 1.8 fusion.150
  787.9 3.4 fusion.53
  792.2 7.5 convert_bitcast_fusion.3
  799.7 18.5 %add_bitcast_fusion = f32[1024,3,2048]{2,0,1:T(8,128)} fusion(bf16[2,3,1024,2048]{3,2,1,0:T(8,128)(2,1)} %bitcast.209), kind=kLoop, calls=%fused_computation.1 | loop fusion | flops 18874368 | bytes 50331648 | tf_op jit(solution)/shard_map/transpose | solution.py:1090
  818.3 4.6 all-gather.13.cloned.1.call-done
  822.8 1.9 convert_add_fusion
  (133 shorter events, 30.6 us)
Async XLA Ops:
  7.2 61.3 %copy-start = (bf16[1,128,2048]{2,1,0:T(8,128)(2,1)S(1)}, bf16[1,128,2048]{2,1,0:T(8,128)(2,1)}, u32[]{:S(2)}) copy-start(bf16[1,128,2048]{2,1,0:T(8,128)(2,1)} %param.10) | copy-start | bytes 1572868
  7.2 62.0 %copy-start.13 = (bf16[2,2048]{1,0:T(2,128)(2,1)S(1)}, bf16[2,2048]{1,0:T(2,128)(2,1)}, u32[]{:S(2)}) copy-start(bf16[2,2048]{1,0:T(2,128)(2,1)} %param.12) | copy-start | bytes 24580
  7.2 140.5 %all-gather.7.cloned.1.call-start = ((), (), s32[]{:S(2)}) async-start(), calls=%async_computation.2 | async-start | bytes 8912896 | tf_op jit(solution)/shard_map/all_gather | solution.py:89
  68.4 302.4 %all-gather.9.cloned.1.call-start = ((), (), s32[]{:S(2)}) async-start(), calls=%async_computation.3 | async-start | bytes 12255232 | tf_op jit(solution)/shard_map/all_gather | solution.py:89
  71.9 8.8 %copy-start.16 = (s32[1,4]{1,0:T(1,128)S(1)}, s32[1,4]{1,0:T(1,128)}, u32[]{:S(2)}) copy-start(s32[1,4]{1,0:T(1,128)} %param.11) | copy-start | bytes 52
  122.2 3.2 copy-start.2
  129.2 630.3 %all-gather.11.cloned.1.call-start = ((), (), s32[]{:S(2)}) async-start(), calls=%async_computation.4 | async-start | bytes 37748736 | tf_op jit(solution)/shard_map/all_gather | solution.py:97
  326.0 12.9 %copy-start.1 = (bf16[3,2048,1024]{2,1,0:T(8,128)(2,1)S(1)}, bf16[3,2048,1024]{2,1,0:T(8,128)(2,1)}, u32[]{:S(2)}) copy-start(bf16[3,2048,1024]{2,1,0:T(8,128)(2,1)} %get-tuple-element.29.refs_0_) | copy-start | bytes 37748740
  372.3 235.1 %all-to-all-start = ((bf16[128,16,128]{2,0,1:T(8,128)(2,1)}), bf16[128,16,128]{2,0,1:T(8,128)(2,1)}, u32[]{:S(2)}, u32[]{:S(2)}) async-start(bf16[128,16,128]{2,0,1:T(8,128)(2,1)} %fusion.144), calls=%async_computation | async-start | bytes 1048576 | tf_op jit(solution)/shard_map/all_to_all | solution.py:105
  381.2 13.1 %copy-start.15 = (bf16[2048,768]{1,0:T(8,128)(2,1)S(1)}, bf16[2048,768]{1,0:T(8,128)(2,1)}, u32[]{:S(2)}) copy-start(bf16[2048,768]{1,0:T(8,128)(2,1)} %get-tuple-element.33) | copy-start | bytes 9437188
  540.9 6.7 copy-start.7
  540.9 9.0 %slice-start = ((s8[8388608]{0:T(1024)(128)(4,1)}), s8[4194304]{0:T(1024)(128)(4,1)S(1)}, s32[]{:S(2)}) async-start(s8[8388608]{0:T(1024)(128)(4,1)} %bitcast.205), calls=%async_computation.6 | async-start | bytes 8388608
  542.9 5.1 copy-start.5
  545.6 4.4 slice-start.1
  547.6 5.9 slice-start.2
  550.0 3.5 slice-start.3
  550.0 3.5 copy-start.3
  562.8 37.0 %slice-start.4 = ((s8[6291456]{0:T(1024)(128)(4,1)}), s8[2097152]{0:T(1024)(128)(4,1)S(1)}, s32[]{:S(2)}) async-start(s8[6291456]{0:T(1024)(128)(4,1)} %bitcast.222), calls=%async_computation.10 | async-start | bytes 4194304
  589.2 10.6 %copy-start.4 = (bf16[128,3712]{1,0:T(8,128)(2,1)}, bf16[128,3712]{1,0:T(8,128)(2,1)S(1)}, u32[]{:S(2)}) copy-start(bf16[128,3712]{1,0:T(8,128)(2,1)S(1)} %get-tuple-element.47) | copy-start | bytes 2850820
  592.2 7.7 slice-start.5
  599.9 14.5 %copy-start.14 = (f32[128]{0:T(128)S(1)}, f32[128]{0:T(128)}, u32[]{:S(2)}) copy-start(f32[128]{0:T(128)} %get-tuple-element.66) | copy-start | bytes 1540
  607.4 18.6 %all-to-all-start.1 = ((bf16[128,16,128]{2,0,1:T(8,128)(2,1)}), bf16[128,16,128]{2,0,1:T(8,128)(2,1)S(1)}, u32[]{:S(2)}, u32[]{:S(2)}) async-start(bf16[128,16,128]{2,0,1:T(8,128)(2,1)} %bitcast.247), calls=%async_computation.1 | async-start | bytes 1048576 | tf_op jit(solution)/shard_map/all_to_all | solution.py:105
  611.6 211.2 %all-gather.13.cloned.1.call-start = ((), (), s32[]{:S(2)}) async-start(), calls=%async_computation.5 | async-start | bytes 3637248 | tf_op jit(solution)/shard_map/all_gather | solution.py:97
  634.3 6.7 copy-start.6
  634.3 6.7 copy-start.11
  634.3 6.7 copy-start.12
  752.6 5.8 slice-start.6
  758.4 8.4 %slice-start.7 = ((s8[15204352]{0:T(1024)(128)(4,1)}), s8[2621440]{0:T(1024)(128)(4,1)S(1)}, s32[]{:S(2)}) async-start(s8[15204352]{0:T(1024)(128)(4,1)} %bitcast.248), calls=%async_computation.13 | async-start | bytes 5242880
  759.5 7.3 slice-start.8
  759.5 7.3 slice-start.9
  759.5 7.7 slice-start.10
  786.0 6.2 copy-start.8
  786.1 6.2 copy-start.9
  786.1 6.2 copy-start.10
Sparse Core Ops, SparseCore 0:
  68.6 79.1 all-gather.6
  150.4 154.3 all-gather.8
  370.9 297.1 all-gather.10
  786.2 36.6 all-gather.12

commit v7 on v6

--- a/solution.py
+++ b/solution.py
@@ -99,6 +99,41 @@
 
 def both_loops(shares):
     return shares[0].astype(f32) + shares[1].astype(f32)
+
+
+def sum_kernel(early_ref, up_ref, o_ref):
+    @pl.when(pl.program_id(0) != 1)
+    def _():
+        o_ref[0] = early_ref[0, 0].astype(f32) + early_ref[1, 0].astype(f32)
+
+    @pl.when(pl.program_id(0) == 1)
+    def _():
+        o_ref[0] = up_ref[0].astype(f32) + up_ref[1].astype(f32)
+
+
+def sum_loops(early, up):
+    _, rows, columns = up.shape
+    tile = min(rows, 256)
+    steps = rows // tile
+    return pl.pallas_call(
+        sum_kernel,
+        grid=(3, steps),
+        out_shape=jax.ShapeDtypeStruct((3, rows, columns), f32),
+        in_specs=[
+            pl.BlockSpec(
+                (2, 1, tile, columns),
+                lambda i, j: (0, i // 2, jnp.where(i == 1, steps - 1, j), 0),
+            ),
+            pl.BlockSpec(
+                (2, tile, columns),
+                lambda i, j: (0, jnp.where(i == 1, j, jnp.where(i < 1, 0, steps - 1)), 0),
+            ),
+        ],
+        out_specs=pl.BlockSpec((1, tile, columns), lambda i, j: (i, j, 0)),
+        compiler_params=pltpu.CompilerParams(vmem_limit_bytes=32 << 20),
+        cost_estimate=busy(17),
+        name="sum_loops",
+    )(early, up)
 
 
 def turn(block):
@@ -329,8 +364,9 @@
 
 def unit_kernel(chips, *refs):
     sources, (planes, squeeze, widen_down, widen_gate, widen_up, narrow) = refs[:2], refs[2:8]
-    outs, (held, rows_v, acts, low) = refs[8:11], refs[11:15]
-    held_sem, own_sem, ring_send, ring_recv, side_send, side_recv, out_sem = refs[15:]
+    two_all, grad_all, acts_all, low_all = refs[8:12]
+    held, acts, low, landed = refs[12], refs[13], refs[14], refs[15:17]
+    held_sem, own_sem, ring_send, ring_recv, side_send, side_recv, out_sem = refs[17:]
     core, device = ring_neighbours(chips)
     rows = sources[0].shape[0]
     reach = chips // 2
@@ -347,7 +383,7 @@
 
     def at(i, way, hops, c, part):
         origin = device(-hops if way == 0 else hops, c)
-        return rows_v.at[i, pl.ds(pl.multiple_of(origin * rows + part[0], 16), part[1])]
+        return landed[i].at[pl.ds(pl.multiple_of(origin * rows + part[0], 16), part[1])]
 
     def hop(i, way, hops):
         part = span(way, hops)
@@ -387,9 +423,14 @@
 
     def leaving(n, first):
         mine = pl.ds(first, 2 * rows)
-        pairs = [(rows_v.at[i, mine], outs[0].at[i, mine]) for i in (0, 1)]
-        pairs += [(acts.at[i, mine], outs[1].at[i, mine]) for i in range(3)]
-        pairs += [(low.at[mine], outs[2].at[mine])]
+        width, under = grad_all.shape[1], low.shape[1]
+        pairs = [
+            (landed[0].at[mine, pl.ds(0, width)], two_all.at[mine]),
+            (landed[0].at[mine, pl.ds(width, ADAPTER_RANK)], low_all.at[mine, pl.ds(under, ADAPTER_RANK)]),
+            (low.at[mine], low_all.at[mine, pl.ds(0, under)]),
+            (landed[1].at[mine], grad_all.at[mine]),
+        ]
+        pairs += [(acts.at[i, mine], acts_all.at[i, mine]) for i in range(3)]
         return [pltpu.make_async_copy(a, b, out_sem.at[n, i]) for i, (a, b) in enumerate(pairs)]
 
     def first_row(shift):
@@ -397,21 +438,21 @@
 
     def work(n, first):
         mine = pl.ds(first, 2 * rows)
-        rank = ADAPTER_RANK
-        low[mine, : 2 * rank] = matrix_product(rows_v[0, mine, :], squeeze[...]).astype(bf16)
-        low[mine, 2 * rank :] = times_transposed(rows_v[1, mine, :], widen_down[...]).astype(bf16)
+        rank, width = ADAPTER_RANK, MODEL_WIDTH
+        low[mine, : 2 * rank] = matrix_product(landed[0][mine, :width], squeeze[...]).astype(bf16)
+        low[mine, 2 * rank :] = times_transposed(landed[1][mine, :], widen_down[...]).astype(bf16)
 
         @pl.loop(0, held.shape[1] // wide)
         def _(t):
             own = pl.ds(pl.multiple_of(t * wide, wide), wide)
-            two = rows_v[0, mine, :]
+            two = landed[0][mine, :width]
             gate = times_transposed(two, held[0, own, :]) + matrix_product(
                 low[mine, :rank], widen_gate[:, own]
             )
             upward = times_transposed(two, held[1, own, :]) + matrix_product(
                 low[mine, rank : 2 * rank], widen_up[:, own]
             )
-            pull = times_transposed(rows_v[1, mine, :], held[2, own, :]) + times_transposed(
+            pull = times_transposed(landed[1][mine, :], held[2, own, :]) + times_transposed(
                 low[mine, 2 * rank :], narrow[own, :]
             )
             scale = math.sqrt(2.0 / math.pi)
@@ -479,6 +520,7 @@
     rank = ADAPTER_RANK
     if size != 16:
         two, grad = gather_rows(two), gather_rows(grad)
+        two, lora_out = two[:, :MODEL_WIDTH], two[:, MODEL_WIDTH:]
         low = matrix_product(two, squeeze).astype(bf16)
         pulled = times_transposed(grad, widen_down).astype(bf16)
         gate = times_transposed(two, planes[0]) + matrix_product(low[:, :rank], widen_gate)
@@ -487,12 +529,13 @@
         units = (gelu_tanh(gate) * upward).astype(bf16)
         gate_grad, up_grad = unit_backward(gate, upward, units_grad)
         return (
-            jnp.stack([two, grad]),
+            two,
+            grad,
             jnp.stack([gate_grad, up_grad, units]),
-            jnp.concatenate([low, pulled], axis=1),
+            jnp.concatenate([low, pulled, lora_out], axis=1),
         )
     chips = size // 2
-    rows, columns = two.shape
+    rows, columns = grad.shape
     all_rows, hidden = size * rows, planes.shape[1]
     anywhere, inside = pl.BlockSpec(memory_space=pl.ANY), pl.BlockSpec(memory_space=pltpu.VMEM)
     pair = pltpu.SemaphoreType.DMA((2, 2, chips // 2))
@@ -500,24 +543,26 @@
     return pl.pallas_call(
         functools.partial(unit_kernel, chips),
         out_shape=(
-            jax.ShapeDtypeStruct((2, all_rows, columns), bf16),
+            jax.ShapeDtypeStruct((all_rows, columns), bf16),
+            jax.ShapeDtypeStruct((all_rows, columns), bf16),
             jax.ShapeDtypeStruct((3, all_rows, hidden), bf16),
-            jax.ShapeDtypeStruct((all_rows, 3 * rank), bf16),
+            jax.ShapeDtypeStruct((all_rows, 4 * rank), bf16),
         ),
         in_specs=[anywhere] * 3 + [inside] * 5,
-        out_specs=(anywhere,) * 3,
+        out_specs=(anywhere,) * 4,
         scratch_shapes=[
             pltpu.VMEM(planes.shape, bf16),
-            pltpu.VMEM((2, all_rows, columns), bf16),
             pltpu.VMEM((3, all_rows, hidden), bf16),
             pltpu.VMEM((all_rows, 3 * rank), bf16),
+            pltpu.VMEM((all_rows, two.shape[1]), bf16),
+            pltpu.VMEM((all_rows, columns), bf16),
             pltpu.SemaphoreType.DMA((3,)),
             pltpu.SemaphoreType.DMA((2,)),
             pair,
             pair,
             sides,
             sides,
-            pltpu.SemaphoreType.DMA((chips, 6)),
+            pltpu.SemaphoreType.DMA((chips, 7)),
         ],
         compiler_params=pltpu.CompilerParams(
             collective_id=ident, has_side_effects=True, vmem_limit_bytes=60 << 20
@@ -560,14 +605,15 @@
             device_id_type=MESH,
         )
 
-    def hop(way, step):
+    def hop(way, step, part):
         target = (reach - step if way == 0 else chips - reach + step) % chips
         cols = pl.ds(way * half, half) if step == 0 else pl.ds(0, columns)
+        here = pl.ds(part * (rows // 2), rows // 2)
         return pltpu.make_async_remote_copy(
-            side_buf.at[target, :, cols],
-            ring_buf.at[way, step, :, cols],
-            ring_send.at[way, step],
-            ring_recv.at[way, step],
+            side_buf.at[target, here, cols],
+            ring_buf.at[way, step, here, cols],
+            ring_send.at[way, step, part],
+            ring_recv.at[way, step, part],
             device_id={"fsdp": ways[way]},
             device_id_type=MESH,
         )
@@ -610,32 +656,35 @@
         last = target == 0
         incoming = [(w, step - 1) for w in ((0, 1) if last else (way,))] if step else []
         across(i).wait_recv()
-        for w, s in incoming:
-            hop(w, s).wait_recv()
-
-        @pl.loop(0, rows // tile)
-        def _(j):
-            here = pl.ds(pl.multiple_of(j * tile, tile), tile)
-            for part in (0, 1):
-                cols = pl.ds(part * half, half)
-                total = mine[i % 2, here, cols].astype(f32) + side_buf[target, here, cols].astype(f32)
-                for w, s in incoming:
-                    if s or w == part:
-                        total = total + ring_buf[w, s, here, cols].astype(f32)
-                if last:
-                    o_ref[here, cols] = total
-                else:
-                    side_buf[target, here, cols] = total.astype(bf16)
-
-        if not last:
-            hop(way, step).start()
-            if step == 0:
-                hop(1, 0).start()
+        for part in (0, 1):
+            for w, s in incoming:
+                hop(w, s, part).wait_recv()
+
+            @pl.loop(0, rows // 2 // tile)
+            def _(j, part=part):
+                here = pl.ds(pl.multiple_of(part * (rows // 2) + j * tile, tile), tile)
+                for side_half in (0, 1):
+                    cols = pl.ds(side_half * half, half)
+                    total = mine[i % 2, here, cols].astype(f32) + side_buf[target, here, cols].astype(f32)
+                    for w, s in incoming:
+                        if s or w == side_half:
+                            total = total + ring_buf[w, s, here, cols].astype(f32)
+                    if last:
+                        o_ref[here, cols] = total
+                    else:
+                        side_buf[target, here, cols] = total.astype(bf16)
+
+            if not last:
+                hop(way, step, part).start()
+                if step == 0:
+                    hop(1, 0, part).start()
 
     for fetch in fetches:
         fetch.wait()
     make(0)
-    for i in range(len(order)):
+    add(0)
+    make(1)
+    for i in range(1, len(order)):
         if i + 1 < len(order):
             make(i + 1)
         add(i)
@@ -643,7 +692,8 @@
         across(i).wait_send()
     for step in range(reach):
         for way in (0, 1):
-            hop(way, step).wait_send()
+            for part in (0, 1):
+                hop(way, step, part).wait_send()
 
 
 def mix_rows(acts, planes, gate_b, up_b, down_a, ident):
@@ -660,7 +710,7 @@
         return scatter_rows(jnp.concatenate(terms, axis=1))
     chips = size // 2
     rows, columns = acts.shape[1] // size, 2 * MODEL_WIDTH + 3 * ADAPTER_RANK
-    pair = pltpu.SemaphoreType.DMA((2, chips // 2))
+    pair = pltpu.SemaphoreType.DMA((2, chips // 2, 2))
     sides = pltpu.SemaphoreType.DMA((chips,))
     return pl.pallas_call(
         functools.partial(mix_kernel, chips),
@@ -915,8 +965,8 @@
     normed_two = (middle * scale_two * gains[1]).astype(bf16)
 
     weight_planes = feedforward_weight.transpose(1, 0, 2)
-    rows_all, acts, low_ffn = unit_rows(
-        normed_two,
+    two_all, grad_all, acts, low_ffn = unit_rows(
+        jnp.concatenate([normed_two, lora_out], axis=1),
         output_gradient[0],
         weight_planes,
         first_factor[:, 4 * rank :],
@@ -926,18 +976,18 @@
         narrow_down,
         2,
     )
-    two_all, grad_all = rows_all[0], rows_all[1]
     gate_grad, up_grad, units = acts[0], acts[1], acts[2]
-    lora_gate, lora_up, hd_grad = low_ffn[:, :rank], low_ffn[:, rank : 2 * rank], low_ffn[:, 2 * rank :]
-    ffn_shares = jnp.stack(
+    lora_gate, lora_up = low_ffn[:, :rank], low_ffn[:, rank : 2 * rank]
+    hd_grad, lora_out_all = low_ffn[:, 2 * rank : 3 * rank], low_ffn[:, 3 * rank :]
+    early_shares = jnp.stack(
         [
-            outer_product_rows(former, latter).astype(bf16)
-            for former, latter in ((gate_grad, two_all), (up_grad, two_all), (units, grad_all))
+            outer_product_rows(gate_grad, two_all).astype(bf16),
+            outer_product_rows(units, grad_all).astype(bf16),
         ]
     )
-    attended_all = gather_rows(jnp.concatenate([attended, lora_qkv], axis=1))
-    ffn_shares, acts, attended_all = lax.optimization_barrier((ffn_shares, acts, attended_all))
-    ffn_both = loop_shares(ffn_shares)
+    early_shares, acts = lax.optimization_barrier((early_shares, acts))
+    early_both = loop_shares(early_shares)
+    up_share = outer_product_rows(acts[1], two_all).astype(bf16)
     rows_sum = mix_rows(
         acts, weight_planes, widen_gate, widen_up, narrow_down, 3
     )
@@ -981,6 +1031,10 @@
     )
     value_part = jnp.einsum("thu,thd->ud", probs_low, heads_grad, preferred_element_type=f32)
     pair_grad = ring_scatter([key_part, value_part], 4)
+    attended_rows, early_both, pair_grad = lax.optimization_barrier(
+        (jnp.concatenate([attended, lora_qkv], axis=1), early_both, pair_grad)
+    )
+    attended_all = gather_rows(attended_rows)
     query_grad = rotate(
         query_rot_grad.reshape(tokens_dev, QUERY_WIDTH), position_own, -1.0
     ).astype(bf16)
@@ -1009,7 +1063,6 @@
     gain_one = jnp.sum(normed_grad * hidden_state * scale_one, axis=0)
 
     lora_qkv_all = attended_all[:, QUERY_WIDTH:]
-    lora_out_all = matrix_product(attended_all[:, :QUERY_WIDTH], narrow_output).astype(bf16)
     normed_turn, branch_turn = turn(normalized), turn(branch_grad)
     out_piece = outer_product_rows(branch_turn, lora_out_all)
     gain_rows = jnp.stack([gain_one, gain_two]).astype(bf16).reshape(tokens_dev, -1)
@@ -1018,9 +1071,10 @@
     proj_rows = jnp.concatenate(
         [proj_grad, lora_out_grad, gate_low, up_low, lora_hd, gain_rows], axis=1
     )
-    proj_rows, normed_turn, branch_turn = lax.optimization_barrier(
-        (proj_rows, normed_turn, branch_turn)
-    )
+    proj_rows, normed_turn, branch_turn, up_share = lax.optimization_barrier(
+        (proj_rows, normed_turn, branch_turn, up_share)
+    )
+    up_both = loop_shares(up_share)
     proj_all, middle_own = share_rows(
         proj_rows, jnp.concatenate([out_piece, gate_piece, up_piece], axis=0).astype(bf16), 5
     )
@@ -1037,7 +1091,7 @@
         ],
         axis=1,
     ).astype(bf16)
-    attn_part, ffn_both, proj_all = lax.optimization_barrier((attn_part, ffn_both, proj_all))
+    attn_part, up_both, proj_all = lax.optimization_barrier((attn_part, up_both, proj_all))
     attn_sum = both_loops(loop_shares(attn_part))
     gain_column = PROJECT_COLUMNS + QUERY_WIDTH
     gain_sum = attn_sum[:2, gain_column : gain_column + width_own]
@@ -1087,7 +1141,7 @@
     expand_own = jnp.where(
         owned < PROJECT_COLUMNS, near, jnp.where(owned < far_start, middle_own, far)
     ).T.astype(f32)
-    ffn_sum = both_loops(ffn_both).transpose(1, 0, 2)
+    ffn_sum = sum_loops(early_both, up_both).transpose(1, 0, 2)
     return (
         hidden_out[None],
         input_grad[None],

time: 844 us -> 814 us (0.964)
  Pallas kernels: 521 us -> 490 us
  waiting for transfers between devices: 22.2 us -> 50.2 us
  other arithmetic: 56.4 us -> 41.6 us
  local copies, waits for them, and re-layouts: 40.6 us -> 31.6 us
    pallas_call x1, Pallas kernels: 167 us -> 101 us  [unit_rows(): pl.pallas_call(functools.partial(unit_kernel, chips), out_shape=(jax.Shap...]
    all_gather x2 -> x3, waiting for transfers between devices: 4.57 us -> 25.7 us  [loop_shares(): return lax.all_gather(partial.astype(bf16), 'loop', axis=0)]
    pallas_call x0 -> x1, Pallas kernels: none -> 20.4 us  [sum_loops(): pl.pallas_call(sum_kernel, grid=(3, steps), out_shape=jax.ShapeDtypeStruc...]
    pallas_call x1, Pallas kernels: 109 us -> 129 us  [share_rows(): pl.pallas_call(functools.partial(share_kernel, size, chunk, own_count), o...]
    transpose x1 -> x0, other arithmetic: 18.5 us -> none  [per_device(): ffn_sum = both_loops(ffn_both).transpose(1, 0, 2)]
    slice x1 -> x0, local copies, waits for them, and re-layouts: 13.1 us -> none  [per_device(): two_all, grad_all = (rows_all[0], rows_all[1])]
    dot_general x16, matrix products: 94.3 us -> 83.5 us  [outer_product_rows(): lax.dot_general(former, latter, (((0,), (0,)), ((), ())), preferred_eleme...]
    pallas_call x1, Pallas kernels: 132 us -> 123 us  [mix_rows(): pl.pallas_call(functools.partial(mix_kernel, chips), out_shape=jax.ShapeD...]
  transfers between devices with their start and end apart: 6 -> 7, of which waited for: 3 -> 3; matrix products, arithmetic and copies ran while one was open for 27% -> 20% of each run, Pallas kernels for 55% -> 41%
where the time goes in v7:
time: 814 us; the launch traced here: 801 us
  Pallas kernels  490 us (60%)
  matrix products  160 us (20%)
  waiting for transfers between devices  50.2 us (6%)
  other arithmetic  41.6 us (5%)
  local copies, waits for them, and re-layouts  31.6 us (4%)
  between operations  15.2 us (2%)
  starting transfers between devices  12.2 us (1%)
    pallas_call x1, Pallas kernels, share_rows(): pl.pallas_call(functools.partial(share_kernel, size, chunk, own_count), o...  129 us
    pallas_call x1, Pallas kernels, mix_rows(): pl.pallas_call(functools.partial(mix_kernel, chips), out_shape=jax.ShapeD...  123 us
    pallas_call x1, Pallas kernels, unit_rows(): pl.pallas_call(functools.partial(unit_kernel, chips), out_shape=(jax.Shap...  101 us
    pallas_call x2, Pallas kernels, ring_gather(): pl.pallas_call(functools.partial(gather_kernel, chips), out_shape=jax.Sha...  91.8 us
    dot_general x16, matrix products, outer_product_rows(): lax.dot_general(former, latter, (((0,), (0,)), ((), ())), preferred_eleme...  83.5 us
    dot_general x13, matrix products, times_transposed(): lax.dot_general(former, latter, (((1,), (1,)), ((), ())), preferred_eleme...  45.9 us
    all_gather x3, waiting for transfers between devices, loop_shares(): return lax.all_gather(partial.astype(bf16), 'loop', axis=0)  25.7 us
    pallas_call x1, Pallas kernels, ring_scatter(): pl.pallas_call(functools.partial(scatter_kernel, chips, count), out_shape...  25.2 us
  transfers between devices with their start and end apart: 7, of which 3 were waited for; matrix products, arithmetic and copies ran while one was open for 20% of the time, Pallas kernels for 41%

profile of v7, /device:TPU:0, one launch (start us, length us, event | category | flops | bytes accessed | tf_op | source)
XLA Modules:
  0.0 801.1 jit_solution(4774532778542819904)
XLA Ops:
  7.2 61.2 %ring_gather.2 = bf16[2048,2560]{1,0:T(8,128)(2,1)} custom-call(bf16[128,2560]{1,0:T(8,128)(2,1)} %x_ref.1), custom_call_target="tpu_custom_call" | custom-call | bytes 3000000 | tf_op jit(solution)/shard_map/ring_gather/pallas_call | solution.py:229
  68.5 2.5 slice.293.refs_4_
  71.0 3.8 slice.292.refs_3_
  75.5 2.7 fusion.95
  78.2 1.7 fusion.163
  79.9 1.5 convolution_add_fusion.5
  85.4 30.6 %ring_gather.3 = bf16[2048,512]{1,0:T(8,128)(2,1)} custom-call(bf16[128,512]{1,0:T(8,128)(2,1)} %pad_maximum_fusion.7.x_ref), custom_call_target="tpu_custom_call" | custom-call | bytes 3000000 | tf_op jit(solution)/shard_map/ring_gather/pallas_call | solution.py:229
  118.4 2.5 fusion.118
  121.0 5.4 fusion.214
  126.3 3.4 copy-done.3
  129.7 2.0 fusion.81
  132.0 1.9 dynamic-slice_bitcast_fusion.refs_7_.refs_4_
  133.9 2.2 dynamic-slice_bitcast_fusion.1
  136.1 1.6 convolution_convert_fusion.8
  137.7 10.0 %all-gather.9.cloned.1.call-done = bf16[2048,2048]{1,0:T(8,128)(2,1)} async-done(((bf16[128,2048]{1,0:T(8,128)(2,1)}), bf16[2048,2048]{1,0:T(8,128)(2,1)}) %all-gather.9.cloned.1.call-update) | async-done | bytes 8388624 | tf_op jit(solution)/shard_map/all_gather | solution.py:89
  147.7 6.6 convolution_add_fusion.6
  154.4 1.6 multiply_reduce_fusion.3
  157.0 101.2 %unit_rows.1 = (bf16[2048,2048]{1,0:T(8,128)(2,1)}, bf16[2048,2048]{1,0:T(8,128)(2,1)}, bf16[3,2048,1024]{2,1,0:T(8,128)(2,1)}, bf16[2048,1024]{1,0:T(8,128)(2,1)}) custom-call(bf16[128,2304]{1,0:T(8,128)(2,1)} %pad_maximum_fusion.3.refs_0_, bf16[128,2048]{1,0:T(8,128)(2,1)} %bitcast.226, bf16[3,1024,2048]{2,1,0:T(8,128)(2,1)} %bitcast.189, ...), custom_call_target="tpu_custom_call" | custom-call | bytes 300000000 | tf_op jit(solution)/shard_map/unit_rows/pallas_call | solution.py:543
  258.3 14.2 %convert_bitcast_fusion = bf16[1,1024,2048]{2,1,0:T(8,128)(2,1)} fusion(bf16[2048,2048]{1,0:T(8,128)(2,1)} %get-tuple-element.33, bf16[3,2048,1024]{2,1,0:T(8,128)(2,1)} %get-tuple-element.34.refs_0_), kind=kOutput, calls=%fused_computation.27 | convolution fusion | flops 8592031744 | bytes 16777216 | tf_op jit(solution)/shard_map/dot_general | solution.py:36
  272.5 12.5 %convert_bitcast_fusion.1 = bf16[1,1024,2048]{2,1,0:T(8,128)(2,1)} fusion(bf16[2048,2048]{1,0:T(8,128)(2,1)S(1)} %copy-done.24, bf16[3,2048,1024]{2,1,0:T(8,128)(2,1)} %get-tuple-element.34.refs_0_), kind=kOutput, calls=%fused_computation.28 | convolution fusion | flops 8592031744 | bytes 16777216 | tf_op jit(solution)/shard_map/dot_general | solution.py:36
  285.0 7.6 pad_maximum_fusion
  294.7 122.8 %mix_rows.1 = f32[128,4864]{1,0:T(8,128)} custom-call(bf16[3,2048,1024]{2,1,0:T(8,128)(2,1)} %get-tuple-element.34.refs_0_, bf16[3,1024,2048]{2,1,0:T(8,128)(2,1)} %bitcast.190, bf16[256,1024]{1,0:T(8,128)(2,1)} %get-tuple-element.58.refs_5_.refs_2_, bf16[256,1024]{1,0:T(8,128)(2,1)} %get-tuple-element.57.refs_6_.refs_3_, ...), custom_call_target="tpu_custom_call" | custom-call | bytes 3000000 | tf_op jit(solution)/shard_map/mix_rows/pallas_call | solution.py:715
  417.5 2.0 convert.97
  419.5 2.6 convolution_add_fusion.2
  422.1 2.0 multiply_reduce_fusion.1
  424.6 1.9 convolution_convert_fusion.7
  427.9 2.1 fusion.66
  432.8 2.0 copy-done.6
  434.8 2.4 fusion.50.refs_0_
  437.2 2.7 fusion.51.refs_1_
  439.9 25.2 %ring_scatter.1 = f32[128,512]{1,0:T(8,128)} custom-call(bf16[2048,256]{1,0:T(8,128)(2,1)} %fusion.50.refs_0_, bf16[2048,256]{1,0:T(8,128)(2,1)} %fusion.51.refs_1_), custom_call_target="tpu_custom_call" | custom-call | bytes 3000000 | tf_op jit(solution)/shard_map/ring_scatter/pallas_call | solution.py:344
  465.1 25.7 %all-gather.13.cloned.1.call-done = bf16[4,1024,2048]{2,1,0:T(8,128)(2,1)} async-done(((bf16[2,1024,2048]{2,1,0:T(8,128)(2,1)}), bf16[4,1024,2048]{2,1,0:T(8,128)(2,1)}) %all-gather.13.cloned.1.call-update) | async-done | bytes 16777232 | tf_op jit(solution)/shard_map/all_gather | solution.py:97
  492.3 5.9 all-to-all-start
  499.2 4.1 convolution_multiply_fusion
  504.4 2.3 convolution_convert_fusion.6
  506.8 14.0 %fusion.29 = bf16[1024,2048]{1,0:T(8,128)(2,1)} fusion(bf16[2048,2048]{1,0:T(8,128)(2,1)} %get-tuple-element.32, bf16[3,2048,1024]{2,1,0:T(8,128)(2,1)} %get-tuple-element.34.refs_0_), kind=kOutput, calls=%fused_computation.33 | convolution fusion | flops 8592031744 | bytes 16777216 | tf_op jit(solution)/shard_map/dot_general | solution.py:36
  521.8 1.7 convolution_convert_fusion.10
  525.3 8.6 %fusion.145 = f32[128,2048]{1,0:T(8,128)} fusion(bf16[2048,2560]{1,0:T(8,128)(2,1)} %ring_gather.2, bf16[128,256]{1,0:T(8,128)(2,1)S(1)} %get-tuple-element.56, bf16[128,256]{1,0:T(8,128)(2,1)S(1)} %maximum_bitcast_fusion.3, bf16[128,2048]{1,0:T(8,128)(2,1)S(1)} %bitcast.209), kind=kOutput, calls=%fused_computation.173 | convolution fusion | flops 1344143360 | bytes 12189696 | tf_op jit(solution)/shard_map/dot_general | solution.py:32
  533.9 6.1 all-to-all-start.1
  540.1 4.4 fusion.108
  545.2 1.6 slice_dynamic-update-slice_fusion
  548.9 14.4 %all-to-all-done.1 = bf16[128,16,128]{2,0,1:T(8,128)(2,1)S(1)} async-done(((bf16[128,16,128]{2,0,1:T(8,128)(2,1)}), bf16[128,16,128]{2,0,1:T(8,128)(2,1)S(1)}, u32[]{:S(2)}, u32[]{:S(2)}) %all-to-all-start.1) | async-done | bytes 524320 | tf_op jit(solution)/shard_map/all_to_all | solution.py:140
  563.3 2.7 fusion.67
  566.0 4.9 fusion.73
  570.9 3.5 fusion.87
  574.4 3.5 fusion.84
  579.4 129.0 %share_rows.1 = (bf16[2048,3712]{1,0:T(8,128)(2,1)}, bf16[2464,256]{1,0:T(8,128)(2,1)}) custom-call(bf16[128,3712]{1,0:T(8,128)(2,1)} %pad_dynamic-update-slice_fusion.x_ref, bf16[2176,256]{1,0:T(8,128)(2,1)} %pad_maximum_fusion.1.mid_ref), custom_call_target="tpu_custom_call" | custom-call | bytes 3000000 | tf_op jit(solution)/shard_map/share_rows/pallas_call | solution.py:852
  710.2 2.5 fusion.105
  712.7 5.7 fusion.36
  718.5 8.2 %fusion.215 = bf16[128,2816]{1,0:T(8,128)(2,1)S(1)} fusion(bf16[2048,128]{1,0:T(8,128)(2,1)S(1)} %bitcast.206, bf16[2048,2816]{0,1:T(8,128)(2,1)} %all-gather.11.cloned.1.call-done), kind=kOutput, calls=%fused_computation.290 | convolution fusion | flops 1476395008 | bytes 12779520 | tf_op jit(solution)/shard_map/dot_general | solution.py:36
  727.9 2.2 fusion.68
  730.1 2.7 convolution_convert_fusion
  732.8 2.7 convolution_convert_fusion.1
  735.5 7.1 fusion.52
  742.7 3.4 copy-done
  746.1 20.4 %sum_loops.1 = f32[3,1024,2048]{2,1,0:T(8,128)} custom-call(bf16[2,2,1024,2048]{3,2,1,0:T(8,128)(2,1)} %bitcast.192, bf16[2,1024,2048]{2,1,0:T(8,128)(2,1)S(1)} %bitcast.186), custom_call_target="tpu_custom_call" | custom-call | bytes 51000000 | tf_op jit(solution)/shard_map/sum_loops/pallas_call | solution.py:118
  766.6 2.4 fusion.39
  768.9 1.8 fusion.124
  771.7 2.0 convolution_convert_fusion.4
  773.8 1.7 convolution_convert_fusion.3
  775.6 2.6 convolution_convert_fusion.2
  778.2 3.7 fusion.55
  782.0 7.5 convert_bitcast_fusion.2
  789.5 1.9 convert_add_fusion
  (168 shorter events, 32.4 us)
Async XLA Ops:
  7.2 67.6 %copy-start.2 = (bf16[1,128,2048]{2,1,0:T(8,128)(2,1)S(1)}, bf16[1,128,2048]{2,1,0:T(8,128)(2,1)}, u32[]{:S(2)}) copy-start(bf16[1,128,2048]{2,1,0:T(8,128)(2,1)} %param.10) | copy-start | bytes 1572868
  7.2 140.5 %all-gather.9.cloned.1.call-start = ((), (), s32[]{:S(2)}) async-start(), calls=%async_computation.2 | async-start | bytes 8912896 | tf_op jit(solution)/shard_map/all_gather | solution.py:89
  68.4 7.1 copy-start.23
  68.4 422.4 %all-gather.13.cloned.1.call-start = ((), (), s32[]{:S(2)}) async-start(), calls=%async_computation.4 | async-start | bytes 25165824 | tf_op jit(solution)/shard_map/all_gather | solution.py:97
  68.5 9.7 %copy-start.1 = (bf16[2048,2560]{1,0:T(8,128)(2,1)S(1)}, bf16[2048,2560]{1,0:T(8,128)(2,1)}, u32[]{:S(2)}) copy-start(bf16[2048,2560]{1,0:T(8,128)(2,1)} %ring_gather.2) | copy-start | bytes 31457284
  78.2 5.5 copy-start.17
  78.2 3.6 copy-start.29
  82.0 36.4 %copy-start.25 = (f32[128]{0:T(128)}, f32[128]{0:T(128)S(1)}, u32[]{:S(2)}) copy-start(f32[128]{0:T(128)S(1)} %multiply_exponential_fusion) | copy-start | bytes 1540
  117.0 1.4 copy-start.19
  117.3 1.2 copy-start.12
  117.3 1.2 copy-start.14
  120.9 8.8 %copy-start.4 = (bf16[2048,512]{1,0:T(8,128)(2,1)S(1)}, bf16[2048,512]{1,0:T(8,128)(2,1)}, u32[]{:S(2)}) copy-start(bf16[2048,512]{1,0:T(8,128)(2,1)} %ring_gather.3) | copy-start | bytes 6291460
  126.3 3.4 copy-start.3
  258.3 14.2 %copy-start.24 = (bf16[2048,2048]{1,0:T(8,128)(2,1)S(1)}, bf16[2048,2048]{1,0:T(8,128)(2,1)}, u32[]{:S(2)}) copy-start(bf16[2048,2048]{1,0:T(8,128)(2,1)} %get-tuple-element.32) | copy-start | bytes 25165828
  292.7 0.9 copy-start.18
  292.7 425.8 %all-gather.11.cloned.1.call-start = ((), (), s32[]{:S(2)}) async-start(), calls=%async_computation.3 | async-start | bytes 12255232 | tf_op jit(solution)/shard_map/all_gather | solution.py:89
  417.5 6.7 copy-start.8
  417.5 9.0 %slice-start = ((s8[8388608]{0:T(1024)(128)(4,1)}), s8[4194304]{0:T(1024)(128)(4,1)S(1)}, s32[]{:S(2)}) async-start(s8[8388608]{0:T(1024)(128)(4,1)} %bitcast.187), calls=%async_computation.7 | async-start | bytes 8388608
  419.5 5.1 copy-start.7
  422.1 4.4 slice-start.1
  424.2 5.9 slice-start.2
  426.5 3.5 slice-start.3
  426.6 3.5 copy-start.5
  426.6 3.5 copy-start.27
  431.6 3.2 copy-start.13
  431.6 3.2 copy-start.15
  432.8 2.0 copy-start.6
  492.3 41.5 %all-to-all-start = ((bf16[128,16,128]{2,0,1:T(8,128)(2,1)}), bf16[128,16,128]{2,0,1:T(8,128)(2,1)}, u32[]{:S(2)}, u32[]{:S(2)}) async-start(bf16[128,16,128]{2,0,1:T(8,128)(2,1)} %fusion.121), calls=%async_computation | async-start | bytes 1048576 | tf_op jit(solution)/shard_map/all_to_all | solution.py:140
  499.1 4.2 copy-start.20
  499.1 4.2 copy-start.22
  506.8 14.0 %copy-start.16 = (f32[128,512]{1,0:T(8,128)S(1)}, f32[128,512]{1,0:T(8,128)}, u32[]{:S(2)}) copy-start(f32[128,512]{1,0:T(8,128)} %ring_scatter.1) | copy-start | bytes 786436
  506.8 14.0 %copy-start.26 = (f32[128]{0:T(128)S(1)}, f32[128]{0:T(128)}, u32[]{:S(2)}) copy-start(f32[128]{0:T(128)} %copy-done.25) | copy-start | bytes 1540
  525.3 14.7 %copy-start.30 = (bf16[128,256]{1,0:T(8,128)(2,1)S(1)}, bf16[128,256]{1,0:T(8,128)(2,1)}, u32[]{:S(2)}) copy-start(bf16[128,256]{1,0:T(8,128)(2,1)} %convolution_convert_fusion.10) | copy-start | bytes 196612
  525.3 14.7 %copy-start.31 = (bf16[128,256]{1,0:T(8,128)(2,1)S(1)}, bf16[128,256]{1,0:T(8,128)(2,1)}, u32[]{:S(2)}) copy-start(bf16[128,256]{1,0:T(8,128)(2,1)} %convolution_convert_fusion.6) | copy-start | bytes 196612
  533.9 29.4 %all-to-all-start.1 = ((bf16[128,16,128]{2,0,1:T(8,128)(2,1)}), bf16[128,16,128]{2,0,1:T(8,128)(2,1)S(1)}, u32[]{:S(2)}, u32[]{:S(2)}) async-start(bf16[128,16,128]{2,0,1:T(8,128)(2,1)} %bitcast.227), calls=%async_computation.1 | async-start | bytes 1048576 | tf_op jit(solution)/shard_map/all_to_all | solution.py:140
  540.0 187.9 %all-gather.15.cloned.1.call-start = ((), (), s32[]{:S(2)}) async-start(), calls=%async_computation.5 | async-start | bytes 12582912 | tf_op jit(solution)/shard_map/all_gather | solution.py:97
  563.3 226.2 %all-gather.17.cloned.1.call-start = ((), (), s32[]{:S(2)}) async-start(), calls=%async_computation.6 | async-start | bytes 3637248 | tf_op jit(solution)/shard_map/all_gather | solution.py:97
  566.0 4.9 copy-start.21
  577.9 132.2 %copy-start.28 = (f32[128]{0:T(128)S(1)}, f32[128]{0:T(128)}, u32[]{:S(2)}) copy-start(f32[128]{0:T(128)} %get-tuple-element.74) | copy-start | bytes 1540
  735.5 38.3 %slice-start.4 = ((s8[15204352]{0:T(1024)(128)(4,1)}), s8[2621440]{0:T(1024)(128)(4,1)S(1)}, s32[]{:S(2)}) async-start(s8[15204352]{0:T(1024)(128)(4,1)} %bitcast.228), calls=%async_computation.11 | async-start | bytes 5242880
  742.7 3.4 copy-start
  746.0 20.5 %copy-start.10 = (bf16[2048,256]{0,1:T(8,128)(2,1)S(1)}, bf16[2048,256]{0,1:T(8,128)(2,1)}, u32[]{:S(2)}) copy-start(bf16[2048,256]{0,1:T(8,128)(2,1)} %convolution_convert_fusion) | copy-start | bytes 3145732
  746.1 20.5 %copy-start.11 = (bf16[2048,256]{0,1:T(8,128)(2,1)S(1)}, bf16[2048,256]{0,1:T(8,128)(2,1)}, u32[]{:S(2)}) copy-start(bf16[2048,256]{0,1:T(8,128)(2,1)} %convolution_convert_fusion.1) | copy-start | bytes 3145732
  746.1 20.5 %copy-start.32 = (bf16[2048,256]{0,1:T(8,128)(2,1)S(1)}, bf16[2048,256]{0,1:T(8,128)(2,1)}, u32[]{:S(2)}) copy-start(bf16[2048,256]{0,1:T(8,128)(2,1)} %fusion.52) | copy-start | bytes 3145732
  746.1 27.7 %slice-start.5 = ((s8[15204352]{0:T(1024)(128)(4,1)}), s8[4194304]{0:T(1024)(128)(4,1)S(1)}, s32[]{:S(2)}) async-start(s8[15204352]{0:T(1024)(128)(4,1)} %bitcast.228), calls=%async_computation.12 | async-start | bytes 8388608
  746.1 27.8 %slice-start.6 = ((s8[15204352]{0:T(1024)(128)(4,1)}), s8[4194304]{0:T(1024)(128)(4,1)S(1)}, s32[]{:S(2)}) async-start(s8[15204352]{0:T(1024)(128)(4,1)} %bitcast.228), calls=%async_computation.13 | async-start | bytes 8388608
  746.1 27.8 %slice-start.7 = ((s8[15204352]{0:T(1024)(128)(4,1)}), s8[4194304]{0:T(1024)(128)(4,1)S(1)}, s32[]{:S(2)}) async-start(s8[15204352]{0:T(1024)(128)(4,1)} %bitcast.228), calls=%async_computation.14 | async-start | bytes 8388608
  766.6 9.0 %slice-start.8 = ((s8[8388608]{0:T(1024)(128)(4,1)}), s8[4194304]{0:T(1024)(128)(4,1)S(1)}, s32[]{:S(2)}) async-start(s8[8388608]{0:T(1024)(128)(4,1)} %bitcast.240), calls=%async_computation.15 | async-start | bytes 8388608
  768.9 6.6 slice-start.9
  778.2 3.7 copy-start.9
Sparse Core Ops, SparseCore 0:
  68.6 79.1 all-gather.8
  292.8 197.9 all-gather.12
  493.6 122.5 all-gather.10
  618.1 109.6 all-gather.14
  742.8 36.9 all-gather.16

commit v8 on v7

--- a/solution.py
+++ b/solution.py
@@ -364,9 +364,9 @@
 
 def unit_kernel(chips, *refs):
     sources, (planes, squeeze, widen_down, widen_gate, widen_up, narrow) = refs[:2], refs[2:8]
-    two_all, grad_all, acts_all, low_all = refs[8:12]
-    held, acts, low, landed = refs[12], refs[13], refs[14], refs[15:17]
-    held_sem, own_sem, ring_send, ring_recv, side_send, side_recv, out_sem = refs[17:]
+    two_all, grad_all, acts_all, low_all, early_out, up_out, piece_out, down_out = refs[8:16]
+    held, turned, acts, low, tiles, landed = refs[16], refs[17], refs[18], refs[19], refs[20], refs[21:23]
+    held_sem, own_sem, ring_send, ring_recv, side_send, side_recv, out_sem, acts_sem, tile_sem = refs[23:]
     core, device = ring_neighbours(chips)
     rows = sources[0].shape[0]
     reach = chips // 2
@@ -430,8 +430,13 @@
             (low.at[mine], low_all.at[mine, pl.ds(0, under)]),
             (landed[1].at[mine], grad_all.at[mine]),
         ]
-        pairs += [(acts.at[i, mine], acts_all.at[i, mine]) for i in range(3)]
         return [pltpu.make_async_copy(a, b, out_sem.at[n, i]) for i, (a, b) in enumerate(pairs)]
+
+    def shown(n, first):
+        mine = pl.ds(first, 2 * rows)
+        return [
+            pltpu.make_async_copy(acts.at[n % 2, i], acts_all.at[i, mine], acts_sem.at[n % 2, i]) for i in range(3)
+        ]
 
     def first_row(shift):
         return pl.multiple_of(device(shift, 0) * rows, 2 * rows)
@@ -439,6 +444,9 @@
     def work(n, first):
         mine = pl.ds(first, 2 * rows)
         rank, width = ADAPTER_RANK, MODEL_WIDTH
+        if n >= 2:
+            for copy in shown(n, first):
+                copy.wait()
         low[mine, : 2 * rank] = matrix_product(landed[0][mine, :width], squeeze[...]).astype(bf16)
         low[mine, 2 * rank :] = times_transposed(landed[1][mine, :], widen_down[...]).astype(bf16)
 
@@ -461,11 +469,11 @@
             rise = 0.5 * (1.0 + bend)
             active = gate * rise
             slope = rise + 0.5 * gate * (1.0 - bend * bend) * (scale * (1.0 + 3 * 0.044715 * square))
-            acts[0, mine, own] = (pull * upward * slope).astype(bf16)
-            acts[1, mine, own] = (pull * active).astype(bf16)
-            acts[2, mine, own] = (active * upward).astype(bf16)
-
-        for copy in leaving(n, first):
+            for i, value in enumerate((pull * upward * slope, pull * active, active * upward)):
+                acts[n % 2, i, :, own] = value.astype(bf16)
+                turned[i, own, mine] = value.T.astype(bf16)
+
+        for copy in leaving(n, first) + shown(n, first):
             copy.start()
 
     for i in (0, 1):
@@ -498,6 +506,31 @@
         for i in (0, 1):
             across(i, way, reach, 1 - core).wait_recv()
     work(2 * reach - 1, first_row(reach))
+    rank = ADAPTER_RANK
+    for kind, out in ((0, early_out.at[0]), (2, early_out.at[1]), (1, up_out)):
+
+        def tile_copy(t, out=out):
+            there = pl.ds(pl.multiple_of(t * wide, wide), wide)
+            return pltpu.make_async_copy(tiles.at[t % 2], out.at[:, there], tile_sem.at[t % 2])
+
+        @pl.loop(0, MODEL_WIDTH // wide)
+        def _(t, kind=kind, tile_copy=tile_copy):
+            @pl.when(t > 1)
+            def _():
+                tile_copy(t - 2).wait()
+
+            cols = pl.ds(pl.multiple_of(t * wide, wide), wide)
+            tiles[t % 2] = matrix_product(
+                turned[kind], landed[1 if kind == 2 else 0][:, cols]
+            ).astype(bf16)
+            tile_copy(t).start()
+
+        if kind == 2:
+            piece_out[0] = matrix_product(turned[0], low[:, :rank]).astype(bf16)
+            piece_out[1] = matrix_product(turned[1], low[:, rank : 2 * rank]).astype(bf16)
+            down_out[...] = matrix_product(turned[2], low[:, 2 * rank :])
+        tile_copy(MODEL_WIDTH // wide - 2).wait()
+        tile_copy(MODEL_WIDTH // wide - 1).wait()
     for i in (0, 1):
         across(i, 0, 0, core).wait_send()
         for hops in range(1, reach + 1):
@@ -513,6 +546,9 @@
             shift = (-1 if n % 2 else 1) * ((n + 1) // 2)
         for copy in leaving(n, first_row(shift)):
             copy.wait()
+        if n >= chips - 2:
+            for copy in shown(n, first_row(shift)):
+                copy.wait()
 
 
 def unit_rows(two, grad, planes, squeeze, widen_down, widen_gate, widen_up, narrow, ident):
@@ -533,6 +569,12 @@
             grad,
             jnp.stack([gate_grad, up_grad, units]),
             jnp.concatenate([low, pulled, lora_out], axis=1),
+            jnp.stack([outer_product_rows(gate_grad, two), outer_product_rows(units, grad)]).astype(bf16),
+            outer_product_rows(up_grad, two).astype(bf16),
+            jnp.stack(
+                [outer_product_rows(gate_grad, low[:, :rank]), outer_product_rows(up_grad, low[:, rank:])]
+            ).astype(bf16),
+            outer_product_rows(units, pulled),
         )
     chips = size // 2
     rows, columns = grad.shape
@@ -547,13 +589,19 @@
             jax.ShapeDtypeStruct((all_rows, columns), bf16),
             jax.ShapeDtypeStruct((3, all_rows, hidden), bf16),
             jax.ShapeDtypeStruct((all_rows, 4 * rank), bf16),
+            jax.ShapeDtypeStruct((2, hidden, columns), bf16),
+            jax.ShapeDtypeStruct((hidden, columns), bf16),
+            jax.ShapeDtypeStruct((2, hidden, rank), bf16),
+            jax.ShapeDtypeStruct((hidden, rank), f32),
         ),
         in_specs=[anywhere] * 3 + [inside] * 5,
-        out_specs=(anywhere,) * 4,
+        out_specs=(anywhere,) * 6 + (inside,) * 2,
         scratch_shapes=[
             pltpu.VMEM(planes.shape, bf16),
-            pltpu.VMEM((3, all_rows, hidden), bf16),
+            pltpu.VMEM((3, hidden, all_rows), bf16),
+            pltpu.VMEM((2, 3, 2 * rows, hidden), bf16),
             pltpu.VMEM((all_rows, 3 * rank), bf16),
+            pltpu.VMEM((2, hidden, 256), bf16),
             pltpu.VMEM((all_rows, two.shape[1]), bf16),
             pltpu.VMEM((all_rows, columns), bf16),
             pltpu.SemaphoreType.DMA((3,)),
@@ -562,7 +610,9 @@
             pair,
             sides,
             sides,
-            pltpu.SemaphoreType.DMA((chips, 7)),
+            pltpu.SemaphoreType.DMA((chips, 4)),
+            pltpu.SemaphoreType.DMA((2, 3)),
+            pltpu.SemaphoreType.DMA((2,)),
         ],
         compiler_params=pltpu.CompilerParams(
             collective_id=ident, has_side_effects=True, vmem_limit_bytes=60 << 20
@@ -965,7 +1015,7 @@
     normed_two = (middle * scale_two * gains[1]).astype(bf16)
 
     weight_planes = feedforward_weight.transpose(1, 0, 2)
-    two_all, grad_all, acts, low_ffn = unit_rows(
+    two_all, grad_all, acts, low_ffn, early_shares, up_share, ffn_pieces, down_own = unit_rows(
         jnp.concatenate([normed_two, lora_out], axis=1),
         output_gradient[0],
         weight_planes,
@@ -976,26 +1026,13 @@
         narrow_down,
         2,
     )
-    gate_grad, up_grad, units = acts[0], acts[1], acts[2]
-    lora_gate, lora_up = low_ffn[:, :rank], low_ffn[:, rank : 2 * rank]
-    hd_grad, lora_out_all = low_ffn[:, 2 * rank : 3 * rank], low_ffn[:, 3 * rank :]
-    early_shares = jnp.stack(
-        [
-            outer_product_rows(gate_grad, two_all).astype(bf16),
-            outer_product_rows(units, grad_all).astype(bf16),
-        ]
-    )
+    lora_out_all = low_ffn[:, 3 * rank :]
     early_shares, acts = lax.optimization_barrier((early_shares, acts))
     early_both = loop_shares(early_shares)
-    up_share = outer_product_rows(acts[1], two_all).astype(bf16)
     rows_sum = mix_rows(
         acts, weight_planes, widen_gate, widen_up, narrow_down, 3
     )
     back_own, out_own = rows_sum[:, : MODEL_WIDTH + 2 * rank], rows_sum[:, MODEL_WIDTH + 2 * rank :]
-    down_own = outer_product_rows(units, hd_grad)
-    gate_piece = outer_product_rows(gate_grad, lora_gate)
-    up_piece = outer_product_rows(up_grad, lora_up)
-
     lora_hd = out_own[:, MODEL_WIDTH:].astype(bf16)
     hidden_out = (middle + out_own[:, :MODEL_WIDTH] + matrix_product(lora_hd, widen_down)).astype(bf16)
 
@@ -1015,6 +1052,9 @@
     gain_two = jnp.sum(two_grad * middle * scale_two, axis=0)
 
     branch_grad = middle_grad.astype(bf16)
+    both = [block.reshape(tokens_dev, size, width_own) for block in (normalized, branch_grad)]
+    turned = turn(jnp.concatenate(both, axis=2).reshape(tokens_dev, -1))
+    normed_turn, branch_turn = turned[:, :width_own], turned[:, width_own:]
     lora_out_grad = times_transposed(branch_grad, widen_output).astype(bf16)
     attended_grad = (
         matrix_product(branch_grad, proj_out) + times_transposed(lora_out_grad, narrow_output)
@@ -1031,8 +1071,8 @@
     )
     value_part = jnp.einsum("thu,thd->ud", probs_low, heads_grad, preferred_element_type=f32)
     pair_grad = ring_scatter([key_part, value_part], 4)
-    attended_rows, early_both, pair_grad = lax.optimization_barrier(
-        (jnp.concatenate([attended, lora_qkv], axis=1), early_both, pair_grad)
+    attended_rows, early_both, pair_grad, normed_turn, branch_turn = lax.optimization_barrier(
+        (jnp.concatenate([attended, lora_qkv], axis=1), early_both, pair_grad, normed_turn, branch_turn)
     )
     attended_all = gather_rows(attended_rows)
     query_grad = rotate(
@@ -1063,7 +1103,6 @@
     gain_one = jnp.sum(normed_grad * hidden_state * scale_one, axis=0)
 
     lora_qkv_all = attended_all[:, QUERY_WIDTH:]
-    normed_turn, branch_turn = turn(normalized), turn(branch_grad)
     out_piece = outer_product_rows(branch_turn, lora_out_all)
     gain_rows = jnp.stack([gain_one, gain_two]).astype(bf16).reshape(tokens_dev, -1)
     gain_count = gain_rows.shape[1]
@@ -1071,12 +1110,10 @@
     proj_rows = jnp.concatenate(
         [proj_grad, lora_out_grad, gate_low, up_low, lora_hd, gain_rows], axis=1
     )
-    proj_rows, normed_turn, branch_turn, up_share = lax.optimization_barrier(
-        (proj_rows, normed_turn, branch_turn, up_share)
-    )
+    proj_rows, up_share = lax.optimization_barrier((proj_rows, up_share))
     up_both = loop_shares(up_share)
     proj_all, middle_own = share_rows(
-        proj_rows, jnp.concatenate([out_piece, gate_piece, up_piece], axis=0).astype(bf16), 5
+        proj_rows, jnp.concatenate([out_piece.astype(bf16), ffn_pieces[0], ffn_pieces[1]], axis=0), 5
     )
     column = place * width_own
     gain_all = proj_all[:, PROJECT_COLUMNS + 4 * rank :][:, :gain_count].reshape(size, 2, MODEL_WIDTH)

time: 814 us -> 835 us (1.026)
  Pallas kernels: 490 us -> 565 us
  matrix products: 160 us -> 108 us
  waiting for transfers between devices: 50.2 us -> 62.2 us
    dot_general x16 -> x10, matrix products: 83.5 us -> 34.4 us  [outer_product_rows(): lax.dot_general(former, latter, (((0,), (0,)), ((), ())), preferred_eleme...]
    pallas_call x1, Pallas kernels: 101 us -> 139 us  [unit_rows(): pl.pallas_call(functools.partial(unit_kernel, chips), out_shape=(jax.Shap...]
    pallas_call x1, Pallas kernels: 129 us -> 161 us  [share_rows(): pl.pallas_call(functools.partial(share_kernel, size, chunk, own_count), o...]
    all_gather x3, waiting for transfers between devices: 25.7 us -> 56.4 us  [loop_shares(): return lax.all_gather(partial.astype(bf16), 'loop', axis=0)]
    all_to_all x2 -> x1, waiting for transfers between devices: 14.4 us -> 0.01 us  [turn(): lax.all_to_all(block, 'fsdp', split_axis=1, concat_axis=0, tiled=True)]
    dot_general x13, matrix products: 45.9 us -> 37.5 us  [times_transposed(): lax.dot_general(former, latter, (((1,), (1,)), ((), ())), preferred_eleme...]
  transfers between devices with their start and end apart: 7 -> 6, of which waited for: 3 -> 3; matrix products, arithmetic and copies ran while one was open for 20% -> 17% of each run, Pallas kernels for 41% -> 44%
where the time goes in v8:
time: 835 us; the launch traced here: 825 us
  Pallas kernels  565 us (68%)
  matrix products  108 us (13%)
  waiting for transfers between devices  62.2 us (7%)
  other arithmetic  34.7 us (4%)
  local copies, waits for them, and re-layouts  34.3 us (4%)
  between operations  15 us (2%)
    pallas_call x1, Pallas kernels, share_rows(): pl.pallas_call(functools.partial(share_kernel, size, chunk, own_count), o...  161 us
    pallas_call x1, Pallas kernels, unit_rows(): pl.pallas_call(functools.partial(unit_kernel, chips), out_shape=(jax.Shap...  139 us
    pallas_call x1, Pallas kernels, mix_rows(): pl.pallas_call(functools.partial(mix_kernel, chips), out_shape=jax.ShapeD...  128 us
    pallas_call x2, Pallas kernels, ring_gather(): pl.pallas_call(functools.partial(gather_kernel, chips), out_shape=jax.Sha...  93.4 us
    all_gather x3, waiting for transfers between devices, loop_shares(): return lax.all_gather(partial.astype(bf16), 'loop', axis=0)  56.4 us
    dot_general x13, matrix products, times_transposed(): lax.dot_general(former, latter, (((1,), (1,)), ((), ())), preferred_eleme...  37.5 us
    dot_general x10, matrix products, outer_product_rows(): lax.dot_general(former, latter, (((0,), (0,)), ((), ())), preferred_eleme...  34.4 us
    pallas_call x1, Pallas kernels, ring_scatter(): pl.pallas_call(functools.partial(scatter_kernel, chips, count), out_shape...  23.9 us
  transfers between devices with their start and end apart: 6, of which 3 were waited for; matrix products, arithmetic and copies ran while one was open for 17% of the time, Pallas kernels for 44%

profile of v8, /device:TPU:0, one launch (start us, length us, event | category | flops | bytes accessed | tf_op | source)
XLA Modules:
  0.0 824.5 jit_solution(11310308435397528343)
XLA Ops:
  7.2 61.2 %ring_gather.2 = bf16[2048,2560]{1,0:T(8,128)(2,1)} custom-call(bf16[128,2560]{1,0:T(8,128)(2,1)} %x_ref.1), custom_call_target="tpu_custom_call" | custom-call | bytes 3000000 | tf_op jit(solution)/shard_map/ring_gather/pallas_call | solution.py:229
  68.5 2.3 slice.281.refs_4_
  70.8 3.0 slice.280.refs_3_
  75.1 2.7 fusion.61
  77.8 5.6 fusion.126
  86.6 32.3 %ring_gather.3 = bf16[2048,512]{1,0:T(8,128)(2,1)} custom-call(bf16[128,512]{1,0:T(8,128)(2,1)} %pad_maximum_fusion.7.x_ref), custom_call_target="tpu_custom_call" | custom-call | bytes 3000000 | tf_op jit(solution)/shard_map/ring_gather/pallas_call | solution.py:229
  118.9 1.7 convolution_add_fusion.5
  123.4 1.3 fusion.84
  124.7 5.3 fusion.178
  130.0 3.4 copy-done.2
  133.4 2.0 fusion.53
  135.7 1.9 dynamic-slice_bitcast_fusion.refs_7_.refs_4_
  137.5 2.2 dynamic-slice_bitcast_fusion.1
  139.8 1.6 convolution_convert_fusion.8
  141.4 5.6 all-gather.9.cloned.1.call-done
  147.0 6.7 convolution_add_fusion.6
  153.8 1.6 multiply_reduce_fusion.3
  156.4 139.3 %unit_rows.1 = (bf16[2048,2048]{1,0:T(8,128)(2,1)}, bf16[2048,2048]{1,0:T(8,128)(2,1)}, bf16[3,2048,1024]{2,1,0:T(8,128)(2,1)}, bf16[2048,1024]{1,0:T(8,128)(2,1...) custom-call(bf16[128,2304]{1,0:T(8,128)(2,1)} %pad_maximum_fusion.3., ...), custom_call_target="tpu_custom_call" | custom-call | bytes 300000000 | tf_op jit(solution)/shard_map/unit_rows/pallas_call | solution.py:585
  298.4 127.7 %mix_rows.1 = f32[128,4864]{1,0:T(8,128)} custom-call(bf16[3,2048,1024]{2,1,0:T(8,128)(2,1)} %get-tuple-element.37.refs_0_, bf16[3,1024,2048]{2,1,0:T(8,128)(2,1)} %bitcast.155, bf16[256,1024]{1,0:T(8,128)(2,1)} %get-tuple-element.66.refs_5_.refs_2_, bf16[256,1024]{1,0:T(8,128)(2,1)} %get-tuple-element.65.refs_6_.refs_3_, ...), custom_call_target="tpu_custom_call" | custom-call | bytes 3000000 | tf_op jit(solution)/shard_map/mix_rows/pallas_call | solution.py:765
  426.2 1.9 convert.88
  428.1 2.5 convolution_add_fusion.2
  430.6 1.9 multiply_reduce_fusion.1
  434.1 4.3 all-to-all-start
  438.5 1.9 convolution_convert_fusion.7
  440.4 4.8 fusion.170
  445.2 1.7 fusion.41
  447.0 1.5 multiply_reduce_fusion
  448.5 1.6 multiply_convert_fusion
  450.1 2.0 copy-done.6
  452.1 2.4 fusion.25.refs_0_
  454.5 2.7 fusion.26.refs_1_
  457.2 23.9 %ring_scatter.1 = f32[128,512]{1,0:T(8,128)} custom-call(bf16[2048,256]{1,0:T(8,128)(2,1)} %fusion.25.refs_0_, bf16[2048,256]{1,0:T(8,128)(2,1)} %fusion.26.refs_1_), custom_call_target="tpu_custom_call" | custom-call | bytes 3000000 | tf_op jit(solution)/shard_map/ring_scatter/pallas_call | solution.py:344
  481.1 2.1 fusion.175
  483.1 11.6 %all-gather.13.cloned.1.call-done = bf16[4,1024,2048]{2,1,0:T(8,128)(2,1)} async-done(((bf16[2,1024,2048]{2,1,0:T(8,128)(2,1)}), bf16[4,1024,2048]{2,1,0:T(8,128)(2,1)}) %all-gather.13.cloned.1.call-update) | async-done | bytes 16777232 | tf_op jit(solution)/shard_map/all_gather | solution.py:97
  494.9 3.9 convolution_multiply_fusion
  499.9 1.7 convolution_convert_fusion.6
  504.4 1.8 convolution_convert_fusion.9
  506.3 4.4 fusion.108
  510.7 3.4 fusion.74
  514.8 1.6 slice_dynamic-update-slice_fusion
  516.4 1.5 slice_dynamic-update-slice_fusion.1
  518.6 2.7 fusion.42
  521.3 1.3 slice_bitcast_fusion.1
  522.6 1.6 convolution_convert_fusion.5
  525.3 161.0 %share_rows.1 = (bf16[2048,3712]{1,0:T(8,128)(2,1)}, bf16[2464,256]{1,0:T(8,128)(2,1)}) custom-call(bf16[128,3712]{1,0:T(8,128)(2,1)} %pad_dynamic-update-slice_fusion.x_ref, bf16[2176,256]{1,0:T(8,128)(2,1)} %pad_maximum_fusion.mid_ref), custom_call_target="tpu_custom_call" | custom-call | bytes 3000000 | tf_op jit(solution)/shard_map/share_rows/pallas_call | solution.py:902
  688.0 2.5 fusion.71
  690.6 5.7 fusion.11
  696.3 8.2 %fusion.179 = bf16[128,2816]{1,0:T(8,128)(2,1)S(1)} fusion(bf16[2048,128]{1,0:T(8,128)(2,1)S(1)} %get-tuple-element.43, bf16[2048,2816]{0,1:T(8,128)(2,1)} %all-gather.11.cloned.1.call-done), kind=kOutput, calls=%fused_computation.266 | convolution fusion | flops 1476395008 | bytes 12779520 | tf_op jit(solution)/shard_map/dot_general | solution.py:36
  705.7 44.8 %all-gather.15.cloned.1.call-done = bf16[2048,2048]{1,0:T(8,128)(2,1)} async-done(((bf16[1024,2048]{1,0:T(8,128)(2,1)}), bf16[2048,2048]{1,0:T(8,128)(2,1)}) %all-gather.15.cloned.1.call-update) | async-done | bytes 8388624 | tf_op jit(solution)/shard_map/all_gather | solution.py:97
  750.6 1.7 convolution_convert_fusion
  752.3 1.7 convolution_convert_fusion.1
  754.0 7.0 fusion.27
  761.0 2.2 fusion.43
  763.3 3.4 copy-done
  766.7 20.1 %sum_loops.1 = f32[3,1024,2048]{2,1,0:T(8,128)} custom-call(bf16[2,2,1024,2048]{3,2,1,0:T(8,128)(2,1)} %bitcast.157, bf16[2,1024,2048]{2,1,0:T(8,128)(2,1)S(1)} %bitcast.151), custom_call_target="tpu_custom_call" | custom-call | bytes 51000000 | tf_op jit(solution)/shard_map/sum_loops/pallas_call | solution.py:118
  786.8 1.2 fusion.14
  788.0 1.8 fusion.89
  790.7 2.0 convolution_convert_fusion.3
  792.8 2.0 convolution_convert_fusion.4
  794.9 5.9 convolution_convert_fusion.2
  800.8 3.7 fusion.30
  804.5 7.5 convert_bitcast_fusion
  812.0 2.0 convert_add_fusion
  814.0 1.2 slice.299
  (157 shorter events, 25.9 us)
Async XLA Ops:
  7.2 66.7 %copy-start.27 = (s32[1,4]{1,0:T(1,128)S(1)}, s32[1,4]{1,0:T(1,128)}, u32[]{:S(2)}) copy-start(s32[1,4]{1,0:T(1,128)} %param.11) | copy-start | bytes 52
  7.2 67.1 %copy-start.1 = (bf16[1,128,2048]{2,1,0:T(8,128)(2,1)S(1)}, bf16[1,128,2048]{2,1,0:T(8,128)(2,1)}, u32[]{:S(2)}) copy-start(bf16[1,128,2048]{2,1,0:T(8,128)(2,1)} %param.10) | copy-start | bytes 1572868
  7.2 139.8 %all-gather.9.cloned.1.call-start = ((), (), s32[]{:S(2)}) async-start(), calls=%async_computation.1 | async-start | bytes 8912896 | tf_op jit(solution)/shard_map/all_gather | solution.py:89
  68.4 6.6 copy-start.22
  68.4 426.3 %all-gather.13.cloned.1.call-start = ((), (), s32[]{:S(2)}) async-start(), calls=%async_computation.3 | async-start | bytes 25165824 | tf_op jit(solution)/shard_map/all_gather | solution.py:97
  74.1 46.8 %copy-start.23 = (f32[128]{0:T(128)}, f32[128]{0:T(128)S(1)}, u32[]{:S(2)}) copy-start(f32[128]{0:T(128)S(1)} %multiply_exponential_fusion) | copy-start | bytes 1540
  77.8 41.1 %copy-start.16 = (bf16[128,768]{1,0:T(8,128)(2,1)}, bf16[128,768]{1,0:T(8,128)(2,1)S(1)}, u32[]{:S(2)}) copy-start(bf16[128,768]{1,0:T(8,128)(2,1)S(1)} %fusion.61) | copy-start | bytes 589828
  118.9 4.5 copy-start.3
  121.9 1.4 copy-start.18
  122.2 1.2 copy-start.11
  122.2 1.2 copy-start.13
  124.7 8.7 %copy-start.4 = (bf16[2048,512]{1,0:T(8,128)(2,1)S(1)}, bf16[2048,512]{1,0:T(8,128)(2,1)}, u32[]{:S(2)}) copy-start(bf16[2048,512]{1,0:T(8,128)(2,1)} %ring_gather.3) | copy-start | bytes 6291460
  130.0 3.4 copy-start.2
  295.7 0.9 copy-start.17
  426.2 6.3 copy-start.8
  428.1 4.9 copy-start.7
  434.1 46.9 %all-to-all-start = ((bf16[128,16,256]{2,0,1:T(8,128)(2,1)}), bf16[128,16,256]{2,0,1:T(8,128)(2,1)}, u32[]{:S(2)}, u32[]{:S(2)}) async-start(bf16[128,16,256]{2,0,1:T(8,128)(2,1)} %pad_maximum_fusion.1), calls=%async_computation | async-start | bytes 2097152 | tf_op jit(solution)/shard_map/all_to_all | solution.py:140
  438.5 257.8 %all-gather.11.cloned.1.call-start = ((), (), s32[]{:S(2)}) async-start(), calls=%async_computation.2 | async-start | bytes 12255232 | tf_op jit(solution)/shard_map/all_gather | solution.py:89
  438.5 8.4 %slice-start.3 = ((s8[8388608]{0:T(1024)(128)(4,1)}), s8[4194304]{0:T(1024)(128)(4,1)S(1)}, s32[]{:S(2)}) async-start(s8[8388608]{0:T(1024)(128)(4,1)} %bitcast.158), calls=%async_computation.9 | async-start | bytes 8388608
  440.4 6.5 slice-start.4
  440.4 6.5 copy-start.5
  440.4 6.5 copy-start.25
  448.5 3.6 copy-start.12
  448.5 3.6 copy-start.14
  450.1 2.0 copy-start.6
  494.8 4.0 copy-start.19
  494.8 4.0 copy-start.21
  494.8 255.8 %all-gather.15.cloned.1.call-start = ((), (), s32[]{:S(2)}) async-start(), calls=%async_computation.4 | async-start | bytes 12582912 | tf_op jit(solution)/shard_map/all_gather | solution.py:97
  494.8 11.4 %slice-start = ((s8[10485760]{0:T(1024)(128)(4,1)}), s8[4194304]{0:T(1024)(128)(4,1)S(1)}, s32[]{:S(2)}) async-start(s8[10485760]{0:T(1024)(128)(4,1)} %bitcast.152), calls=%async_computation.6 | async-start | bytes 8388608
  494.8 11.4 %slice-start.1 = ((s8[10485760]{0:T(1024)(128)(4,1)}), s8[4194304]{0:T(1024)(128)(4,1)S(1)}, s32[]{:S(2)}) async-start(s8[10485760]{0:T(1024)(128)(4,1)} %bitcast.152), calls=%async_computation.7 | async-start | bytes 8388608
  498.8 2.9 copy-start.15
  498.8 2.9 copy-start.24
  498.8 7.4 slice-start.2
  503.8 6.9 slice-start.5
  506.2 4.4 slice-start.6
  518.5 293.5 %all-gather.17.cloned.1.call-start = ((), (), s32[]{:S(2)}) async-start(), calls=%async_computation.5 | async-start | bytes 3637248 | tf_op jit(solution)/shard_map/all_gather | solution.py:97
  521.3 166.7 %copy-start.26 = (f32[128]{0:T(128)S(1)}, f32[128]{0:T(128)}, u32[]{:S(2)}) copy-start(f32[128]{0:T(128)} %get-tuple-element.86) | copy-start | bytes 1540
  763.3 3.4 copy-start
  766.7 20.1 %copy-start.20 = (bf16[2048,128]{1,0:T(8,128)(2,1)S(1)}, bf16[2048,128]{1,0:T(8,128)(2,1)}, u32[]{:S(2)}) copy-start(bf16[2048,128]{1,0:T(8,128)(2,1)} %get-tuple-element.40) | copy-start | bytes 1572868
  766.7 20.1 %copy-start.28 = (bf16[2048,256]{0,1:T(8,128)(2,1)S(1)}, bf16[2048,256]{0,1:T(8,128)(2,1)}, u32[]{:S(2)}) copy-start(bf16[2048,256]{0,1:T(8,128)(2,1)} %fusion.27) | copy-start | bytes 3145732
  766.7 28.1 %slice-start.7 = ((s8[15204352]{0:T(1024)(128)(4,1)}), s8[2621440]{0:T(1024)(128)(4,1)S(1)}, s32[]{:S(2)}) async-start(s8[15204352]{0:T(1024)(128)(4,1)} %bitcast.193), calls=%async_computation.13 | async-start | bytes 5242880
  766.7 28.1 %slice-start.8 = ((s8[15204352]{0:T(1024)(128)(4,1)}), s8[4194304]{0:T(1024)(128)(4,1)S(1)}, s32[]{:S(2)}) async-start(s8[15204352]{0:T(1024)(128)(4,1)} %bitcast.193), calls=%async_computation.14 | async-start | bytes 8388608
  766.7 28.2 %slice-start.9 = ((s8[15204352]{0:T(1024)(128)(4,1)}), s8[4194304]{0:T(1024)(128)(4,1)S(1)}, s32[]{:S(2)}) async-start(s8[15204352]{0:T(1024)(128)(4,1)} %bitcast.193), calls=%async_computation.15 | async-start | bytes 8388608
  786.8 8.0 slice-start.10
  800.8 3.7 copy-start.9
  812.0 4.8 copy-start.10
Sparse Core Ops, SparseCore 0:
  68.6 78.3 all-gather.8
  295.9 198.8 all-gather.12
  497.5 141.4 all-gather.10
  640.3 110.2 all-gather.14
  763.4 36.8 all-gather.16

commit v9 on v8

--- a/solution.py
+++ b/solution.py
@@ -99,41 +99,6 @@
 
 def both_loops(shares):
     return shares[0].astype(f32) + shares[1].astype(f32)
-
-
-def sum_kernel(early_ref, up_ref, o_ref):
-    @pl.when(pl.program_id(0) != 1)
-    def _():
-        o_ref[0] = early_ref[0, 0].astype(f32) + early_ref[1, 0].astype(f32)
-
-    @pl.when(pl.program_id(0) == 1)
-    def _():
-        o_ref[0] = up_ref[0].astype(f32) + up_ref[1].astype(f32)
-
-
-def sum_loops(early, up):
-    _, rows, columns = up.shape
-    tile = min(rows, 256)
-    steps = rows // tile
-    return pl.pallas_call(
-        sum_kernel,
-        grid=(3, steps),
-        out_shape=jax.ShapeDtypeStruct((3, rows, columns), f32),
-        in_specs=[
-            pl.BlockSpec(
-                (2, 1, tile, columns),
-                lambda i, j: (0, i // 2, jnp.where(i == 1, steps - 1, j), 0),
-            ),
-            pl.BlockSpec(
-                (2, tile, columns),
-                lambda i, j: (0, jnp.where(i == 1, j, jnp.where(i < 1, 0, steps - 1)), 0),
-            ),
-        ],
-        out_specs=pl.BlockSpec((1, tile, columns), lambda i, j: (i, j, 0)),
-        compiler_params=pltpu.CompilerParams(vmem_limit_bytes=32 << 20),
-        cost_estimate=busy(17),
-        name="sum_loops",
-    )(early, up)
 
 
 def turn(block):
@@ -363,10 +328,11 @@
 
 
 def unit_kernel(chips, *refs):
-    sources, (planes, squeeze, widen_down, widen_gate, widen_up, narrow) = refs[:2], refs[2:8]
-    two_all, grad_all, acts_all, low_all, early_out, up_out, piece_out, down_out = refs[8:16]
-    held, turned, acts, low, tiles, landed = refs[16], refs[17], refs[18], refs[19], refs[20], refs[21:23]
-    held_sem, own_sem, ring_send, ring_recv, side_send, side_recv, out_sem, acts_sem, tile_sem = refs[23:]
+    sources, (planes, squeeze, widen_down, widen_gate, widen_up, narrow) = refs[:3], refs[3:9]
+    two_all, grad_all, later_all, acts_all, low_all, share_out, piece_out, down_out = refs[9:17]
+    held, turned, acts, low, tiles = refs[17:22]
+    landed = (refs[22], refs[23], later_all)
+    held_sem, own_sem, ring_send, ring_recv, side_send, side_recv, out_sem, acts_sem, tile_sem = refs[24:]
     core, device = ring_neighbours(chips)
     rows = sources[0].shape[0]
     reach = chips // 2
@@ -481,7 +447,7 @@
             hop(i, way, 1).start()
         across(i, 0, 0, core).start()
     keeps = [
-        pltpu.make_async_copy(sources[i], at(i, 0, 0, core, (0, rows)), own_sem.at[i]) for i in (0, 1)
+        pltpu.make_async_copy(sources[i], at(i, 0, 0, core, (0, rows)), own_sem.at[i]) for i in range(3)
     ]
     for keep in keeps:
         keep.start()
@@ -497,7 +463,11 @@
                 if hops < reach:
                     hop(i, way, hops + 1).start()
                 across(i, way, hops, core).start()
-        if hops < reach:
+        if hops == reach:
+            for way in (0, 1):
+                hop(2, way, 1).start()
+            across(2, 0, 0, core).start()
+        else:
             for way in (0, 1):
                 for i in (0, 1):
                     across(i, way, hops, 1 - core).wait_recv()
@@ -507,11 +477,21 @@
             across(i, way, reach, 1 - core).wait_recv()
     work(2 * reach - 1, first_row(reach))
     rank = ADAPTER_RANK
-    for kind, out in ((0, early_out.at[0]), (2, early_out.at[1]), (1, up_out)):
-
-        def tile_copy(t, out=out):
+
+    def relay(hops):
+        for way in (0, 1):
+            arriving(2, way, hops).wait_recv()
+            if hops < reach:
+                hop(2, way, hops + 1).start()
+            across(2, way, hops, core).start()
+
+    for kind in range(3):
+
+        def tile_copy(t, kind=kind):
             there = pl.ds(pl.multiple_of(t * wide, wide), wide)
-            return pltpu.make_async_copy(tiles.at[t % 2], out.at[:, there], tile_sem.at[t % 2])
+            return pltpu.make_async_copy(
+                tiles.at[t % 2], share_out.at[kind, :, there], tile_sem.at[t % 2]
+            )
 
         @pl.loop(0, MODEL_WIDTH // wide)
         def _(t, kind=kind, tile_copy=tile_copy):
@@ -525,13 +505,20 @@
             ).astype(bf16)
             tile_copy(t).start()
 
+        relay(kind + 1)
         if kind == 2:
             piece_out[0] = matrix_product(turned[0], low[:, :rank]).astype(bf16)
             piece_out[1] = matrix_product(turned[1], low[:, rank : 2 * rank]).astype(bf16)
             down_out[...] = matrix_product(turned[2], low[:, 2 * rank :])
         tile_copy(MODEL_WIDTH // wide - 2).wait()
         tile_copy(MODEL_WIDTH // wide - 1).wait()
-    for i in (0, 1):
+    for hops in range(4, reach + 1):
+        relay(hops)
+    across(2, 0, 0, 1 - core).wait_recv()
+    for hops in range(1, reach + 1):
+        for way in (0, 1):
+            across(2, way, hops, 1 - core).wait_recv()
+    for i in range(3):
         across(i, 0, 0, core).wait_send()
         for hops in range(1, reach + 1):
             for way in (0, 1):
@@ -551,7 +538,7 @@
                 copy.wait()
 
 
-def unit_rows(two, grad, planes, squeeze, widen_down, widen_gate, widen_up, narrow, ident):
+def unit_rows(two, grad, later, planes, squeeze, widen_down, widen_gate, widen_up, narrow, ident):
     size = lax.axis_size("fsdp")
     rank = ADAPTER_RANK
     if size != 16:
@@ -567,10 +554,16 @@
         return (
             two,
             grad,
+            gather_rows(later),
             jnp.stack([gate_grad, up_grad, units]),
             jnp.concatenate([low, pulled, lora_out], axis=1),
-            jnp.stack([outer_product_rows(gate_grad, two), outer_product_rows(units, grad)]).astype(bf16),
-            outer_product_rows(up_grad, two).astype(bf16),
+            jnp.stack(
+                [
+                    outer_product_rows(gate_grad, two),
+                    outer_product_rows(up_grad, two),
+                    outer_product_rows(units, grad),
+                ]
+            ).astype(bf16),
             jnp.stack(
                 [outer_product_rows(gate_grad, low[:, :rank]), outer_product_rows(up_grad, low[:, rank:])]
             ).astype(bf16),
@@ -580,21 +573,21 @@
     rows, columns = grad.shape
     all_rows, hidden = size * rows, planes.shape[1]
     anywhere, inside = pl.BlockSpec(memory_space=pl.ANY), pl.BlockSpec(memory_space=pltpu.VMEM)
-    pair = pltpu.SemaphoreType.DMA((2, 2, chips // 2))
-    sides = pltpu.SemaphoreType.DMA((2, 2, chips // 2 + 1))
+    pair = pltpu.SemaphoreType.DMA((3, 2, chips // 2))
+    sides = pltpu.SemaphoreType.DMA((3, 2, chips // 2 + 1))
     return pl.pallas_call(
         functools.partial(unit_kernel, chips),
         out_shape=(
             jax.ShapeDtypeStruct((all_rows, columns), bf16),
             jax.ShapeDtypeStruct((all_rows, columns), bf16),
+            jax.ShapeDtypeStruct((all_rows, later.shape[1]), bf16),
             jax.ShapeDtypeStruct((3, all_rows, hidden), bf16),
             jax.ShapeDtypeStruct((all_rows, 4 * rank), bf16),
-            jax.ShapeDtypeStruct((2, hidden, columns), bf16),
-            jax.ShapeDtypeStruct((hidden, columns), bf16),
+            jax.ShapeDtypeStruct((3, hidden, columns), bf16),
             jax.ShapeDtypeStruct((2, hidden, rank), bf16),
             jax.ShapeDtypeStruct((hidden, rank), f32),
         ),
-        in_specs=[anywhere] * 3 + [inside] * 5,
+        in_specs=[anywhere] * 4 + [inside] * 5,
         out_specs=(anywhere,) * 6 + (inside,) * 2,
         scratch_shapes=[
             pltpu.VMEM(planes.shape, bf16),
@@ -605,7 +598,7 @@
             pltpu.VMEM((all_rows, two.shape[1]), bf16),
             pltpu.VMEM((all_rows, columns), bf16),
             pltpu.SemaphoreType.DMA((3,)),
-            pltpu.SemaphoreType.DMA((2,)),
+            pltpu.SemaphoreType.DMA((3,)),
             pair,
             pair,
             sides,
@@ -619,7 +612,7 @@
         ),
         cost_estimate=busy(100),
         name="unit_rows",
-    )(two, grad, planes, squeeze, widen_down, widen_gate, widen_up, narrow)
+    )(two, grad, later, planes, squeeze, widen_down, widen_gate, widen_up, narrow)
 
 
 def mix_kernel(chips, *refs):
@@ -1015,9 +1008,10 @@
     normed_two = (middle * scale_two * gains[1]).astype(bf16)
 
     weight_planes = feedforward_weight.transpose(1, 0, 2)
-    two_all, grad_all, acts, low_ffn, early_shares, up_share, ffn_pieces, down_own = unit_rows(
+    two_all, grad_all, attended_all, acts, low_ffn, ffn_shares, ffn_pieces, down_own = unit_rows(
         jnp.concatenate([normed_two, lora_out], axis=1),
         output_gradient[0],
+        jnp.concatenate([attended, lora_qkv], axis=1),
         weight_planes,
         first_factor[:, 4 * rank :],
         widen_down,
@@ -1027,8 +1021,7 @@
         2,
     )
     lora_out_all = low_ffn[:, 3 * rank :]
-    early_shares, acts = lax.optimization_barrier((early_shares, acts))
-    early_both = loop_shares(early_shares)
+    ffn_both = loop_shares(ffn_shares)
     rows_sum = mix_rows(
         acts, weight_planes, widen_gate, widen_up, narrow_down, 3
     )
@@ -1071,10 +1064,7 @@
     )
     value_part = jnp.einsum("thu,thd->ud", probs_low, heads_grad, preferred_element_type=f32)
     pair_grad = ring_scatter([key_part, value_part], 4)
-    attended_rows, early_both, pair_grad, normed_turn, branch_turn = lax.optimization_barrier(
-        (jnp.concatenate([attended, lora_qkv], axis=1), early_both, pair_grad, normed_turn, branch_turn)
-    )
-    attended_all = gather_rows(attended_rows)
+    pair_grad, normed_turn, branch_turn = lax.optimization_barrier((pair_grad, normed_turn, branch_turn))
     query_grad = rotate(
         query_rot_grad.reshape(tokens_dev, QUERY_WIDTH), position_own, -1.0
     ).astype(bf16)
@@ -1110,8 +1100,6 @@
     proj_rows = jnp.concatenate(
         [proj_grad, lora_out_grad, gate_low, up_low, lora_hd, gain_rows], axis=1
     )
-    proj_rows, up_share = lax.optimization_barrier((proj_rows, up_share))
-    up_both = loop_shares(up_share)
     proj_all, middle_own = share_rows(
         proj_rows, jnp.concatenate([out_piece.astype(bf16), ffn_pieces[0], ffn_pieces[1]], axis=0), 5
     )
@@ -1128,7 +1116,7 @@
         ],
         axis=1,
     ).astype(bf16)
-    attn_part, up_both, proj_all = lax.optimization_barrier((attn_part, up_both, proj_all))
+    attn_part, ffn_both, proj_all = lax.optimization_barrier((attn_part, ffn_both, proj_all))
     attn_sum = both_loops(loop_shares(attn_part))
     gain_column = PROJECT_COLUMNS + QUERY_WIDTH
     gain_sum = attn_sum[:2, gain_column : gain_column + width_own]
@@ -1178,7 +1166,7 @@
     expand_own = jnp.where(
         owned < PROJECT_COLUMNS, near, jnp.where(owned < far_start, middle_own, far)
     ).T.astype(f32)
-    ffn_sum = sum_loops(early_both, up_both).transpose(1, 0, 2)
+    ffn_sum = both_loops(ffn_both).transpose(1, 0, 2)
     return (
         hidden_out[None],
         input_grad[None],

time: 835 us -> 749 us (0.90)
  waiting for transfers between devices: 62.2 us -> 15.9 us
  Pallas kernels: 565 us -> 519 us
  other arithmetic: 34.7 us -> 51.9 us
  local copies, waits for them, and re-layouts: 34.3 us -> 23.9 us
    pallas_call x1, Pallas kernels: 161 us -> 109 us  [share_rows(): pl.pallas_call(functools.partial(share_kernel, size, chunk, own_count), o...]
    all_gather x3 -> x2, waiting for transfers between devices: 56.4 us -> 6.43 us  [loop_shares(): return lax.all_gather(partial.astype(bf16), 'loop', axis=0)]
    pallas_call x1, Pallas kernels: 139 us -> 164 us  [unit_rows(): pl.pallas_call(functools.partial(unit_kernel, chips), out_shape=(jax.Shap...]
    pallas_call x1 -> x0, Pallas kernels: 20.1 us -> none  [sum_loops(): pl.pallas_call(sum_kernel, grid=(3, steps), out_shape=jax.ShapeDtypeStruc...]
    transpose x0 -> x1, other arithmetic: none -> 18.5 us  [per_device(): ffn_sum = both_loops(ffn_both).transpose(1, 0, 2)]
    unnamed x88 -> x92, local copies, waits for them, and re-layouts: 16.5 us -> 6.87 us
  transfers between devices with their start and end apart: 6 -> 4, of which waited for: 3 -> 2; matrix products, arithmetic and copies ran while one was open for 17% -> 19% of each run, Pallas kernels for 44% -> 40%
where the time goes in v9:
time: 749 us; the launch traced here: 739 us
  Pallas kernels  519 us (69%)
  matrix products  109 us (15%)
  other arithmetic  51.9 us (7%)
  local copies, waits for them, and re-layouts  23.9 us (3%)
  waiting for transfers between devices  15.9 us (2%)
  between operations  14.9 us (2%)
    pallas_call x1, Pallas kernels, unit_rows(): pl.pallas_call(functools.partial(unit_kernel, chips), out_shape=(jax.Shap...  164 us
    pallas_call x1, Pallas kernels, mix_rows(): pl.pallas_call(functools.partial(mix_kernel, chips), out_shape=jax.ShapeD...  128 us
    pallas_call x1, Pallas kernels, share_rows(): pl.pallas_call(functools.partial(share_kernel, size, chunk, own_count), o...  109 us
    pallas_call x2, Pallas kernels, ring_gather(): pl.pallas_call(functools.partial(gather_kernel, chips), out_shape=jax.Sha...  93.5 us
    dot_general x13, matrix products, times_transposed(): lax.dot_general(former, latter, (((1,), (1,)), ((), ())), preferred_eleme...  37.5 us
    dot_general x10, matrix products, outer_product_rows(): lax.dot_general(former, latter, (((0,), (0,)), ((), ())), preferred_eleme...  36.2 us
    pallas_call x1, Pallas kernels, ring_scatter(): pl.pallas_call(functools.partial(scatter_kernel, chips, count), out_shape...  24 us
    dot_general x9, matrix products, matrix_product(): return jnp.dot(former, latter, preferred_element_type=f32)  22.7 us
  transfers between devices with their start and end apart: 4, of which 2 were waited for; matrix products, arithmetic and copies ran while one was open for 19% of the time, Pallas kernels for 40%

profile of v9, /device:TPU:0, one launch (start us, length us, event | category | flops | bytes accessed | tf_op | source)
XLA Modules:
  0.0 738.6 jit_solution(8621540019610233701)
XLA Ops:
  7.2 61.2 %ring_gather.2 = bf16[2048,2560]{1,0:T(8,128)(2,1)} custom-call(bf16[128,2560]{1,0:T(8,128)(2,1)} %x_ref.1), custom_call_target="tpu_custom_call" | custom-call | bytes 3000000 | tf_op jit(solution)/shard_map/ring_gather/pallas_call | solution.py:194
  68.5 2.3 slice.289.refs_5_
  70.8 3.0 slice.288.refs_4_
  75.1 2.7 fusion.64
  77.8 5.6 fusion.129
  86.5 32.4 %ring_gather.3 = bf16[2048,512]{1,0:T(8,128)(2,1)} custom-call(bf16[128,512]{1,0:T(8,128)(2,1)} %pad_maximum_fusion.7.x_ref), custom_call_target="tpu_custom_call" | custom-call | bytes 3000000 | tf_op jit(solution)/shard_map/ring_gather/pallas_call | solution.py:194
  118.9 1.7 convolution_add_fusion.5
  122.6 1.3 fusion.84
  123.9 3.5 fusion.181
  127.5 3.4 fusion.60
  130.9 1.9 dynamic-slice_bitcast_fusion.refs_8_.refs_4_
  132.8 2.3 dynamic-slice_bitcast_fusion.1
  135.1 1.5 convolution_convert_fusion.8
  137.5 9.5 %all-gather.6.cloned.1.call-done = bf16[2048,2048]{1,0:T(8,128)(2,1)} async-done(((bf16[128,2048]{1,0:T(8,128)(2,1)}), bf16[2048,2048]{1,0:T(8,128)(2,1)}) %all-gather.6.cloned.1.call-update) | async-done | bytes 8388624 | tf_op jit(solution)/shard_map/all_gather | solution.py:89
  147.0 6.7 convolution_add_fusion.6
  153.7 1.6 multiply_reduce_fusion.3
  156.4 163.8 %unit_rows.1 = (bf16[2048,2048]{1,0:T(8,128)(2,1)}, bf16[2048,2048]{1,0:T(8,128)(2,1)}, bf16[2048,2816]{1,0:T(8,128)(2,1)}, bf16[3,2048,1024]{2,1,0:T(8,128)(2,1...) custom-call(bf16[128,2304]{1,0:T(8,128)(2,1)} %pad_maximum_fusion.3., ...), custom_call_target="tpu_custom_call" | custom-call | bytes 300000000 | tf_op jit(solution)/shard_map/unit_rows/pallas_call | solution.py:578
  321.5 128.4 %mix_rows.1 = f32[128,4864]{1,0:T(8,128)} custom-call(bf16[3,2048,1024]{2,1,0:T(8,128)(2,1)} %get-tuple-element.29.refs_0_, bf16[3,1024,2048]{2,1,0:T(8,128)(2,1)} %bitcast.156, bf16[256,1024]{1,0:T(8,128)(2,1)} %get-tuple-element.54.refs_6_.refs_2_, bf16[256,1024]{1,0:T(8,128)(2,1)} %get-tuple-element.53.refs_7_.refs_3_, ...), custom_call_target="tpu_custom_call" | custom-call | bytes 3000000 | tf_op jit(solution)/shard_map/mix_rows/pallas_call | solution.py:758
  449.9 1.9 convert.88
  451.9 2.5 convolution_add_fusion.2
  454.3 2.4 multiply_reduce_fusion.1
  457.3 1.1 pad_maximum_fusion.1
  458.4 4.3 all-to-all-start
  462.9 1.9 convolution_convert_fusion.7
  464.8 4.8 fusion.173
  469.5 1.7 fusion.41
  471.3 1.5 multiply_reduce_fusion
  472.8 1.6 multiply_convert_fusion
  474.4 1.3 convolution_multiply_fusion
  476.0 2.4 fusion.25.refs_0_
  478.4 2.7 fusion.26.refs_1_
  481.1 24.0 %ring_scatter.1 = f32[128,512]{1,0:T(8,128)} custom-call(bf16[2048,256]{1,0:T(8,128)(2,1)} %fusion.25.refs_0_, bf16[2048,256]{1,0:T(8,128)(2,1)} %fusion.26.refs_1_), custom_call_target="tpu_custom_call" | custom-call | bytes 3000000 | tf_op jit(solution)/shard_map/ring_scatter/pallas_call | solution.py:309
  505.9 2.7 fusion.42
  509.5 2.3 convolution_convert_fusion.6
  511.8 2.1 fusion.178
  515.6 1.1 convolution_convert_fusion.10
  517.4 1.4 convolution_convert_fusion.9
  518.8 7.6 %fusion.111 = f32[128,2048]{1,0:T(8,128)S(1)} fusion(bf16[2048,2560]{1,0:T(8,128)(2,1)} %ring_gather.2, bf16[128,256]{1,0:T(8,128)(2,1)S(1)} %get-tuple-element.50, bf16[128,256]{1,0:T(8,128)(2,1)S(1)} %maximum_bitcast_fusion.3, bf16[128,2048]{1,0:T(8,128)(2,1)S(1)} %bitcast.162), kind=kOutput, calls=%fused_computation.148 | convolution fusion | flops 1344143360 | bytes 12189696 | tf_op jit(solution)/shard_map/dot_general | solution.py:32
  526.5 2.2 fusion.77
  528.8 6.0 fusion.182
  535.6 1.6 slice_dynamic-update-slice_fusion
  537.1 1.5 slice_dynamic-update-slice_fusion.1
  539.2 1.6 convolution_convert_fusion.5
  541.9 108.9 %share_rows.1 = (bf16[2048,3712]{1,0:T(8,128)(2,1)}, bf16[2464,256]{1,0:T(8,128)(2,1)}) custom-call(bf16[128,3712]{1,0:T(8,128)(2,1)} %pad_dynamic-update-slice_fusion.x_ref, bf16[2176,256]{1,0:T(8,128)(2,1)} %pad_maximum_fusion.mid_ref), custom_call_target="tpu_custom_call" | custom-call | bytes 3000000 | tf_op jit(solution)/shard_map/share_rows/pallas_call | solution.py:895
  650.8 1.1 slice_convert_fusion.1
  652.6 2.5 fusion.74
  655.1 5.7 fusion.11
  660.8 1.1 fusion.63
  661.9 2.7 convolution_convert_fusion.3
  664.6 2.8 convolution_convert_fusion.4
  667.5 7.3 fusion.30
  674.8 1.5 convolution_convert_fusion
  676.3 1.4 convolution_convert_fusion.1
  677.7 4.8 fusion.27
  682.5 3.6 convolution_convert_fusion.2
  686.0 1.6 fusion.92
  687.7 2.2 fusion.43
  690.0 2.7 fusion.14
  693.7 7.5 %convert_bitcast_fusion = f32[1,256,2464]{1,2,0:T(8,128)} fusion(bf16[2464,256]{1,0:T(8,128)(2,1)S(1)} %copy-done.7, s32[]{:T(128)S(6)} %max.3, bf16[2048,256]{1,0:T(8,128)(2,1)S(1)} %copy-done.14, s32[]{:T(128)S(6)} %select_n.49, bf16[2048,256]{1,0:T(8,128)(2,1)S(1)} %copy-done.13, bf16[256,256]{1,0:T(8,128)(2,1)S(1)} %copy-done.18, ...), kind=kLoop, calls=%fused_computation.45 | loop fusion | flops 8830976 | bytes 6150464 | tf_op jit(solution)/shard_map/broadcast_in_dim | solution.py:1178
  701.2 18.5 %add_bitcast_fusion = f32[1024,3,2048]{2,0,1:T(8,128)} fusion(bf16[2,3,1024,2048]{3,2,1,0:T(8,128)(2,1)} %bitcast.157), kind=kLoop, calls=%fused_computation.1 | loop fusion | flops 18874368 | bytes 50331648 | tf_op jit(solution)/shard_map/transpose | solution.py:1169
  719.7 6.4 all-gather.10.cloned.1.call-done
  726.2 1.9 convert_add_fusion
  728.0 1.2 slice.307
  729.2 1.1 slice.308
  (154 shorter events, 20.4 us)
Async XLA Ops:
  7.2 66.7 %copy-start.30 = (s32[1,4]{1,0:T(1,128)S(1)}, s32[1,4]{1,0:T(1,128)}, u32[]{:S(2)}) copy-start(s32[1,4]{1,0:T(1,128)} %param.11) | copy-start | bytes 52
  7.2 67.1 %copy-start = (bf16[1,128,2048]{2,1,0:T(8,128)(2,1)S(1)}, bf16[1,128,2048]{2,1,0:T(8,128)(2,1)}, u32[]{:S(2)}) copy-start(bf16[1,128,2048]{2,1,0:T(8,128)(2,1)} %param.10) | copy-start | bytes 1572868
  7.2 139.8 %all-gather.6.cloned.1.call-start = ((), (), s32[]{:S(2)}) async-start(), calls=%async_computation.1 | async-start | bytes 8912896 | tf_op jit(solution)/shard_map/all_gather | solution.py:89
  68.4 6.6 copy-start.19
  68.4 593.5 %all-gather.8.cloned.1.call-start = ((), (), s32[]{:S(2)}) async-start(), calls=%async_computation.2 | async-start | bytes 37748736 | tf_op jit(solution)/shard_map/all_gather | solution.py:97
  74.1 46.8 %copy-start.26 = (f32[128]{0:T(128)}, f32[128]{0:T(128)S(1)}, u32[]{:S(2)}) copy-start(f32[128]{0:T(128)S(1)} %multiply_exponential_fusion) | copy-start | bytes 1540
  74.3 46.6 %copy-start.25 = (f32[128]{0:T(128)}, f32[128]{0:T(128)S(1)}, u32[]{:S(2)}) copy-start(f32[128]{0:T(128)S(1)} %fusion.165) | copy-start | bytes 1540
  75.0 246.1 %copy-start.23 = (f32[128]{0:T(128)}, f32[128]{0:T(128)S(1)}, u32[]{:S(2)}) copy-start(f32[128]{0:T(128)S(1)} %get-tuple-element.75) | copy-start | bytes 1540
  118.9 3.8 copy-start.2
  122.2 5.3 copy-start.10
  127.5 3.4 copy-start.1
  127.5 345.3 %copy-start.27 = (f32[128,8]{0,1:T(8,128)}, f32[128,8]{0,1:T(8,128)S(1)}, u32[]{:S(2)}) copy-start(f32[128,8]{0,1:T(8,128)S(1)} %get-tuple-element.78) | copy-start | bytes 12292
  449.9 6.8 copy-start.5
  451.8 5.5 copy-start.4
  458.4 53.4 %all-to-all-start = ((bf16[128,16,256]{2,0,1:T(8,128)(2,1)}), bf16[128,16,256]{2,0,1:T(8,128)(2,1)}, u32[]{:S(2)}, u32[]{:S(2)}) async-start(bf16[128,16,256]{2,0,1:T(8,128)(2,1)} %pad_maximum_fusion.1), calls=%async_computation | async-start | bytes 2097152 | tf_op jit(solution)/shard_map/all_to_all | solution.py:105
  462.8 263.4 %all-gather.10.cloned.1.call-start = ((), (), s32[]{:S(2)}) async-start(), calls=%async_computation.3 | async-start | bytes 3637248 | tf_op jit(solution)/shard_map/all_gather | solution.py:97
  462.9 8.4 %slice-start = ((s8[8388608]{0:T(1024)(128)(4,1)}), s8[4194304]{0:T(1024)(128)(4,1)S(1)}, s32[]{:S(2)}) async-start(s8[8388608]{0:T(1024)(128)(4,1)} %bitcast.158), calls=%async_computation.4 | async-start | bytes 8388608
  464.7 6.5 slice-start.1
  464.7 6.5 copy-start.3
  474.4 1.3 copy-start.16
  474.4 1.6 copy-start.20
  474.4 1.6 copy-start.11
  475.8 2.5 copy-start.28
  481.1 27.5 %copy-start.9 = (bf16[2,1024,256]{2,1,0:T(8,128)(2,1)S(1)}, bf16[2,1024,256]{2,1,0:T(8,128)(2,1)}, u32[]{:S(2)}) copy-start(bf16[2,1024,256]{2,1,0:T(8,128)(2,1)} %get-tuple-element.34) | copy-start | bytes 3145732
  505.1 8.8 %copy-start.15 = (f32[128,512]{1,0:T(8,128)S(1)}, f32[128,512]{1,0:T(8,128)}, u32[]{:S(2)}) copy-start(f32[128,512]{1,0:T(8,128)} %ring_scatter.1) | copy-start | bytes 786436
  516.7 9.8 %slice-start.2 = ((s8[6291456]{0:T(1024)(128)(4,1)}), s8[4194304]{0:T(1024)(128)(4,1)S(1)}, s32[]{:S(2)}) async-start(s8[6291456]{0:T(1024)(128)(4,1)} %bitcast.172), calls=%async_computation.6 | async-start | bytes 8388608
  516.7 9.8 %copy-start.24 = (f32[128]{0:T(128)S(1)}, f32[128]{0:T(128)}, u32[]{:S(2)}) copy-start(f32[128]{0:T(128)} %copy-done.23) | copy-start | bytes 1540
  516.7 9.8 %copy-start.31 = (bf16[128,256]{1,0:T(8,128)(2,1)S(1)}, bf16[128,256]{1,0:T(8,128)(2,1)}, u32[]{:S(2)}) copy-start(bf16[128,256]{1,0:T(8,128)(2,1)} %convolution_convert_fusion.6) | copy-start | bytes 196612
  518.8 7.7 %slice-start.3 = ((s8[6291456]{0:T(1024)(128)(4,1)}), s8[2097152]{0:T(1024)(128)(4,1)S(1)}, s32[]{:S(2)}) async-start(s8[6291456]{0:T(1024)(128)(4,1)} %bitcast.172), calls=%async_computation.7 | async-start | bytes 4194304
  528.8 12.0 %copy-start.6 = (bf16[1024,256]{1,0:T(8,128)(2,1)S(1)}, bf16[1024,256]{1,0:T(8,128)(2,1)}, u32[]{:S(2)}) copy-start(bf16[1024,256]{1,0:T(8,128)(2,1)} %get-tuple-element.60) | copy-start | bytes 1572868
  534.9 117.7 %copy-start.29 = (f32[128]{0:T(128)S(1)}, f32[128]{0:T(128)}, u32[]{:S(2)}) copy-start(f32[128]{0:T(128)} %get-tuple-element.74) | copy-start | bytes 1540
  664.6 10.1 %slice-start.4 = ((s8[15204352]{0:T(1024)(128)(4,1)}), s8[4194304]{0:T(1024)(128)(4,1)S(1)}, s32[]{:S(2)}) async-start(s8[15204352]{0:T(1024)(128)(4,1)} %bitcast.191), calls=%async_computation.8 | async-start | bytes 8388608
  667.5 7.3 slice-start.5
  667.5 7.3 slice-start.6
  667.5 7.3 slice-start.7
  674.8 7.7 %slice-start.8 = ((s8[8388608]{0:T(1024)(128)(4,1)}), s8[4194304]{0:T(1024)(128)(4,1)S(1)}, s32[]{:S(2)}) async-start(s8[8388608]{0:T(1024)(128)(4,1)} %bitcast.206), calls=%async_computation.12 | async-start | bytes 8388608
  677.7 4.8 slice-start.9
  689.9 3.8 copy-start.7
  689.9 3.8 copy-start.21
  689.9 3.8 copy-start.22
  689.9 2.8 copy-start.12
  689.9 3.7 copy-start.13
  689.9 3.7 copy-start.14
  690.0 3.7 copy-start.17
  690.0 3.7 copy-start.18
  719.7 11.1 %copy-start.8 = (f32[1024,256]{1,0:T(8,128)S(1)}, f32[1024,256]{1,0:T(8,128)}, u32[]{:S(2)}) copy-start(f32[1024,256]{1,0:T(8,128)} %get-tuple-element.44) | copy-start | bytes 3145732
Sparse Core Ops, SparseCore 0:
  68.6 78.3 all-gather.5
  320.3 293.5 all-gather.7
  690.0 36.0 all-gather.9

commit v10 on v9

--- a/solution.py
+++ b/solution.py
@@ -125,7 +125,7 @@
         pl.semaphore_signal(barrier, inc=1, device_id={"fsdp": d}, device_id_type=MESH)
     pl.semaphore_wait(barrier, len(devices))
 
-def gather_kernel(chips, x_ref, o_ref, own_sem, ring_send, ring_recv, side_send, side_recv, greet=None, also=None):
+def gather_kernel(chips, x_ref, o_ref, own_sem, ring_send, ring_recv, side_send, side_recv, greet, also, work):
     core, device = ring_neighbours(chips)
     rows = x_ref.shape[0]
     reach = chips // 2
@@ -166,20 +166,35 @@
     own.start()
     if also is not None:
         also()
+    if work is not None:
+        own.wait()
+        across(0, 0, 1 - core).wait_recv()
+        work(0)
     for hops in range(1, reach + 1):
         for way in (0, 1):
             arriving(way, hops).wait_recv()
             if hops < reach:
                 hop(way, hops + 1).start()
             across(way, hops, core).start()
-    across(0, 0, 1 - core).wait_recv()
+        if work is not None:
+            for way in (0, 1):
+                across(way, hops, 1 - core).wait_recv()
+                if hops < reach:
+                    work(-hops if way == 0 else hops)
+                elif way:
+                    work(reach)
+    if work is None:
+        own.wait()
+        across(0, 0, 1 - core).wait_recv()
+        for hops in range(1, reach + 1):
+            for way in (0, 1):
+                across(way, hops, 1 - core).wait_recv()
     across(0, 0, core).wait_send()
     for hops in range(1, reach + 1):
         for way in (0, 1):
-            across(way, hops, 1 - core).wait_recv()
             across(way, hops, core).wait_send()
             hop(way, hops).wait_send()
-    own.wait()
+
 
 def busy(us):
     return pl.CostEstimate(flops=0, bytes_accessed=int(us * 3.0e6), transcendentals=0)
@@ -192,7 +207,7 @@
     pair = pltpu.SemaphoreType.DMA((2, chips // 2))
     sides = pltpu.SemaphoreType.DMA((2, chips // 2 + 1))
     return pl.pallas_call(
-        functools.partial(gather_kernel, chips),
+        functools.partial(gather_kernel, chips, greet=None, also=None, work=None),
         out_shape=jax.ShapeDtypeStruct((size * rows, columns), block.dtype),
         in_specs=[pl.BlockSpec(memory_space=pl.ANY)],
         out_specs=pl.BlockSpec(memory_space=pl.ANY),
@@ -619,10 +634,6 @@
     acts_ref, planes, gate_b, up_b, down_a, o_ref = refs[:6]
     acts, held, side_buf, ring_buf, stage, mine = refs[6:12]
     held_sem, side_send, side_recv, ring_send, ring_recv = refs[12:]
-    fetches = [pltpu.make_async_copy(planes.at[i], held.at[i], held_sem.at[0, i]) for i in range(3)]
-    fetches += [pltpu.make_async_copy(acts_ref.at[i], acts.at[i], held_sem.at[1, i]) for i in range(3)]
-    for fetch in fetches:
-        fetch.start()
     core, device = ring_neighbours(chips)
     rows, columns = o_ref.shape
     reach = chips // 2
@@ -631,11 +642,19 @@
     wide = 256
     ways = (device(1, core), device(-1, core))
     side = device(0, 1 - core)
-    meet((*ways, side))
     order = [(reach, 0, 0)]
     for step in range(1, reach):
         order += [(reach - step, 0, step), (chips - reach + step, 1, step)]
     order.append((0, 0, reach))
+    fetches = [pltpu.make_async_copy(planes.at[i], held.at[i], held_sem.at[chips, i]) for i in range(3)]
+
+    def fetched(i):
+        here = pl.ds(pl.multiple_of(device(order[i][0], 0) * rows, 2 * rows), 2 * rows)
+        return [pltpu.make_async_copy(acts_ref.at[k, here], acts.at[k, here], held_sem.at[i, k]) for k in range(3)]
+
+    for copy in fetched(0) + fetches + [copy for i in range(1, chips) for copy in fetched(i)]:
+        copy.start()
+    meet((*ways, side))
 
     def across(i):
         target = order[i][0]
@@ -663,6 +682,8 @@
 
     def make(i):
         target, slot = order[i][0], i % 2
+        for copy in fetched(i):
+            copy.wait()
         if i >= 2:
             across(i - 2).wait_send()
         theirs = pl.ds(pl.multiple_of(device(target, 1 - core) * rows, rows), rows)
@@ -726,11 +747,12 @@
         fetch.wait()
     make(0)
     add(0)
-    make(1)
-    for i in range(1, len(order)):
-        if i + 1 < len(order):
-            make(i + 1)
-        add(i)
+    for i in range(1, len(order), 2):
+        both = range(i, min(i + 2, len(order)))
+        for j in both:
+            make(j)
+        for j in both:
+            add(j)
     for i in range(len(order) - 2, len(order)):
         across(i).wait_send()
     for step in range(reach):
@@ -768,7 +790,7 @@
             pltpu.VMEM((2, chips // 2, rows, columns), bf16),
             pltpu.VMEM((2, rows, columns), bf16),
             pltpu.VMEM((2, rows, columns), bf16),
-            pltpu.SemaphoreType.DMA((2, 3)),
+            pltpu.SemaphoreType.DMA((chips + 1, 3)),
             sides,
             sides,
             pair,
@@ -782,8 +804,11 @@
     )(acts, planes, gate_b, up_b, down_a)
 
 
-def share_kernel(size, chunk, own_count, x_ref, mid_ref, all_ref, o_ref, *sems):
+def share_kernel(size, chunk, own_count, *refs):
+    x_ref, mid_ref, turned, lora, grad, widen, o_ref, in_ref, a_ref, near_ref, far_ref, gain_ref, all_ref = refs[:13]
+    sems = refs[13:]
     send_sem, recv_sem, own_sem = sems[5:]
+    _, device = ring_neighbours(size // 2)
     me = lax.axis_index("fsdp")
     hidden = HIDDEN_COUNT // size
     width = MODEL_WIDTH // size
@@ -844,7 +869,45 @@
 
             lax.fori_loop(0, length // chunk, send, 0)
 
-    gather_kernel(size // 2, x_ref, all_ref, *sems[:5], greet=greet, also=send_all)
+    def work(shift):
+        first = shift == 0
+        count = 2 * x_ref.shape[0]
+        here = pl.ds(pl.multiple_of(device(shift, 0) * x_ref.shape[0], count), count)
+        rank = ADAPTER_RANK
+
+        def put(ref, cols, value):
+            ref[:, cols] = value if first else ref[:, cols] + value
+
+        normed = turned[0, :, here]
+        wide = PROJECT_COLUMNS // rank
+
+        @pl.loop(0, wide)
+        def _(t):
+            cols = pl.ds(pl.multiple_of(t * rank, rank), rank)
+            part = jnp.maximum(t - (wide - 3), 0)
+            low = lora[pl.ds(pl.multiple_of(part * rank, rank), rank), here]
+            total = matrix_product(jnp.concatenate([normed, low], axis=0), all_ref[here, cols])
+            put(in_ref, cols, total[: normed.shape[0]])
+            put(near_ref, cols, total[normed.shape[0] :])
+
+        spans = ((0, QUERY_WIDTH), (QUERY_WIDTH, HEAD_WIDTH), (QUERY_WIDTH + HEAD_WIDTH, HEAD_WIDTH))
+        for i, (start, width) in enumerate(spans):
+            cols = pl.ds(start, width)
+            low = times_transposed(all_ref[here, cols], widen[:, cols]).astype(bf16)
+            put(a_ref, pl.ds(i * rank, rank), matrix_product(normed, low))
+        lows = [all_ref[here, pl.ds(PROJECT_COLUMNS + i * rank, rank)] for i in range(4)]
+        for i, kind in ((0, 1), (1, 2), (2, 2)):
+            put(a_ref, pl.ds((3 + i) * rank, rank), matrix_product(turned[kind, :, here], lows[i]))
+        pulled = lows[3].astype(f32).T.astype(bf16)
+
+        @pl.loop(0, MODEL_WIDTH // rank)
+        def _(t):
+            cols = pl.ds(pl.multiple_of(t * rank, rank), rank)
+            put(far_ref, cols, matrix_product(pulled, grad[here, cols]))
+
+        gain_ref[here, :] = all_ref[here, pl.ds(PROJECT_COLUMNS + 4 * rank, gain_ref.shape[1])]
+
+    gather_kernel(size // 2, x_ref, all_ref, *sems[:5], greet=greet, also=send_all, work=work)
 
     def arrive(j, carry):
         column = me * own_count + j * chunk
@@ -884,23 +947,59 @@
         lax.fori_loop(0, length // chunk, sent, 0)
 
 
-def share_rows(block, middle, ident):
+def share_rows(block, middle, turned, lora, grad, widen, ident):
     size = lax.axis_size("fsdp")
+    rank = ADAPTER_RANK
     rows, columns = block.shape
     own_count = ADAPTER_COLUMNS // size
-    chunk = math.gcd(own_count, MODEL_WIDTH // size, HIDDEN_COUNT // size, PROJECT_COLUMNS, GATE_START)
-    anywhere = pl.BlockSpec(memory_space=pl.ANY)
+    gain_width = columns - PROJECT_COLUMNS - 4 * rank
+    width = MODEL_WIDTH // size
+    chunk = math.gcd(own_count, width, HIDDEN_COUNT // size, PROJECT_COLUMNS, GATE_START)
+    if size != 16:
+        every = gather_rows(block)
+        spans = ((0, QUERY_WIDTH), (QUERY_WIDTH, HEAD_WIDTH), (QUERY_WIDTH + HEAD_WIDTH, HEAD_WIDTH))
+        parts = [every[:, a : a + n] for a, n in spans]
+        lows = [every[:, PROJECT_COLUMNS + i * rank :][:, :rank] for i in range(4)]
+        squeezed = [
+            matrix_product(turned[0], times_transposed(part, widen[:, a : a + n]).astype(bf16))
+            for part, (a, n) in zip(parts, spans)
+        ]
+        squeezed += [matrix_product(turned[kind], lows[i]) for i, kind in ((0, 1), (1, 2), (2, 2))]
+        near = [matrix_product(lora[i * rank : (i + 1) * rank], part) for i, part in enumerate(parts)]
+        middle_all = gather_rows(middle).reshape(size, -1, rank)
+        hidden = HIDDEN_COUNT // size
+        cuts = ((0, width), (width, width + hidden), (width + hidden, width + 2 * hidden))
+        middle_all = jnp.concatenate(
+            [jnp.zeros((PROJECT_COLUMNS, rank), bf16)]
+            + [middle_all[:, a:b].reshape(-1, rank) for a, b in cuts]
+            + [jnp.zeros((MODEL_WIDTH, rank), bf16)],
+            axis=0,
+        )
+        return (
+            lax.dynamic_slice_in_dim(middle_all, lax.axis_index("fsdp") * own_count, own_count, 0),
+            matrix_product(turned[0], every[:, :PROJECT_COLUMNS]),
+            jnp.concatenate(squeezed, axis=1),
+            jnp.concatenate(near, axis=1),
+            outer_product_rows(lows[3], grad),
+            every[:, columns - gain_width :],
+        )
+    anywhere, inside = pl.BlockSpec(memory_space=pl.ANY), pl.BlockSpec(memory_space=pltpu.VMEM)
     pair = pltpu.SemaphoreType.DMA((2, size // 4))
     sides = pltpu.SemaphoreType.DMA((2, size // 4 + 1))
     return pl.pallas_call(
         functools.partial(share_kernel, size, chunk, own_count),
         out_shape=(
-            jax.ShapeDtypeStruct((size * rows, columns), block.dtype),
-            jax.ShapeDtypeStruct((own_count, ADAPTER_RANK), bf16),
+            jax.ShapeDtypeStruct((own_count, rank), bf16),
+            jax.ShapeDtypeStruct((width, PROJECT_COLUMNS), f32),
+            jax.ShapeDtypeStruct((width, 6 * rank), f32),
+            jax.ShapeDtypeStruct((rank, PROJECT_COLUMNS), f32),
+            jax.ShapeDtypeStruct((rank, MODEL_WIDTH), f32),
+            jax.ShapeDtypeStruct((size * rows, gain_width), bf16),
         ),
-        in_specs=[anywhere] * 2,
-        out_specs=(anywhere, anywhere),
+        in_specs=[anywhere] * 2 + [inside] * 4,
+        out_specs=(anywhere,) + (inside,) * 5,
         scratch_shapes=[
+            pltpu.VMEM((size * rows, columns), bf16),
             pltpu.SemaphoreType.DMA,
             pair,
             pair,
@@ -910,10 +1009,12 @@
             pltpu.SemaphoreType.DMA((own_count // chunk,)),
             pltpu.SemaphoreType.DMA((own_count // chunk,)),
         ],
-        compiler_params=pltpu.CompilerParams(collective_id=ident, has_side_effects=True),
+        compiler_params=pltpu.CompilerParams(
+            collective_id=ident, has_side_effects=True, vmem_limit_bytes=56 << 20
+        ),
         cost_estimate=busy(1),
         name="share_rows",
-    )(block, middle)
+    )(block, middle, turned, lora, grad, widen)
 
 
 def per_device(
@@ -1100,64 +1201,41 @@
     proj_rows = jnp.concatenate(
         [proj_grad, lora_out_grad, gate_low, up_low, lora_hd, gain_rows], axis=1
     )
-    proj_all, middle_own = share_rows(
-        proj_rows, jnp.concatenate([out_piece.astype(bf16), ffn_pieces[0], ffn_pieces[1]], axis=0), 5
-    )
     column = place * width_own
-    gain_all = proj_all[:, PROJECT_COLUMNS + 4 * rank :][:, :gain_count].reshape(size, 2, MODEL_WIDTH)
+    attended_turn = lax.dynamic_slice_in_dim(attended_all, column, width_own, 1)
+    two_turn = lax.dynamic_slice_in_dim(two_all, column, width_own, 1)
+    middle_own, attn_in_part, squeeze_own, near, far, gain_all = share_rows(
+        proj_rows,
+        jnp.concatenate([out_piece.astype(bf16), ffn_pieces[0], ffn_pieces[1]], axis=0),
+        jnp.stack([normed_turn.T, attended_turn.T, two_turn.T]),
+        lora_qkv_all.T,
+        grad_all,
+        second_factor[:, :PROJECT_COLUMNS],
+        5,
+    )
+    gain_all = gain_all[:, :gain_count].reshape(size, 2, MODEL_WIDTH)
     gain_all = jnp.sum(gain_all.astype(f32), axis=0)
     gain_own = lax.dynamic_slice_in_dim(gain_all, column, width_own, 1)
     gain_part = jnp.pad(gain_own, ((0, width_own - 2), (0, -width_own % 128)))
     attn_part = jnp.concatenate(
         [
-            outer_product_rows(normed_turn, proj_all[:, :PROJECT_COLUMNS]),
+            attn_in_part,
             outer_product_rows(branch_turn, attended_all)[:, :QUERY_WIDTH],
             gain_part,
         ],
         axis=1,
     ).astype(bf16)
-    attn_part, ffn_both, proj_all = lax.optimization_barrier((attn_part, ffn_both, proj_all))
+    attn_part, ffn_both = lax.optimization_barrier((attn_part, ffn_both))
     attn_sum = both_loops(loop_shares(attn_part))
     gain_column = PROJECT_COLUMNS + QUERY_WIDTH
     gain_sum = attn_sum[:2, gain_column : gain_column + width_own]
-    low_all = proj_all[:, PROJECT_COLUMNS : PROJECT_COLUMNS + 4 * rank]
-    proj_all = proj_all[:, :PROJECT_COLUMNS]
-    qkv_low_all = jnp.concatenate(
-        [
-            times_transposed(proj_all[:, :QUERY_WIDTH], widen_query),
-            times_transposed(proj_all[:, QUERY_WIDTH : QUERY_WIDTH + HEAD_WIDTH], widen_key),
-            times_transposed(proj_all[:, QUERY_WIDTH + HEAD_WIDTH :], widen_value),
-        ],
-        axis=1,
-    ).astype(bf16)
-    attended_turn = lax.dynamic_slice_in_dim(attended_all, column, width_own, 1)
-    two_turn = lax.dynamic_slice_in_dim(two_all, column, width_own, 1)
-    squeeze_own = jnp.concatenate(
-        [
-            outer_product_rows(normed_turn, qkv_low_all),
-            outer_product_rows(attended_turn, low_all[:, :rank]),
-            outer_product_rows(two_turn, low_all[:, rank : 3 * rank]),
-        ],
-        axis=1,
-    )
-    near = jnp.concatenate(
-        [
-            outer_product_rows(proj_all[:, :QUERY_WIDTH], lora_qkv_all[:, :rank]),
-            outer_product_rows(
-                proj_all[:, QUERY_WIDTH : QUERY_WIDTH + HEAD_WIDTH], lora_qkv_all[:, rank : 2 * rank]
-            ),
-            outer_product_rows(proj_all[:, QUERY_WIDTH + HEAD_WIDTH :], lora_qkv_all[:, 2 * rank :]),
-        ],
-        axis=0,
-    )
-    far = outer_product_rows(grad_all, low_all[:, 3 * rank :])
     first = place * columns_own
     far_start = GATE_START + 2 * HIDDEN_COUNT
     near = lax.dynamic_slice_in_dim(
-        jnp.pad(near.astype(bf16), ((0, columns_own), (0, 0))), jnp.minimum(first, PROJECT_COLUMNS), columns_own, 0
+        jnp.pad(near.T.astype(bf16), ((0, columns_own), (0, 0))), jnp.minimum(first, PROJECT_COLUMNS), columns_own, 0
     )
     far = lax.dynamic_slice_in_dim(
-        jnp.pad(far.astype(bf16), ((columns_own, 0), (0, 0))),
+        jnp.pad(far.T.astype(bf16), ((columns_own, 0), (0, 0))),
         jnp.maximum(first - far_start + columns_own, 0),
         columns_own,
         0,

time: 749 us -> 771 us (1.029)
  local copies, waits for them, and re-layouts: 23.9 us -> 70.6 us
  matrix products: 109 us -> 71.4 us
    pallas_call x0 -> x3, local copies, waits for them, and re-layouts: none -> 30.3 us  [the longest x2 27.5 us: unit_rows(): pl.pallas_call(functools.partial(unit_kernel, chips), out_shape=(jax.Shap...]
    dot_general x10 -> x2, matrix products: 36.2 us -> 7.58 us  [outer_product_rows(): lax.dot_general(former, latter, (((0,), (0,)), ((), ())), preferred_eleme...]
    pallas_call x1, Pallas kernels: 109 us -> 122 us  [share_rows(): pl.pallas_call(functools.partial(share_kernel, size, chunk, own_count), o...]
    pallas_call x1, Pallas kernels: 128 us -> 119 us  [mix_rows(): pl.pallas_call(functools.partial(mix_kernel, chips), out_shape=jax.ShapeD...]
    dot_general x13 -> x10, matrix products: 37.5 us -> 28.8 us  [times_transposed(): lax.dot_general(former, latter, (((1,), (1,)), ((), ())), preferred_eleme...]
  transfers between devices with their start and end apart: 4 -> 4, of which waited for: 2 -> 2; matrix products, arithmetic and copies ran while one was open for 19% -> 24% of each run, Pallas kernels for 40% -> 39%
where the time goes in v10:
time: 771 us; the launch traced here: 760 us
  Pallas kernels  522 us (68%)
  matrix products  71.4 us (9%)
  local copies, waits for them, and re-layouts  70.6 us (9%)
  other arithmetic  58.5 us (8%)
  waiting for transfers between devices  18.3 us (2%)
  between operations  14.9 us (2%)
    pallas_call x1, Pallas kernels, unit_rows(): pl.pallas_call(functools.partial(unit_kernel, chips), out_shape=(jax.Shap...  163 us
    pallas_call x1, Pallas kernels, share_rows(): pl.pallas_call(functools.partial(share_kernel, size, chunk, own_count), o...  122 us
    pallas_call x1, Pallas kernels, mix_rows(): pl.pallas_call(functools.partial(mix_kernel, chips), out_shape=jax.ShapeD...  119 us
    pallas_call x2, Pallas kernels, ring_gather(): pl.pallas_call(functools.partial(gather_kernel, chips, greet=None, also=N...  93.5 us
    dot_general x10, matrix products, times_transposed(): lax.dot_general(former, latter, (((1,), (1,)), ((), ())), preferred_eleme...  28.8 us
    pallas_call x2, local copies, waits for them, and re-layouts, unit_rows(): pl.pallas_call(functools.partial(unit_kernel, chips), out_shape=(jax.Shap...  27.5 us
    pallas_call x1, Pallas kernels, ring_scatter(): pl.pallas_call(functools.partial(scatter_kernel, chips, count), out_shape...  23.9 us
    dot_general x9, matrix products, matrix_product(): return jnp.dot(former, latter, preferred_element_type=f32)  22.6 us
  transfers between devices with their start and end apart: 4, of which 2 were waited for; matrix products, arithmetic and copies ran while one was open for 24% of the time, Pallas kernels for 39%

profile of v10, /device:TPU:0, one launch (start us, length us, event | category | flops | bytes accessed | tf_op | source)
XLA Modules:
  0.0 760.2 jit_solution(13784759332657933712)
XLA Ops:
  7.2 61.2 %ring_gather.2 = bf16[2048,2560]{1,0:T(8,128)(2,1)} custom-call(bf16[128,2560]{1,0:T(8,128)(2,1)} %x_ref.1), custom_call_target="tpu_custom_call" | custom-call | bytes 3000000 | tf_op jit(solution)/shard_map/ring_gather/pallas_call | solution.py:209
  68.5 3.1 slice.239.refs_4_
  71.6 2.3 slice.240.refs_5_
  75.1 2.7 fusion.31
  77.8 5.6 fusion.81
  86.6 32.3 %ring_gather.3 = bf16[2048,512]{1,0:T(8,128)(2,1)} custom-call(bf16[128,512]{1,0:T(8,128)(2,1)} %pad_maximum_fusion.8.x_ref), custom_call_target="tpu_custom_call" | custom-call | bytes 3000000 | tf_op jit(solution)/shard_map/ring_gather/pallas_call | solution.py:209
  118.9 1.7 convolution_add_fusion.5
  123.0 1.3 fusion.42
  124.3 3.6 fusion.126
  127.9 3.3 fusion.27
  131.3 1.9 dynamic-slice_bitcast_fusion.2.refs_8_.refs_4_
  133.2 2.3 dynamic-slice_bitcast_fusion.3
  135.5 1.5 convolution_convert_fusion.3
  138.0 9.1 %all-gather.6.cloned.1.call-done = bf16[2048,2048]{1,0:T(8,128)(2,1)} async-done(((bf16[128,2048]{1,0:T(8,128)(2,1)}), bf16[2048,2048]{1,0:T(8,128)(2,1)}) %all-gather.6.cloned.1.call-update) | async-done | bytes 8388624 | tf_op jit(solution)/shard_map/all_gather | solution.py:89
  147.0 6.7 convolution_add_fusion.6
  153.7 1.6 multiply_reduce_fusion.3
  157.0 163.5 %unit_rows.1 = (bf16[2048,2048]{1,0:T(8,128)(2,1)}, bf16[2048,2048]{1,0:T(8,128)(2,1)}, bf16[2048,2816]{1,0:T(8,128)(2,1)}, bf16[3,2048,1024]{2,1,0:T(8,128)(2,1...) custom-call(bf16[128,2304]{1,0:T(8,128)(2,1)} %pad_maximum_fusion.4., ...), custom_call_target="tpu_custom_call" | custom-call | bytes 300000000 | tf_op jit(solution)/shard_map/unit_rows/pallas_call | solution.py:593
  320.7 2.5 slice.255.refs_5_
  323.8 1.1 multiply_convert_fusion.1
  324.9 119.3 %mix_rows.1 = f32[128,4864]{1,0:T(8,128)} custom-call(bf16[3,2048,1024]{2,1,0:T(8,128)(2,1)} %get-tuple-element.32.refs_0_, bf16[3,1024,2048]{2,1,0:T(8,128)(2,1)} %bitcast.160, bf16[256,1024]{1,0:T(8,128)(2,1)} %get-tuple-element.96.refs_6_.refs_2_, bf16[256,1024]{1,0:T(8,128)(2,1)} %get-tuple-element.95.refs_7_.refs_3_, ...), custom_call_target="tpu_custom_call" | custom-call | bytes 3000000 | tf_op jit(solution)/shard_map/mix_rows/pallas_call | solution.py:780
  444.2 2.0 convert.70
  446.6 2.2 convolution_add_fusion.2
  448.8 2.5 multiply_reduce_fusion.1
  451.3 1.5 fusion.122
  452.8 2.0 copy.86
  454.8 2.3 pad_maximum_fusion.2
  457.1 4.3 all-to-all-start
  461.5 2.0 convolution_convert_fusion.2
  463.6 4.9 fusion.127
  468.6 1.7 fusion.17
  470.3 1.5 multiply_reduce_fusion
  471.8 1.6 multiply_convert_fusion
  473.4 1.3 convolution_multiply_fusion
  474.9 2.4 fusion.10.refs_0_
  477.2 2.7 fusion.11.refs_1_
  480.9 12.3 %copy.79 = bf16[2048,2048]{0,1:T(8,128)(2,1)} copy(bf16[2048,2048]{1,0:T(8,128)(2,1)} %get-tuple-element.39) | data formatting | bytes 16777216 | tf_op jit(solution)/shard_map/unit_rows/pallas_call | solution.py:593
  493.2 15.2 %copy.78 = bf16[2048,2816]{0,1:T(8,128)(2,1)} copy(bf16[2048,2816]{1,0:T(8,128)(2,1)} %get-tuple-element.38) | data formatting | bytes 23068672 | tf_op jit(solution)/shard_map/unit_rows/pallas_call | solution.py:593
  508.4 23.9 %ring_scatter.1 = f32[128,512]{1,0:T(8,128)} custom-call(bf16[2048,256]{1,0:T(8,128)(2,1)} %fusion.10.refs_0_, bf16[2048,256]{1,0:T(8,128)(2,1)} %fusion.11.refs_1_), custom_call_target="tpu_custom_call" | custom-call | bytes 3000000 | tf_op jit(solution)/shard_map/ring_scatter/pallas_call | solution.py:324
  532.4 1.9 constant_dynamic-update-slice_fusion.3
  534.3 2.4 fusion.18
  536.7 2.1 dynamic-slice_bitcast_fusion
  538.9 1.7 convolution_convert_fusion.1
  540.6 4.0 slice_bitcast_fusion.refs_3_
  544.6 1.5 copy_bitcast_fusion
  550.9 7.6 fusion.65
  558.6 2.2 fusion.52
  561.5 1.6 slice_dynamic-update-slice_fusion
  563.1 1.5 slice_dynamic-update-slice_fusion.1
  565.2 2.4 pad_maximum_fusion.refs_2_
  567.6 1.5 convolution_convert_fusion
  570.2 121.9 %share_rows.1 = (bf16[2464,256]{1,0:T(8,128)(2,1)}, f32[128,2560]{1,0:T(8,128)}, f32[128,1536]{1,0:T(8,128)}, f32[256,2560]{1,0:T(8,128)}, f32[256,2048]{1,0:T(8,128)}, /*index=5*/bf16[2048,128]{1,0:T(8,128)(2,1)}) custom-call(bf16[128,3712]{1,0:T(8,128)(2,1)} %pad_dynamic-update-slice_fusion.refs_0_, bf16[2176,256]{1,0:T(8,128)(2,1)} %pad_maximum_fusion.1.refs_1_, ...), custom_call_target="tpu_custom_call" | custom-call | bytes 3000000 | tf_op jit(solution)/shard_map/share_rows/pallas_call | solution.py:989
  692.1 1.1 slice_convert_fusion.1
  693.8 6.1 fusion.128
  701.6 2.7 copy.81
  704.5 2.7 convert_bitcast_fusion.2
  707.2 2.4 fusion.30
  709.6 1.2 convert_bitcast_fusion.1
  710.8 3.0 convert_bitcast_fusion
  713.8 2.1 copy.82
  715.8 3.1 fusion.49
  718.9 18.8 %add_bitcast_fusion = f32[1024,3,2048]{2,0,1:T(8,128)} fusion(bf16[2,3,1024,2048]{3,2,1,0:T(8,128)(2,1)} %bitcast.161), kind=kLoop, calls=%fused_computation.1 | loop fusion | flops 18874368 | bytes 50331648 | tf_op jit(solution)/shard_map/transpose | solution.py:1247
  737.7 9.2 %all-gather.10.cloned.1.call-done = bf16[256,4736]{1,0:T(8,128)(2,1)} async-done(((bf16[128,4736]{1,0:T(8,128)(2,1)}), bf16[256,4736]{1,0:T(8,128)(2,1)}) %all-gather.10.cloned.1.call-update) | async-done | bytes 2424848 | tf_op jit(solution)/shard_map/all_gather | solution.py:97
  746.9 1.9 convert_add_fusion
  749.4 1.2 slice.260
  (162 shorter events, 25.0 us)
Async XLA Ops:
  7.2 139.8 %all-gather.6.cloned.1.call-start = ((), (), s32[]{:S(2)}) async-start(), calls=%async_computation.1 | async-start | bytes 8912896 | tf_op jit(solution)/shard_map/all_gather | solution.py:89
  68.4 5.5 copy-start.42
  68.4 6.0 copy-start.1
  68.4 6.7 copy-start.26
  68.4 642.3 %all-gather.8.cloned.1.call-start = ((), (), s32[]{:S(2)}) async-start(), calls=%async_computation.2 | async-start | bytes 37748736 | tf_op jit(solution)/shard_map/all_gather | solution.py:97
  74.2 46.8 %copy-start.34 = (f32[128]{0:T(128)}, f32[128]{0:T(128)S(1)}, u32[]{:S(2)}) copy-start(f32[128]{0:T(128)S(1)} %multiply_exponential_fusion) | copy-start | bytes 1540
  74.4 46.6 %copy-start.32 = (f32[128]{0:T(128)}, f32[128]{0:T(128)S(1)}, u32[]{:S(2)}) copy-start(f32[128]{0:T(128)S(1)} %fusion.113) | copy-start | bytes 1540
  75.1 248.7 %copy-start.30 = (f32[128]{0:T(128)}, f32[128]{0:T(128)S(1)}, u32[]{:S(2)}) copy-start(f32[128]{0:T(128)S(1)} %get-tuple-element.117) | copy-start | bytes 1540
  118.9 4.1 copy-start.4
  121.9 2.4 copy-start.21
  122.2 0.7 copy-start.15
  122.2 0.8 copy-start.17
  127.9 3.4 copy-start.3
  127.9 3.4 copy-start.38
  155.9 164.5 %copy-start.36 = (f32[128]{0:T(128)}, f32[128]{0:T(128)S(1)}, u32[]{:S(2)}) copy-start(f32[128]{0:T(128)S(1)} %get-tuple-element.119) | copy-start | bytes 1540
  444.2 2.5 copy-start
  444.2 4.6 copy-start.37
  446.6 6.2 copy-start.9
  446.6 4.7 copy-start.10
  446.6 4.7 copy-start.41
  457.1 87.5 %all-to-all-start = ((bf16[128,16,256]{0,2,1:T(8,128)(2,1)}), bf16[128,16,256]{0,2,1:T(8,128)(2,1)}, u32[]{:S(2)}, u32[]{:S(2)}) async-start(bf16[128,16,256]{0,2,1:T(8,128)(2,1)} %pad_maximum_fusion.2), calls=%async_computation | async-start | bytes 2097152 | tf_op jit(solution)/shard_map/all_to_all | solution.py:105
  461.5 285.4 %all-gather.10.cloned.1.call-start = ((), (), s32[]{:S(2)}) async-start(), calls=%async_computation.3 | async-start | bytes 3637248 | tf_op jit(solution)/shard_map/all_gather | solution.py:97
  461.5 8.8 %slice-start = ((s8[8388608]{0:T(1024)(128)(4,1)}), s8[4194304]{0:T(1024)(128)(4,1)S(1)}, s32[]{:S(2)}) async-start(s8[8388608]{0:T(1024)(128)(4,1)} %bitcast.162), calls=%async_computation.4 | async-start | bytes 8388608
  463.6 5.0 copy-start.24
  463.6 6.7 slice-start.1
  463.6 6.7 copy-start.5
  463.6 6.7 copy-start.39
  473.4 1.3 copy-start.22
  473.4 1.3 copy-start.23
  473.4 1.5 copy-start.16
  473.4 1.5 copy-start.18
  477.2 3.6 copy-start.27
  508.4 30.4 %copy-start.14 = (bf16[2,1024,256]{2,1,0:T(8,128)(2,1)S(1)}, bf16[2,1024,256]{2,1,0:T(8,128)(2,1)}, u32[]{:S(2)}) copy-start(bf16[2,1024,256]{2,1,0:T(8,128)(2,1)} %get-tuple-element.36) | copy-start | bytes 3145732
  534.3 4.6 copy-start.6
  540.6 6.4 copy-start.19
  540.6 6.4 copy-start.33
  540.6 6.4 copy-start.35
  544.6 6.3 copy-start.7
  544.6 13.9 %slice-start.2 = ((s8[6291456]{0:T(1024)(128)(4,1)}), s8[4194304]{0:T(1024)(128)(4,1)S(1)}, s32[]{:S(2)}) async-start(s8[6291456]{0:T(1024)(128)(4,1)} %bitcast.176), calls=%async_computation.6 | async-start | bytes 8388608
  550.9 7.7 %copy-start.2 = (bf16[1,128,2048]{2,1,0:T(8,128)(2,1)S(1)}, bf16[1,128,2048]{2,1,0:T(8,128)(2,1)}, u32[]{:S(2)}) copy-start(bf16[1,128,2048]{2,1,0:T(8,128)(2,1)} %param.10) | copy-start | bytes 1572868
  550.9 7.6 %slice-start.3 = ((s8[6291456]{0:T(1024)(128)(4,1)}), s8[2097152]{0:T(1024)(128)(4,1)S(1)}, s32[]{:S(2)}) async-start(s8[6291456]{0:T(1024)(128)(4,1)} %bitcast.176), calls=%async_computation.7 | async-start | bytes 4194304
  550.9 7.6 %copy-start.31 = (f32[128]{0:T(128)S(1)}, f32[128]{0:T(128)}, u32[]{:S(2)}) copy-start(f32[128]{0:T(128)} %copy-done.30) | copy-start | bytes 1540
  558.5 2.4 copy-start.25
  558.6 6.7 copy-start.11
  693.8 6.9 copy-start.12
  701.6 7.9 %copy-start.8 = (f32[256,2560]{1,0:T(8,128)S(1)}, f32[256,2560]{1,0:T(8,128)}, u32[]{:S(2)}) copy-start(f32[256,2560]{1,0:T(8,128)} %get-tuple-element.47) | copy-start | bytes 7864324
  707.2 3.6 copy-start.28
  707.2 3.6 copy-start.29
  710.8 5.0 copy-start.40
  737.7 13.9 %copy-start.20 = (f32[128,1536]{1,0:T(8,128)S(1)}, f32[128,1536]{1,0:T(8,128)}, u32[]{:S(2)}) copy-start(f32[128,1536]{1,0:T(8,128)} %get-tuple-element.46) | copy-start | bytes 2359300
  748.8 3.7 copy-start.13
Sparse Core Ops, SparseCore 0:
  68.6 78.3 all-gather.5
  320.6 293.4 all-gather.7
  710.9 35.9 all-gather.9

commit v11 on v10

--- a/solution.py
+++ b/solution.py
@@ -805,8 +805,8 @@
 
 
 def share_kernel(size, chunk, own_count, *refs):
-    x_ref, mid_ref, turned, lora, grad, widen, o_ref, in_ref, a_ref, near_ref, far_ref, gain_ref, all_ref = refs[:13]
-    sems = refs[13:]
+    x_ref, mid_ref, turned, lora, grad, widen, o_ref, in_ref, a_ref, near_ref, far_ref, gain_ref, all_ref, low_t = refs[:14]
+    sems = refs[14:]
     send_sem, recv_sem, own_sem = sems[5:]
     _, device = ring_neighbours(size // 2)
     me = lax.axis_index("fsdp")
@@ -878,15 +878,19 @@
         def put(ref, cols, value):
             ref[:, cols] = value if first else ref[:, cols] + value
 
-        normed = turned[0, :, here]
+        def flip(block):
+            return block.astype(f32).T.astype(bf16)
+
+        normed = flip(turned[0, here, :])
         wide = PROJECT_COLUMNS // rank
+        for i in range(3):
+            low_t[i] = flip(lora[here, pl.ds(i * rank, rank)])
 
         @pl.loop(0, wide)
         def _(t):
             cols = pl.ds(pl.multiple_of(t * rank, rank), rank)
             part = jnp.maximum(t - (wide - 3), 0)
-            low = lora[pl.ds(pl.multiple_of(part * rank, rank), rank), here]
-            total = matrix_product(jnp.concatenate([normed, low], axis=0), all_ref[here, cols])
+            total = matrix_product(jnp.concatenate([normed, low_t[part]], axis=0), all_ref[here, cols])
             put(in_ref, cols, total[: normed.shape[0]])
             put(near_ref, cols, total[normed.shape[0] :])
 
@@ -897,8 +901,8 @@
             put(a_ref, pl.ds(i * rank, rank), matrix_product(normed, low))
         lows = [all_ref[here, pl.ds(PROJECT_COLUMNS + i * rank, rank)] for i in range(4)]
         for i, kind in ((0, 1), (1, 2), (2, 2)):
-            put(a_ref, pl.ds((3 + i) * rank, rank), matrix_product(turned[kind, :, here], lows[i]))
-        pulled = lows[3].astype(f32).T.astype(bf16)
+            put(a_ref, pl.ds((3 + i) * rank, rank), matrix_product(flip(turned[kind, here, :]), lows[i]))
+        pulled = flip(lows[3])
 
         @pl.loop(0, MODEL_WIDTH // rank)
         def _(t):
@@ -961,11 +965,11 @@
         parts = [every[:, a : a + n] for a, n in spans]
         lows = [every[:, PROJECT_COLUMNS + i * rank :][:, :rank] for i in range(4)]
         squeezed = [
-            matrix_product(turned[0], times_transposed(part, widen[:, a : a + n]).astype(bf16))
+            outer_product_rows(turned[0], times_transposed(part, widen[:, a : a + n]).astype(bf16))
             for part, (a, n) in zip(parts, spans)
         ]
-        squeezed += [matrix_product(turned[kind], lows[i]) for i, kind in ((0, 1), (1, 2), (2, 2))]
-        near = [matrix_product(lora[i * rank : (i + 1) * rank], part) for i, part in enumerate(parts)]
+        squeezed += [outer_product_rows(turned[kind], lows[i]) for i, kind in ((0, 1), (1, 2), (2, 2))]
+        near = [outer_product_rows(lora[:, i * rank :][:, :rank], part) for i, part in enumerate(parts)]
         middle_all = gather_rows(middle).reshape(size, -1, rank)
         hidden = HIDDEN_COUNT // size
         cuts = ((0, width), (width, width + hidden), (width + hidden, width + 2 * hidden))
@@ -977,7 +981,7 @@
         )
         return (
             lax.dynamic_slice_in_dim(middle_all, lax.axis_index("fsdp") * own_count, own_count, 0),
-            matrix_product(turned[0], every[:, :PROJECT_COLUMNS]),
+            outer_product_rows(turned[0], every[:, :PROJECT_COLUMNS]),
             jnp.concatenate(squeezed, axis=1),
             jnp.concatenate(near, axis=1),
             outer_product_rows(lows[3], grad),
@@ -1000,6 +1004,7 @@
         out_specs=(anywhere,) + (inside,) * 5,
         scratch_shapes=[
             pltpu.VMEM((size * rows, columns), bf16),
+            pltpu.VMEM((3, rank, rank), bf16),
             pltpu.SemaphoreType.DMA,
             pair,
             pair,
@@ -1128,7 +1133,6 @@
     )
     back_own, out_own = rows_sum[:, : MODEL_WIDTH + 2 * rank], rows_sum[:, MODEL_WIDTH + 2 * rank :]
     lora_hd = out_own[:, MODEL_WIDTH:].astype(bf16)
-    hidden_out = (middle + out_own[:, :MODEL_WIDTH] + matrix_product(lora_hd, widen_down)).astype(bf16)
 
     gate_low = back_own[:, MODEL_WIDTH : MODEL_WIDTH + rank].astype(bf16)
     up_low = back_own[:, MODEL_WIDTH + rank :].astype(bf16)
@@ -1202,13 +1206,20 @@
         [proj_grad, lora_out_grad, gate_low, up_low, lora_hd, gain_rows], axis=1
     )
     column = place * width_own
-    attended_turn = lax.dynamic_slice_in_dim(attended_all, column, width_own, 1)
-    two_turn = lax.dynamic_slice_in_dim(two_all, column, width_own, 1)
+    attended_turn, two_turn, attn_out_part, lora_qkv_all, proj_rows = lax.optimization_barrier(
+        (
+            lax.dynamic_slice_in_dim(attended_all, column, width_own, 1),
+            lax.dynamic_slice_in_dim(two_all, column, width_own, 1),
+            outer_product_rows(branch_turn, attended_all)[:, :QUERY_WIDTH],
+            lora_qkv_all,
+            proj_rows,
+        )
+    )
     middle_own, attn_in_part, squeeze_own, near, far, gain_all = share_rows(
         proj_rows,
         jnp.concatenate([out_piece.astype(bf16), ffn_pieces[0], ffn_pieces[1]], axis=0),
-        jnp.stack([normed_turn.T, attended_turn.T, two_turn.T]),
-        lora_qkv_all.T,
+        jnp.stack([normed_turn, attended_turn, two_turn]),
+        lora_qkv_all,
         grad_all,
         second_factor[:, :PROJECT_COLUMNS],
         5,
@@ -1220,12 +1231,14 @@
     attn_part = jnp.concatenate(
         [
             attn_in_part,
-            outer_product_rows(branch_turn, attended_all)[:, :QUERY_WIDTH],
+            attn_out_part,
             gain_part,
         ],
         axis=1,
     ).astype(bf16)
-    attn_part, ffn_both = lax.optimization_barrier((attn_part, ffn_both))
+    attn_part, ffn_both, near, far, middle_own, out_own = lax.optimization_barrier(
+        (attn_part, ffn_both, near, far, middle_own, out_own)
+    )
     attn_sum = both_loops(loop_shares(attn_part))
     gain_column = PROJECT_COLUMNS + QUERY_WIDTH
     gain_sum = attn_sum[:2, gain_column : gain_column + width_own]
@@ -1244,6 +1257,7 @@
     expand_own = jnp.where(
         owned < PROJECT_COLUMNS, near, jnp.where(owned < far_start, middle_own, far)
     ).T.astype(f32)
+    hidden_out = (middle + out_own[:, :MODEL_WIDTH] + matrix_product(lora_hd, widen_down)).astype(bf16)
     ffn_sum = both_loops(ffn_both).transpose(1, 0, 2)
     return (
         hidden_out[None],

time: 771 us -> 743 us (0.964)
  local copies, waits for them, and re-layouts: 70.6 us -> 40.9 us
    pallas_call x3 -> x0, local copies, waits for them, and re-layouts: 30.3 us -> none  [the longest x2 27.5 us: unit_rows(): pl.pallas_call(functools.partial(unit_kernel, chips), out_shape=(jax.Shap...]
  transfers between devices with their start and end apart: 4 -> 4, of which waited for: 2 -> 2; matrix products, arithmetic and copies ran while one was open for 24% -> 21% of each run, Pallas kernels for 39% -> 40%
where the time goes in v11:
time: 743 us; the launch traced here: 733 us
  Pallas kernels  522 us (70%)
  matrix products  73.9 us (10%)
  other arithmetic  59.5 us (8%)
  local copies, waits for them, and re-layouts  40.9 us (6%)
  waiting for transfers between devices  17.9 us (2%)
  between operations  14.8 us (2%)
    pallas_call x1, Pallas kernels, unit_rows(): pl.pallas_call(functools.partial(unit_kernel, chips), out_shape=(jax.Shap...  164 us
    pallas_call x1, Pallas kernels, share_rows(): pl.pallas_call(functools.partial(share_kernel, size, chunk, own_count), o...  122 us
    pallas_call x1, Pallas kernels, mix_rows(): pl.pallas_call(functools.partial(mix_kernel, chips), out_shape=jax.ShapeD...  118 us
    pallas_call x2, Pallas kernels, ring_gather(): pl.pallas_call(functools.partial(gather_kernel, chips, greet=None, also=N...  93.3 us
    dot_general x10, matrix products, times_transposed(): lax.dot_general(former, latter, (((1,), (1,)), ((), ())), preferred_eleme...  31.2 us
    pallas_call x1, Pallas kernels, ring_scatter(): pl.pallas_call(functools.partial(scatter_kernel, chips, count), out_shape...  23.9 us
    dot_general x9, matrix products, matrix_product(): return jnp.dot(former, latter, preferred_element_type=f32)  23 us
    transpose x1, other arithmetic, per_device(): ffn_sum = both_loops(ffn_both).transpose(1, 0, 2)  18.7 us
  transfers between devices with their start and end apart: 4, of which 2 were waited for; matrix products, arithmetic and copies ran while one was open for 21% of the time, Pallas kernels for 40%

profile of v11, /device:TPU:0, one launch (start us, length us, event | category | flops | bytes accessed | tf_op | source)
XLA Modules:
  0.0 733.3 jit_solution(12714107717155041267)
XLA Ops:
  7.2 61.2 %ring_gather.2 = bf16[2048,2560]{1,0:T(8,128)(2,1)} custom-call(bf16[128,2560]{1,0:T(8,128)(2,1)} %x_ref.1), custom_call_target="tpu_custom_call" | custom-call | bytes 3000000 | tf_op jit(solution)/shard_map/ring_gather/pallas_call | solution.py:209
  68.5 2.4 slice.242.refs_5_
  70.9 3.0 slice.241.refs_4_
  75.1 2.7 fusion.38
  77.8 5.6 fusion.90
  83.4 1.2 fusion.41
  86.7 32.1 %ring_gather.3 = bf16[2048,512]{1,0:T(8,128)(2,1)} custom-call(bf16[128,512]{1,0:T(8,128)(2,1)} %pad_maximum_fusion.8.x_ref), custom_call_target="tpu_custom_call" | custom-call | bytes 3000000 | tf_op jit(solution)/shard_map/ring_gather/pallas_call | solution.py:209
  118.9 2.0 convolution_add_fusion.5
  123.0 1.3 fusion.58
  124.3 3.6 fusion.137
  127.8 3.3 fusion.34
  131.3 1.9 dynamic-slice_bitcast_fusion.refs_8_.refs_4_
  133.2 2.3 dynamic-slice_bitcast_fusion.1
  135.4 1.5 convolution_convert_fusion.3
  137.9 9.1 %all-gather.6.cloned.1.call-done = bf16[2048,2048]{1,0:T(8,128)(2,1)} async-done(((bf16[128,2048]{1,0:T(8,128)(2,1)}), bf16[2048,2048]{1,0:T(8,128)(2,1)}) %all-gather.6.cloned.1.call-update) | async-done | bytes 8388624 | tf_op jit(solution)/shard_map/all_gather | solution.py:89
  147.0 6.7 convolution_add_fusion.6
  153.7 1.6 multiply_reduce_fusion.3
  156.4 163.8 %unit_rows.1 = (bf16[2048,2048]{1,0:T(8,128)(2,1)}, bf16[2048,2048]{1,0:T(8,128)(2,1)}, bf16[2048,2816]{1,0:T(8,128)(2,1)}, bf16[3,2048,1024]{2,1,0:T(8,128)(2,1...) custom-call(bf16[128,2304]{1,0:T(8,128)(2,1)} %pad_maximum_fusion.4., ...), custom_call_target="tpu_custom_call" | custom-call | bytes 300000000 | tf_op jit(solution)/shard_map/unit_rows/pallas_call | solution.py:593
  320.2 2.5 slice.256.refs_5_
  324.0 118.5 %mix_rows.1 = f32[128,4864]{1,0:T(8,128)} custom-call(bf16[3,2048,1024]{2,1,0:T(8,128)(2,1)} %get-tuple-element.43.refs_0_, bf16[3,1024,2048]{2,1,0:T(8,128)(2,1)} %bitcast.158, bf16[256,1024]{1,0:T(8,128)(2,1)} %get-tuple-element.114.refs_6_.refs_2_, bf16[256,1024]{1,0:T(8,128)(2,1)} %get-tuple-element.113.refs_7_.refs_3_, ...), custom_call_target="tpu_custom_call" | custom-call | bytes 3000000 | tf_op jit(solution)/shard_map/mix_rows/pallas_call | solution.py:780
  442.4 2.0 convert.69
  444.9 1.8 convolution_add_fusion.3
  446.7 2.5 multiply_reduce_fusion.1
  449.7 1.1 pad_maximum_fusion.2
  450.8 4.4 all-to-all-start
  455.2 1.9 convolution_convert_fusion.2
  457.1 4.8 fusion.129
  461.9 1.7 fusion.18
  463.6 1.5 multiply_reduce_fusion
  465.1 1.6 multiply_convert_fusion
  466.7 1.3 convolution_multiply_fusion
  468.3 3.8 slice.197.refs_3_
  472.1 2.4 fusion.12.refs_0_
  474.5 2.7 fusion.13.refs_1_
  477.2 23.9 %ring_scatter.1 = f32[128,512]{1,0:T(8,128)} custom-call(bf16[2048,256]{1,0:T(8,128)(2,1)} %fusion.12.refs_0_, bf16[2048,256]{1,0:T(8,128)(2,1)} %fusion.13.refs_1_), custom_call_target="tpu_custom_call" | custom-call | bytes 3000000 | tf_op jit(solution)/shard_map/ring_scatter/pallas_call | solution.py:324
  501.9 2.3 constant_dynamic-slice_fusion.1
  505.3 2.3 convolution_convert_fusion.1
  507.6 2.2 fusion.134
  511.6 1.1 convolution_convert_fusion.5
  513.3 1.1 convolution_convert_fusion.4
  514.4 7.5 %fusion.74 = f32[128,2048]{1,0:T(8,128)S(1)} fusion(bf16[2048,2560]{1,0:T(8,128)(2,1)} %ring_gather.2, bf16[128,256]{1,0:T(8,128)(2,1)S(1)} %get-tuple-element.110, bf16[128,256]{1,0:T(8,128)(2,1)S(1)} %maximum_bitcast_fusion.2, bf16[128,2048]{1,0:T(8,128)(2,1)S(1)} %bitcast.164), kind=kOutput, calls=%fused_computation.110 | convolution fusion | flops 1344143360 | bytes 12189696 | tf_op jit(solution)/shard_map/dot_general | solution.py:32
  522.0 4.7 fusion.51
  527.5 1.6 slice_dynamic-update-slice_fusion
  529.0 1.5 slice_dynamic-update-slice_fusion.1
  531.1 5.6 fusion.1
  536.8 1.3 pad_maximum_fusion.refs_2_
  538.1 1.6 convolution_convert_fusion
  539.7 1.1 pad_maximum_fusion.1.refs_1_
  540.8 122.3 %share_rows.1 = (bf16[2464,256]{1,0:T(8,128)(2,1)}, f32[128,2560]{1,0:T(8,128)}, f32[128,1536]{1,0:T(8,128)}, f32[256,2560]{1,0:T(8,128)}, f32[256,2048]{1,0:T(8,128)}, /*index=5*/bf16[2048,128]{1,0:T(8,128)(2,1)}) custom-call(bf16[128,3712]{1,0:T(8,128)(2,1)} %pad_dynamic-update-slice_fusion.refs_0_, bf16[2176,256]{1,0:T(8,128)(2,1)} %pad_maximum_fusion.1.refs_1_, ...), custom_call_target="tpu_custom_call" | custom-call | bytes 3000000 | tf_op jit(solution)/shard_map/share_rows/pallas_call | solution.py:993
  663.1 2.1 slice_convert_fusion
  665.2 1.8 reshape.325
  667.0 1.4 convert.80
  670.4 2.5 fusion.50
  672.9 2.2 fusion.37
  675.1 2.9 convert_bitcast_fusion.3
  678.0 1.8 copy.65
  679.8 2.7 convert_bitcast_fusion.4
  682.6 4.2 convert_bitcast_fusion
  686.8 3.2 copy.66
  690.0 2.5 fusion.20
  692.5 18.7 %add_bitcast_fusion = f32[1024,3,2048]{2,0,1:T(8,128)} fusion(bf16[2,3,1024,2048]{3,2,1,0:T(8,128)(2,1)} %bitcast.159), kind=kLoop, calls=%fused_computation.1 | loop fusion | flops 18874368 | bytes 50331648 | tf_op jit(solution)/shard_map/transpose | solution.py:1261
  711.2 8.7 %all-gather.10.cloned.1.call-done = bf16[256,4736]{1,0:T(8,128)(2,1)} async-done(((bf16[128,4736]{1,0:T(8,128)(2,1)}), bf16[256,4736]{1,0:T(8,128)(2,1)}) %all-gather.10.cloned.1.call-update) | async-done | bytes 2424848 | tf_op jit(solution)/shard_map/all_gather | solution.py:97
  719.9 1.9 convert_add_fusion
  721.8 1.2 slice.260
  (140 shorter events, 21.2 us)
Async XLA Ops:
  7.2 139.8 %all-gather.6.cloned.1.call-start = ((), (), s32[]{:S(2)}) async-start(), calls=%async_computation.1 | async-start | bytes 8912896 | tf_op jit(solution)/shard_map/all_gather | solution.py:89
  68.4 5.5 copy-start.33
  68.4 6.0 copy-start.1
  68.4 6.7 copy-start.21
  68.4 606.6 %all-gather.8.cloned.1.call-start = ((), (), s32[]{:S(2)}) async-start(), calls=%async_computation.2 | async-start | bytes 37748736 | tf_op jit(solution)/shard_map/all_gather | solution.py:97
  74.2 47.1 %copy-start.29 = (f32[128]{0:T(128)}, f32[128]{0:T(128)S(1)}, u32[]{:S(2)}) copy-start(f32[128]{0:T(128)S(1)} %multiply_exponential_fusion) | copy-start | bytes 1540
  74.4 46.9 %copy-start.28 = (f32[128]{0:T(128)}, f32[128]{0:T(128)S(1)}, u32[]{:S(2)}) copy-start(f32[128]{0:T(128)S(1)} %fusion.122) | copy-start | bytes 1540
  75.1 248.5 %copy-start.25 = (f32[128]{0:T(128)}, f32[128]{0:T(128)S(1)}, u32[]{:S(2)}) copy-start(f32[128]{0:T(128)S(1)} %get-tuple-element.135) | copy-start | bytes 1540
  83.4 1.6 copy-start.3
  118.9 4.1 copy-start.4
  122.5 1.8 copy-start.16
  127.8 3.4 copy-start.2
  127.8 337.3 %copy-start.30 = (f32[128,8]{0,1:T(8,128)}, f32[128,8]{0,1:T(8,128)S(1)}, u32[]{:S(2)}) copy-start(f32[128,8]{0,1:T(8,128)S(1)} %get-tuple-element.138) | copy-start | bytes 12292
  442.4 2.5 copy-start
  444.4 4.7 copy-start.6
  444.9 4.2 copy-start.7
  450.8 56.9 %all-to-all-start = ((bf16[128,16,256]{2,0,1:T(8,128)(2,1)}), bf16[128,16,256]{2,0,1:T(8,128)(2,1)}, u32[]{:S(2)}, u32[]{:S(2)}) async-start(bf16[128,16,256]{2,0,1:T(8,128)(2,1)} %pad_maximum_fusion.2), calls=%async_computation | async-start | bytes 2097152 | tf_op jit(solution)/shard_map/all_to_all | solution.py:105
  455.1 264.8 %all-gather.10.cloned.1.call-start = ((), (), s32[]{:S(2)}) async-start(), calls=%async_computation.3 | async-start | bytes 3637248 | tf_op jit(solution)/shard_map/all_gather | solution.py:97
  455.2 8.4 %slice-start.1 = ((s8[8388608]{0:T(1024)(128)(4,1)}), s8[4194304]{0:T(1024)(128)(4,1)S(1)}, s32[]{:S(2)}) async-start(s8[8388608]{0:T(1024)(128)(4,1)} %bitcast.160), calls=%async_computation.5 | async-start | bytes 8388608
  457.1 6.5 slice-start.2
  457.1 6.5 copy-start.5
  466.7 1.3 copy-start.20
  466.7 1.6 copy-start.22
  468.2 3.9 copy-start.17
  472.1 2.4 copy-start.31
  477.2 27.1 %copy-start.15 = (bf16[2,1024,256]{2,1,0:T(8,128)(2,1)S(1)}, bf16[2,1024,256]{2,1,0:T(8,128)(2,1)}, u32[]{:S(2)}) copy-start(bf16[2,1024,256]{2,1,0:T(8,128)(2,1)} %get-tuple-element.48) | copy-start | bytes 3145732
  501.9 7.9 %copy-start.18 = (f32[128,512]{1,0:T(8,128)S(1)}, f32[128,512]{1,0:T(8,128)}, u32[]{:S(2)}) copy-start(f32[128,512]{1,0:T(8,128)} %ring_scatter.1) | copy-start | bytes 786436
  514.4 7.5 %copy-start.26 = (f32[128]{0:T(128)S(1)}, f32[128]{0:T(128)}, u32[]{:S(2)}) copy-start(f32[128]{0:T(128)} %copy-done.25) | copy-start | bytes 1540
  514.4 7.5 %copy-start.34 = (bf16[128,256]{1,0:T(8,128)(2,1)S(1)}, bf16[128,256]{1,0:T(8,128)(2,1)}, u32[]{:S(2)}) copy-start(bf16[128,256]{1,0:T(8,128)(2,1)} %convolution_convert_fusion.1) | copy-start | bytes 196612
  522.0 9.2 %copy-start.10 = (bf16[2048,128]{1,0:T(8,128)(2,1)S(1)}, bf16[2048,128]{1,0:T(8,128)(2,1)}, u32[]{:S(2)}) copy-start(bf16[2048,128]{1,0:T(8,128)(2,1)} %get-tuple-element.44) | copy-start | bytes 1572868
  531.1 5.6 copy-start.11
  531.1 5.6 copy-start.12
  531.1 5.6 copy-start.13
  536.7 2.9 copy-start.8
  536.8 2.9 copy-start.9
  663.1 7.3 copy-start.27
  663.1 7.3 copy-start.32
  678.0 4.6 copy-start.23
  678.0 4.6 copy-start.24
  682.6 7.4 %slice-start = ((f32[128,4864]{1,0:T(8,128)}), f32[128,2304]{1,0:T(8,128)S(1)}, s32[]{:S(2)}) async-start(f32[128,4864]{1,0:T(8,128)} %mix_rows.1), calls=%async_computation.4 | async-start | bytes 2359296 | tf_op jit(solution)/shard_map/slice | solution.py:1134
  711.2 13.5 %copy-start.19 = (f32[128,1536]{1,0:T(8,128)S(1)}, f32[128,1536]{1,0:T(8,128)}, u32[]{:S(2)}) copy-start(f32[128,1536]{1,0:T(8,128)} %get-tuple-element.64) | copy-start | bytes 2359300
  721.8 3.7 copy-start.14
Sparse Core Ops, SparseCore 0:
  68.6 78.3 all-gather.5
  320.3 294.2 all-gather.7
  682.7 37.1 all-gather.9

commit v12 on v11

--- a/solution.py
+++ b/solution.py
@@ -99,6 +99,25 @@
 
 def both_loops(shares):
     return shares[0].astype(f32) + shares[1].astype(f32)
+
+
+def sum_kernel(x_ref, o_ref):
+    o_ref[...] = x_ref[0].astype(f32) + x_ref[1].astype(f32)
+
+
+def sum_loops(shares):
+    _, planes, rows, columns = shares.shape
+    tile = min(rows, 256)
+    return pl.pallas_call(
+        sum_kernel,
+        grid=(planes, rows // tile),
+        out_shape=jax.ShapeDtypeStruct((planes, rows, columns), f32),
+        in_specs=[pl.BlockSpec((2, 1, tile, columns), lambda i, j: (0, i, j, 0))],
+        out_specs=pl.BlockSpec((1, tile, columns), lambda i, j: (i, j, 0)),
+        compiler_params=pltpu.CompilerParams(vmem_limit_bytes=32 << 20),
+        cost_estimate=busy(1),
+        name="sum_loops",
+    )(shares)
 
 
 def turn(block):
@@ -342,12 +361,43 @@
     )(*terms)
 
 
+def adapter_parts(first_factor, second_factor, down_first):
+    own = HIDDEN_COUNT // lax.axis_size("fsdp")
+    start = lax.axis_index("fsdp") * own
+    return (
+        first_factor[:, 4 * ADAPTER_RANK :],
+        second_factor[:, GATE_START + 2 * HIDDEN_COUNT :],
+        lax.dynamic_slice_in_dim(second_factor, GATE_START + start, own, 1),
+        lax.dynamic_slice_in_dim(second_factor, GATE_START + HIDDEN_COUNT + start, own, 1),
+        lax.dynamic_slice_in_dim(down_first, start, own, 0),
+    )
+
+
+def part_copies(first_ref, second_ref, down_ref, parts, sems):
+    own = parts[4].shape[0]
+    start = pl.multiple_of(lax.axis_index("fsdp") * own, own)
+    sources = (
+        lambda: first_ref.at[:, pl.ds(4 * ADAPTER_RANK, 2 * ADAPTER_RANK)],
+        lambda: second_ref.at[:, pl.ds(GATE_START + 2 * HIDDEN_COUNT, MODEL_WIDTH)],
+        lambda: second_ref.at[:, pl.ds(pl.multiple_of(GATE_START + start, 128), own)],
+        lambda: second_ref.at[:, pl.ds(pl.multiple_of(GATE_START + HIDDEN_COUNT + start, 128), own)],
+        lambda: down_ref.at[pl.ds(start, own)],
+    )
+    return [
+        pltpu.make_async_copy(source(), part, sems.at[i])
+        for i, (source, part) in enumerate(zip(sources, parts))
+        if part is not None
+    ]
+
+
 def unit_kernel(chips, *refs):
-    sources, (planes, squeeze, widen_down, widen_gate, widen_up, narrow) = refs[:3], refs[3:9]
-    two_all, grad_all, later_all, acts_all, low_all, share_out, piece_out, down_out = refs[9:17]
-    held, turned, acts, low, tiles = refs[17:22]
-    landed = (refs[22], refs[23], later_all)
-    held_sem, own_sem, ring_send, ring_recv, side_send, side_recv, out_sem, acts_sem, tile_sem = refs[24:]
+    sources, planes, adapters = refs[:3], refs[3], refs[4:7]
+    two_all, grad_all, later_all, acts_all, low_all, share_out, piece_out, down_out = refs[7:15]
+    held, turned, acts, low, tiles = refs[15:20]
+    landed = (refs[20], refs[21], later_all)
+    parts, part_sem = refs[22:27], refs[27]
+    squeeze, widen_down, widen_gate, widen_up, narrow = parts
+    held_sem, own_sem, ring_send, ring_recv, side_send, side_recv, out_sem, acts_sem, tile_sem = refs[28:]
     core, device = ring_neighbours(chips)
     rows = sources[0].shape[0]
     reach = chips // 2
@@ -355,6 +405,7 @@
     ways = (device(1, core), device(-1, core))
     side = device(0, 1 - core)
     fetches = [pltpu.make_async_copy(planes.at[i], held.at[i], held_sem.at[i]) for i in range(3)]
+    fetches += part_copies(*adapters, parts, part_sem)
     for fetch in fetches:
         fetch.start()
     meet((*ways, side))
@@ -553,10 +604,11 @@
                 copy.wait()
 
 
-def unit_rows(two, grad, later, planes, squeeze, widen_down, widen_gate, widen_up, narrow, ident):
+def unit_rows(two, grad, later, planes, adapters, ident):
     size = lax.axis_size("fsdp")
     rank = ADAPTER_RANK
     if size != 16:
+        squeeze, widen_down, widen_gate, widen_up, narrow = adapter_parts(*adapters)
         two, grad = gather_rows(two), gather_rows(grad)
         two, lora_out = two[:, :MODEL_WIDTH], two[:, MODEL_WIDTH:]
         low = matrix_product(two, squeeze).astype(bf16)
@@ -602,7 +654,7 @@
             jax.ShapeDtypeStruct((2, hidden, rank), bf16),
             jax.ShapeDtypeStruct((hidden, rank), f32),
         ),
-        in_specs=[anywhere] * 4 + [inside] * 5,
+        in_specs=[anywhere] * 7,
         out_specs=(anywhere,) * 6 + (inside,) * 2,
         scratch_shapes=[
             pltpu.VMEM(planes.shape, bf16),
@@ -612,6 +664,12 @@
             pltpu.VMEM((2, hidden, 256), bf16),
             pltpu.VMEM((all_rows, two.shape[1]), bf16),
             pltpu.VMEM((all_rows, columns), bf16),
+            pltpu.VMEM((columns, 2 * rank), bf16),
+            pltpu.VMEM((rank, columns), bf16),
+            pltpu.VMEM((rank, hidden), bf16),
+            pltpu.VMEM((rank, hidden), bf16),
+            pltpu.VMEM((hidden, rank), bf16),
+            pltpu.SemaphoreType.DMA((5,)),
             pltpu.SemaphoreType.DMA((3,)),
             pltpu.SemaphoreType.DMA((3,)),
             pair,
@@ -627,13 +685,13 @@
         ),
         cost_estimate=busy(100),
         name="unit_rows",
-    )(two, grad, later, planes, squeeze, widen_down, widen_gate, widen_up, narrow)
+    )(two, grad, later, planes, *adapters)
 
 
 def mix_kernel(chips, *refs):
-    acts_ref, planes, gate_b, up_b, down_a, o_ref = refs[:6]
-    acts, held, side_buf, ring_buf, stage, mine = refs[6:12]
-    held_sem, side_send, side_recv, ring_send, ring_recv = refs[12:]
+    acts_ref, planes, adapters, o_ref = refs[0], refs[1], refs[2:5], refs[5]
+    acts, held, gate_b, up_b, down_a, side_buf, ring_buf, stage, mine = refs[6:15]
+    part_sem, held_sem, side_send, side_recv, ring_send, ring_recv = refs[15:]
     core, device = ring_neighbours(chips)
     rows, columns = o_ref.shape
     reach = chips // 2
@@ -647,6 +705,7 @@
         order += [(reach - step, 0, step), (chips - reach + step, 1, step)]
     order.append((0, 0, reach))
     fetches = [pltpu.make_async_copy(planes.at[i], held.at[i], held_sem.at[chips, i]) for i in range(3)]
+    fetches += part_copies(*adapters, (None, None, gate_b, up_b, down_a), part_sem)
 
     def fetched(i):
         here = pl.ds(pl.multiple_of(device(order[i][0], 0) * rows, 2 * rows), 2 * rows)
@@ -761,10 +820,11 @@
                 hop(way, step, part).wait_send()
 
 
-def mix_rows(acts, planes, gate_b, up_b, down_a, ident):
+def mix_rows(acts, planes, adapters, ident):
     size = lax.axis_size("fsdp")
     if size != 16:
         gate_grad, up_grad, units = acts[0], acts[1], acts[2]
+        gate_b, up_b, down_a = adapter_parts(*adapters)[2:]
         terms = [
             matrix_product(gate_grad, planes[0]) + matrix_product(up_grad, planes[1]),
             times_transposed(gate_grad, gate_b),
@@ -780,16 +840,19 @@
     return pl.pallas_call(
         functools.partial(mix_kernel, chips),
         out_shape=jax.ShapeDtypeStruct((rows, columns), f32),
-        in_specs=[pl.BlockSpec(memory_space=pl.ANY)] * 2
-        + [pl.BlockSpec(memory_space=pltpu.VMEM)] * 3,
+        in_specs=[pl.BlockSpec(memory_space=pl.ANY)] * 5,
         out_specs=pl.BlockSpec(memory_space=pltpu.VMEM),
         scratch_shapes=[
             pltpu.VMEM(acts.shape, bf16),
             pltpu.VMEM(planes.shape, bf16),
+            pltpu.VMEM((ADAPTER_RANK, planes.shape[1]), bf16),
+            pltpu.VMEM((ADAPTER_RANK, planes.shape[1]), bf16),
+            pltpu.VMEM((planes.shape[1], ADAPTER_RANK), bf16),
             pltpu.VMEM((chips, rows, columns), bf16),
             pltpu.VMEM((2, chips // 2, rows, columns), bf16),
             pltpu.VMEM((2, rows, columns), bf16),
             pltpu.VMEM((2, rows, columns), bf16),
+            pltpu.SemaphoreType.DMA((5,)),
             pltpu.SemaphoreType.DMA((chips + 1, 3)),
             sides,
             sides,
@@ -801,12 +864,21 @@
         ),
         cost_estimate=busy(1),
         name="mix_rows",
-    )(acts, planes, gate_b, up_b, down_a)
+    )(acts, planes, *adapters)
 
 
 def share_kernel(size, chunk, own_count, *refs):
-    x_ref, mid_ref, turned, lora, grad, widen, o_ref, in_ref, a_ref, near_ref, far_ref, gain_ref, all_ref, low_t = refs[:14]
-    sems = refs[14:]
+    x_ref, mid_ref, turned, later_ref, grad, second_ref = refs[:6]
+    o_ref, in_ref, a_ref, near_ref, far_ref, gain_ref, all_ref, low_t, lora, widen, load_sem = refs[6:17]
+    sems = refs[17:]
+    loads = [
+        pltpu.make_async_copy(
+            later_ref.at[:, pl.ds(QUERY_WIDTH, 3 * ADAPTER_RANK)], lora, load_sem.at[0]
+        ),
+        pltpu.make_async_copy(second_ref.at[:, pl.ds(0, PROJECT_COLUMNS)], widen, load_sem.at[1]),
+    ]
+    for load in loads:
+        load.start()
     send_sem, recv_sem, own_sem = sems[5:]
     _, device = ring_neighbours(size // 2)
     me = lax.axis_index("fsdp")
@@ -871,6 +943,9 @@
 
     def work(shift):
         first = shift == 0
+        if first:
+            for load in loads:
+                load.wait()
         count = 2 * x_ref.shape[0]
         here = pl.ds(pl.multiple_of(device(shift, 0) * x_ref.shape[0], count), count)
         rank = ADAPTER_RANK
@@ -951,7 +1026,7 @@
         lax.fori_loop(0, length // chunk, sent, 0)
 
 
-def share_rows(block, middle, turned, lora, grad, widen, ident):
+def share_rows(block, middle, turned, later, grad, second_factor, ident):
     size = lax.axis_size("fsdp")
     rank = ADAPTER_RANK
     rows, columns = block.shape
@@ -961,6 +1036,7 @@
     chunk = math.gcd(own_count, width, HIDDEN_COUNT // size, PROJECT_COLUMNS, GATE_START)
     if size != 16:
         every = gather_rows(block)
+        lora, widen = later[:, QUERY_WIDTH:], second_factor[:, :PROJECT_COLUMNS]
         spans = ((0, QUERY_WIDTH), (QUERY_WIDTH, HEAD_WIDTH), (QUERY_WIDTH + HEAD_WIDTH, HEAD_WIDTH))
         parts = [every[:, a : a + n] for a, n in spans]
         lows = [every[:, PROJECT_COLUMNS + i * rank :][:, :rank] for i in range(4)]
@@ -1000,11 +1076,14 @@
             jax.ShapeDtypeStruct((rank, MODEL_WIDTH), f32),
             jax.ShapeDtypeStruct((size * rows, gain_width), bf16),
         ),
-        in_specs=[anywhere] * 2 + [inside] * 4,
+        in_specs=[anywhere] * 2 + [inside, anywhere, inside, anywhere],
         out_specs=(anywhere,) + (inside,) * 5,
         scratch_shapes=[
             pltpu.VMEM((size * rows, columns), bf16),
             pltpu.VMEM((3, rank, rank), bf16),
+            pltpu.VMEM((size * rows, 3 * rank), bf16),
+            pltpu.VMEM((rank, PROJECT_COLUMNS), bf16),
+            pltpu.SemaphoreType.DMA((2,)),
             pltpu.SemaphoreType.DMA,
             pair,
             pair,
@@ -1019,7 +1098,7 @@
         ),
         cost_estimate=busy(1),
         name="share_rows",
-    )(block, middle, turned, lora, grad, widen)
+    )(block, middle, turned, later, grad, second_factor)
 
 
 def per_device(
@@ -1058,17 +1137,11 @@
     narrow_output = first_factor[:, 3 * rank : 4 * rank]
     squeeze_gate = first_factor[:, 4 * rank : 5 * rank]
     squeeze_up = first_factor[:, 5 * rank :]
-    narrow_down = lax.dynamic_slice_in_dim(adapter_down_first[0], place * hidden_own, hidden_own, 0)
+    adapters = (first_factor, second_factor, adapter_down_first[0])
     widen_query = second_factor[:, :QUERY_WIDTH]
     widen_key = second_factor[:, QUERY_WIDTH : QUERY_WIDTH + HEAD_WIDTH]
     widen_value = second_factor[:, QUERY_WIDTH + HEAD_WIDTH : PROJECT_COLUMNS]
     widen_output = second_factor[:, PROJECT_COLUMNS:GATE_START]
-    widen_gate = lax.dynamic_slice_in_dim(
-        second_factor, GATE_START + place * hidden_own, hidden_own, 1
-    )
-    widen_up = lax.dynamic_slice_in_dim(
-        second_factor, GATE_START + HIDDEN_COUNT + place * hidden_own, hidden_own, 1
-    )
     widen_down = second_factor[:, GATE_START + 2 * HIDDEN_COUNT :]
     scaling = HEAD_WIDTH ** (-0.5)
 
@@ -1119,17 +1192,13 @@
         output_gradient[0],
         jnp.concatenate([attended, lora_qkv], axis=1),
         weight_planes,
-        first_factor[:, 4 * rank :],
-        widen_down,
-        widen_gate,
-        widen_up,
-        narrow_down,
+        adapters,
         2,
     )
     lora_out_all = low_ffn[:, 3 * rank :]
     ffn_both = loop_shares(ffn_shares)
     rows_sum = mix_rows(
-        acts, weight_planes, widen_gate, widen_up, narrow_down, 3
+        acts, weight_planes, adapters, 3
     )
     back_own, out_own = rows_sum[:, : MODEL_WIDTH + 2 * rank], rows_sum[:, MODEL_WIDTH + 2 * rank :]
     lora_hd = out_own[:, MODEL_WIDTH:].astype(bf16)
@@ -1197,7 +1266,6 @@
     )
     gain_one = jnp.sum(normed_grad * hidden_state * scale_one, axis=0)
 
-    lora_qkv_all = attended_all[:, QUERY_WIDTH:]
     out_piece = outer_product_rows(branch_turn, lora_out_all)
     gain_rows = jnp.stack([gain_one, gain_two]).astype(bf16).reshape(tokens_dev, -1)
     gain_count = gain_rows.shape[1]
@@ -1206,12 +1274,11 @@
         [proj_grad, lora_out_grad, gate_low, up_low, lora_hd, gain_rows], axis=1
     )
     column = place * width_own
-    attended_turn, two_turn, attn_out_part, lora_qkv_all, proj_rows = lax.optimization_barrier(
+    attended_turn, two_turn, attn_out_part, proj_rows = lax.optimization_barrier(
         (
             lax.dynamic_slice_in_dim(attended_all, column, width_own, 1),
             lax.dynamic_slice_in_dim(two_all, column, width_own, 1),
             outer_product_rows(branch_turn, attended_all)[:, :QUERY_WIDTH],
-            lora_qkv_all,
             proj_rows,
         )
     )
@@ -1219,9 +1286,9 @@
         proj_rows,
         jnp.concatenate([out_piece.astype(bf16), ffn_pieces[0], ffn_pieces[1]], axis=0),
         jnp.stack([normed_turn, attended_turn, two_turn]),
-        lora_qkv_all,
+        attended_all,
         grad_all,
-        second_factor[:, :PROJECT_COLUMNS],
+        second_factor,
         5,
     )
     gain_all = gain_all[:, :gain_count].reshape(size, 2, MODEL_WIDTH)
@@ -1258,7 +1325,7 @@
         owned < PROJECT_COLUMNS, near, jnp.where(owned < far_start, middle_own, far)
     ).T.astype(f32)
     hidden_out = (middle + out_own[:, :MODEL_WIDTH] + matrix_product(lora_hd, widen_down)).astype(bf16)
-    ffn_sum = both_loops(ffn_both).transpose(1, 0, 2)
+    ffn_sum = sum_loops(ffn_both).transpose(1, 0, 2)
     return (
         hidden_out[None],
         input_grad[None],

time: 743 us -> 728 us (0.980)
  other arithmetic: 59.5 us -> 41.9 us
  Pallas kernels: 522 us -> 539 us
  local copies, waits for them, and re-layouts: 40.9 us -> 27.3 us
    pallas_call x0 -> x1, Pallas kernels: none -> 21.4 us  [sum_loops(): pl.pallas_call(sum_kernel, grid=(planes, rows // tile), out_shape=jax.Sha...]
    transpose x1 -> x0, other arithmetic: 18.7 us -> none  [per_device(): ffn_sum = both_loops(ffn_both).transpose(1, 0, 2)]
    slice x4 -> x0, local copies, waits for them, and re-layouts: 11.6 us -> none  [the longest x1 3.76 us: per_device(): lora_qkv_all = attended_all[:, QUERY_WIDTH:]]
    all_gather x2, waiting for transfers between devices: 8.75 us -> 0.01 us  [loop_shares(): return lax.all_gather(partial.astype(bf16), 'loop', axis=0)]
  transfers between devices with their start and end apart: 4 -> 4, of which waited for: 2 -> 1; matrix products, arithmetic and copies ran while one was open for 21% -> 17% of each run, Pallas kernels for 40% -> 44%
where the time goes in v12:
time: 728 us; the launch traced here: 717 us
  Pallas kernels  539 us (74%)
  matrix products  72.9 us (10%)
  other arithmetic  41.9 us (6%)
  local copies, waits for them, and re-layouts  27.3 us (4%)
  waiting for transfers between devices  16.1 us (2%)
  between operations  14.9 us (2%)
    pallas_call x1, Pallas kernels, unit_rows(): pl.pallas_call(functools.partial(unit_kernel, chips), out_shape=(jax.Shap...  160 us
    pallas_call x1, Pallas kernels, mix_rows(): pl.pallas_call(functools.partial(mix_kernel, chips), out_shape=jax.ShapeD...  122 us
    pallas_call x1, Pallas kernels, share_rows(): pl.pallas_call(functools.partial(share_kernel, size, chunk, own_count), o...  121 us
    pallas_call x2, Pallas kernels, ring_gather(): pl.pallas_call(functools.partial(gather_kernel, chips, greet=None, also=N...  90.5 us
    dot_general x10, matrix products, times_transposed(): lax.dot_general(former, latter, (((1,), (1,)), ((), ())), preferred_eleme...  29.1 us
    pallas_call x1, Pallas kernels, ring_scatter(): pl.pallas_call(functools.partial(scatter_kernel, chips, count), out_shape...  24.1 us
    dot_general x9, matrix products, matrix_product(): return jnp.dot(former, latter, preferred_element_type=f32)  22.6 us
    pallas_call x1, Pallas kernels, sum_loops(): pl.pallas_call(sum_kernel, grid=(planes, rows // tile), out_shape=jax.Sha...  21.4 us
  transfers between devices with their start and end apart: 4, of which 1 were waited for; matrix products, arithmetic and copies ran while one was open for 17% of the time, Pallas kernels for 44%

profile of v12, /device:TPU:0, one launch (start us, length us, event | category | flops | bytes accessed | tf_op | source)
XLA Modules:
  0.0 716.5 jit_solution(8234269499849285989)
XLA Ops:
  7.3 61.2 %ring_gather.2 = bf16[2048,2560]{1,0:T(8,128)(2,1)} custom-call(bf16[128,2560]{1,0:T(8,128)(2,1)} %x_ref.1), custom_call_target="tpu_custom_call" | custom-call | bytes 3000000 | tf_op jit(solution)/shard_map/ring_gather/pallas_call | solution.py:228
  69.7 2.5 fusion.38
  72.2 5.9 fusion.91
  78.2 1.1 fusion.41
  79.6 1.1 fusion.42
  81.4 29.4 %ring_gather.3 = bf16[2048,512]{1,0:T(8,128)(2,1)} custom-call(bf16[128,512]{1,0:T(8,128)(2,1)} %pad_maximum_fusion.8.x_ref), custom_call_target="tpu_custom_call" | custom-call | bytes 3000000 | tf_op jit(solution)/shard_map/ring_gather/pallas_call | solution.py:228
  110.7 1.7 convolution_add_fusion.5
  112.8 0.9 broadcast_multiply_fusion
  114.5 4.7 fusion.59
  119.2 9.2 %fusion.137 = (f32[128,8]{0,1:T(8,128)S(1)}, f32[128,8,2048]{2,0,1:T(8,128)S(1)}) fusion(f32[128,8,2048]{2,0,1:T(8,128)} %fusion.59, pred[128,2048]{1,0:T(8,128)(4,1)S(1)} %fusion.64), kind=kOutput, calls=%fused_computation.220 | output fusion | flops 12584959 | bytes 17043456 | tf_op jit(solution)/shard_map/sub | solution.py:1171
  128.4 1.3 fusion.34
  129.7 2.1 copy-done.6
  131.8 1.5 convolution_convert_fusion.3
  133.4 0.9 pad_maximum_fusion.3.refs_2_
  134.3 16.0 %all-gather.6.cloned.1.call-done = bf16[2048,2048]{1,0:T(8,128)(2,1)} async-done(((bf16[128,2048]{1,0:T(8,128)(2,1)}), bf16[2048,2048]{1,0:T(8,128)(2,1)}) %all-gather.6.cloned.1.call-update) | async-done | bytes 8388624 | tf_op jit(solution)/shard_map/all_gather | solution.py:89
  150.3 6.7 convolution_add_fusion.6
  157.0 1.6 multiply_reduce_fusion.3
  160.2 159.6 %unit_rows.1 = (bf16[2048,2048]{1,0:T(8,128)(2,1)}, bf16[2048,2048]{1,0:T(8,128)(2,1)}, bf16[2048,2816]{1,0:T(8,128)(2,1)}, bf16[3,2048,1024]{2,1,0:T(8,128)(2,1...) custom-call(bf16[128,2304]{1,0:T(8,128)(2,1)} %pad_maximum_fusion.4., ...), custom_call_target="tpu_custom_call" | custom-call | bytes 300000000 | tf_op jit(solution)/shard_map/unit_rows/pallas_call | solution.py:645
  321.2 122.0 %mix_rows.1 = f32[128,4864]{1,0:T(8,128)} custom-call(bf16[3,2048,1024]{2,1,0:T(8,128)(2,1)} %get-tuple-element.42.refs_0_, bf16[3,1024,2048]{2,1,0:T(8,128)(2,1)} %bitcast.162, bf16[2048,1536]{1,0:T(8,128)(2,1)} %bitcast.166, bf16[256,39424]{1,0:T(8,128)(2,1)} %bitcast.154, bf16[16384,256]{1,0:T(8,128)(2,1)} %bitcast.174), custom_call_target="tpu_custom_call" | custom-call | bytes 3000000 | tf_op jit(solution)/shard_map/mix_rows/pallas_call | solution.py:840
  443.1 2.0 convert.69
  445.6 1.8 convolution_add_fusion.3
  447.4 2.5 multiply_reduce_fusion.1
  450.4 1.2 pad_maximum_fusion.2
  451.6 4.4 all-to-all-start
  456.0 1.9 convolution_convert_fusion.2
  457.9 4.8 fusion.130
  462.7 1.7 fusion.18
  464.4 1.5 multiply_reduce_fusion
  465.9 1.6 multiply_convert_fusion
  467.6 1.3 convolution_multiply_fusion
  469.2 2.3 fusion.12.refs_0_
  471.5 2.7 fusion.13.refs_1_
  474.2 24.1 %ring_scatter.1 = f32[128,512]{1,0:T(8,128)} custom-call(bf16[2048,256]{1,0:T(8,128)(2,1)} %fusion.12.refs_0_, bf16[2048,256]{1,0:T(8,128)(2,1)} %fusion.13.refs_1_), custom_call_target="tpu_custom_call" | custom-call | bytes 3000000 | tf_op jit(solution)/shard_map/ring_scatter/pallas_call | solution.py:343
  499.1 2.3 constant_dynamic-slice_fusion.1
  501.5 1.0 slice_bitcast_fusion.1
  502.5 2.5 convolution_convert_fusion.1
  505.0 2.2 fusion.134
  507.3 1.0 fusion.107
  508.9 1.1 convolution_convert_fusion.5
  510.6 1.1 convolution_convert_fusion.4
  511.8 7.7 %fusion.75 = f32[128,2048]{1,0:T(8,128)S(1)} fusion(bf16[2048,2560]{1,0:T(8,128)(2,1)} %ring_gather.2, bf16[128,256]{1,0:T(8,128)(2,1)S(1)} %get-tuple-element.108, bf16[128,256]{1,0:T(8,128)(2,1)S(1)} %maximum_bitcast_fusion.2, bf16[128,2048]{1,0:T(8,128)(2,1)} %bitcast.181), kind=kOutput, calls=%fused_computation.110 | convolution fusion | flops 1344143360 | bytes 12189696 | tf_op jit(solution)/shard_map/dot_general | solution.py:32
  519.6 2.2 fusion.51
  522.6 1.6 slice_dynamic-update-slice_fusion
  524.1 1.5 slice_dynamic-update-slice_fusion.1
  526.2 5.8 fusion.1
  532.0 1.3 pad_maximum_fusion.refs_2_
  533.3 1.6 convolution_convert_fusion
  535.0 1.1 pad_maximum_fusion.1.refs_1_
  536.0 121.4 %share_rows.1 = (bf16[2464,256]{1,0:T(8,128)(2,1)}, f32[128,2560]{1,0:T(8,128)}, f32[128,1536]{1,0:T(8,128)}, f32[256,2560]{1,0:T(8,128)}, f32[256,2048]{1,0:T(8,128)}, /*index=5*/bf16[2048,128]{1,0:T(8,128)(2,1)}) custom-call(bf16[128,3712]{1,0:T(8,128)(2,1)} %pad_dynamic-update-slice_fusion.refs_0_, bf16[2176,256]{1,0:T(8,128)(2,1)} %pad_maximum_fusion.1.refs_1_, ...), custom_call_target="tpu_custom_call" | custom-call | bytes 3000000 | tf_op jit(solution)/shard_map/share_rows/pallas_call | solution.py:1069
  657.4 2.2 slice_convert_fusion
  659.6 1.8 reshape.319
  661.4 2.2 convert.80
  663.7 2.4 fusion.37
  666.2 2.5 fusion.50
  668.7 21.4 %sum_loops.1 = f32[3,1024,2048]{2,1,0:T(8,128)} custom-call(bf16[2,3,1024,2048]{3,2,1,0:T(8,128)(2,1)} %bitcast.175), custom_call_target="tpu_custom_call" | custom-call | bytes 3000000 | tf_op jit(solution)/shard_map/sum_loops/pallas_call | solution.py:111
  690.1 2.6 copy.65
  692.9 1.9 convert_bitcast_fusion.3
  694.8 2.7 convert_bitcast_fusion
  697.6 3.2 copy.66
  700.7 2.4 fusion.20
  703.1 2.0 convert_add_fusion
  705.6 1.2 slice.238
  706.8 1.1 slice.239
  708.8 1.0 copy.107
  (157 shorter events, 13.0 us)
Async XLA Ops:
  7.2 61.3 %copy-start.42 = (s32[1,4]{1,0:T(1,128)S(1)}, s32[1,4]{1,0:T(1,128)}, u32[]{:S(2)}) copy-start(s32[1,4]{1,0:T(1,128)} %param.11) | copy-start | bytes 52
  7.2 61.8 %copy-start.3 = (bf16[1,128,2048]{2,1,0:T(8,128)(2,1)S(1)}, bf16[1,128,2048]{2,1,0:T(8,128)(2,1)}, u32[]{:S(2)}) copy-start(bf16[1,128,2048]{2,1,0:T(8,128)(2,1)} %param.10) | copy-start | bytes 1572868
  7.2 62.5 %copy-start.27 = (bf16[2,2048]{1,0:T(2,128)(2,1)S(1)}, bf16[2,2048]{1,0:T(2,128)(2,1)}, u32[]{:S(2)}) copy-start(bf16[2,2048]{1,0:T(2,128)(2,1)} %param.12) | copy-start | bytes 24580
  7.2 143.1 %all-gather.6.cloned.1.call-start = ((), (), s32[]{:S(2)}) async-start(), calls=%async_computation.1 | async-start | bytes 8912896 | tf_op jit(solution)/shard_map/all_gather | solution.py:89
  68.4 597.7 %all-gather.8.cloned.1.call-start = ((), (), s32[]{:S(2)}) async-start(), calls=%async_computation.2 | async-start | bytes 37748736 | tf_op jit(solution)/shard_map/all_gather | solution.py:97
  68.8 44.0 %copy-start.35 = (f32[128]{0:T(128)}, f32[128]{0:T(128)S(1)}, u32[]{:S(2)}) copy-start(f32[128]{0:T(128)S(1)} %multiply_exponential_fusion) | copy-start | bytes 1540
  69.0 43.8 %copy-start.34 = (f32[128]{0:T(128)}, f32[128]{0:T(128)S(1)}, u32[]{:S(2)}) copy-start(f32[128]{0:T(128)S(1)} %fusion.123) | copy-start | bytes 1540
  69.7 8.5 %copy-start.31 = (f32[128]{0:T(128)}, f32[128]{0:T(128)S(1)}, u32[]{:S(2)}) copy-start(f32[128]{0:T(128)S(1)} %get-tuple-element.131) | copy-start | bytes 1540
  110.7 3.8 copy-start.8
  114.0 5.1 copy-start.22
  128.4 3.4 copy-start.6
  128.4 3.4 copy-start.38
  159.2 160.6 %copy-start.36 = (f32[128]{0:T(128)}, f32[128]{0:T(128)S(1)}, u32[]{:S(2)}) copy-start(f32[128]{0:T(128)S(1)} %get-tuple-element.133) | copy-start | bytes 1540
  319.8 1.0 copy-start.32
  443.1 2.5 copy-start.2
  443.1 4.2 copy-start.37
  445.1 4.7 copy-start.11
  445.6 4.2 copy-start.12
  445.6 4.2 copy-start.41
  450.2 12.4 %copy-start = (f32[128,2048]{1,0:T(8,128)}, f32[128,2048]{1,0:T(8,128)S(1)}, u32[]{:S(2)}) copy-start(f32[128,2048]{1,0:T(8,128)S(1)} %get-tuple-element.110) | copy-start | bytes 3145732
  451.6 53.4 %all-to-all-start = ((bf16[128,16,256]{2,0,1:T(8,128)(2,1)}), bf16[128,16,256]{2,0,1:T(8,128)(2,1)}, u32[]{:S(2)}, u32[]{:S(2)}) async-start(bf16[128,16,256]{2,0,1:T(8,128)(2,1)} %pad_maximum_fusion.2), calls=%async_computation | async-start | bytes 2097152 | tf_op jit(solution)/shard_map/all_to_all | solution.py:124
  455.9 247.2 %all-gather.10.cloned.1.call-start = ((), (), s32[]{:S(2)}) async-start(), calls=%async_computation.3 | async-start | bytes 3637248 | tf_op jit(solution)/shard_map/all_gather | solution.py:97
  456.0 8.4 %slice-start.3 = ((s8[8388608]{0:T(1024)(128)(4,1)}), s8[4194304]{0:T(1024)(128)(4,1)S(1)}, s32[]{:S(2)}) async-start(s8[8388608]{0:T(1024)(128)(4,1)} %bitcast.177), calls=%async_computation.7 | async-start | bytes 8388608
  457.8 6.6 slice-start.4
  457.9 6.6 copy-start.9
  457.9 6.6 copy-start.39
  467.5 1.3 copy-start.26
  467.5 1.6 copy-start.28
  467.5 1.6 copy-start.23
  469.1 33.4 %copy-start.10 = (bf16[8,16,8,256]{3,2,0,1:T(8,128)(2,1)}, bf16[8,16,8,256]{3,2,0,1:T(8,128)(2,1)S(1)}, u32[]{:S(2)}) copy-start(bf16[8,16,8,256]{3,2,0,1:T(8,128)(2,1)S(1)} %copy.74) | copy-start | bytes 1572868
  474.2 27.3 %copy-start.21 = (bf16[2,1024,256]{2,1,0:T(8,128)(2,1)S(1)}, bf16[2,1024,256]{2,1,0:T(8,128)(2,1)}, u32[]{:S(2)}) copy-start(bf16[2,1024,256]{2,1,0:T(8,128)(2,1)} %get-tuple-element.47) | copy-start | bytes 3145732
  499.1 8.1 %copy-start.24 = (f32[128,512]{1,0:T(8,128)S(1)}, f32[128,512]{1,0:T(8,128)}, u32[]{:S(2)}) copy-start(f32[128,512]{1,0:T(8,128)} %ring_scatter.1) | copy-start | bytes 786436
  502.5 17.0 %slice-start = ((s8[6291456]{0:T(1024)(128)(4,1)}), s8[2097152]{0:T(1024)(128)(4,1)S(1)}, s32[]{:S(2)}) async-start(s8[6291456]{0:T(1024)(128)(4,1)} %bitcast.170), calls=%async_computation.4 | async-start | bytes 4194304
  511.7 7.8 %slice-start.1 = ((s8[6291456]{0:T(1024)(128)(4,1)}), s8[4194304]{0:T(1024)(128)(4,1)S(1)}, s32[]{:S(2)}) async-start(s8[6291456]{0:T(1024)(128)(4,1)} %bitcast.170), calls=%async_computation.5 | async-start | bytes 8388608
  511.7 7.8 %copy-start.4 = (bf16[1,128,2048]{2,1,0:T(8,128)(2,1)S(1)}, bf16[1,128,2048]{2,1,0:T(8,128)(2,1)}, u32[]{:S(2)}) copy-start(bf16[1,128,2048]{2,1,0:T(8,128)(2,1)} %param.10) | copy-start | bytes 1572868
  511.8 7.8 %copy-start.33 = (f32[128]{0:T(128)S(1)}, f32[128]{0:T(128)}, u32[]{:S(2)}) copy-start(f32[128]{0:T(128)} %copy-done.31) | copy-start | bytes 1540
  511.8 7.8 %copy-start.43 = (bf16[128,256]{1,0:T(8,128)(2,1)S(1)}, bf16[128,256]{1,0:T(8,128)(2,1)}, u32[]{:S(2)}) copy-start(bf16[128,256]{1,0:T(8,128)(2,1)} %convolution_convert_fusion.1) | copy-start | bytes 196612
  526.2 5.8 copy-start.17
  526.2 5.8 copy-start.18
  526.2 5.8 copy-start.19
  526.2 7.1 copy-start.16
  532.0 2.9 copy-start.14
  532.0 3.0 copy-start.15
  657.4 8.7 %copy-start.1 = (f32[128,2048]{1,0:T(8,128)S(1)}, f32[128,2048]{1,0:T(8,128)}, u32[]{:S(2)}) copy-start(f32[128,2048]{1,0:T(8,128)} %copy-done) | copy-start | bytes 3145732
  657.4 8.7 %copy-start.5 = (bf16[1,128,2048]{2,1,0:T(8,128)(2,1)S(1)}, bf16[1,128,2048]{2,1,0:T(8,128)(2,1)}, u32[]{:S(2)}) copy-start(bf16[1,128,2048]{2,1,0:T(8,128)(2,1)} %param.10) | copy-start | bytes 1572868
  657.4 8.7 %copy-start.40 = (f32[128]{0:T(128)S(1)}, f32[128]{0:T(128)}, u32[]{:S(2)}) copy-start(f32[128]{0:T(128)} %get-tuple-element.130) | copy-start | bytes 1540
  668.7 24.0 %copy-start.13 = (f32[256,2048]{1,0:T(8,128)S(1)}, f32[256,2048]{1,0:T(8,128)}, u32[]{:S(2)}) copy-start(f32[256,2048]{1,0:T(8,128)} %get-tuple-element.65) | copy-start | bytes 6291460
  690.1 4.7 copy-start.29
  690.1 4.7 copy-start.30
  692.7 2.1 copy-start.7
  694.8 5.9 slice-start.2
  703.1 4.8 copy-start.25
  705.1 3.7 copy-start.20
Sparse Core Ops, SparseCore 0:
  68.6 81.6 all-gather.5
  320.0 292.6 all-gather.7
  666.3 35.3 all-gather.9

commit v13 on v12

--- a/solution.py
+++ b/solution.py
@@ -183,8 +183,6 @@
     across(0, 0, core).start()
     own = pltpu.make_async_copy(x_ref, at(0, 0, core, (0, rows)), own_sem)
     own.start()
-    if also is not None:
-        also()
     if work is not None:
         own.wait()
         across(0, 0, 1 - core).wait_recv()
@@ -195,6 +193,8 @@
             if hops < reach:
                 hop(way, hops + 1).start()
             across(way, hops, core).start()
+        if also is not None and hops == reach - 1:
+            also()
         if work is not None:
             for way in (0, 1):
                 across(way, hops, 1 - core).wait_recv()

time: 728 us -> 719 us (0.988)
  Pallas kernels: 539 us -> 521 us
  waiting for transfers between devices: 16.1 us -> 25.6 us
    pallas_call x1, Pallas kernels: 121 us -> 104 us  [share_rows(): pl.pallas_call(functools.partial(share_kernel, size, chunk, own_count), o...]
    all_gather x2, waiting for transfers between devices: 0.01 us -> 9.55 us  [loop_shares(): return lax.all_gather(partial.astype(bf16), 'loop', axis=0)]
  transfers between devices with their start and end apart: 4 -> 4, of which waited for: 1 -> 2; matrix products, arithmetic and copies ran while one was open for 17% -> 17% of each run, Pallas kernels for 44% -> 42%
where the time goes in v13:
time: 719 us; the launch traced here: 708 us
  Pallas kernels  521 us (72%)
  matrix products  72.9 us (10%)
  other arithmetic  41.9 us (6%)
  local copies, waits for them, and re-layouts  27.3 us (4%)
  waiting for transfers between devices  25.6 us (4%)
  between operations  14.9 us (2%)
    pallas_call x1, Pallas kernels, unit_rows(): pl.pallas_call(functools.partial(unit_kernel, chips), out_shape=(jax.Shap...  160 us
    pallas_call x1, Pallas kernels, mix_rows(): pl.pallas_call(functools.partial(mix_kernel, chips), out_shape=jax.ShapeD...  122 us
    pallas_call x1, Pallas kernels, share_rows(): pl.pallas_call(functools.partial(share_kernel, size, chunk, own_count), o...  104 us
    pallas_call x2, Pallas kernels, ring_gather(): pl.pallas_call(functools.partial(gather_kernel, chips, greet=None, also=N...  90.5 us
    dot_general x10, matrix products, times_transposed(): lax.dot_general(former, latter, (((1,), (1,)), ((), ())), preferred_eleme...  29.1 us
    pallas_call x1, Pallas kernels, ring_scatter(): pl.pallas_call(functools.partial(scatter_kernel, chips, count), out_shape...  24.1 us
    dot_general x9, matrix products, matrix_product(): return jnp.dot(former, latter, preferred_element_type=f32)  22.6 us
    pallas_call x1, Pallas kernels, sum_loops(): pl.pallas_call(sum_kernel, grid=(planes, rows // tile), out_shape=jax.Sha...  21.2 us
  transfers between devices with their start and end apart: 4, of which 2 were waited for; matrix products, arithmetic and copies ran while one was open for 17% of the time, Pallas kernels for 42%

profile of v13, /device:TPU:0, one launch (start us, length us, event | category | flops | bytes accessed | tf_op | source)
XLA Modules:
  0.0 708.0 jit_solution(563843979263951003)
XLA Ops:
  7.3 61.2 %ring_gather.2 = bf16[2048,2560]{1,0:T(8,128)(2,1)} custom-call(bf16[128,2560]{1,0:T(8,128)(2,1)} %x_ref.1), custom_call_target="tpu_custom_call" | custom-call | bytes 3000000 | tf_op jit(solution)/shard_map/ring_gather/pallas_call | solution.py:228
  69.7 2.5 fusion.38
  72.2 5.9 fusion.91
  78.2 1.1 fusion.41
  79.6 1.1 fusion.42
  81.4 29.4 %ring_gather.3 = bf16[2048,512]{1,0:T(8,128)(2,1)} custom-call(bf16[128,512]{1,0:T(8,128)(2,1)} %pad_maximum_fusion.8.x_ref), custom_call_target="tpu_custom_call" | custom-call | bytes 3000000 | tf_op jit(solution)/shard_map/ring_gather/pallas_call | solution.py:228
  110.7 1.7 convolution_add_fusion.5
  112.8 0.9 broadcast_multiply_fusion
  114.5 4.7 fusion.59
  119.2 9.2 %fusion.137 = (f32[128,8]{0,1:T(8,128)S(1)}, f32[128,8,2048]{2,0,1:T(8,128)S(1)}) fusion(f32[128,8,2048]{2,0,1:T(8,128)} %fusion.59, pred[128,2048]{1,0:T(8,128)(4,1)S(1)} %fusion.64), kind=kOutput, calls=%fused_computation.220 | output fusion | flops 12584959 | bytes 17043456 | tf_op jit(solution)/shard_map/sub | solution.py:1171
  128.4 1.3 fusion.34
  129.7 2.1 copy-done.6
  131.8 1.5 convolution_convert_fusion.3
  134.3 16.0 %all-gather.6.cloned.1.call-done = bf16[2048,2048]{1,0:T(8,128)(2,1)} async-done(((bf16[128,2048]{1,0:T(8,128)(2,1)}), bf16[2048,2048]{1,0:T(8,128)(2,1)}) %all-gather.6.cloned.1.call-update) | async-done | bytes 8388624 | tf_op jit(solution)/shard_map/all_gather | solution.py:89
  150.3 6.7 convolution_add_fusion.6
  157.0 1.6 multiply_reduce_fusion.3
  160.2 159.6 %unit_rows.1 = (bf16[2048,2048]{1,0:T(8,128)(2,1)}, bf16[2048,2048]{1,0:T(8,128)(2,1)}, bf16[2048,2816]{1,0:T(8,128)(2,1)}, bf16[3,2048,1024]{2,1,0:T(8,128)(2,1...) custom-call(bf16[128,2304]{1,0:T(8,128)(2,1)} %pad_maximum_fusion.4., ...), custom_call_target="tpu_custom_call" | custom-call | bytes 300000000 | tf_op jit(solution)/shard_map/unit_rows/pallas_call | solution.py:645
  321.2 122.0 %mix_rows.1 = f32[128,4864]{1,0:T(8,128)} custom-call(bf16[3,2048,1024]{2,1,0:T(8,128)(2,1)} %get-tuple-element.42.refs_0_, bf16[3,1024,2048]{2,1,0:T(8,128)(2,1)} %bitcast.162, bf16[2048,1536]{1,0:T(8,128)(2,1)} %bitcast.166, bf16[256,39424]{1,0:T(8,128)(2,1)} %bitcast.154, bf16[16384,256]{1,0:T(8,128)(2,1)} %bitcast.174), custom_call_target="tpu_custom_call" | custom-call | bytes 3000000 | tf_op jit(solution)/shard_map/mix_rows/pallas_call | solution.py:840
  443.1 2.0 convert.69
  445.6 1.8 convolution_add_fusion.3
  447.4 2.5 multiply_reduce_fusion.1
  450.4 1.2 pad_maximum_fusion.2
  451.6 4.4 all-to-all-start
  456.0 1.9 convolution_convert_fusion.2
  457.9 4.8 fusion.130
  462.7 1.7 fusion.18
  464.4 1.5 multiply_reduce_fusion
  465.9 1.6 multiply_convert_fusion
  467.6 1.3 convolution_multiply_fusion
  469.2 2.3 fusion.12.refs_0_
  471.5 2.7 fusion.13.refs_1_
  474.2 24.1 %ring_scatter.1 = f32[128,512]{1,0:T(8,128)} custom-call(bf16[2048,256]{1,0:T(8,128)(2,1)} %fusion.12.refs_0_, bf16[2048,256]{1,0:T(8,128)(2,1)} %fusion.13.refs_1_), custom_call_target="tpu_custom_call" | custom-call | bytes 3000000 | tf_op jit(solution)/shard_map/ring_scatter/pallas_call | solution.py:343
  499.1 2.3 constant_dynamic-slice_fusion.1
  501.5 1.0 slice_bitcast_fusion.1
  502.5 2.5 convolution_convert_fusion.1
  505.0 2.2 fusion.134
  507.3 1.0 fusion.107
  508.9 1.1 convolution_convert_fusion.5
  510.6 1.1 convolution_convert_fusion.4
  511.8 7.7 %fusion.75 = f32[128,2048]{1,0:T(8,128)S(1)} fusion(bf16[2048,2560]{1,0:T(8,128)(2,1)} %ring_gather.2, bf16[128,256]{1,0:T(8,128)(2,1)S(1)} %get-tuple-element.108, bf16[128,256]{1,0:T(8,128)(2,1)S(1)} %maximum_bitcast_fusion.2, bf16[128,2048]{1,0:T(8,128)(2,1)} %bitcast.181), kind=kOutput, calls=%fused_computation.110 | convolution fusion | flops 1344143360 | bytes 12189696 | tf_op jit(solution)/shard_map/dot_general | solution.py:32
  519.6 2.2 fusion.51
  522.6 1.6 slice_dynamic-update-slice_fusion
  524.1 1.5 slice_dynamic-update-slice_fusion.1
  526.2 5.8 fusion.1
  532.0 1.3 pad_maximum_fusion.refs_2_
  533.3 1.6 convolution_convert_fusion
  535.0 1.1 pad_maximum_fusion.1.refs_1_
  536.0 103.6 %share_rows.1 = (bf16[2464,256]{1,0:T(8,128)(2,1)}, f32[128,2560]{1,0:T(8,128)}, f32[128,1536]{1,0:T(8,128)}, f32[256,2560]{1,0:T(8,128)}, f32[256,2048]{1,0:T(8,128)}, /*index=5*/bf16[2048,128]{1,0:T(8,128)(2,1)}) custom-call(bf16[128,3712]{1,0:T(8,128)(2,1)} %pad_dynamic-update-slice_fusion.refs_0_, bf16[2176,256]{1,0:T(8,128)(2,1)} %pad_maximum_fusion.1.refs_1_, ...), custom_call_target="tpu_custom_call" | custom-call | bytes 3000000 | tf_op jit(solution)/shard_map/share_rows/pallas_call | solution.py:1069
  639.6 2.2 slice_convert_fusion
  641.8 1.8 reshape.319
  643.6 2.2 convert.80
  645.9 2.4 fusion.37
  648.4 2.5 fusion.50
  650.9 21.2 %sum_loops.1 = f32[3,1024,2048]{2,1,0:T(8,128)} custom-call(bf16[2,3,1024,2048]{3,2,1,0:T(8,128)(2,1)} %bitcast.175), custom_call_target="tpu_custom_call" | custom-call | bytes 3000000 | tf_op jit(solution)/shard_map/sum_loops/pallas_call | solution.py:111
  672.1 2.6 copy.65
  674.9 1.9 convert_bitcast_fusion.3
  676.9 2.7 convert_bitcast_fusion
  679.6 3.2 copy.66
  682.8 2.4 fusion.20
  685.1 9.6 %all-gather.10.cloned.1.call-done = bf16[256,4736]{1,0:T(8,128)(2,1)} async-done(((bf16[128,4736]{1,0:T(8,128)(2,1)}), bf16[256,4736]{1,0:T(8,128)(2,1)}) %all-gather.10.cloned.1.call-update) | async-done | bytes 2424848 | tf_op jit(solution)/shard_map/all_gather | solution.py:97
  694.7 1.9 convert_add_fusion
  697.2 1.2 slice.238
  698.3 1.1 slice.239
  700.3 1.0 copy.107
  (157 shorter events, 13.9 us)
Async XLA Ops:
  7.2 61.3 %copy-start.42 = (s32[1,4]{1,0:T(1,128)S(1)}, s32[1,4]{1,0:T(1,128)}, u32[]{:S(2)}) copy-start(s32[1,4]{1,0:T(1,128)} %param.11) | copy-start | bytes 52
  7.2 61.8 %copy-start.3 = (bf16[1,128,2048]{2,1,0:T(8,128)(2,1)S(1)}, bf16[1,128,2048]{2,1,0:T(8,128)(2,1)}, u32[]{:S(2)}) copy-start(bf16[1,128,2048]{2,1,0:T(8,128)(2,1)} %param.10) | copy-start | bytes 1572868
  7.2 62.5 %copy-start.27 = (bf16[2,2048]{1,0:T(2,128)(2,1)S(1)}, bf16[2,2048]{1,0:T(2,128)(2,1)}, u32[]{:S(2)}) copy-start(bf16[2,2048]{1,0:T(2,128)(2,1)} %param.12) | copy-start | bytes 24580
  7.2 143.1 %all-gather.6.cloned.1.call-start = ((), (), s32[]{:S(2)}) async-start(), calls=%async_computation.1 | async-start | bytes 8912896 | tf_op jit(solution)/shard_map/all_gather | solution.py:89
  68.4 579.9 %all-gather.8.cloned.1.call-start = ((), (), s32[]{:S(2)}) async-start(), calls=%async_computation.2 | async-start | bytes 37748736 | tf_op jit(solution)/shard_map/all_gather | solution.py:97
  68.8 44.0 %copy-start.35 = (f32[128]{0:T(128)}, f32[128]{0:T(128)S(1)}, u32[]{:S(2)}) copy-start(f32[128]{0:T(128)S(1)} %multiply_exponential_fusion) | copy-start | bytes 1540
  69.0 43.8 %copy-start.34 = (f32[128]{0:T(128)}, f32[128]{0:T(128)S(1)}, u32[]{:S(2)}) copy-start(f32[128]{0:T(128)S(1)} %fusion.123) | copy-start | bytes 1540
  69.7 8.5 %copy-start.31 = (f32[128]{0:T(128)}, f32[128]{0:T(128)S(1)}, u32[]{:S(2)}) copy-start(f32[128]{0:T(128)S(1)} %get-tuple-element.131) | copy-start | bytes 1540
  110.7 3.8 copy-start.8
  114.0 5.1 copy-start.22
  128.4 3.4 copy-start.6
  128.4 3.4 copy-start.38
  159.2 160.6 %copy-start.36 = (f32[128]{0:T(128)}, f32[128]{0:T(128)S(1)}, u32[]{:S(2)}) copy-start(f32[128]{0:T(128)S(1)} %get-tuple-element.133) | copy-start | bytes 1540
  319.8 1.0 copy-start.32
  443.1 2.5 copy-start.2
  443.1 4.2 copy-start.37
  445.1 4.7 copy-start.11
  445.6 4.2 copy-start.12
  445.6 4.2 copy-start.41
  450.2 12.4 %copy-start = (f32[128,2048]{1,0:T(8,128)}, f32[128,2048]{1,0:T(8,128)S(1)}, u32[]{:S(2)}) copy-start(f32[128,2048]{1,0:T(8,128)S(1)} %get-tuple-element.110) | copy-start | bytes 3145732
  451.6 53.4 %all-to-all-start = ((bf16[128,16,256]{2,0,1:T(8,128)(2,1)}), bf16[128,16,256]{2,0,1:T(8,128)(2,1)}, u32[]{:S(2)}, u32[]{:S(2)}) async-start(bf16[128,16,256]{2,0,1:T(8,128)(2,1)} %pad_maximum_fusion.2), calls=%async_computation | async-start | bytes 2097152 | tf_op jit(solution)/shard_map/all_to_all | solution.py:124
  455.9 238.8 %all-gather.10.cloned.1.call-start = ((), (), s32[]{:S(2)}) async-start(), calls=%async_computation.3 | async-start | bytes 3637248 | tf_op jit(solution)/shard_map/all_gather | solution.py:97
  456.0 8.4 %slice-start.3 = ((s8[8388608]{0:T(1024)(128)(4,1)}), s8[4194304]{0:T(1024)(128)(4,1)S(1)}, s32[]{:S(2)}) async-start(s8[8388608]{0:T(1024)(128)(4,1)} %bitcast.177), calls=%async_computation.7 | async-start | bytes 8388608
  457.8 6.6 slice-start.4
  457.9 6.6 copy-start.9
  457.9 6.6 copy-start.39
  467.5 1.3 copy-start.26
  467.5 1.6 copy-start.28
  467.5 1.6 copy-start.23
  469.1 33.4 %copy-start.10 = (bf16[8,16,8,256]{3,2,0,1:T(8,128)(2,1)}, bf16[8,16,8,256]{3,2,0,1:T(8,128)(2,1)S(1)}, u32[]{:S(2)}) copy-start(bf16[8,16,8,256]{3,2,0,1:T(8,128)(2,1)S(1)} %copy.74) | copy-start | bytes 1572868
  474.2 27.3 %copy-start.21 = (bf16[2,1024,256]{2,1,0:T(8,128)(2,1)S(1)}, bf16[2,1024,256]{2,1,0:T(8,128)(2,1)}, u32[]{:S(2)}) copy-start(bf16[2,1024,256]{2,1,0:T(8,128)(2,1)} %get-tuple-element.47) | copy-start | bytes 3145732
  499.1 8.1 %copy-start.24 = (f32[128,512]{1,0:T(8,128)S(1)}, f32[128,512]{1,0:T(8,128)}, u32[]{:S(2)}) copy-start(f32[128,512]{1,0:T(8,128)} %ring_scatter.1) | copy-start | bytes 786436
  502.5 17.0 %slice-start = ((s8[6291456]{0:T(1024)(128)(4,1)}), s8[2097152]{0:T(1024)(128)(4,1)S(1)}, s32[]{:S(2)}) async-start(s8[6291456]{0:T(1024)(128)(4,1)} %bitcast.170), calls=%async_computation.4 | async-start | bytes 4194304
  511.7 7.8 %slice-start.1 = ((s8[6291456]{0:T(1024)(128)(4,1)}), s8[4194304]{0:T(1024)(128)(4,1)S(1)}, s32[]{:S(2)}) async-start(s8[6291456]{0:T(1024)(128)(4,1)} %bitcast.170), calls=%async_computation.5 | async-start | bytes 8388608
  511.7 7.8 %copy-start.4 = (bf16[1,128,2048]{2,1,0:T(8,128)(2,1)S(1)}, bf16[1,128,2048]{2,1,0:T(8,128)(2,1)}, u32[]{:S(2)}) copy-start(bf16[1,128,2048]{2,1,0:T(8,128)(2,1)} %param.10) | copy-start | bytes 1572868
  511.8 7.8 %copy-start.33 = (f32[128]{0:T(128)S(1)}, f32[128]{0:T(128)}, u32[]{:S(2)}) copy-start(f32[128]{0:T(128)} %copy-done.31) | copy-start | bytes 1540
  511.8 7.8 %copy-start.43 = (bf16[128,256]{1,0:T(8,128)(2,1)S(1)}, bf16[128,256]{1,0:T(8,128)(2,1)}, u32[]{:S(2)}) copy-start(bf16[128,256]{1,0:T(8,128)(2,1)} %convolution_convert_fusion.1) | copy-start | bytes 196612
  526.2 5.8 copy-start.17
  526.2 5.8 copy-start.18
  526.2 5.8 copy-start.19
  526.2 7.1 %copy-start.16 = (bf16[2048,128]{1,0:T(8,128)(2,1)S(1)}, bf16[2048,128]{1,0:T(8,128)(2,1)}, u32[]{:S(2)}) copy-start(bf16[2048,128]{1,0:T(8,128)(2,1)} %get-tuple-element.43) | copy-start | bytes 1572868
  532.0 2.9 copy-start.14
  532.0 3.0 copy-start.15
  639.6 8.7 %copy-start.1 = (f32[128,2048]{1,0:T(8,128)S(1)}, f32[128,2048]{1,0:T(8,128)}, u32[]{:S(2)}) copy-start(f32[128,2048]{1,0:T(8,128)} %copy-done) | copy-start | bytes 3145732
  639.6 8.7 %copy-start.5 = (bf16[1,128,2048]{2,1,0:T(8,128)(2,1)S(1)}, bf16[1,128,2048]{2,1,0:T(8,128)(2,1)}, u32[]{:S(2)}) copy-start(bf16[1,128,2048]{2,1,0:T(8,128)(2,1)} %param.10) | copy-start | bytes 1572868
  639.6 8.7 %copy-start.40 = (f32[128]{0:T(128)S(1)}, f32[128]{0:T(128)}, u32[]{:S(2)}) copy-start(f32[128]{0:T(128)} %get-tuple-element.130) | copy-start | bytes 1540
  650.9 23.8 %copy-start.13 = (f32[256,2048]{1,0:T(8,128)S(1)}, f32[256,2048]{1,0:T(8,128)}, u32[]{:S(2)}) copy-start(f32[256,2048]{1,0:T(8,128)} %get-tuple-element.65) | copy-start | bytes 6291460
  672.1 4.7 copy-start.29
  672.1 4.7 copy-start.30
  674.7 2.1 copy-start.7
  676.9 5.9 slice-start.2
  685.1 14.3 %copy-start.25 = (f32[128,1536]{1,0:T(8,128)S(1)}, f32[128,1536]{1,0:T(8,128)}, u32[]{:S(2)}) copy-start(f32[128,1536]{1,0:T(8,128)} %get-tuple-element.62) | copy-start | bytes 2359300
  696.6 3.7 copy-start.20
Sparse Core Ops, SparseCore 0:
  68.6 81.6 all-gather.5
  320.0 292.6 all-gather.7
  648.5 46.1 all-gather.9
